TPU v7x, 512 devices: a whole 4x8x8 slice. The times are simulated.
512 devices in a mesh: row: 16 (over x, z_hi), col: 32 (over z_lo, y, core).
Axes of the slice: x: 4, y: 8, z: 8 (z_hi: 4, z_lo: 2; z = z_hi * 2 + z_lo), core: 2. Of those that a mesh axis runs over, the one named last changes fastest.
Arguments:
- bin_features: bfloat16 [4096, 512], P('row'), may hold values from -6 to 6
- w_left: bfloat16 [512, 32], replicated, may hold values from -0.25 to 0.25
- w_right: bfloat16 [512, 32], replicated, may hold values from -0.25 to 0.25
- depth_kernel: float32 [9, 32], replicated, may hold values from -2 to 2
- w_point: bfloat16 [32, 32], replicated, may hold values from -1 to 1
- w_head: bfloat16 [32, 24], replicated, may hold values from -1 to 1
- cotangent: bfloat16 [24, 4096, 4096], P(None, 'row', 'col'), may hold values from -6 to 6
Outputs:
- grad_features: bfloat16 [4096, 512], P('row')
- grad_w_left: float32 [512, 32], replicated
- grad_w_right: float32 [512, 32], replicated
- grad_kernel: float32 [9, 32], replicated
- grad_point: float32 [32, 32], replicated
- grad_head: float32 [32, 24], replicated
All inputs are finite; a program needn't handle non-finite values.
Results may differ from a plain program's by a relative error of at most 0.019.
Values may be sent and summed in bfloat16 or wider, within the bound.
No kernel may reach another device: no remote copies, remote signals or barrier semaphores. Data moves between devices by JAX's collectives and lax.ppermute only.
A program may use at most 64 MiB of HBM per device.

v0:
```python
import math

import jax
import jax.numpy as jnp
from jax import lax
from jax.sharding import PartitionSpec as P

DILATION_STEP = 4


def from_root(block, axis, source):
    block = jnp.where(lax.axis_index(axis) == source, block, jnp.zeros_like(block))
    return lax.psum(block, axis)


def extended(x, sides, width):
    for axis, dim in sides:
        count, length = (lax.axis_size(axis), x.shape[dim])
        up = [(i, (i + 1) % count) for i in range(count - 1)]
        down = [(j, i) for i, j in up]
        last = lax.slice_in_dim(x, length - width, length, axis=dim)
        first = lax.slice_in_dim(x, 0, width, axis=dim)
        before = lax.ppermute(last, axis, up)
        after = lax.ppermute(first, axis, down)
        x = jnp.concatenate([before, x, after], axis=dim)
    return x


def silu_slope(values):
    logistic = jax.nn.sigmoid(values)
    return logistic * (1.0 + values * (1.0 - logistic))


def depthwise(kernel_taps, padded, output_rows, output_columns):
    result = jnp.zeros((padded.shape[0], output_rows, output_columns), jnp.float32)
    for kernel_tap_row in range(3):
        for kernel_tap_column in range(3):
            result = result + kernel_taps[3 * kernel_tap_row + kernel_tap_column][
                :, None, None
            ] * padded[
                :,
                DILATION_STEP * kernel_tap_row : DILATION_STEP * kernel_tap_row + output_rows,
                DILATION_STEP * kernel_tap_column : DILATION_STEP * kernel_tap_column
                + output_columns,
            ].astype(
                jnp.float32
            )
    return result


def body(bin_features, w_left, w_right, depth_kernel, w_point, w_head, cotangent):
    rows_per_tile = bin_features.shape[0]
    columns_per_tile = cotangent.shape[2]
    chans = w_left.shape[1]
    row_count = lax.axis_size("row")
    col_count = lax.axis_size("col")
    panel_ratio = col_count // row_count
    contact_map_bins = rows_per_tile * row_count
    grad_scale = 1.0 / math.sqrt(contact_map_bins)
    row_index = lax.axis_index("row")
    col_index = lax.axis_index("col")
    left_panel = jnp.dot(bin_features, w_left, preferred_element_type=jnp.float32).astype(
        jnp.bfloat16
    )
    offset = col_index % panel_ratio * columns_per_tile
    own_rows = lax.dynamic_slice_in_dim(bin_features, offset, columns_per_tile, 0)
    right_own = jnp.dot(own_rows, w_right, preferred_element_type=jnp.float32).astype(jnp.bfloat16)
    right_panel = from_root(right_own, "row", col_index // panel_ratio)
    pair_matrix = (
        left_panel.astype(jnp.float32).T[:, :, None] + right_panel.astype(jnp.float32).T[:, None, :]
    ).astype(jnp.bfloat16)
    extended_pair = extended(pair_matrix, (("row", 1), ("col", 2)), DILATION_STEP)
    convolved_map = depthwise(depth_kernel, extended_pair, rows_per_tile, columns_per_tile)
    trunk_gradient = (
        grad_scale
        * jnp.einsum("ch,hij->cij", w_head, cotangent, preferred_element_type=jnp.float32)
    ).astype(jnp.bfloat16)
    grad_hidden = jnp.einsum(
        "co,oij->cij", w_point, trunk_gradient, preferred_element_type=jnp.float32
    )
    convolved_gradient = (grad_hidden * silu_slope(convolved_map)).astype(jnp.bfloat16)
    extended_gradient = extended(convolved_gradient, (("row", 1), ("col", 2)), DILATION_STEP)
    hidden_state = jax.nn.silu(convolved_map).astype(jnp.bfloat16)
    mixed_out = jnp.einsum("co,cij->oij", w_point, hidden_state, preferred_element_type=jnp.float32)
    centre_offset = extended_pair[
        :,
        DILATION_STEP : DILATION_STEP + rows_per_tile,
        DILATION_STEP : DILATION_STEP + columns_per_tile,
    ]
    trunk_matrix = (centre_offset.astype(jnp.float32) + mixed_out).astype(jnp.bfloat16)
    conv_f32 = convolved_gradient.astype(jnp.float32)
    backward_pass = jnp.zeros((chans, rows_per_tile, columns_per_tile), jnp.float32)
    kern_terms = []
    for kernel_tap_row in range(3):
        for kernel_tap_column in range(3):
            backward_pass = backward_pass + depth_kernel[3 * kernel_tap_row + kernel_tap_column][
                :, None, None
            ] * extended_gradient[
                :,
                DILATION_STEP * (2 - kernel_tap_row) : DILATION_STEP * (2 - kernel_tap_row)
                + rows_per_tile,
                DILATION_STEP * (2 - kernel_tap_column) : DILATION_STEP * (2 - kernel_tap_column)
                + columns_per_tile,
            ].astype(
                jnp.float32
            )
            shifted_window = extended_pair[
                :,
                DILATION_STEP * kernel_tap_row : DILATION_STEP * kernel_tap_row + rows_per_tile,
                DILATION_STEP * kernel_tap_column : DILATION_STEP * kernel_tap_column
                + columns_per_tile,
            ].astype(jnp.float32)
            kern_terms.append(jnp.sum(conv_f32 * shifted_window, axis=(1, 2)))
    kernel_part = jnp.stack(kern_terms)
    pair_gradient = trunk_gradient.astype(jnp.float32) + backward_pass
    left_part = jnp.sum(pair_gradient, axis=2).T
    right_part = jnp.sum(pair_gradient, axis=1).T
    point_part = jnp.einsum(
        "fsk,gsk->fg", hidden_state, trunk_gradient, preferred_element_type=jnp.float32
    )
    head_part = jnp.einsum(
        "ydq,gdq->yg", trunk_matrix, cotangent, preferred_element_type=jnp.float32
    )
    grad_left = lax.psum(left_part, "col").astype(jnp.bfloat16)
    column_total = lax.psum(right_part, "row").astype(jnp.bfloat16)
    all_panels = lax.all_gather(column_total, "col", axis=0, tiled=True)
    grad_right = lax.dynamic_slice_in_dim(all_panels, row_index * rows_per_tile, rows_per_tile, 0)
    grad_features = (
        jnp.dot(grad_left, w_left.T, preferred_element_type=jnp.float32)
        + jnp.dot(grad_right, w_right.T, preferred_element_type=jnp.float32)
    ).astype(jnp.bfloat16)
    contract = (((0,), (0,)), ((), ()))
    wleft_part = lax.dot_general(
        bin_features, grad_left, contract, preferred_element_type=jnp.float32
    )
    wright_part = lax.dot_general(
        bin_features, grad_right, contract, preferred_element_type=jnp.float32
    )
    kernel_sum, point_sum, head_sum = lax.psum((kernel_part, point_part, head_part), ("row", "col"))
    wleft_sum, wright_sum = lax.psum((wleft_part, wright_part), "row")
    return (
        grad_features,
        grad_scale * wleft_sum,
        grad_scale * wright_sum,
        grad_scale * kernel_sum,
        grad_scale * point_sum,
        grad_scale * head_sum,
    )


def solution(mesh):
    placed = (P("row", None), P(), P(), P(), P(), P(), P(None, "row", "col"))
    return jax.shard_map(
        body,
        mesh=mesh,
        in_specs=placed,
        out_specs=(P("row", None), P(), P(), P(), P(), P()),
        check_vma=False,
    )
```

profile of v0, /device:TPU:6, one launch (start us, length us, event | category | flops | bytes accessed | tf_op | source)
XLA Modules:
  0.0 670.2 jit_solution(18254187634809960480)
XLA Ops:
  7.3 1.1 fusion.34
  8.4 44.1 %psum.56 = bf16[32,128]{1,0:T(8,128)(2,1)S(1)} all-reduce(bf16[32,128]{1,0:T(8,128)(2,1)S(1)} %fusion.34), channel_id=1, replica_groups=mesh['row'=16,'col'=32] {'row'}, use_global_device_ids=true, to_apply=%region_0.1 | all-reduce | flops 4096 | bytes 16384 | tf_op jit(solution)/shard_map/psum | solution.py:13
  52.5 1.1 fusion.29
  53.8 1.7 add_convert_fusion
  55.5 2.9 collective-permute-start
  58.4 6.0 collective-permute-start.1
  64.4 3.5 multiply_convert_fusion.1
  68.2 2.9 fusion.51
  71.1 3.6 copy.20
  74.7 3.6 copy.22
  78.4 1.3 collective-permute-start.3
  79.7 3.2 collective-permute-start.2
  82.9 0.7 collective-permute-done.2
  83.7 3.0 copy.21
  86.7 3.0 copy.23
  89.7 7.2 %maximum_maximum_fusion = (bf16[32,264,132]{2,0,1:T(8,128)(2,1)S(1)}, bf16[32,264,132]{2,0,1:T(8,128)(2,1)S(1)}) fusion(bf16[32,4,128]{2,0,1:T(8,128)(2,1)S(1)} %collective-permute-done.1, bf16[32,256,128]{2,0,1:T(8,128)(2,1)} %copy-done.1, bf16[32,4,128]{2,0,1:T(8,128)(2,1)S(1)} %collective-permute-done, bf16[32,264,4]{2,0,1:T(8,128)(2,1)} %copy.21, ...), kind=kLoop, calls=%fused_computation.20 | loop fusion | flops 17842176 | bytes 6758400 | tf_op jit(solution)/shard_map/concatenate | solution.py:25
  97.0 10.2 %multiply_convert_fusion = (bf16[32,256,128]{2,0,1:T(8,128)(2,1)}, f32[32,256,128]{2,0,1:T(8,128)}) fusion(bf16[32,264,132]{2,0,1:T(8,128)(2,1)S(1)} %get-tuple-element.34, f32[32]{0:T(128)S(1)} %get-tuple-element.48, bf16[32,4,128]{2,0,1:T(8,128)(2,1)S(1)} %collective-permute-done.1, bf16[32,256,128]{2,0,1:T(8,128)(2,1)S(1)} %copy-done.2, ...), kind=kLoop, calls=%fused_computation.50 | loop fusion | flops 36700160 | bytes 21087360 | tf_op jit(solution)/shard_map/convert_element_type | solution.py:83
  107.1 3.4 fusion.30
  110.6 3.1 convolution_bitcast_fusion.2
  113.7 0.4 copy-done.7
  114.1 13.2 %fusion.23 = (f32[32]{0:T(128)S(1)}, f32[32]{0:T(128)S(1)}, f32[32]{0:T(128)S(1)}, f32[32]{0:T(128)S(1)}, f32[32]{0:T(128)S(1)}, /*index=5*/f32[32]{0:T(128)S(1)...) fusion(bf16[32,264,132]{2,0,1:T(8,128)(2,1)} %copy-done.5, ...), kind=kOutput, calls=%fused_computation.47 | convolution fusion | flops 110100192 | bytes 23186560 | tf_op jit(solution)/shard_map/co,oij->cij/dot_general | solution.py:78
  127.3 101.2 %all-reduce = (f32[9,32]{1,0:T(8,128)S(1)}, f32[32,32]{1,0:T(8,128)S(1)}, f32[32,24]{0,1:T(8,128)S(1)}) all-reduce(f32[9,32]{1,0:T(8,128)S(1)} %stack.39, f32[32,32]{1,0:T(8,128)S(1)} %convolution_bitcast_fusion.2, f32[32,24]{0,1:T(8,128)S(1)} %fusion.30), channel_id=1, replica_groups=mesh['row'=16,'col'=32] {'row','col'}, use_global_device_ids=true, to_apply=%region_16.17 | all-reduce | flops 2080 | bytes 16640 | tf_op jit(solution)/shard_map/psum | solution.py:139
  228.5 0.6 broadcast_multiply_fusion.2
  229.1 0.8 fusion.52
  229.9 3.8 collective-permute-start.4
  233.7 5.3 collective-permute-start.5
  239.0 0.6 broadcast_multiply_fusion.3
  239.6 1.0 collective-permute-done.5
  240.6 1.9 pad_maximum_fusion.3
  242.4 2.9 fusion.50
  245.4 3.6 copy.24
  249.0 3.6 copy.26
  252.6 1.3 collective-permute-start.7
  253.9 1.3 collective-permute-start.6
  255.2 0.6 broadcast_multiply_fusion.4
  255.8 2.0 collective-permute-done.6
  257.8 3.0 copy.25
  260.8 3.0 copy.27
  263.9 7.2 %pad_maximum_fusion.1 = (bf16[32,264,132]{2,0,1:T(8,128)(2,1)S(1)}, bf16[32,264,132]{2,0,1:T(8,128)(2,1)S(1)}) fusion(bf16[32,264,4]{2,0,1:T(8,128)(2,1)} %copy.25, bf16[32,4,128]{2,0,1:T(8,128)(2,1)S(1)} %collective-permute-done.5, bf16[32,256,128]{2,0,1:T(8,128)(2,1)} %get-tuple-element.50, bf16[32,4,128]{2,0,1:T(8,128)(2,1)S(1)} %collective-permute-done.4, ...), kind=kLoop, calls=%fused_computation.22 | loop fusion | flops 17842176 | bytes 6758400 | tf_op jit(solution)/shard_map/concatenate | solution.py:25
  271.2 7.2 %fusion.48 = (f32[32,128]{1,0:T(8,128)S(1)}, f32[32,256]{0,1:T(8,128)S(1)}) fusion(bf16[32,264,132]{2,0,1:T(8,128)(2,1)S(1)} %get-tuple-element.30, f32[32]{0:T(128)S(1)} %get-tuple-element.48, bf16[32,256,128]{2,0,1:T(8,128)(2,1)S(1)} %copy-done.6, bf16[32,4,128]{2,0,1:T(8,128)(2,1)S(1)} %collective-permute-done.4, f32[32]{0:T(128)S(1)} %get-tuple-element.49, ...), kind=kLoop, calls=%fused_computation.100 | loop fusion | flops 33542144 | bytes 16893056 | tf_op jit(solution)/shard_map/reduce_sum | solution.py:117
  278.4 107.7 %psum.57 = bf16[256,32]{1,0:T(8,128)(2,1)S(1)} all-reduce(f32[256,32]{1,0:T(8,128)S(1)} %bitcast.73), channel_id=1, replica_groups=mesh['row'=16,'col'=32] {'col'}, use_global_device_ids=true, to_apply=%region_2.3 | all-reduce | flops 8192 | bytes 49152 | tf_op jit(solution)/shard_map/psum | solution.py:124
  386.1 0.8 convolution_bitcast_fusion.1
  387.1 74.2 %psum.58 = bf16[128,32]{0,1:T(8,128)(2,1)S(1)} all-reduce(f32[128,32]{0,1:T(8,128)S(1)} %bitcast.74), channel_id=1, replica_groups=mesh['row'=16,'col'=32] {'row'}, use_global_device_ids=true, to_apply=%region_4.5 | all-reduce | flops 4096 | bytes 24576 | tf_op jit(solution)/shard_map/psum | solution.py:125
  461.4 31.1 %all_gather.3 = bf16[4096,32]{0,1:T(8,128)(2,1)S(1)} all-gather(bf16[128,32]{0,1:T(8,128)(2,1)S(1)} %psum.58), channel_id=1, replica_groups=mesh['row'=16,'col'=32] {'col'}, dimensions={0}, use_global_device_ids=true | all-gather | bytes 270336 | tf_op jit(solution)/shard_map/all_gather | solution.py:126
  492.4 0.8 convolution_bitcast_fusion
  493.3 1.0 fusion.28
  494.2 167.6 %all-reduce.4.cloned.1.call-done = (f32[512,32]{0,1:T(8,128)}, f32[512,32]{0,1:T(8,128)}) async-done(((f32[512,32]{0,1:T(8,128)}, f32[512,32]{0,1:T(8,128)}), (f32[512,32]{0,1:T(8,128)}, f32[512,32]{0,1:T(8,128)})) %all-reduce.4.cloned.1.call-update) | async-done | bytes 131088 | tf_op jit(solution)/shard_map/psum | solution.py:140
  661.8 1.5 broadcast_multiply_fusion
  (41 shorter events, 0.8 us)
Async XLA Ops:
  7.2 57.2 %copy-start = (bf16[24,256,128]{2,1,0:T(8,128)(2,1)S(1)}, bf16[24,256,128]{2,1,0:T(8,128)(2,1)}, u32[]{:S(2)}) copy-start(bf16[24,256,128]{2,1,0:T(8,128)(2,1)} %param.13) | copy-start | bytes 4718596
  7.2 654.6 %all-reduce.4.cloned.1.call-start = ((), (), s32[]{:S(2)}) async-start(), calls=%async_computation | async-start | bytes 262144 | tf_op jit(solution)/shard_map/psum | solution.py:140
  55.5 12.4 %copy-start.1 = (bf16[32,256,128]{2,0,1:T(8,128)(2,1)}, bf16[32,256,128]{2,0,1:T(8,128)(2,1)S(1)}, u32[]{:S(2)}) copy-start(bf16[32,256,128]{2,0,1:T(8,128)(2,1)S(1)} %add_convert_fusion) | copy-start | bytes 6291460
  55.5 12.4 %collective-permute-start = (bf16[32,4,128]{2,0,1:T(8,128)(2,1)S(1)}, bf16[32,4,128]{2,0,1:T(8,128)(2,1)S(1)}, u32[]{:S(2)}, u32[]{:S(2)}) collective-permute-start(bf16[32,4,128]{2,0,1:T(8,128)(2,1)S(1)} %get-tuple-element.39), channel_id=1, source_target_pairs={{0,32},{32,64},{64,96},{96,128},{128,160},{160,192},{192,224},{224... | collective-permute-start | bytes 98312 | tf_op jit(solution)/shard_map/ppermute | solution.py:23
  58.4 9.5 %collective-permute-start.1 = (bf16[32,4,128]{2,0,1:T(8,128)(2,1)S(1)}, bf16[32,4,128]{2,0,1:T(8,128)(2,1)S(1)}, u32[]{:S(2)}, u32[]{:S(2)}) collective-permute-start(bf16[32,4,128]{2,0,1:T(8,128)(2,1)S(1)} %get-tuple-element.40), channel_id=1, source_target_pairs={{32,0},{64,32},{96,64},{128,96},{160,128},{192,160},{224,192},{256... | collective-permute-start | bytes 98312 | tf_op jit(solution)/shard_map/ppermute | solution.py:24
  71.1 11.8 %copy-start.12 = (f32[9,32]{1,0:T(8,128)S(1)}, f32[9,32]{1,0:T(8,128)}, u32[]{:S(2)}) copy-start(f32[9,32]{1,0:T(8,128)} %param.10) | copy-start | bytes 3460
  78.4 8.3 %collective-permute-start.3 = (bf16[32,264,4]{1,0,2:T(8,128)(2,1)S(1)}, bf16[32,264,4]{1,0,2:T(8,128)(2,1)S(1)}, u32[]{:S(2)}, u32[]{:S(2)}) collective-permute-start(bf16[32,264,4]{1,0,2:T(8,128)(2,1)S(1)} %copy.22), channel_id=1, source_target_pairs={{1,0},{2,1},{3,2},{4,3},{5,4},{6,5},{7,6},{8,7},{9,8},{10,9},{11,1... | collective-permute-start | bytes 202760 | tf_op jit(solution)/shard_map/ppermute | solution.py:24
  79.7 4.0 collective-permute-start.2
  89.7 7.2 %copy-start.2 = (bf16[32,256,128]{2,0,1:T(8,128)(2,1)S(1)}, bf16[32,256,128]{2,0,1:T(8,128)(2,1)}, u32[]{:S(2)}) copy-start(bf16[32,256,128]{2,0,1:T(8,128)(2,1)} %copy-done.1) | copy-start | bytes 6291460
  96.9 10.2 %copy-start.4 = (bf16[32,264,132]{2,0,1:T(8,128)(2,1)}, bf16[32,264,132]{2,0,1:T(8,128)(2,1)S(1)}, u32[]{:S(2)}) copy-start(bf16[32,264,132]{2,0,1:T(8,128)(2,1)S(1)} %get-tuple-element.33) | copy-start | bytes 6690820
  96.9 10.2 %copy-start.5 = (bf16[32,264,132]{2,0,1:T(8,128)(2,1)}, bf16[32,264,132]{2,0,1:T(8,128)(2,1)S(1)}, u32[]{:S(2)}) copy-start(bf16[32,264,132]{2,0,1:T(8,128)(2,1)S(1)} %get-tuple-element.34) | copy-start | bytes 6690820
  97.0 10.2 %copy-start.13 = (bf16[32,32]{1,0:T(8,128)(2,1)S(1)}, bf16[32,32]{1,0:T(8,128)(2,1)}, u32[]{:S(2)}) copy-start(bf16[32,32]{1,0:T(8,128)(2,1)} %param.11) | copy-start | bytes 6148
  110.6 3.1 copy-start.3
  110.6 3.5 copy-start.7
  229.9 9.7 %collective-permute-start.4 = (bf16[32,4,128]{2,0,1:T(8,128)(2,1)S(1)}, bf16[32,4,128]{2,0,1:T(8,128)(2,1)S(1)}, u32[]{:S(2)}, u32[]{:S(2)}) collective-permute-start(bf16[32,4,128]{2,0,1:T(8,128)(2,1)S(1)} %get-tuple-element.37), channel_id=1, source_target_pairs={{0,32},{32,64},{64,96},{96,128},{128,160},{160,192},{192,224},{224... | collective-permute-start | bytes 98312 | tf_op jit(solution)/shard_map/ppermute | solution.py:23
  233.7 6.9 %collective-permute-start.5 = (bf16[32,4,128]{2,0,1:T(8,128)(2,1)S(1)}, bf16[32,4,128]{2,0,1:T(8,128)(2,1)S(1)}, u32[]{:S(2)}, u32[]{:S(2)}) collective-permute-start(bf16[32,4,128]{2,0,1:T(8,128)(2,1)S(1)} %get-tuple-element.38), channel_id=1, source_target_pairs={{32,0},{64,32},{96,64},{128,96},{160,128},{192,160},{224,192},{256... | collective-permute-start | bytes 98312 | tf_op jit(solution)/shard_map/ppermute | solution.py:24
  252.6 8.2 %collective-permute-start.7 = (bf16[32,264,4]{1,0,2:T(8,128)(2,1)S(1)}, bf16[32,264,4]{1,0,2:T(8,128)(2,1)S(1)}, u32[]{:S(2)}, u32[]{:S(2)}) collective-permute-start(bf16[32,264,4]{1,0,2:T(8,128)(2,1)S(1)} %copy.26), channel_id=1, source_target_pairs={{0,1},{1,2},{2,3},{3,4},{4,5},{5,6},{6,7},{7,8},{8,9},{9,10},{10,1... | collective-permute-start | bytes 202760 | tf_op jit(solution)/shard_map/ppermute | solution.py:23
  253.9 3.9 collective-permute-start.6
  263.9 7.3 %copy-start.6 = (bf16[32,256,128]{2,0,1:T(8,128)(2,1)S(1)}, bf16[32,256,128]{2,0,1:T(8,128)(2,1)}, u32[]{:S(2)}) copy-start(bf16[32,256,128]{2,0,1:T(8,128)(2,1)} %get-tuple-element.50) | copy-start | bytes 6291460
  263.9 7.3 %copy-start.8 = (bf16[32,256,128]{2,0,1:T(8,128)(2,1)S(1)}, bf16[32,256,128]{2,0,1:T(8,128)(2,1)}, u32[]{:S(2)}) copy-start(bf16[32,256,128]{2,0,1:T(8,128)(2,1)} %multiply_convert_fusion.1) | copy-start | bytes 6291460
  271.1 115.0 %copy-start.9 = (bf16[256,512]{1,0:T(8,128)(2,1)S(1)}, bf16[256,512]{1,0:T(8,128)(2,1)}, u32[]{:S(2)}) copy-start(bf16[256,512]{1,0:T(8,128)(2,1)} %param.7) | copy-start | bytes 786436
  271.2 115.7 %copy-start.10 = (bf16[512,32]{0,1:T(8,128)(2,1)S(1)}, bf16[512,32]{0,1:T(8,128)(2,1)}, u32[]{:S(2)}) copy-start(bf16[512,32]{0,1:T(8,128)(2,1)} %param.8) | copy-start | bytes 98308
  271.2 222.1 %copy-start.11 = (bf16[512,32]{0,1:T(8,128)(2,1)S(1)}, bf16[512,32]{0,1:T(8,128)(2,1)}, u32[]{:S(2)}) copy-start(bf16[512,32]{0,1:T(8,128)(2,1)} %param.9) | copy-start | bytes 98308
Sparse Core Ops, SparseCore 0:
  493.4 168.3 all-reduce.3
where the time goes:
time: 675 us; the launch traced here: 670 us
  blocking collectives  358 us (53%)
  waiting for transfers between devices  171 us (25%)
  other arithmetic  39 us (6%)
  local copies, waits for them, and re-layouts  34 us (5%)
  matrix products  28.2 us (4%)
  starting transfers between devices  25 us (4%)
  between operations  14.4 us (2%)
    psum x1, waiting for transfers between devices, body(): wleft_sum, wright_sum = lax.psum((wleft_part, wright_part), 'row')  168 us
    psum x1, blocking collectives, body(): grad_left = lax.psum(left_part, 'col').astype(jnp.bfloat16)  108 us
    psum x1, blocking collectives, body(): lax.psum((kernel_part, point_part, head_part), ('row', 'col'))  101 us
    psum x1, blocking collectives, body(): column_total = lax.psum(right_part, 'row').astype(jnp.bfloat16)  74.2 us
    psum x1, blocking collectives, from_root(): return lax.psum(block, axis)  44.1 us
    all_gather x1, blocking collectives, body(): all_panels = lax.all_gather(column_total, 'col', axis=0, tiled=True)  31.1 us
    concatenate x4, other arithmetic, extended(): x = jnp.concatenate([before, x, after], axis=dim)  16.6 us
    ppermute x4, starting transfers between devices, extended(): after = lax.ppermute(first, axis, down)  13.8 us
  transfers between devices with their start and end apart: 9, of which 4 were waited for; matrix products, arithmetic and copies ran while one was open for 2% of the time, Pallas kernels for 0%

commit v1 on v0

v1 whole, which is shorter than its diff:
```python
import math

import jax
import jax.numpy as jnp
from jax import lax
from jax.sharding import PartitionSpec as P

DILATION_STEP = 4


def silu_slope(values):
    logistic = jax.nn.sigmoid(values)
    return logistic * (1.0 + values * (1.0 - logistic))


def shifted(x, axis, step, count):
    pairs = [(i, i + step) for i in range(count) if 0 <= i + step < count]
    return lax.ppermute(x, axis, pairs)


def butterfly(values, axis, count):
    bit = 1
    while bit < count:
        pairs = [(i, i ^ bit) for i in range(count)]
        values = jax.tree.map(lambda a, b: a + b, values, lax.ppermute(values, axis, pairs))
        bit *= 2
    return values


def body(bin_features, w_left, w_right, depth_kernel, w_point, w_head, cotangent):
    rows = bin_features.shape[0]
    cols = cotangent.shape[2]
    row_count = lax.axis_size("row")
    col_count = lax.axis_size("col")
    ratio = col_count // row_count
    bins = rows * row_count
    grad_scale = 1.0 / math.sqrt(bins)
    step = DILATION_STEP
    halo = 2 * step
    r = lax.axis_index("row")
    k = lax.axis_index("col")
    part = k % ratio

    left_proj = jnp.dot(bin_features, w_left, preferred_element_type=jnp.float32).astype(jnp.bfloat16)
    right_proj = jnp.dot(bin_features, w_right, preferred_element_type=jnp.float32).astype(jnp.bfloat16)

    cot_rows = jnp.concatenate(
        [
            shifted(cotangent[:, rows - step :, :], "row", 1, row_count),
            cotangent,
            shifted(cotangent[:, :step, :], "row", -1, row_count),
        ],
        axis=1,
    )
    cot_ext = jnp.concatenate(
        [
            shifted(cot_rows[:, :, cols - step :], "col", 1, col_count),
            cot_rows,
            shifted(cot_rows[:, :, :step], "col", -1, col_count),
        ],
        axis=2,
    )

    left_ext = jnp.concatenate(
        [
            shifted(left_proj[rows - halo :], "row", 1, row_count),
            left_proj,
            shifted(left_proj[:halo], "row", -1, row_count),
        ],
        axis=0,
    )

    def target(a, b, shift):
        tile = ratio * a + b % ratio + shift
        return (b // ratio) * col_count + tile if 0 <= tile < col_count else None

    def perm(shift):
        pairs = []
        for a in range(row_count):
            for b in range(col_count):
                t = target(a, b, shift)
                if t is not None:
                    pairs.append((a * col_count + b, t))
        return pairs

    own_tile = lax.dynamic_slice_in_dim(right_proj, part * cols, cols, 0)
    right_main = lax.ppermute(own_tile, ("row", "col"), perm(0))
    right_before = lax.ppermute(own_tile[cols - halo :], ("row", "col"), perm(1))
    right_after = lax.ppermute(own_tile[:halo], ("row", "col"), perm(-1))
    right_ext = jnp.concatenate([right_before, right_main, right_after], axis=0)

    row_place = r * rows - halo + lax.broadcasted_iota(jnp.int32, (rows + 2 * halo, 1), 0)
    col_place = k * cols - halo + lax.broadcasted_iota(jnp.int32, (1, cols + 2 * halo), 1)
    valid = (row_place >= 0) & (row_place < bins) & (col_place >= 0) & (col_place < bins)
    pair_sum = left_ext.astype(jnp.float32).T[:, :, None] + right_ext.astype(jnp.float32).T[:, None, :]
    pair_ext = jnp.where(valid[None], pair_sum, 0.0).astype(jnp.bfloat16)

    ext_rows = rows + 2 * step
    ext_cols = cols + 2 * step
    conv_ext = jnp.zeros((pair_ext.shape[0], ext_rows, ext_cols), jnp.float32)
    for a in range(3):
        for b in range(3):
            conv_ext = conv_ext + depth_kernel[3 * a + b][:, None, None] * pair_ext[
                :, step * a : step * a + ext_rows, step * b : step * b + ext_cols
            ].astype(jnp.float32)
    conv_tile = conv_ext[:, step : step + rows, step : step + cols]
    hidden_state = jax.nn.silu(conv_tile).astype(jnp.bfloat16)
    mixed_out = jnp.einsum("co,cij->oij", w_point, hidden_state, preferred_element_type=jnp.float32)
    pair_tile = pair_ext[:, halo : halo + rows, halo : halo + cols]
    trunk_matrix = (pair_tile.astype(jnp.float32) + mixed_out).astype(jnp.bfloat16)

    trunk_gradient = (
        grad_scale * jnp.einsum("ch,hij->cij", w_head, cot_ext, preferred_element_type=jnp.float32)
    ).astype(jnp.bfloat16)
    grad_hidden = jnp.einsum("co,oij->cij", w_point, trunk_gradient, preferred_element_type=jnp.float32)
    conv_grad = (grad_hidden * silu_slope(conv_ext)).astype(jnp.bfloat16)
    conv_grad_tile = conv_grad[:, step : step + rows, step : step + cols].astype(jnp.float32)
    trunk_grad_tile = trunk_gradient[:, step : step + rows, step : step + cols]

    backward_pass = trunk_grad_tile.astype(jnp.float32)
    kern_terms = []
    for a in range(3):
        for b in range(3):
            backward_pass = backward_pass + depth_kernel[3 * a + b][:, None, None] * conv_grad[
                :, step * (2 - a) : step * (2 - a) + rows, step * (2 - b) : step * (2 - b) + cols
            ].astype(jnp.float32)
            window = pair_ext[
                :, step + step * a : step + step * a + rows, step + step * b : step + step * b + cols
            ].astype(jnp.float32)
            kern_terms.append(jnp.sum(conv_grad_tile * window, axis=(1, 2)))
    kernel_part = jnp.stack(kern_terms)
    left_part = jnp.sum(backward_pass, axis=2).T
    right_part = jnp.sum(backward_pass, axis=1).T
    point_part = jnp.einsum(
        "fsk,gsk->fg", hidden_state, trunk_grad_tile, preferred_element_type=jnp.float32
    )
    head_part = jnp.einsum("ydq,gdq->yg", trunk_matrix, cotangent, preferred_element_type=jnp.float32)
    small = jnp.concatenate([kernel_part.ravel(), point_part.ravel(), head_part.ravel()])

    left_total, small = butterfly((left_part, small), "col", col_count)
    column_total = butterfly(right_part, "row", row_count)

    def redistribute(shift):
        pairs = []
        for a in range(row_count):
            for b in range(col_count):
                src = (b // ratio) * col_count + ratio * a + (b % ratio + shift) % ratio
                pairs.append((src, a * col_count + b))
        return lax.ppermute(column_total, ("row", "col"), pairs)

    received = jnp.stack([redistribute(q) for q in range(ratio)])
    grad_right = jnp.concatenate(
        [received[(m - part) % ratio] for m in range(ratio)], axis=0
    ).astype(jnp.bfloat16)
    grad_left = left_total.astype(jnp.bfloat16)

    grad_features = (
        jnp.dot(grad_left, w_left.T, preferred_element_type=jnp.float32)
        + jnp.dot(grad_right, w_right.T, preferred_element_type=jnp.float32)
    ).astype(jnp.bfloat16)
    contract = (((0,), (0,)), ((), ()))
    wleft_part = lax.dot_general(bin_features, grad_left, contract, preferred_element_type=jnp.float32)
    wright_part = lax.dot_general(bin_features, grad_right, contract, preferred_element_type=jnp.float32)
    wleft_sum, wright_sum, small = butterfly((wleft_part, wright_part, small), "row", row_count)

    chans = w_left.shape[1]
    heads = w_head.shape[1]
    taps = kernel_part.size
    kernel_sum = small[:taps].reshape(kernel_part.shape)
    point_sum = small[taps : taps + chans * chans].reshape(chans, chans)
    head_sum = small[taps + chans * chans :].reshape(chans, heads)
    return (
        grad_features,
        grad_scale * wleft_sum,
        grad_scale * wright_sum,
        grad_scale * kernel_sum,
        grad_scale * point_sum,
        grad_scale * head_sum,
    )


def solution(mesh):
    placed = (P("row", None), P(), P(), P(), P(), P(), P(None, "row", "col"))
    return jax.shard_map(
        body,
        mesh=mesh,
        in_specs=placed,
        out_specs=(P("row", None), P(), P(), P(), P(), P()),
        check_vma=False,
    )
```

time: 675 us -> 242 us (0.36)
  blocking collectives: 358 us -> 0 us
  waiting for transfers between devices: 171 us -> 24.9 us
  starting transfers between devices: 25 us -> 143 us
  local copies, waits for them, and re-layouts: 34 us -> 12.2 us
  between operations: 14.4 us -> 1.86 us
  matrix products: 28.2 us -> 15.7 us
    psum x4 -> x0, blocking collectives: 327 us -> none  [the longest x1 108 us: body(): grad_left = lax.psum(left_part, 'col').astype(jnp.bfloat16)]
    psum x1 -> x0, waiting for transfers between devices: 168 us -> none  [body(): wleft_sum, wright_sum = lax.psum((wleft_part, wright_part), 'row')]
    ppermute x8 -> x37, starting transfers between devices: 25 us -> 143 us  [the longest x26 93.3 us: butterfly(): lax.ppermute(values, axis, pairs)]
    all_gather x1 -> x0, blocking collectives: 31.1 us -> none  [body(): all_panels = lax.all_gather(column_total, 'col', axis=0, tiled=True)]
    ppermute x8 -> x37, waiting for transfers between devices: 3.65 us -> 24.9 us  [the longest x26 24.8 us: butterfly(): lax.ppermute(values, axis, pairs)]
    slice x8 -> x3, local copies, waits for them, and re-layouts: 21.2 us -> 1.03 us  [the longest x1 0.85 us: body(): cotangent[:, rows - step:, :]]
    reduce_sum x1 -> x2, other arithmetic: 7.23 us -> 26.7 us  [the longest x1 19.4 us: body(): left_part = jnp.sum(backward_pass, axis=2).T]
    concatenate x4 -> x0, other arithmetic: 16.6 us -> none  [extended(): x = jnp.concatenate([before, x, after], axis=dim)]
  transfers between devices with their start and end apart: 9 -> 37, of which waited for: 4 -> 10; matrix products, arithmetic and copies ran while one was open for 2% -> 20% of each run, Pallas kernels for 0% -> 0%
where the time goes in v1:
time: 242 us; the launch traced here: 240 us
  starting transfers between devices  143 us (59%)
  other arithmetic  42.4 us (18%)
  waiting for transfers between devices  24.9 us (10%)
  matrix products  15.7 us (6%)
  local copies, waits for them, and re-layouts  12.2 us (5%)
    ppermute x26, starting transfers between devices, butterfly(): lax.ppermute(values, axis, pairs)  93.3 us
    ppermute x26, waiting for transfers between devices, butterfly(): lax.ppermute(values, axis, pairs)  24.8 us
    ppermute x6, starting transfers between devices, shifted(): return lax.ppermute(x, axis, pairs)  20.6 us
    reduce_sum x1, other arithmetic, body(): left_part = jnp.sum(backward_pass, axis=2).T  19.4 us
    ppermute x1, starting transfers between devices, body(): right_main = lax.ppermute(own_tile, ('row', 'col'), perm(0))  9.46 us
    ppermute x1, starting transfers between devices, body(): right_after = lax.ppermute(own_tile[:halo], ('row', 'col'), perm(-1))  9.07 us
    add x1, other arithmetic, body(): conv_ext + depth_kernel[3 * a + b][:, None, None] * pair_ext[:, step * a:...  8.34 us
    ppermute x2, starting transfers between devices, redistribute(): return lax.ppermute(column_total, ('row', 'col'), pairs)  7.35 us
  transfers between devices with their start and end apart: 37, of which 10 were waited for; matrix products, arithmetic and copies ran while one was open for 20% of the time, Pallas kernels for 0%

profile of v1, /device:TPU:6, one launch (start us, length us, event | category | flops | bytes accessed | tf_op | source)
XLA Modules:
  0.0 240.1 jit_solution(15677649748167143040)
XLA Ops:
  2.5 9.5 %collective-permute-start.7 = (bf16[128,32]{0,1:T(8,128)(2,1)S(1)}, bf16[128,32]{0,1:T(8,128)(2,1)S(1)}, u32[]{:S(2)}, u32[]{:S(2)}) collective-permute-start(bf16[128,32]{0,1:T(8,128)(2,1)S(1)} %dynamic-slice_convert_fusion), channel_id=1, source_target_pairs={{0,0},{1,1},{2,32},{3,33},{4,64},{5,65},{6,96},{7,97},{8,128},{9,1... | collective-permute-start | bytes 24584 | tf_op jit(solution)/shard_map/ppermute | solution.py:87
  12.1 9.1 %collective-permute-start.8 = (bf16[8,32]{0,1:T(8,128)(2,1)S(1)}, bf16[8,32]{0,1:T(8,128)(2,1)S(1)}, u32[]{:S(2)}, u32[]{:S(2)}) collective-permute-start(bf16[8,32]{0,1:T(8,128)(2,1)S(1)} %get-tuple-element.53), channel_id=1, source_target_pairs={{1,0},{3,32},{5,64},{7,96},{9,128},{11,160},{13,192},{15,224},{17,... | collective-permute-start | bytes 1544 | tf_op jit(solution)/shard_map/ppermute | solution.py:89
  21.2 3.4 %collective-permute-start.6 = (bf16[8,32]{0,1:T(8,128)(2,1)S(1)}, bf16[8,32]{0,1:T(8,128)(2,1)S(1)}, u32[]{:S(2)}, u32[]{:S(2)}) collective-permute-start(bf16[8,32]{0,1:T(8,128)(2,1)S(1)} %get-tuple-element.52), channel_id=1, source_target_pairs={{0,1},{1,2},{2,33},{3,34},{4,65},{5,66},{6,97},{7,98},{8,129},{9,1... | collective-permute-start | bytes 1544 | tf_op jit(solution)/shard_map/ppermute | solution.py:88
  25.6 4.9 %collective-permute-start.5 = (bf16[8,32]{0,1:T(8,128)(2,1)S(1)}, bf16[8,32]{0,1:T(8,128)(2,1)S(1)}, u32[]{:S(2)}, u32[]{:S(2)}) collective-permute-start(bf16[8,32]{0,1:T(8,128)(2,1)S(1)} %get-tuple-element.42), channel_id=1, source_target_pairs={{32,0},{64,32},{96,64},{128,96},{160,128},{192,160},{224,192},{256... | collective-permute-start | bytes 1544 | tf_op jit(solution)/shard_map/ppermute | solution.py:18
  30.4 1.9 collective-permute-start.4
  34.5 2.2 copy.40
  36.7 6.9 %collective-permute-start.1 = (bf16[24,4,128]{2,0,1:T(8,128)(2,1)S(1)}, bf16[24,4,128]{2,0,1:T(8,128)(2,1)S(1)}, u32[]{:S(2)}, u32[]{:S(2)}) collective-permute-start(bf16[24,4,128]{2,0,1:T(8,128)(2,1)S(1)} %copy.54), channel_id=1, source_target_pairs={{32,0},{64,32},{96,64},{128,96},{160,128},{192,160},{224,192},{256... | collective-permute-start | bytes 73736 | tf_op jit(solution)/shard_map/ppermute | solution.py:18
  43.6 1.9 collective-permute-start
  47.3 8.3 %multiply_add_fusion = f32[32,264,136]{1,0,2:T(8,128)S(1)} fusion(bf16[32,272,144]{1,0,2:T(8,128)(2,1)S(1)} %select_convert_fusion, f32[32]{0:T(128)S(1)} %get-tuple-element.50, f32[32]{0:T(128)S(1)} %get-tuple-element.51, f32[32]{0:T(128)S(1)} %get-tuple-element.44, f32[32]{0:T(128)S(1)} %get-tuple-element.45, f32[32]{0:T(128)S(1)} %get-tuple-element.46, ...), kind=kLoop, calls=%fused_computation.13 | loop fusion | flops 29872128 | bytes 25277568 | tf_op jit(solution)/shard_map/add | solution.py:103
  55.8 3.1 %multiply_convert_fusion.1 = bf16[32,256,128]{1,0,2:T(8,128)(2,1)} fusion(f32[32,264,136]{1,0,2:T(8,128)S(1)} %multiply_add_fusion), kind=kLoop, calls=%fused_computation.31 | loop fusion | flops 5242880 | bytes 6291456 | tf_op jit(solution)/shard_map/convert_element_type | solution.py:107
  62.4 3.7 %collective-permute-start.2 = (bf16[24,264,4]{1,0,2:T(8,128)(2,1)}, bf16[24,264,4]{1,0,2:T(8,128)(2,1)}, u32[]{:S(2)}, u32[]{:S(2)}) collective-permute-start(bf16[24,264,4]{1,0,2:T(8,128)(2,1)} %get-tuple-element.35), channel_id=1, source_target_pairs={{0,1},{1,2},{2,3},{3,4},{4,5},{5,6},{6,7},{7,8},{8,9},{9,10},{10,1... | collective-permute-start | bytes 152072 | tf_op jit(solution)/shard_map/ppermute | solution.py:18
  66.1 4.6 %fusion.30 = f32[32,24]{1,0:T(8,128)S(1)} fusion(bf16[24,256,128]{1,0,2:T(8,128)(2,1)S(1)} %copy.40, bf16[32,256,128]{1,0,2:T(8,128)(2,1)} %multiply_convert_fusion.1, bf16[32,272,144]{1,0,2:T(8,128)(2,1)} %copy-done.1, bf16[32,32]{1,0:T(8,128)(2,1)S(1)} %copy-done.30), kind=kOutput, calls=%fused_computation.50 | convolution fusion | flops 120586240 | bytes 5772288 | tf_op jit(solution)/shard_map/ydq,gdq->yg/dot_general | solution.py:137
  71.4 3.5 %fusion.16 = bf16[32,264,136]{1,0,2:T(8,128)(2,1)S(1)} fusion(bf16[24,264,4]{1,0,2:T(8,128)(2,1)} %collective-permute-done.3, bf16[24,4,128]{1,0,2:T(8,128)(2,1)S(1)} %copy.41, bf16[24,256,128]{1,0,2:T(8,128)(2,1)} %copy-done.5, bf16[24,4,128]{1,0,2:T(8,128)(2,1)} %copy-done.6, bf16[24,264,4]{1,0,2:T(8,128)(2,1)} %collective-permute-done.2, ...), kind=kOutput, calls=%fused_computation.32 | convolution fusion | flops 66063360 | bytes 4022784 | tf_op jit(solution)/shard_map/ch,hij->cij/dot_general | solution.py:113
  75.0 3.3 %fusion = bf16[32,264,136]{1,0,2:T(8,128)(2,1)S(1)} fusion(f32[32,264,136]{1,0,2:T(8,128)S(1)} %bitcast.86, bf16[32,264,136]{1,0,2:T(8,128)(2,1)S(1)} %fusion.16, bf16[32,32]{1,0:T(8,128)(2,1)S(1)} %copy-done.31), kind=kOutput, calls=%fused_computation.12 | convolution fusion | flops 83871744 | bytes 9193472 | tf_op jit(solution)/shard_map/co,oij->cij/dot_general | solution.py:115
  79.3 2.2 copy-done.2
  81.6 7.3 %fusion.15 = (f32[32]{0:T(128)S(1)}, f32[32]{0:T(128)S(1)}, f32[32]{0:T(128)S(1)}, f32[32]{0:T(128)S(1)}, f32[32]{0:T(128)S(1)}, /*index=5*/f32[32]{0:T(128)S(1)}, f32[32]{0:T(128)S(1)}, f32[32]{0:T(128)S(1)}, f32[32]{0:T(128)S(1)}) fusion(bf16[32,272,144]{1,0,2:T(8,128)(2,1)S(1)} %copy-done.2, bf16[32,264,136]{1,0,2:T(8,128)(2,1)S(1)} %fusion), kind=kLoop, calls=%fused_computation.30 | loop fusion | flops 29359840 | bytes 20972672 | tf_op jit(solution)/shard_map/reduce_sum | solution.py:130
  89.1 4.4 %collective-permute-start.28 = (f32[2080]{0:T(1024)S(1)}, f32[2080]{0:T(1024)S(1)}, u32[]{:S(2)}, u32[]{:S(2)}) collective-permute-start(f32[2080]{0:T(1024)S(1)} %concatenate.24), channel_id=1, source_target_pairs={{0,1},{1,0},{2,3},{3,2},{4,5},{5,4},{6,7},{7,6},{8,9},{9,8},{10,11... | collective-permute-start | bytes 24968 | tf_op jit(solution)/shard_map/ppermute | solution.py:25
  93.6 19.4 %fusion.53 = (f32[32,256]{1,0:T(8,128)S(1)}, f32[32,128]{0,1:T(8,128)S(1)}) fusion(bf16[32,264,136]{1,0,2:T(8,128)(2,1)} %copy-done.3, f32[32]{0:T(128)S(1)} %copy-done.27, f32[32]{0:T(128)S(1)} %copy-done.29, f32[32]{0:T(128)S(1)} %copy-done.15, f32[32]{0:T(128)S(1)} %copy-done.17, f32[32]{0:T(128)S(1)} %copy-done.19, f32[32]{0:T(128)S(1)} %copy-done.21, ...), kind=kLoop, calls=%fused_computation.101 | loop fusion | flops 31444992 | bytes 21021824 | tf_op jit(solution)/shard_map/reduce_sum | solution.py:132
  113.0 4.1 %collective-permute-start.14 = (f32[128,32]{1,0:T(8,128)S(1)}, f32[128,32]{1,0:T(8,128)S(1)}, u32[]{:S(2)}, u32[]{:S(2)}) collective-permute-start(f32[128,32]{1,0:T(8,128)S(1)} %bitcast.87), channel_id=1, source_target_pairs={{0,32},{32,0},{64,96},{96,64},{128,160},{160,128},{192,224},{224,1... | collective-permute-start | bytes 49160 | tf_op jit(solution)/shard_map/ppermute | solution.py:25
  117.2 8.5 %collective-permute-start.29 = (f32[2080]{0:T(1024)S(1)}, f32[2080]{0:T(1024)S(1)}, u32[]{:S(2)}, u32[]{:S(2)}) collective-permute-start(f32[2080]{0:T(1024)S(1)} %add.256), channel_id=1, source_target_pairs={{0,2},{1,3},{2,0},{3,1},{4,6},{5,7},{6,4},{7,5},{8,10},{9,11},{10,... | collective-permute-start | bytes 24968 | tf_op jit(solution)/shard_map/ppermute | solution.py:25
  127.6 3.6 %collective-permute-start.30 = (f32[2080]{0:T(1024)S(1)}, f32[2080]{0:T(1024)S(1)}, u32[]{:S(2)}, u32[]{:S(2)}) collective-permute-start(f32[2080]{0:T(1024)S(1)} %add.257), channel_id=1, source_target_pairs={{0,4},{1,5},{2,6},{3,7},{4,0},{5,1},{6,2},{7,3},{8,12},{9,13},{10,... | collective-permute-start | bytes 24968 | tf_op jit(solution)/shard_map/ppermute | solution.py:25
  134.1 3.4 %collective-permute-start.31 = (f32[2080]{0:T(1024)S(1)}, f32[2080]{0:T(1024)S(1)}, u32[]{:S(2)}, u32[]{:S(2)}) collective-permute-start(f32[2080]{0:T(1024)S(1)} %add.258), channel_id=1, source_target_pairs={{0,8},{1,9},{2,10},{3,11},{4,12},{5,13},{6,14},{7,15},{8,0},{9,1},... | collective-permute-start | bytes 24968 | tf_op jit(solution)/shard_map/ppermute | solution.py:25
  137.6 4.4 %collective-permute-done.15 = f32[128,32]{1,0:T(8,128)S(1)} collective-permute-done((f32[128,32]{1,0:T(8,128)S(1)}, f32[128,32]{1,0:T(8,128)S(1)}, u32[]{:S(2)}, u32[]{:S(2)}) %collective-permute-start.15) | collective-permute-done | bytes 16416 | tf_op jit(solution)/shard_map/ppermute | solution.py:25
  142.0 1.9 collective-permute-start.16
  144.0 2.9 %collective-permute-start.32 = (f32[2080]{0:T(1024)S(1)}, f32[2080]{0:T(1024)S(1)}, u32[]{:S(2)}, u32[]{:S(2)}) collective-permute-start(f32[2080]{0:T(1024)S(1)} %add.259), channel_id=1, source_target_pairs={{0,16},{1,17},{2,18},{3,19},{4,20},{5,21},{6,22},{7,23},{8,24},{9,... | collective-permute-start | bytes 24968 | tf_op jit(solution)/shard_map/ppermute | solution.py:25
  146.8 3.3 %collective-permute-start.10 = (f32[256,32]{0,1:T(8,128)S(1)}, f32[256,32]{0,1:T(8,128)S(1)}, u32[]{:S(2)}, u32[]{:S(2)}) collective-permute-start(f32[256,32]{0,1:T(8,128)S(1)} %bitcast_add_fusion.1), channel_id=1, source_target_pairs={{0,2},{1,3},{2,0},{3,1},{4,6},{5,7},{6,4},{7,5},{8,10},{9,11},{10,... | collective-permute-start | bytes 98312 | tf_op jit(solution)/shard_map/ppermute | solution.py:25
  150.1 2.7 %collective-permute-start.33 = (f32[2080]{0:T(1024)S(1)}, f32[2080]{0:T(1024)S(1)}, u32[]{:S(2)}, u32[]{:S(2)}) collective-permute-start(f32[2080]{0:T(1024)S(1)} %add.260), channel_id=1, source_target_pairs={{0,32},{32,0},{64,96},{96,64},{128,160},{160,128},{192,224},{224,1... | collective-permute-start | bytes 24968 | tf_op jit(solution)/shard_map/ppermute | solution.py:25
  152.9 3.0 %collective-permute-start.17 = (f32[128,32]{1,0:T(8,128)S(1)}, f32[128,32]{1,0:T(8,128)S(1)}, u32[]{:S(2)}, u32[]{:S(2)}) collective-permute-start(f32[128,32]{1,0:T(8,128)S(1)} %add.239), channel_id=1, source_target_pairs={{0,256},{32,288},{64,320},{96,352},{128,384},{160,416},{192,448},{... | collective-permute-start | bytes 49160 | tf_op jit(solution)/shard_map/ppermute | solution.py:25
  156.6 6.2 %collective-permute-start.34 = (f32[2080]{0:T(1024)S(1)}, f32[2080]{0:T(1024)S(1)}, u32[]{:S(2)}, u32[]{:S(2)}) collective-permute-start(f32[2080]{0:T(1024)S(1)} %add.261), channel_id=1, source_target_pairs={{0,64},{32,96},{64,0},{96,32},{128,192},{160,224},{192,128},{224,1... | collective-permute-start | bytes 24968 | tf_op jit(solution)/shard_map/ppermute | solution.py:25
  162.9 3.3 %collective-permute-done.34 = f32[2080]{0:T(1024)S(1)} collective-permute-done((f32[2080]{0:T(1024)S(1)}, f32[2080]{0:T(1024)S(1)}, u32[]{:S(2)}, u32[]{:S(2)}) %collective-permute-start.34) | collective-permute-done | bytes 8352 | tf_op jit(solution)/shard_map/ppermute | solution.py:25
  166.1 4.0 %collective-permute-start.35 = (f32[2080]{0:T(1024)S(1)}, f32[2080]{0:T(1024)S(1)}, u32[]{:S(2)}, u32[]{:S(2)}) collective-permute-start(f32[2080]{0:T(1024)S(1)} %add.262), channel_id=1, source_target_pairs={{0,128},{32,160},{64,192},{96,224},{128,0},{160,32},{192,64},{224,... | collective-permute-start | bytes 24968 | tf_op jit(solution)/shard_map/ppermute | solution.py:25
  172.1 5.4 %collective-permute-start.18 = (bf16[128,32]{1,0:T(8,128)(2,1)S(1)}, bf16[128,32]{1,0:T(8,128)(2,1)S(1)}, u32[]{:S(2)}, u32[]{:S(2)}) collective-permute-start(bf16[128,32]{1,0:T(8,128)(2,1)S(1)} %add.240), channel_id=1, source_target_pairs={{0,0},{1,1},{32,2},{33,3},{64,4},{65,5},{96,6},{97,7},{128,8},{129... | collective-permute-start | bytes 24584 | tf_op jit(solution)/shard_map/ppermute | solution.py:149
  177.6 4.0 %collective-permute-start.11 = (f32[256,32]{0,1:T(8,128)S(1)}, f32[256,32]{0,1:T(8,128)S(1)}, u32[]{:S(2)}, u32[]{:S(2)}) collective-permute-start(f32[256,32]{0,1:T(8,128)S(1)} %add.233), channel_id=1, source_target_pairs={{0,4},{1,5},{2,6},{3,7},{4,0},{5,1},{6,2},{7,3},{8,12},{9,13},{10,... | collective-permute-start | bytes 98312 | tf_op jit(solution)/shard_map/ppermute | solution.py:25
  181.6 4.6 %collective-permute-start.36 = (f32[2080]{0:T(1024)S(1)}, f32[2080]{0:T(1024)S(1)}, u32[]{:S(2)}, u32[]{:S(2)}) collective-permute-start(f32[2080]{0:T(1024)S(1)} %add.263), channel_id=1, source_target_pairs={{0,256},{32,288},{64,320},{96,352},{128,384},{160,416},{192,448},{... | collective-permute-start | bytes 24968 | tf_op jit(solution)/shard_map/ppermute | solution.py:25
  186.8 3.0 %collective-permute-start.12 = (f32[256,32]{0,1:T(8,128)S(1)}, f32[256,32]{0,1:T(8,128)S(1)}, u32[]{:S(2)}, u32[]{:S(2)}) collective-permute-start(f32[256,32]{0,1:T(8,128)S(1)} %add.234), channel_id=1, source_target_pairs={{0,8},{1,9},{2,10},{3,11},{4,12},{5,13},{6,14},{7,15},{8,0},{9,1},... | collective-permute-start | bytes 98312 | tf_op jit(solution)/shard_map/ppermute | solution.py:25
  190.0 2.2 collective-permute-start.24
  192.2 4.2 %collective-permute-done.12 = f32[256,32]{0,1:T(8,128)S(1)} collective-permute-done((f32[256,32]{0,1:T(8,128)S(1)}, f32[256,32]{0,1:T(8,128)S(1)}, u32[]{:S(2)}, u32[]{:S(2)}) %collective-permute-start.12) | collective-permute-done | bytes 32800 | tf_op jit(solution)/shard_map/ppermute | solution.py:25
  196.5 2.2 collective-permute-start.13
  198.8 5.8 %collective-permute-start.25 = (f32[512,32]{0,1:T(8,128)S(1)}, f32[512,32]{0,1:T(8,128)S(1)}, u32[]{:S(2)}, u32[]{:S(2)}) collective-permute-start(f32[512,32]{0,1:T(8,128)S(1)} %add.250), channel_id=1, source_target_pairs={{0,64},{32,96},{64,0},{96,32},{128,192},{160,224},{192,128},{224,1... | collective-permute-start | bytes 196616 | tf_op jit(solution)/shard_map/ppermute | solution.py:25
  204.8 2.3 collective-permute-start.20
  208.9 3.4 %collective-permute-start.26 = (f32[512,32]{0,1:T(8,128)S(1)}, f32[512,32]{0,1:T(8,128)S(1)}, u32[]{:S(2)}, u32[]{:S(2)}) collective-permute-start(f32[512,32]{0,1:T(8,128)S(1)} %add.251), channel_id=1, source_target_pairs={{0,128},{32,160},{64,192},{96,224},{128,0},{160,32},{192,64},{224,... | collective-permute-start | bytes 196616 | tf_op jit(solution)/shard_map/ppermute | solution.py:25
  212.3 2.0 collective-permute-done.20
  214.2 4.6 %collective-permute-start.21 = (f32[512,32]{0,1:T(8,128)S(1)}, f32[512,32]{0,1:T(8,128)S(1)}, u32[]{:S(2)}, u32[]{:S(2)}) collective-permute-start(f32[512,32]{0,1:T(8,128)S(1)} %add.246), channel_id=1, source_target_pairs={{0,64},{32,96},{64,0},{96,32},{128,192},{160,224},{192,128},{224,1... | collective-permute-start | bytes 196616 | tf_op jit(solution)/shard_map/ppermute | solution.py:25
  221.0 4.0 %collective-permute-start.27 = (f32[512,32]{0,1:T(8,128)S(1)}, f32[512,32]{0,1:T(8,128)S(1)}, u32[]{:S(2)}, u32[]{:S(2)}) collective-permute-start(f32[512,32]{0,1:T(8,128)S(1)} %add.252), channel_id=1, source_target_pairs={{0,256},{32,288},{64,320},{96,352},{128,384},{160,416},{192,448},{... | collective-permute-start | bytes 196616 | tf_op jit(solution)/shard_map/ppermute | solution.py:25
  225.6 2.2 collective-permute-start.22
  228.8 2.9 %collective-permute-done.22 = f32[512,32]{0,1:T(8,128)S(1)} collective-permute-done((f32[512,32]{0,1:T(8,128)S(1)}, f32[512,32]{0,1:T(8,128)S(1)}, u32[]{:S(2)}, u32[]{:S(2)}) %collective-permute-start.22) | collective-permute-done | bytes 65568 | tf_op jit(solution)/shard_map/ppermute | solution.py:25
  231.8 2.8 %collective-permute-start.23 = (f32[512,32]{0,1:T(8,128)S(1)}, f32[512,32]{0,1:T(8,128)S(1)}, u32[]{:S(2)}, u32[]{:S(2)}) collective-permute-start(f32[512,32]{0,1:T(8,128)S(1)} %add.248), channel_id=1, source_target_pairs={{0,256},{32,288},{64,320},{96,352},{128,384},{160,416},{192,448},{... | collective-permute-start | bytes 196616 | tf_op jit(solution)/shard_map/ppermute | solution.py:25
  235.2 4.2 %collective-permute-done.23 = f32[512,32]{0,1:T(8,128)S(1)} collective-permute-done((f32[512,32]{0,1:T(8,128)S(1)}, f32[512,32]{0,1:T(8,128)S(1)}, u32[]{:S(2)}, u32[]{:S(2)}) %collective-permute-start.23) | collective-permute-done | bytes 65568 | tf_op jit(solution)/shard_map/ppermute | solution.py:25
  (168 shorter events, 27.2 us)
Async XLA Ops:
  2.5 43.1 %collective-permute-start.7 = (bf16[128,32]{0,1:T(8,128)(2,1)S(1)}, bf16[128,32]{0,1:T(8,128)(2,1)S(1)}, u32[]{:S(2)}, u32[]{:S(2)}) collective-permute-start(bf16[128,32]{0,1:T(8,128)(2,1)S(1)} %dynamic-slice_convert_fusion), channel_id=1, source_target_pairs={{0,0},{1,1},{2,32},{3,33},{4,64},{5,65},{6,96},{7,97},{8,128},{9,1... | collective-permute-start | bytes 24584 | tf_op jit(solution)/shard_map/ppermute | solution.py:87
  12.1 33.6 %collective-permute-start.8 = (bf16[8,32]{0,1:T(8,128)(2,1)S(1)}, bf16[8,32]{0,1:T(8,128)(2,1)S(1)}, u32[]{:S(2)}, u32[]{:S(2)}) collective-permute-start(bf16[8,32]{0,1:T(8,128)(2,1)S(1)} %get-tuple-element.53), channel_id=1, source_target_pairs={{1,0},{3,32},{5,64},{7,96},{9,128},{11,160},{13,192},{15,224},{17,... | collective-permute-start | bytes 1544 | tf_op jit(solution)/shard_map/ppermute | solution.py:89
  21.2 24.5 %collective-permute-start.6 = (bf16[8,32]{0,1:T(8,128)(2,1)S(1)}, bf16[8,32]{0,1:T(8,128)(2,1)S(1)}, u32[]{:S(2)}, u32[]{:S(2)}) collective-permute-start(bf16[8,32]{0,1:T(8,128)(2,1)S(1)} %get-tuple-element.52), channel_id=1, source_target_pairs={{0,1},{1,2},{2,33},{3,34},{4,65},{5,66},{6,97},{7,98},{8,129},{9,1... | collective-permute-start | bytes 1544 | tf_op jit(solution)/shard_map/ppermute | solution.py:88
  25.6 11.1 %collective-permute-start.5 = (bf16[8,32]{0,1:T(8,128)(2,1)S(1)}, bf16[8,32]{0,1:T(8,128)(2,1)S(1)}, u32[]{:S(2)}, u32[]{:S(2)}) collective-permute-start(bf16[8,32]{0,1:T(8,128)(2,1)S(1)} %get-tuple-element.42), channel_id=1, source_target_pairs={{32,0},{64,32},{96,64},{128,96},{160,128},{192,160},{224,192},{256... | collective-permute-start | bytes 1544 | tf_op jit(solution)/shard_map/ppermute | solution.py:18
  30.4 13.2 %collective-permute-start.4 = (bf16[8,32]{0,1:T(8,128)(2,1)S(1)}, bf16[8,32]{0,1:T(8,128)(2,1)S(1)}, u32[]{:S(2)}, u32[]{:S(2)}) collective-permute-start(bf16[8,32]{0,1:T(8,128)(2,1)S(1)} %get-tuple-element.41), channel_id=1, source_target_pairs={{0,32},{32,64},{64,96},{96,128},{128,160},{160,192},{192,224},{224... | collective-permute-start | bytes 1544 | tf_op jit(solution)/shard_map/ppermute | solution.py:18
  34.4 21.3 %copy-start.12 = (f32[32]{0:T(128)}, f32[32]{0:T(128)S(1)}, u32[]{:S(2)}) copy-start(f32[32]{0:T(128)S(1)} %get-tuple-element.43) | copy-start | bytes 388
  34.4 21.3 %copy-start.14 = (f32[32]{0:T(128)}, f32[32]{0:T(128)S(1)}, u32[]{:S(2)}) copy-start(f32[32]{0:T(128)S(1)} %get-tuple-element.44) | copy-start | bytes 388
  34.4 21.3 %copy-start.16 = (f32[32]{0:T(128)}, f32[32]{0:T(128)S(1)}, u32[]{:S(2)}) copy-start(f32[32]{0:T(128)S(1)} %get-tuple-element.45) | copy-start | bytes 388
  34.4 21.3 %copy-start.18 = (f32[32]{0:T(128)}, f32[32]{0:T(128)S(1)}, u32[]{:S(2)}) copy-start(f32[32]{0:T(128)S(1)} %get-tuple-element.46) | copy-start | bytes 388
  34.4 21.3 %copy-start.20 = (f32[32]{0:T(128)}, f32[32]{0:T(128)S(1)}, u32[]{:S(2)}) copy-start(f32[32]{0:T(128)S(1)} %get-tuple-element.47) | copy-start | bytes 388
  34.4 21.3 %copy-start.22 = (f32[32]{0:T(128)}, f32[32]{0:T(128)S(1)}, u32[]{:S(2)}) copy-start(f32[32]{0:T(128)S(1)} %get-tuple-element.48) | copy-start | bytes 388
  34.4 21.3 %copy-start.24 = (f32[32]{0:T(128)}, f32[32]{0:T(128)S(1)}, u32[]{:S(2)}) copy-start(f32[32]{0:T(128)S(1)} %get-tuple-element.49) | copy-start | bytes 388
  34.4 21.3 %copy-start.26 = (f32[32]{0:T(128)}, f32[32]{0:T(128)S(1)}, u32[]{:S(2)}) copy-start(f32[32]{0:T(128)S(1)} %get-tuple-element.50) | copy-start | bytes 388
  36.6 29.4 %copy-start.5 = (bf16[24,256,128]{1,0,2:T(8,128)(2,1)}, bf16[24,256,128]{1,0,2:T(8,128)(2,1)S(1)}, u32[]{:S(2)}) copy-start(bf16[24,256,128]{1,0,2:T(8,128)(2,1)S(1)} %copy.40) | copy-start | bytes 4718596
  36.7 22.5 %collective-permute-start.1 = (bf16[24,4,128]{2,0,1:T(8,128)(2,1)S(1)}, bf16[24,4,128]{2,0,1:T(8,128)(2,1)S(1)}, u32[]{:S(2)}, u32[]{:S(2)}) collective-permute-start(bf16[24,4,128]{2,0,1:T(8,128)(2,1)S(1)} %copy.54), channel_id=1, source_target_pairs={{32,0},{64,32},{96,64},{128,96},{160,128},{192,160},{224,192},{256... | collective-permute-start | bytes 73736 | tf_op jit(solution)/shard_map/ppermute | solution.py:18
  43.6 16.1 %collective-permute-start = (bf16[24,4,128]{2,0,1:T(8,128)(2,1)S(1)}, bf16[24,4,128]{2,0,1:T(8,128)(2,1)S(1)}, u32[]{:S(2)}, u32[]{:S(2)}) collective-permute-start(bf16[24,4,128]{2,0,1:T(8,128)(2,1)S(1)} %copy.53), channel_id=1, source_target_pairs={{0,32},{32,64},{64,96},{96,128},{128,160},{160,192},{192,224},{224... | collective-permute-start | bytes 73736 | tf_op jit(solution)/shard_map/ppermute | solution.py:18
  61.1 10.3 %collective-permute-start.3 = (bf16[24,264,4]{1,0,2:T(8,128)(2,1)}, bf16[24,264,4]{1,0,2:T(8,128)(2,1)}, u32[]{:S(2)}, u32[]{:S(2)}) collective-permute-start(bf16[24,264,4]{1,0,2:T(8,128)(2,1)} %get-tuple-element.36), channel_id=1, source_target_pairs={{1,0},{2,1},{3,2},{4,3},{5,4},{6,5},{7,6},{8,7},{9,8},{10,9},{11,1... | collective-permute-start | bytes 152072 | tf_op jit(solution)/shard_map/ppermute | solution.py:18
  62.4 9.0 %collective-permute-start.2 = (bf16[24,264,4]{1,0,2:T(8,128)(2,1)}, bf16[24,264,4]{1,0,2:T(8,128)(2,1)}, u32[]{:S(2)}, u32[]{:S(2)}) collective-permute-start(bf16[24,264,4]{1,0,2:T(8,128)(2,1)} %get-tuple-element.35), channel_id=1, source_target_pairs={{0,1},{1,2},{2,3},{3,4},{4,5},{5,6},{6,7},{7,8},{8,9},{9,10},{10,1... | collective-permute-start | bytes 152072 | tf_op jit(solution)/shard_map/ppermute | solution.py:18
  89.1 97.4 %copy-start.9 = (bf16[512,32]{0,1:T(8,128)(2,1)S(1)}, bf16[512,32]{0,1:T(8,128)(2,1)}, u32[]{:S(2)}) copy-start(bf16[512,32]{0,1:T(8,128)(2,1)} %param.9) | copy-start | bytes 98308
  89.1 138.7 %copy-start.10 = (bf16[512,32]{0,1:T(8,128)(2,1)S(1)}, bf16[512,32]{0,1:T(8,128)(2,1)}, u32[]{:S(2)}) copy-start(bf16[512,32]{0,1:T(8,128)(2,1)} %param.8) | copy-start | bytes 98308
  89.1 28.0 %collective-permute-start.28 = (f32[2080]{0:T(1024)S(1)}, f32[2080]{0:T(1024)S(1)}, u32[]{:S(2)}, u32[]{:S(2)}) collective-permute-start(f32[2080]{0:T(1024)S(1)} %concatenate.24), channel_id=1, source_target_pairs={{0,1},{1,0},{2,3},{3,2},{4,5},{5,4},{6,7},{7,6},{8,9},{9,8},{10,11... | collective-permute-start | bytes 24968 | tf_op jit(solution)/shard_map/ppermute | solution.py:25
  113.0 18.3 %collective-permute-start.14 = (f32[128,32]{1,0:T(8,128)S(1)}, f32[128,32]{1,0:T(8,128)S(1)}, u32[]{:S(2)}, u32[]{:S(2)}) collective-permute-start(f32[128,32]{1,0:T(8,128)S(1)} %bitcast.87), channel_id=1, source_target_pairs={{0,32},{32,0},{64,96},{96,64},{128,160},{160,128},{192,224},{224,1... | collective-permute-start | bytes 49160 | tf_op jit(solution)/shard_map/ppermute | solution.py:25
  117.2 10.5 %collective-permute-start.29 = (f32[2080]{0:T(1024)S(1)}, f32[2080]{0:T(1024)S(1)}, u32[]{:S(2)}, u32[]{:S(2)}) collective-permute-start(f32[2080]{0:T(1024)S(1)} %add.256), channel_id=1, source_target_pairs={{0,2},{1,3},{2,0},{3,1},{4,6},{5,7},{6,4},{7,5},{8,10},{9,11},{10,... | collective-permute-start | bytes 24968 | tf_op jit(solution)/shard_map/ppermute | solution.py:25
  125.7 21.1 %collective-permute-start.9 = (f32[256,32]{0,1:T(8,128)S(1)}, f32[256,32]{0,1:T(8,128)S(1)}, u32[]{:S(2)}, u32[]{:S(2)}) collective-permute-start(f32[256,32]{0,1:T(8,128)S(1)} %bitcast.88), channel_id=1, source_target_pairs={{0,1},{1,0},{2,3},{3,2},{4,5},{5,4},{6,7},{7,6},{8,9},{9,8},{10,11... | collective-permute-start | bytes 98312 | tf_op jit(solution)/shard_map/ppermute | solution.py:25
  127.6 6.5 %collective-permute-start.30 = (f32[2080]{0:T(1024)S(1)}, f32[2080]{0:T(1024)S(1)}, u32[]{:S(2)}, u32[]{:S(2)}) collective-permute-start(f32[2080]{0:T(1024)S(1)} %add.257), channel_id=1, source_target_pairs={{0,4},{1,5},{2,6},{3,7},{4,0},{5,1},{6,2},{7,3},{8,12},{9,13},{10,... | collective-permute-start | bytes 24968 | tf_op jit(solution)/shard_map/ppermute | solution.py:25
  131.3 10.7 %collective-permute-start.15 = (f32[128,32]{1,0:T(8,128)S(1)}, f32[128,32]{1,0:T(8,128)S(1)}, u32[]{:S(2)}, u32[]{:S(2)}) collective-permute-start(f32[128,32]{1,0:T(8,128)S(1)} %bitcast_add_fusion), channel_id=1, source_target_pairs={{0,64},{32,96},{64,0},{96,32},{128,192},{160,224},{192,128},{224,1... | collective-permute-start | bytes 49160 | tf_op jit(solution)/shard_map/ppermute | solution.py:25
  134.1 9.8 %collective-permute-start.31 = (f32[2080]{0:T(1024)S(1)}, f32[2080]{0:T(1024)S(1)}, u32[]{:S(2)}, u32[]{:S(2)}) collective-permute-start(f32[2080]{0:T(1024)S(1)} %add.258), channel_id=1, source_target_pairs={{0,8},{1,9},{2,10},{3,11},{4,12},{5,13},{6,14},{7,15},{8,0},{9,1},... | collective-permute-start | bytes 24968 | tf_op jit(solution)/shard_map/ppermute | solution.py:25
  142.0 10.8 %collective-permute-start.16 = (f32[128,32]{1,0:T(8,128)S(1)}, f32[128,32]{1,0:T(8,128)S(1)}, u32[]{:S(2)}, u32[]{:S(2)}) collective-permute-start(f32[128,32]{1,0:T(8,128)S(1)} %add.238), channel_id=1, source_target_pairs={{0,128},{32,160},{64,192},{96,224},{128,0},{160,32},{192,64},{224,... | collective-permute-start | bytes 49160 | tf_op jit(solution)/shard_map/ppermute | solution.py:25
  144.0 6.2 %collective-permute-start.32 = (f32[2080]{0:T(1024)S(1)}, f32[2080]{0:T(1024)S(1)}, u32[]{:S(2)}, u32[]{:S(2)}) collective-permute-start(f32[2080]{0:T(1024)S(1)} %add.259), channel_id=1, source_target_pairs={{0,16},{1,17},{2,18},{3,19},{4,20},{5,21},{6,22},{7,23},{8,24},{9,... | collective-permute-start | bytes 24968 | tf_op jit(solution)/shard_map/ppermute | solution.py:25
  146.8 30.7 %collective-permute-start.10 = (f32[256,32]{0,1:T(8,128)S(1)}, f32[256,32]{0,1:T(8,128)S(1)}, u32[]{:S(2)}, u32[]{:S(2)}) collective-permute-start(f32[256,32]{0,1:T(8,128)S(1)} %bitcast_add_fusion.1), channel_id=1, source_target_pairs={{0,2},{1,3},{2,0},{3,1},{4,6},{5,7},{6,4},{7,5},{8,10},{9,11},{10,... | collective-permute-start | bytes 98312 | tf_op jit(solution)/shard_map/ppermute | solution.py:25
  150.1 6.5 %collective-permute-start.33 = (f32[2080]{0:T(1024)S(1)}, f32[2080]{0:T(1024)S(1)}, u32[]{:S(2)}, u32[]{:S(2)}) collective-permute-start(f32[2080]{0:T(1024)S(1)} %add.260), channel_id=1, source_target_pairs={{0,32},{32,0},{64,96},{96,64},{128,160},{160,128},{192,224},{224,1... | collective-permute-start | bytes 24968 | tf_op jit(solution)/shard_map/ppermute | solution.py:25
  152.9 17.3 %collective-permute-start.17 = (f32[128,32]{1,0:T(8,128)S(1)}, f32[128,32]{1,0:T(8,128)S(1)}, u32[]{:S(2)}, u32[]{:S(2)}) collective-permute-start(f32[128,32]{1,0:T(8,128)S(1)} %add.239), channel_id=1, source_target_pairs={{0,256},{32,288},{64,320},{96,352},{128,384},{160,416},{192,448},{... | collective-permute-start | bytes 49160 | tf_op jit(solution)/shard_map/ppermute | solution.py:25
  156.6 9.5 %collective-permute-start.34 = (f32[2080]{0:T(1024)S(1)}, f32[2080]{0:T(1024)S(1)}, u32[]{:S(2)}, u32[]{:S(2)}) collective-permute-start(f32[2080]{0:T(1024)S(1)} %add.261), channel_id=1, source_target_pairs={{0,64},{32,96},{64,0},{96,32},{128,192},{160,224},{192,128},{224,1... | collective-permute-start | bytes 24968 | tf_op jit(solution)/shard_map/ppermute | solution.py:25
  166.1 15.5 %collective-permute-start.35 = (f32[2080]{0:T(1024)S(1)}, f32[2080]{0:T(1024)S(1)}, u32[]{:S(2)}, u32[]{:S(2)}) collective-permute-start(f32[2080]{0:T(1024)S(1)} %add.262), channel_id=1, source_target_pairs={{0,128},{32,160},{64,192},{96,224},{128,0},{160,32},{192,64},{224,... | collective-permute-start | bytes 24968 | tf_op jit(solution)/shard_map/ppermute | solution.py:25
  170.2 16.1 %collective-permute-start.19 = (bf16[128,32]{1,0:T(8,128)(2,1)S(1)}, bf16[128,32]{1,0:T(8,128)(2,1)S(1)}, u32[]{:S(2)}, u32[]{:S(2)}) collective-permute-start(bf16[128,32]{1,0:T(8,128)(2,1)S(1)} %add.240), channel_id=1, source_target_pairs={{1,0},{0,1},{33,2},{32,3},{65,4},{64,5},{97,6},{96,7},{129,8},{128... | collective-permute-start | bytes 24584 | tf_op jit(solution)/shard_map/ppermute | solution.py:149
  172.1 14.3 %collective-permute-start.18 = (bf16[128,32]{1,0:T(8,128)(2,1)S(1)}, bf16[128,32]{1,0:T(8,128)(2,1)S(1)}, u32[]{:S(2)}, u32[]{:S(2)}) collective-permute-start(bf16[128,32]{1,0:T(8,128)(2,1)S(1)} %add.240), channel_id=1, source_target_pairs={{0,0},{1,1},{32,2},{33,3},{64,4},{65,5},{96,6},{97,7},{128,8},{129... | collective-permute-start | bytes 24584 | tf_op jit(solution)/shard_map/ppermute | solution.py:149
  177.6 9.2 %collective-permute-start.11 = (f32[256,32]{0,1:T(8,128)S(1)}, f32[256,32]{0,1:T(8,128)S(1)}, u32[]{:S(2)}, u32[]{:S(2)}) collective-permute-start(f32[256,32]{0,1:T(8,128)S(1)} %add.233), channel_id=1, source_target_pairs={{0,4},{1,5},{2,6},{3,7},{4,0},{5,1},{6,2},{7,3},{8,12},{9,13},{10,... | collective-permute-start | bytes 98312 | tf_op jit(solution)/shard_map/ppermute | solution.py:25
  181.6 10.6 %collective-permute-start.36 = (f32[2080]{0:T(1024)S(1)}, f32[2080]{0:T(1024)S(1)}, u32[]{:S(2)}, u32[]{:S(2)}) collective-permute-start(f32[2080]{0:T(1024)S(1)} %add.263), channel_id=1, source_target_pairs={{0,256},{32,288},{64,320},{96,352},{128,384},{160,416},{192,448},{... | collective-permute-start | bytes 24968 | tf_op jit(solution)/shard_map/ppermute | solution.py:25
  186.8 9.7 %collective-permute-start.12 = (f32[256,32]{0,1:T(8,128)S(1)}, f32[256,32]{0,1:T(8,128)S(1)}, u32[]{:S(2)}, u32[]{:S(2)}) collective-permute-start(f32[256,32]{0,1:T(8,128)S(1)} %add.234), channel_id=1, source_target_pairs={{0,8},{1,9},{2,10},{3,11},{4,12},{5,13},{6,14},{7,15},{8,0},{9,1},... | collective-permute-start | bytes 98312 | tf_op jit(solution)/shard_map/ppermute | solution.py:25
  190.0 8.8 %collective-permute-start.24 = (f32[512,32]{0,1:T(8,128)S(1)}, f32[512,32]{0,1:T(8,128)S(1)}, u32[]{:S(2)}, u32[]{:S(2)}) collective-permute-start(f32[512,32]{0,1:T(8,128)S(1)} %convolution_bitcast_fusion), channel_id=1, source_target_pairs={{0,32},{32,0},{64,96},{96,64},{128,160},{160,128},{192,224},{224,1... | collective-permute-start | bytes 196616 | tf_op jit(solution)/shard_map/ppermute | solution.py:25
  196.5 8.1 %collective-permute-start.13 = (f32[256,32]{0,1:T(8,128)S(1)}, f32[256,32]{0,1:T(8,128)S(1)}, u32[]{:S(2)}, u32[]{:S(2)}) collective-permute-start(f32[256,32]{0,1:T(8,128)S(1)} %add.235), channel_id=1, source_target_pairs={{0,16},{1,17},{2,18},{3,19},{4,20},{5,21},{6,22},{7,23},{8,24},{9,... | collective-permute-start | bytes 98312 | tf_op jit(solution)/shard_map/ppermute | solution.py:25
  198.8 10.1 %collective-permute-start.25 = (f32[512,32]{0,1:T(8,128)S(1)}, f32[512,32]{0,1:T(8,128)S(1)}, u32[]{:S(2)}, u32[]{:S(2)}) collective-permute-start(f32[512,32]{0,1:T(8,128)S(1)} %add.250), channel_id=1, source_target_pairs={{0,64},{32,96},{64,0},{96,32},{128,192},{160,224},{192,128},{224,1... | collective-permute-start | bytes 196616 | tf_op jit(solution)/shard_map/ppermute | solution.py:25
  204.8 9.5 %collective-permute-start.20 = (f32[512,32]{0,1:T(8,128)S(1)}, f32[512,32]{0,1:T(8,128)S(1)}, u32[]{:S(2)}, u32[]{:S(2)}) collective-permute-start(f32[512,32]{0,1:T(8,128)S(1)} %convolution_bitcast_fusion.1), channel_id=1, source_target_pairs={{0,32},{32,0},{64,96},{96,64},{128,160},{160,128},{192,224},{224,1... | collective-permute-start | bytes 196616 | tf_op jit(solution)/shard_map/ppermute | solution.py:25
  208.9 12.1 %collective-permute-start.26 = (f32[512,32]{0,1:T(8,128)S(1)}, f32[512,32]{0,1:T(8,128)S(1)}, u32[]{:S(2)}, u32[]{:S(2)}) collective-permute-start(f32[512,32]{0,1:T(8,128)S(1)} %add.251), channel_id=1, source_target_pairs={{0,128},{32,160},{64,192},{96,224},{128,0},{160,32},{192,64},{224,... | collective-permute-start | bytes 196616 | tf_op jit(solution)/shard_map/ppermute | solution.py:25
  214.2 11.3 %collective-permute-start.21 = (f32[512,32]{0,1:T(8,128)S(1)}, f32[512,32]{0,1:T(8,128)S(1)}, u32[]{:S(2)}, u32[]{:S(2)}) collective-permute-start(f32[512,32]{0,1:T(8,128)S(1)} %add.246), channel_id=1, source_target_pairs={{0,64},{32,96},{64,0},{96,32},{128,192},{160,224},{192,128},{224,1... | collective-permute-start | bytes 196616 | tf_op jit(solution)/shard_map/ppermute | solution.py:25
  221.0 13.6 %collective-permute-start.27 = (f32[512,32]{0,1:T(8,128)S(1)}, f32[512,32]{0,1:T(8,128)S(1)}, u32[]{:S(2)}, u32[]{:S(2)}) collective-permute-start(f32[512,32]{0,1:T(8,128)S(1)} %add.252), channel_id=1, source_target_pairs={{0,256},{32,288},{64,320},{96,352},{128,384},{160,416},{192,448},{... | collective-permute-start | bytes 196616 | tf_op jit(solution)/shard_map/ppermute | solution.py:25
  225.6 6.2 %collective-permute-start.22 = (f32[512,32]{0,1:T(8,128)S(1)}, f32[512,32]{0,1:T(8,128)S(1)}, u32[]{:S(2)}, u32[]{:S(2)}) collective-permute-start(f32[512,32]{0,1:T(8,128)S(1)} %add.247), channel_id=1, source_target_pairs={{0,128},{32,160},{64,192},{96,224},{128,0},{160,32},{192,64},{224,... | collective-permute-start | bytes 196616 | tf_op jit(solution)/shard_map/ppermute | solution.py:25
  231.8 7.7 %collective-permute-start.23 = (f32[512,32]{0,1:T(8,128)S(1)}, f32[512,32]{0,1:T(8,128)S(1)}, u32[]{:S(2)}, u32[]{:S(2)}) collective-permute-start(f32[512,32]{0,1:T(8,128)S(1)} %add.248), channel_id=1, source_target_pairs={{0,256},{32,288},{64,320},{96,352},{128,384},{160,416},{192,448},{... | collective-permute-start | bytes 196616 | tf_op jit(solution)/shard_map/ppermute | solution.py:25
  (23 other events, 198.0 us)

commit v2 on v1

--- a/solution.py
+++ b/solution.py
@@ -18,13 +18,20 @@
     return lax.ppermute(x, axis, pairs)
 
 
-def butterfly(values, axis, count):
-    bit = 1
-    while bit < count:
-        pairs = [(i, i ^ bit) for i in range(count)]
-        values = jax.tree.map(lambda a, b: a + b, values, lax.ppermute(values, axis, pairs))
-        bit *= 2
-    return values
+def packed(parts):
+    return jnp.concatenate([p.ravel() for p in parts])
+
+
+def unpacked(flat, likes):
+    out, at = [], 0
+    for like in likes:
+        out.append(flat[at : at + like.size].reshape(like.shape))
+        at += like.size
+    return out
+
+
+def xor_round(flat, axis, count, bit):
+    return lax.ppermute(flat, axis, [(i, i ^ bit) for i in range(count)])
 
 
 def body(bin_features, w_left, w_right, depth_kernel, w_point, w_head, cotangent):
@@ -44,14 +51,13 @@
     left_proj = jnp.dot(bin_features, w_left, preferred_element_type=jnp.float32).astype(jnp.bfloat16)
     right_proj = jnp.dot(bin_features, w_right, preferred_element_type=jnp.float32).astype(jnp.bfloat16)
 
-    cot_rows = jnp.concatenate(
-        [
-            shifted(cotangent[:, rows - step :, :], "row", 1, row_count),
-            cotangent,
-            shifted(cotangent[:, :step, :], "row", -1, row_count),
-        ],
-        axis=1,
-    )
+    tail = (cotangent[:, rows - step :, :], left_proj[rows - halo :], right_proj[rows - halo :])
+    head = (cotangent[:, :step, :], left_proj[:halo], right_proj[:halo])
+    before = unpacked(shifted(packed(tail), "row", 1, row_count), tail)
+    after = unpacked(shifted(packed(head), "row", -1, row_count), head)
+    cot_rows = jnp.concatenate([before[0], cotangent, after[0]], axis=1)
+    left_ext = jnp.concatenate([before[1], left_proj, after[1]], axis=0)
+    right_panel = jnp.concatenate([before[2], right_proj, after[2]], axis=0)
     cot_ext = jnp.concatenate(
         [
             shifted(cot_rows[:, :, cols - step :], "col", 1, col_count),
@@ -61,33 +67,15 @@
         axis=2,
     )
 
-    left_ext = jnp.concatenate(
-        [
-            shifted(left_proj[rows - halo :], "row", 1, row_count),
-            left_proj,
-            shifted(left_proj[:halo], "row", -1, row_count),
-        ],
-        axis=0,
-    )
-
-    def target(a, b, shift):
-        tile = ratio * a + b % ratio + shift
-        return (b // ratio) * col_count + tile if 0 <= tile < col_count else None
-
-    def perm(shift):
+    def transpose_pairs():
         pairs = []
         for a in range(row_count):
             for b in range(col_count):
-                t = target(a, b, shift)
-                if t is not None:
-                    pairs.append((a * col_count + b, t))
+                pairs.append((a * col_count + b, (b // ratio) * col_count + ratio * a + b % ratio))
         return pairs
 
-    own_tile = lax.dynamic_slice_in_dim(right_proj, part * cols, cols, 0)
-    right_main = lax.ppermute(own_tile, ("row", "col"), perm(0))
-    right_before = lax.ppermute(own_tile[cols - halo :], ("row", "col"), perm(1))
-    right_after = lax.ppermute(own_tile[:halo], ("row", "col"), perm(-1))
-    right_ext = jnp.concatenate([right_before, right_main, right_after], axis=0)
+    own_tile = lax.dynamic_slice_in_dim(right_panel, part * cols, cols + 2 * halo, 0)
+    right_ext = lax.ppermute(own_tile, ("row", "col"), transpose_pairs())
 
     row_place = r * rows - halo + lax.broadcasted_iota(jnp.int32, (rows + 2 * halo, 1), 0)
     col_place = k * cols - halo + lax.broadcasted_iota(jnp.int32, (1, cols + 2 * halo), 1)
@@ -135,24 +123,30 @@
         "fsk,gsk->fg", hidden_state, trunk_grad_tile, preferred_element_type=jnp.float32
     )
     head_part = jnp.einsum("ydq,gdq->yg", trunk_matrix, cotangent, preferred_element_type=jnp.float32)
-    small = jnp.concatenate([kernel_part.ravel(), point_part.ravel(), head_part.ravel()])
+    small = packed((kernel_part, point_part, head_part))
 
-    left_total, small = butterfly((left_part, small), "col", col_count)
-    column_total = butterfly(right_part, "row", row_count)
-
-    def redistribute(shift):
-        pairs = []
-        for a in range(row_count):
-            for b in range(col_count):
-                src = (b // ratio) * col_count + ratio * a + (b % ratio + shift) % ratio
-                pairs.append((src, a * col_count + b))
-        return lax.ppermute(column_total, ("row", "col"), pairs)
-
-    received = jnp.stack([redistribute(q) for q in range(ratio)])
-    grad_right = jnp.concatenate(
-        [received[(m - part) % ratio] for m in range(ratio)], axis=0
-    ).astype(jnp.bfloat16)
-    grad_left = left_total.astype(jnp.bfloat16)
+    right_moved = lax.ppermute(right_part, ("row", "col"), transpose_pairs())
+    bit = ratio
+    while bit < col_count:
+        likes = (left_part, right_moved, small)
+        flat = packed(likes)
+        left_part, right_moved, small = unpacked(flat + xor_round(flat, "col", col_count, bit), likes)
+        bit *= 2
+    right_block = right_moved
+    bit = 1
+    while bit < ratio:
+        likes = (left_part, right_block, small)
+        flat = packed(likes)
+        got = unpacked(xor_round(flat, "col", col_count, bit), likes)
+        left_part = left_part + got[0]
+        small = small + got[2]
+        upper = (k & bit) != 0
+        right_block = jnp.concatenate(
+            [jnp.where(upper, got[1], right_block), jnp.where(upper, right_block, got[1])], axis=0
+        )
+        bit *= 2
+    grad_left = left_part.astype(jnp.bfloat16)
+    grad_right = right_block.astype(jnp.bfloat16)
 
     grad_features = (
         jnp.dot(grad_left, w_left.T, preferred_element_type=jnp.float32)
@@ -161,18 +155,18 @@
     contract = (((0,), (0,)), ((), ()))
     wleft_part = lax.dot_general(bin_features, grad_left, contract, preferred_element_type=jnp.float32)
     wright_part = lax.dot_general(bin_features, grad_right, contract, preferred_element_type=jnp.float32)
-    wleft_sum, wright_sum, small = butterfly((wleft_part, wright_part, small), "row", row_count)
+    bit = 1
+    while bit < row_count:
+        likes = (wleft_part, wright_part, small)
+        flat = packed(likes)
+        wleft_part, wright_part, small = unpacked(flat + xor_round(flat, "row", row_count, bit), likes)
+        bit *= 2
 
-    chans = w_left.shape[1]
-    heads = w_head.shape[1]
-    taps = kernel_part.size
-    kernel_sum = small[:taps].reshape(kernel_part.shape)
-    point_sum = small[taps : taps + chans * chans].reshape(chans, chans)
-    head_sum = small[taps + chans * chans :].reshape(chans, heads)
+    kernel_sum, point_sum, head_sum = unpacked(small, (kernel_part, point_part, head_part))
     return (
         grad_features,
-        grad_scale * wleft_sum,
-        grad_scale * wright_sum,
+        grad_scale * wleft_part,
+        grad_scale * wright_part,
         grad_scale * kernel_sum,
         grad_scale * point_sum,
         grad_scale * head_sum,

time: 242 us -> 182 us (0.75)
  starting transfers between devices: 143 us -> 68.7 us
  waiting for transfers between devices: 24.9 us -> 46.1 us
  other arithmetic: 42.4 us -> 31.3 us
  local copies, waits for them, and re-layouts: 12.2 us -> 17.8 us
    ppermute x31 -> x11, starting transfers between devices: 123 us -> 50.6 us  [the longest x9 37.2 us: xor_round(): return lax.ppermute(flat, axis, [(i, i ^ bit) for i in range(count)])]
    ppermute x31 -> x11, waiting for transfers between devices: 24.9 us -> 46.1 us  [the longest x9 40.6 us: xor_round(): return lax.ppermute(flat, axis, [(i, i ^ bit) for i in range(count)])]
    reduce_sum x1, other arithmetic: 19.4 us -> 6.95 us  [body(): right_part = jnp.sum(backward_pass, axis=1).T]
    ppermute x6 -> x4, starting transfers between devices: 20.6 us -> 18.1 us  [shifted(): return lax.ppermute(x, axis, pairs)]
    unnamed x72 -> x50, local copies, waits for them, and re-layouts: 6.53 us -> 8.12 us
  transfers between devices with their start and end apart: 37 -> 15, of which waited for: 10 -> 10; matrix products, arithmetic and copies ran while one was open for 20% -> 17% of each run, Pallas kernels for 0% -> 0%
where the time goes in v2:
time: 182 us; the launch traced here: 181 us
  starting transfers between devices  68.7 us (38%)
  waiting for transfers between devices  46.1 us (25%)
  other arithmetic  31.3 us (17%)
  local copies, waits for them, and re-layouts  17.8 us (10%)
  matrix products  15.7 us (9%)
    ppermute x9, waiting for transfers between devices, xor_round(): return lax.ppermute(flat, axis, [(i, i ^ bit) for i in range(count)])  40.6 us
    ppermute x9, starting transfers between devices, xor_round(): return lax.ppermute(flat, axis, [(i, i ^ bit) for i in range(count)])  37.2 us
    ppermute x4, starting transfers between devices, shifted(): return lax.ppermute(x, axis, pairs)  18.1 us
    add x1, other arithmetic, body(): conv_ext + depth_kernel[3 * a + b][:, None, None] * pair_ext[:, step * a:...  9.32 us
    unnamed x50, local copies, waits for them, and re-layouts  8.12 us
    reduce_sum x1, other arithmetic, body(): kern_terms.append(jnp.sum(conv_grad_tile * window, axis=(1, 2)))  7.48 us
    ppermute x1, starting transfers between devices, body(): right_moved = lax.ppermute(right_part, ('row', 'col'), transpose_pairs())  6.99 us
    reduce_sum x1, other arithmetic, body(): right_part = jnp.sum(backward_pass, axis=1).T  6.95 us
  transfers between devices with their start and end apart: 15, of which 10 were waited for; matrix products, arithmetic and copies ran while one was open for 17% of the time, Pallas kernels for 0%

profile of v2, /device:TPU:6, one launch (start us, length us, event | category | flops | bytes accessed | tf_op | source)
XLA Modules:
  0.0 181.1 jit_solution(13263790080062522069)
XLA Ops:
  0.6 0.9 copy-done
  1.6 0.9 convolution_convert_fusion
  2.8 0.9 convolution_convert_fusion.1
  4.0 0.9 fusion.52
  4.9 6.1 %collective-permute-start = (bf16[12800]{0:T(1024)(128)(2,1)S(1)}, bf16[12800]{0:T(1024)(128)(2,1)S(1)}, u32[]{:S(2)}, u32[]{:S(2)}) collective-permute-start(bf16[12800]{0:T(1024)(128)(2,1)S(1)} %pad_maximum_fusion.4), channel_id=1, source_target_pairs={{0,32},{32,64},{64,96},{96,128},{128,160},{160,192},{192,224},{224... | collective-permute-start | bytes 76808 | tf_op jit(solution)/shard_map/ppermute | solution.py:18
  11.3 7.0 %collective-permute-start.1 = (bf16[12800]{0:T(1024)(128)(2,1)S(1)}, bf16[12800]{0:T(1024)(128)(2,1)S(1)}, u32[]{:S(2)}, u32[]{:S(2)}) collective-permute-start(bf16[12800]{0:T(1024)(128)(2,1)S(1)} %pad_maximum_fusion.5), channel_id=1, source_target_pairs={{32,0},{64,32},{96,64},{128,96},{160,128},{192,160},{224,192},{256... | collective-permute-start | bytes 76808 | tf_op jit(solution)/shard_map/ppermute | solution.py:18
  18.5 1.6 slice_bitcast_fusion.8
  20.1 2.1 %copy.42 = bf16[24,256,128]{1,0,2:T(8,128)(2,1)S(1)} copy(bf16[24,256,128]{2,1,0:T(8,128)(2,1)} %param.13) | data formatting | bytes 3145728 | tf_op args[6]
  22.8 6.5 %collective-permute-start.4 = (bf16[144,32]{0,1:T(8,128)(2,1)S(1)}, bf16[144,32]{0,1:T(8,128)(2,1)S(1)}, u32[]{:S(2)}, u32[]{:S(2)}) collective-permute-start(bf16[144,32]{0,1:T(8,128)(2,1)S(1)} %fusion.36), channel_id=1, source_target_pairs={{0,0},{1,1},{2,32},{3,33},{4,64},{5,65},{6,96},{7,97},{8,128},{9,1... | collective-permute-start | bytes 27656 | tf_op jit(solution)/shard_map/ppermute | solution.py:78
  30.6 0.9 pad_maximum_fusion.3
  31.5 1.3 collective-permute-start.3
  32.8 3.7 %collective-permute-start.2 = (bf16[24,264,4]{1,0,2:T(8,128)(2,1)}, bf16[24,264,4]{1,0,2:T(8,128)(2,1)}, u32[]{:S(2)}, u32[]{:S(2)}) collective-permute-start(bf16[24,264,4]{1,0,2:T(8,128)(2,1)} %get-tuple-element.29), channel_id=1, source_target_pairs={{0,1},{1,2},{2,3},{3,4},{4,5},{5,6},{6,7},{7,8},{8,9},{9,10},{10,1... | collective-permute-start | bytes 152072 | tf_op jit(solution)/shard_map/ppermute | solution.py:18
  36.5 0.7 convert_bitcast_fusion
  37.8 0.9 copy.48
  38.6 2.2 %select_convert_fusion = bf16[32,272,144]{1,0,2:T(8,128)(2,1)S(1)} fusion(f32[32,144]{0,1:T(8,128)S(1)} %copy.48, f32[32,272]{1,0:T(8,128)} %convert_bitcast_fusion, pred[272,144]{0,1:T(8,128)(4,1)S(1)} %and_and_fusion), kind=kLoop, calls=%fused_computation.10 | loop fusion | flops 3760128 | bytes 2599168 | tf_op jit(solution)/shard_map/convert_element_type | solution.py:84
  40.9 9.3 %multiply_add_fusion = f32[32,264,136]{1,0,2:T(8,128)S(1)} fusion(bf16[32,272,144]{1,0,2:T(8,128)(2,1)S(1)} %select_convert_fusion, f32[32]{0:T(128)} %get-tuple-element.52, f32[32]{0:T(128)} %get-tuple-element.53, f32[32]{0:T(128)} %get-tuple-element.46, f32[32]{0:T(128)} %get-tuple-element.47, f32[32]{0:T(128)} %get-tuple-element.48, ...), kind=kLoop, calls=%fused_computation.13 | loop fusion | flops 29872128 | bytes 25277568 | tf_op jit(solution)/shard_map/add | solution.py:91
  50.2 2.8 %copy-done.3 = f32[32,264,136]{1,0,2:T(8,128)} copy-done((f32[32,264,136]{1,0,2:T(8,128)}, f32[32,264,136]{1,0,2:T(8,128)S(1)}, u32[]{:S(2)}) %copy-start.3) | copy-done | bytes 4595736
  53.0 2.6 %multiply_convert_fusion.1 = bf16[32,256,128]{1,0,2:T(8,128)(2,1)} fusion(f32[32,264,136]{1,0,2:T(8,128)S(1)} %multiply_add_fusion), kind=kLoop, calls=%fused_computation.31 | loop fusion | flops 5242880 | bytes 6291456 | tf_op jit(solution)/shard_map/convert_element_type | solution.py:95
  55.6 4.6 %fusion.30 = f32[32,24]{1,0:T(8,128)S(1)} fusion(bf16[24,256,128]{1,0,2:T(8,128)(2,1)S(1)} %copy.42, bf16[32,256,128]{1,0,2:T(8,128)(2,1)} %multiply_convert_fusion.1, bf16[32,272,144]{1,0,2:T(8,128)(2,1)} %copy-done.1, bf16[32,32]{1,0:T(8,128)(2,1)S(1)} %copy-done.19), kind=kOutput, calls=%fused_computation.51 | convolution fusion | flops 120586240 | bytes 5772288 | tf_op jit(solution)/shard_map/ydq,gdq->yg/dot_general | solution.py:125
  60.2 0.7 reshape.300
  60.9 3.5 %fusion.16 = bf16[32,264,136]{1,0,2:T(8,128)(2,1)S(1)} fusion(bf16[24,264,4]{1,0,2:T(8,128)(2,1)} %collective-permute-done.3, bf16[24,4,128]{1,0,2:T(8,128)(2,1)S(1)} %copy.43, bf16[24,256,128]{1,0,2:T(8,128)(2,1)} %copy-done.4, bf16[24,4,128]{1,0,2:T(8,128)(2,1)} %copy-done.5, bf16[24,264,4]{1,0,2:T(8,128)(2,1)} %collective-permute-done.2, ...), kind=kOutput, calls=%fused_computation.32 | convolution fusion | flops 66063360 | bytes 4022784 | tf_op jit(solution)/shard_map/ch,hij->cij/dot_general | solution.py:101
  64.5 3.3 %fusion = bf16[32,264,136]{1,0,2:T(8,128)(2,1)S(1)} fusion(f32[32,264,136]{1,0,2:T(8,128)S(1)} %bitcast.82, bf16[32,264,136]{1,0,2:T(8,128)(2,1)S(1)} %fusion.16, bf16[32,32]{1,0:T(8,128)(2,1)S(1)} %copy-done.20), kind=kOutput, calls=%fused_computation.12 | convolution fusion | flops 83871744 | bytes 9193472 | tf_op jit(solution)/shard_map/co,oij->cij/dot_general | solution.py:103
  68.0 7.0 %fusion.51 = (f32[32,128]{0,1:T(8,128)S(1)}, f32[32,256]{1,0:T(8,128)S(1)}) fusion(bf16[32,264,136]{1,0,2:T(8,128)(2,1)S(1)} %fusion, f32[32]{0:T(128)S(1)} %copy-done.17, f32[32]{0:T(128)S(1)} %copy-done.18, f32[32]{0:T(128)S(1)} %copy-done.11, f32[32]{0:T(128)S(1)} %copy-done.12, f32[32]{0:T(128)S(1)} %copy-done.13, f32[32]{0:T(128)S(1)} %copy-done.14, ...), kind=kLoop, calls=%fused_computation.102 | loop fusion | flops 31444992 | bytes 21021824 | tf_op jit(solution)/shard_map/reduce_sum | solution.py:121
  74.9 7.5 %fusion.15 = (f32[32]{0:T(128)S(1)}, f32[32]{0:T(128)S(1)}, f32[32]{0:T(128)S(1)}, f32[32]{0:T(128)S(1)}, f32[32]{0:T(128)S(1)}, /*index=5*/f32[32]{0:T(128)S(1)}, f32[32]{0:T(128)S(1)}, f32[32]{0:T(128)S(1)}, f32[32]{0:T(128)S(1)}) fusion(bf16[32,272,144]{1,0,2:T(8,128)(2,1)S(1)} %copy-done.2, bf16[32,264,136]{1,0,2:T(8,128)(2,1)S(1)} %fusion), kind=kLoop, calls=%fused_computation.30 | loop fusion | flops 29359840 | bytes 20972672 | tf_op jit(solution)/shard_map/reduce_sum | solution.py:118
  82.4 7.0 %collective-permute-start.5 = (f32[128,32]{1,0:T(8,128)S(1)}, f32[128,32]{1,0:T(8,128)S(1)}, u32[]{:S(2)}, u32[]{:S(2)}) collective-permute-start(f32[128,32]{1,0:T(8,128)S(1)} %bitcast.88), channel_id=1, source_target_pairs={{0,0},{1,1},{2,32},{3,33},{4,64},{5,65},{6,96},{7,97},{8,128},{9,1... | collective-permute-start | bytes 49160 | tf_op jit(solution)/shard_map/ppermute | solution.py:128
  89.5 1.0 fusion.31
  90.9 5.5 %collective-permute-done.5 = f32[128,32]{1,0:T(8,128)S(1)} collective-permute-done((f32[128,32]{1,0:T(8,128)S(1)}, f32[128,32]{1,0:T(8,128)S(1)}, u32[]{:S(2)}, u32[]{:S(2)}) %collective-permute-start.5) | collective-permute-done | bytes 16416 | tf_op jit(solution)/shard_map/ppermute | solution.py:128
  96.5 7.0 %collective-permute-start.6 = (f32[14368]{0:T(1024)S(1)}, f32[14368]{0:T(1024)S(1)}, u32[]{:S(2)}, u32[]{:S(2)}) collective-permute-start(f32[14368]{0:T(1024)S(1)} %concatenate.48), channel_id=1, source_target_pairs={{0,2},{1,3},{2,0},{3,1},{4,6},{5,7},{6,4},{7,5},{8,10},{9,11},{10,... | collective-permute-start | bytes 172424 | tf_op jit(solution)/shard_map/ppermute | solution.py:34
  103.6 2.3 %collective-permute-done.6 = f32[14368]{0:T(1024)S(1)} collective-permute-done((f32[14368]{0:T(1024)S(1)}, f32[14368]{0:T(1024)S(1)}, u32[]{:S(2)}, u32[]{:S(2)}) %collective-permute-start.6) | collective-permute-done | bytes 57504 | tf_op jit(solution)/shard_map/ppermute | solution.py:34
  105.9 5.7 %collective-permute-start.7 = (f32[14368]{0:T(1024)S(1)}, f32[14368]{0:T(1024)S(1)}, u32[]{:S(2)}, u32[]{:S(2)}) collective-permute-start(f32[14368]{0:T(1024)S(1)} %add.175), channel_id=1, source_target_pairs={{0,4},{1,5},{2,6},{3,7},{4,0},{5,1},{6,2},{7,3},{8,12},{9,13},{10,... | collective-permute-start | bytes 172424 | tf_op jit(solution)/shard_map/ppermute | solution.py:34
  111.6 2.8 %collective-permute-done.7 = f32[14368]{0:T(1024)S(1)} collective-permute-done((f32[14368]{0:T(1024)S(1)}, f32[14368]{0:T(1024)S(1)}, u32[]{:S(2)}, u32[]{:S(2)}) %collective-permute-start.7) | collective-permute-done | bytes 57504 | tf_op jit(solution)/shard_map/ppermute | solution.py:34
  114.5 5.7 %collective-permute-start.8 = (f32[14368]{0:T(1024)S(1)}, f32[14368]{0:T(1024)S(1)}, u32[]{:S(2)}, u32[]{:S(2)}) collective-permute-start(f32[14368]{0:T(1024)S(1)} %add.176), channel_id=1, source_target_pairs={{0,8},{1,9},{2,10},{3,11},{4,12},{5,13},{6,14},{7,15},{8,0},{9,1},... | collective-permute-start | bytes 172424 | tf_op jit(solution)/shard_map/ppermute | solution.py:34
  120.2 4.9 %collective-permute-done.8 = f32[14368]{0:T(1024)S(1)} collective-permute-done((f32[14368]{0:T(1024)S(1)}, f32[14368]{0:T(1024)S(1)}, u32[]{:S(2)}, u32[]{:S(2)}) %collective-permute-start.8) | collective-permute-done | bytes 57504 | tf_op jit(solution)/shard_map/ppermute | solution.py:34
  125.2 3.0 %collective-permute-start.9 = (f32[14368]{0:T(1024)S(1)}, f32[14368]{0:T(1024)S(1)}, u32[]{:S(2)}, u32[]{:S(2)}) collective-permute-start(f32[14368]{0:T(1024)S(1)} %add.177), channel_id=1, source_target_pairs={{0,16},{1,17},{2,18},{3,19},{4,20},{5,21},{6,22},{7,23},{8,24},{9,... | collective-permute-start | bytes 172424 | tf_op jit(solution)/shard_map/ppermute | solution.py:34
  128.2 3.1 %collective-permute-done.9 = f32[14368]{0:T(1024)S(1)} collective-permute-done((f32[14368]{0:T(1024)S(1)}, f32[14368]{0:T(1024)S(1)}, u32[]{:S(2)}, u32[]{:S(2)}) %collective-permute-start.9) | collective-permute-done | bytes 57504 | tf_op jit(solution)/shard_map/ppermute | solution.py:34
  131.3 1.9 %collective-permute-start.10 = (f32[14368]{0:T(1024)S(1)}, f32[14368]{0:T(1024)S(1)}, u32[]{:S(2)}, u32[]{:S(2)}) collective-permute-start(f32[14368]{0:T(1024)S(1)} %add.178), channel_id=1, source_target_pairs={{0,1},{1,0},{2,3},{3,2},{4,5},{5,4},{6,7},{7,6},{8,9},{9,8},{10,11... | collective-permute-start | bytes 172424 | tf_op jit(solution)/shard_map/ppermute | solution.py:34
  133.2 1.2 collective-permute-done.10
  135.8 3.1 %collective-permute-start.11 = (f32[34848]{0:T(1024)S(1)}, f32[34848]{0:T(1024)S(1)}, u32[]{:S(2)}, u32[]{:S(2)}) collective-permute-start(f32[34848]{0:T(1024)S(1)} %pad_maximum_fusion), channel_id=1, source_target_pairs={{0,32},{32,0},{64,96},{96,64},{128,160},{160,128},{192,224},{224,1... | collective-permute-start | bytes 418184 | tf_op jit(solution)/shard_map/ppermute | solution.py:34
  138.9 8.5 %collective-permute-done.11 = f32[34848]{0:T(1024)S(1)} collective-permute-done((f32[34848]{0:T(1024)S(1)}, f32[34848]{0:T(1024)S(1)}, u32[]{:S(2)}, u32[]{:S(2)}) %collective-permute-start.11) | collective-permute-done | bytes 139424 | tf_op jit(solution)/shard_map/ppermute | solution.py:34
  147.5 6.2 %collective-permute-start.12 = (f32[34848]{0:T(1024)S(1)}, f32[34848]{0:T(1024)S(1)}, u32[]{:S(2)}, u32[]{:S(2)}) collective-permute-start(f32[34848]{0:T(1024)S(1)} %fusion.50), channel_id=1, source_target_pairs={{0,64},{32,96},{64,0},{96,32},{128,192},{160,224},{192,128},{224,1... | collective-permute-start | bytes 418184 | tf_op jit(solution)/shard_map/ppermute | solution.py:34
  153.7 7.8 %collective-permute-done.12 = f32[34848]{0:T(1024)S(1)} collective-permute-done((f32[34848]{0:T(1024)S(1)}, f32[34848]{0:T(1024)S(1)}, u32[]{:S(2)}, u32[]{:S(2)}) %collective-permute-start.12) | collective-permute-done | bytes 139424 | tf_op jit(solution)/shard_map/ppermute | solution.py:34
  161.5 1.9 %collective-permute-start.13 = (f32[34848]{0:T(1024)S(1)}, f32[34848]{0:T(1024)S(1)}, u32[]{:S(2)}, u32[]{:S(2)}) collective-permute-start(f32[34848]{0:T(1024)S(1)} %add.183), channel_id=1, source_target_pairs={{0,128},{32,160},{64,192},{96,224},{128,0},{160,32},{192,64},{224,... | collective-permute-start | bytes 418184 | tf_op jit(solution)/shard_map/ppermute | solution.py:34
  163.7 4.8 %collective-permute-done.13 = f32[34848]{0:T(1024)S(1)} collective-permute-done((f32[34848]{0:T(1024)S(1)}, f32[34848]{0:T(1024)S(1)}, u32[]{:S(2)}, u32[]{:S(2)}) %collective-permute-start.13) | collective-permute-done | bytes 139424 | tf_op jit(solution)/shard_map/ppermute | solution.py:34
  168.5 2.4 %collective-permute-start.14 = (f32[34848]{0:T(1024)S(1)}, f32[34848]{0:T(1024)S(1)}, u32[]{:S(2)}, u32[]{:S(2)}) collective-permute-start(f32[34848]{0:T(1024)S(1)} %add.184), channel_id=1, source_target_pairs={{0,256},{32,288},{64,320},{96,352},{128,384},{160,416},{192,448},{... | collective-permute-start | bytes 418184 | tf_op jit(solution)/shard_map/ppermute | solution.py:34
  171.0 0.9 fusion.29
  171.9 5.2 %collective-permute-done.14 = f32[34848]{0:T(1024)S(1)} collective-permute-done((f32[34848]{0:T(1024)S(1)}, f32[34848]{0:T(1024)S(1)}, u32[]{:S(2)}, u32[]{:S(2)}) %collective-permute-start.14) | collective-permute-done | bytes 139424 | tf_op jit(solution)/shard_map/ppermute | solution.py:34
  177.4 0.7 copy.57
  178.2 0.7 copy.58
  (122 shorter events, 8.2 us)
Async XLA Ops:
  0.6 1.0 copy-start
  4.9 17.4 %collective-permute-start = (bf16[12800]{0:T(1024)(128)(2,1)S(1)}, bf16[12800]{0:T(1024)(128)(2,1)S(1)}, u32[]{:S(2)}, u32[]{:S(2)}) collective-permute-start(bf16[12800]{0:T(1024)(128)(2,1)S(1)} %pad_maximum_fusion.4), channel_id=1, source_target_pairs={{0,32},{32,64},{64,96},{96,128},{128,160},{160,192},{192,224},{224... | collective-permute-start | bytes 76808 | tf_op jit(solution)/shard_map/ppermute | solution.py:18
  11.3 11.2 %collective-permute-start.1 = (bf16[12800]{0:T(1024)(128)(2,1)S(1)}, bf16[12800]{0:T(1024)(128)(2,1)S(1)}, u32[]{:S(2)}, u32[]{:S(2)}) collective-permute-start(bf16[12800]{0:T(1024)(128)(2,1)S(1)} %pad_maximum_fusion.5), channel_id=1, source_target_pairs={{32,0},{64,32},{96,64},{128,96},{160,128},{192,160},{224,192},{256... | collective-permute-start | bytes 76808 | tf_op jit(solution)/shard_map/ppermute | solution.py:18
  22.3 33.3 %copy-start.4 = (bf16[24,256,128]{1,0,2:T(8,128)(2,1)}, bf16[24,256,128]{1,0,2:T(8,128)(2,1)S(1)}, u32[]{:S(2)}) copy-start(bf16[24,256,128]{1,0,2:T(8,128)(2,1)S(1)} %copy.42) | copy-start | bytes 4718596
  22.8 14.4 %collective-permute-start.4 = (bf16[144,32]{0,1:T(8,128)(2,1)S(1)}, bf16[144,32]{0,1:T(8,128)(2,1)S(1)}, u32[]{:S(2)}, u32[]{:S(2)}) collective-permute-start(bf16[144,32]{0,1:T(8,128)(2,1)S(1)} %fusion.36), channel_id=1, source_target_pairs={{0,0},{1,1},{2,32},{3,33},{4,64},{5,65},{6,96},{7,97},{8,128},{9,1... | collective-permute-start | bytes 27656 | tf_op jit(solution)/shard_map/ppermute | solution.py:78
  30.6 19.6 %copy-start.5 = (bf16[24,4,128]{1,0,2:T(8,128)(2,1)}, bf16[24,4,128]{1,0,2:T(8,128)(2,1)S(1)}, u32[]{:S(2)}) copy-start(bf16[24,4,128]{1,0,2:T(8,128)(2,1)S(1)} %copy.41) | copy-start | bytes 73732
  31.5 29.4 %collective-permute-start.3 = (bf16[24,264,4]{1,0,2:T(8,128)(2,1)}, bf16[24,264,4]{1,0,2:T(8,128)(2,1)}, u32[]{:S(2)}, u32[]{:S(2)}) collective-permute-start(bf16[24,264,4]{1,0,2:T(8,128)(2,1)} %get-tuple-element.30), channel_id=1, source_target_pairs={{1,0},{2,1},{3,2},{4,3},{5,4},{6,5},{7,6},{8,7},{9,8},{10,9},{11,1... | collective-permute-start | bytes 152072 | tf_op jit(solution)/shard_map/ppermute | solution.py:18
  32.8 28.1 %collective-permute-start.2 = (bf16[24,264,4]{1,0,2:T(8,128)(2,1)}, bf16[24,264,4]{1,0,2:T(8,128)(2,1)}, u32[]{:S(2)}, u32[]{:S(2)}) collective-permute-start(bf16[24,264,4]{1,0,2:T(8,128)(2,1)} %get-tuple-element.29), channel_id=1, source_target_pairs={{0,1},{1,2},{2,3},{3,4},{4,5},{5,6},{6,7},{7,8},{8,9},{9,10},{10,1... | collective-permute-start | bytes 152072 | tf_op jit(solution)/shard_map/ppermute | solution.py:18
  40.9 9.3 %copy-start.1 = (bf16[32,272,144]{1,0,2:T(8,128)(2,1)}, bf16[32,272,144]{1,0,2:T(8,128)(2,1)S(1)}, u32[]{:S(2)}) copy-start(bf16[32,272,144]{1,0,2:T(8,128)(2,1)S(1)} %select_convert_fusion) | copy-start | bytes 7520260
  50.2 2.8 %copy-start.3 = (f32[32,264,136]{1,0,2:T(8,128)}, f32[32,264,136]{1,0,2:T(8,128)S(1)}, u32[]{:S(2)}) copy-start(f32[32,264,136]{1,0,2:T(8,128)S(1)} %multiply_add_fusion) | copy-start | bytes 13787140
  53.0 2.6 %copy-start.19 = (bf16[32,32]{1,0:T(8,128)(2,1)S(1)}, bf16[32,32]{1,0:T(8,128)(2,1)}, u32[]{:S(2)}) copy-start(bf16[32,32]{1,0:T(8,128)(2,1)} %param.11) | copy-start | bytes 6148
  60.2 4.2 %slice-start = ((s8[6684672]{0:T(1024)(128)(4,1)}), s8[2490368]{0:T(1024)(128)(4,1)S(1)}, s32[]{:S(2)}) async-start(s8[6684672]{0:T(1024)(128)(4,1)} %bitcast.81), calls=%async_computation | async-start | bytes 4980736
  60.9 3.5 %slice-start.1 = ((s8[6684672]{0:T(1024)(128)(4,1)}), s8[4194304]{0:T(1024)(128)(4,1)S(1)}, s32[]{:S(2)}) async-start(s8[6684672]{0:T(1024)(128)(4,1)} %bitcast.81), calls=%async_computation.1 | async-start | bytes 8388608
  60.9 3.6 %copy-start.20 = (bf16[32,32]{1,0:T(8,128)(2,1)S(1)}, bf16[32,32]{1,0:T(8,128)(2,1)}, u32[]{:S(2)}) copy-start(bf16[32,32]{1,0:T(8,128)(2,1)} %param.11) | copy-start | bytes 6148
  64.4 3.4 %copy-start.10 = (f32[32]{0:T(128)S(1)}, f32[32]{0:T(128)}, u32[]{:S(2)}) copy-start(f32[32]{0:T(128)} %get-tuple-element.45) | copy-start | bytes 388
  64.5 3.4 %copy-start.11 = (f32[32]{0:T(128)S(1)}, f32[32]{0:T(128)}, u32[]{:S(2)}) copy-start(f32[32]{0:T(128)} %get-tuple-element.46) | copy-start | bytes 388
  64.5 3.4 %copy-start.12 = (f32[32]{0:T(128)S(1)}, f32[32]{0:T(128)}, u32[]{:S(2)}) copy-start(f32[32]{0:T(128)} %get-tuple-element.47) | copy-start | bytes 388
  64.5 3.4 %copy-start.13 = (f32[32]{0:T(128)S(1)}, f32[32]{0:T(128)}, u32[]{:S(2)}) copy-start(f32[32]{0:T(128)} %get-tuple-element.48) | copy-start | bytes 388
  64.5 3.4 %copy-start.14 = (f32[32]{0:T(128)S(1)}, f32[32]{0:T(128)}, u32[]{:S(2)}) copy-start(f32[32]{0:T(128)} %get-tuple-element.49) | copy-start | bytes 388
  64.5 3.4 %copy-start.15 = (f32[32]{0:T(128)S(1)}, f32[32]{0:T(128)}, u32[]{:S(2)}) copy-start(f32[32]{0:T(128)} %get-tuple-element.50) | copy-start | bytes 388
  64.5 3.4 %copy-start.16 = (f32[32]{0:T(128)S(1)}, f32[32]{0:T(128)}, u32[]{:S(2)}) copy-start(f32[32]{0:T(128)} %get-tuple-element.51) | copy-start | bytes 388
  64.5 3.4 %copy-start.17 = (f32[32]{0:T(128)S(1)}, f32[32]{0:T(128)}, u32[]{:S(2)}) copy-start(f32[32]{0:T(128)} %get-tuple-element.52) | copy-start | bytes 388
  64.5 3.4 %copy-start.18 = (f32[32]{0:T(128)S(1)}, f32[32]{0:T(128)}, u32[]{:S(2)}) copy-start(f32[32]{0:T(128)} %get-tuple-element.53) | copy-start | bytes 388
  67.9 7.0 %copy-start.2 = (bf16[32,272,144]{1,0,2:T(8,128)(2,1)S(1)}, bf16[32,272,144]{1,0,2:T(8,128)(2,1)}, u32[]{:S(2)}) copy-start(bf16[32,272,144]{1,0,2:T(8,128)(2,1)} %copy-done.1) | copy-start | bytes 7520260
  74.9 14.5 %copy-start.6 = (bf16[32,256,128]{1,0,2:T(8,128)(2,1)S(1)}, bf16[32,256,128]{1,0,2:T(8,128)(2,1)}, u32[]{:S(2)}) copy-start(bf16[32,256,128]{1,0,2:T(8,128)(2,1)} %multiply_convert_fusion.1) | copy-start | bytes 6291460
  82.4 14.0 %copy-start.9 = (f32[768]{0:T(1024)S(1)}, f32[768]{0:T(1024)}, u32[]{:S(2)}) copy-start(f32[768]{0:T(1024)} %reshape.300) | copy-start | bytes 9220
  82.4 81.0 %copy-start.8 = (bf16[512,32]{0,1:T(8,128)(2,1)S(1)}, bf16[512,32]{0,1:T(8,128)(2,1)}, u32[]{:S(2)}) copy-start(bf16[512,32]{0,1:T(8,128)(2,1)} %param.9) | copy-start | bytes 98308
  82.4 88.5 %copy-start.7 = (bf16[512,32]{0,1:T(8,128)(2,1)S(1)}, bf16[512,32]{0,1:T(8,128)(2,1)}, u32[]{:S(2)}) copy-start(bf16[512,32]{0,1:T(8,128)(2,1)} %param.8) | copy-start | bytes 98308
  82.4 13.9 %collective-permute-start.5 = (f32[128,32]{1,0:T(8,128)S(1)}, f32[128,32]{1,0:T(8,128)S(1)}, u32[]{:S(2)}, u32[]{:S(2)}) collective-permute-start(f32[128,32]{1,0:T(8,128)S(1)} %bitcast.88), channel_id=1, source_target_pairs={{0,0},{1,1},{2,32},{3,33},{4,64},{5,65},{6,96},{7,97},{8,128},{9,1... | collective-permute-start | bytes 49160 | tf_op jit(solution)/shard_map/ppermute | solution.py:128
  96.5 9.3 %collective-permute-start.6 = (f32[14368]{0:T(1024)S(1)}, f32[14368]{0:T(1024)S(1)}, u32[]{:S(2)}, u32[]{:S(2)}) collective-permute-start(f32[14368]{0:T(1024)S(1)} %concatenate.48), channel_id=1, source_target_pairs={{0,2},{1,3},{2,0},{3,1},{4,6},{5,7},{6,4},{7,5},{8,10},{9,11},{10,... | collective-permute-start | bytes 172424 | tf_op jit(solution)/shard_map/ppermute | solution.py:34
  105.9 8.6 %collective-permute-start.7 = (f32[14368]{0:T(1024)S(1)}, f32[14368]{0:T(1024)S(1)}, u32[]{:S(2)}, u32[]{:S(2)}) collective-permute-start(f32[14368]{0:T(1024)S(1)} %add.175), channel_id=1, source_target_pairs={{0,4},{1,5},{2,6},{3,7},{4,0},{5,1},{6,2},{7,3},{8,12},{9,13},{10,... | collective-permute-start | bytes 172424 | tf_op jit(solution)/shard_map/ppermute | solution.py:34
  114.5 10.7 %collective-permute-start.8 = (f32[14368]{0:T(1024)S(1)}, f32[14368]{0:T(1024)S(1)}, u32[]{:S(2)}, u32[]{:S(2)}) collective-permute-start(f32[14368]{0:T(1024)S(1)} %add.176), channel_id=1, source_target_pairs={{0,8},{1,9},{2,10},{3,11},{4,12},{5,13},{6,14},{7,15},{8,0},{9,1},... | collective-permute-start | bytes 172424 | tf_op jit(solution)/shard_map/ppermute | solution.py:34
  125.2 6.1 %collective-permute-start.9 = (f32[14368]{0:T(1024)S(1)}, f32[14368]{0:T(1024)S(1)}, u32[]{:S(2)}, u32[]{:S(2)}) collective-permute-start(f32[14368]{0:T(1024)S(1)} %add.177), channel_id=1, source_target_pairs={{0,16},{1,17},{2,18},{3,19},{4,20},{5,21},{6,22},{7,23},{8,24},{9,... | collective-permute-start | bytes 172424 | tf_op jit(solution)/shard_map/ppermute | solution.py:34
  131.3 3.1 %collective-permute-start.10 = (f32[14368]{0:T(1024)S(1)}, f32[14368]{0:T(1024)S(1)}, u32[]{:S(2)}, u32[]{:S(2)}) collective-permute-start(f32[14368]{0:T(1024)S(1)} %add.178), channel_id=1, source_target_pairs={{0,1},{1,0},{2,3},{3,2},{4,5},{5,4},{6,7},{7,6},{8,9},{9,8},{10,11... | collective-permute-start | bytes 172424 | tf_op jit(solution)/shard_map/ppermute | solution.py:34
  135.8 11.7 %collective-permute-start.11 = (f32[34848]{0:T(1024)S(1)}, f32[34848]{0:T(1024)S(1)}, u32[]{:S(2)}, u32[]{:S(2)}) collective-permute-start(f32[34848]{0:T(1024)S(1)} %pad_maximum_fusion), channel_id=1, source_target_pairs={{0,32},{32,0},{64,96},{96,64},{128,160},{160,128},{192,224},{224,1... | collective-permute-start | bytes 418184 | tf_op jit(solution)/shard_map/ppermute | solution.py:34
  147.5 14.0 %collective-permute-start.12 = (f32[34848]{0:T(1024)S(1)}, f32[34848]{0:T(1024)S(1)}, u32[]{:S(2)}, u32[]{:S(2)}) collective-permute-start(f32[34848]{0:T(1024)S(1)} %fusion.50), channel_id=1, source_target_pairs={{0,64},{32,96},{64,0},{96,32},{128,192},{160,224},{192,128},{224,1... | collective-permute-start | bytes 418184 | tf_op jit(solution)/shard_map/ppermute | solution.py:34
  161.5 7.0 %collective-permute-start.13 = (f32[34848]{0:T(1024)S(1)}, f32[34848]{0:T(1024)S(1)}, u32[]{:S(2)}, u32[]{:S(2)}) collective-permute-start(f32[34848]{0:T(1024)S(1)} %add.183), channel_id=1, source_target_pairs={{0,128},{32,160},{64,192},{96,224},{128,0},{160,32},{192,64},{224,... | collective-permute-start | bytes 418184 | tf_op jit(solution)/shard_map/ppermute | solution.py:34
  168.5 8.5 %collective-permute-start.14 = (f32[34848]{0:T(1024)S(1)}, f32[34848]{0:T(1024)S(1)}, u32[]{:S(2)}, u32[]{:S(2)}) collective-permute-start(f32[34848]{0:T(1024)S(1)} %add.184), channel_id=1, source_target_pairs={{0,256},{32,288},{64,320},{96,352},{128,384},{160,416},{192,448},{... | collective-permute-start | bytes 418184 | tf_op jit(solution)/shard_map/ppermute | solution.py:34

commit v3 on v2

--- a/solution.py
+++ b/solution.py
@@ -3,14 +3,108 @@
 import jax
 import jax.numpy as jnp
 from jax import lax
+from jax.experimental import pallas as pl
+from jax.experimental.pallas import tpu as pltpu
 from jax.sharding import PartitionSpec as P
 
 DILATION_STEP = 4
+LANES = 256
+FWD = 24
+BWD = 32
 
 
 def silu_slope(values):
     logistic = jax.nn.sigmoid(values)
     return logistic * (1.0 + values * (1.0 - logistic))
+
+
+def shift_left(x, n):
+    return x if n == 0 else pltpu.roll(x, LANES - n, 1)
+
+
+def depth_kernel_body(taps_ref, pair_ref, gh_ref, gt_ref, hid_ref, gp_ref, kern_ref, pair_s, gh_s, conv_s, gc_s):
+    c = pl.program_id(0)
+    chans = pl.num_programs(0)
+    pcol = pair_ref.shape[2]
+    erow, ecol = gh_ref.shape[1], gh_ref.shape[2]
+    rows, cols = gt_ref.shape[1], gt_ref.shape[2]
+    tap = [taps_ref[t * chans + c] for t in range(9)]
+    pair_s[...] = jnp.zeros_like(pair_s)
+    pair_s[:, :pcol] = pair_ref[0].astype(jnp.float32)
+    gh_s[...] = jnp.zeros_like(gh_s)
+    gh_s[:, :ecol] = gh_ref[0]
+
+    def forward(s, carry):
+        conv = None
+        for a in range(3):
+            window = pair_s[pl.ds(FWD * s + DILATION_STEP * a, FWD), :]
+            for b in range(3):
+                term = tap[3 * a + b] * shift_left(window, DILATION_STEP * b)
+                conv = term if conv is None else conv + term
+        at = FWD * s
+        conv_s[pl.ds(at, FWD), :] = conv
+        gc = gh_s[pl.ds(at, FWD), :] * silu_slope(conv)
+        gc_s[pl.ds(at, FWD), :] = gc.astype(jnp.bfloat16).astype(jnp.float32)
+        return carry
+
+    for s in range(erow // FWD):
+        forward(s, 0)
+
+    def backward(s, sums):
+        at = BWD * s
+        conv_tile = shift_left(conv_s[pl.ds(at + DILATION_STEP, BWD), :], DILATION_STEP)[:, :cols]
+        hid_ref[0, pl.ds(at, BWD), :] = jax.nn.silu(conv_tile).astype(hid_ref.dtype)
+        gc_tile = shift_left(gc_s[pl.ds(at + DILATION_STEP, BWD), :], DILATION_STEP)[:, :cols]
+        grad = gt_ref[0, pl.ds(at, BWD), :].astype(jnp.float32)
+        out = []
+        for a in range(3):
+            gc_rows = gc_s[pl.ds(at + DILATION_STEP * (2 - a), BWD), :]
+            pair_rows = pair_s[pl.ds(at + DILATION_STEP + DILATION_STEP * a, BWD), :]
+            for b in range(3):
+                grad = grad + tap[3 * a + b] * shift_left(gc_rows, DILATION_STEP * (2 - b))[:, :cols]
+                window = shift_left(pair_rows, DILATION_STEP + DILATION_STEP * b)[:, :cols]
+                out.append(sums[3 * a + b] + gc_tile * window)
+        gp_ref[0, pl.ds(at, BWD), :] = grad
+        return tuple(out)
+
+    zero = jnp.zeros((BWD, cols), jnp.float32)
+    sums = (zero,) * 9
+    for s in range(rows // BWD):
+        sums = backward(s, sums)
+    for t in range(9):
+        kern_ref[0, pl.ds(t, 1), :] = jnp.sum(sums[t], axis=0, keepdims=True)
+
+
+def depth_call(taps, pair_ext, grad_hidden, trunk_grad_tile):
+    chans, prow, pcol = pair_ext.shape
+    _, erow, ecol = grad_hidden.shape
+    _, rows, cols = trunk_grad_tile.shape
+    return pl.pallas_call(
+        depth_kernel_body,
+        grid=(chans,),
+        in_specs=[
+            pl.BlockSpec(memory_space=pltpu.SMEM),
+            pl.BlockSpec((1, prow, pcol), lambda c: (c, 0, 0)),
+            pl.BlockSpec((1, erow, ecol), lambda c: (c, 0, 0)),
+            pl.BlockSpec((1, rows, cols), lambda c: (c, 0, 0)),
+        ],
+        out_specs=[
+            pl.BlockSpec((1, rows, cols), lambda c: (c, 0, 0)),
+            pl.BlockSpec((1, rows, cols), lambda c: (c, 0, 0)),
+            pl.BlockSpec((1, 9, cols), lambda c: (c, 0, 0)),
+        ],
+        out_shape=[
+            jax.ShapeDtypeStruct((chans, rows, cols), jnp.bfloat16),
+            jax.ShapeDtypeStruct((chans, rows, cols), jnp.float32),
+            jax.ShapeDtypeStruct((chans, 9, cols), jnp.float32),
+        ],
+        scratch_shapes=[
+            pltpu.VMEM((prow, LANES), jnp.float32),
+            pltpu.VMEM((erow, LANES), jnp.float32),
+            pltpu.VMEM((erow, LANES), jnp.float32),
+            pltpu.VMEM((erow, LANES), jnp.float32),
+        ],
+    )(taps.ravel(), pair_ext, grad_hidden, trunk_grad_tile)
 
 
 def shifted(x, axis, step, count):
@@ -83,40 +177,16 @@
     pair_sum = left_ext.astype(jnp.float32).T[:, :, None] + right_ext.astype(jnp.float32).T[:, None, :]
     pair_ext = jnp.where(valid[None], pair_sum, 0.0).astype(jnp.bfloat16)
 
-    ext_rows = rows + 2 * step
-    ext_cols = cols + 2 * step
-    conv_ext = jnp.zeros((pair_ext.shape[0], ext_rows, ext_cols), jnp.float32)
-    for a in range(3):
-        for b in range(3):
-            conv_ext = conv_ext + depth_kernel[3 * a + b][:, None, None] * pair_ext[
-                :, step * a : step * a + ext_rows, step * b : step * b + ext_cols
-            ].astype(jnp.float32)
-    conv_tile = conv_ext[:, step : step + rows, step : step + cols]
-    hidden_state = jax.nn.silu(conv_tile).astype(jnp.bfloat16)
-    mixed_out = jnp.einsum("co,cij->oij", w_point, hidden_state, preferred_element_type=jnp.float32)
-    pair_tile = pair_ext[:, halo : halo + rows, halo : halo + cols]
-    trunk_matrix = (pair_tile.astype(jnp.float32) + mixed_out).astype(jnp.bfloat16)
-
     trunk_gradient = (
         grad_scale * jnp.einsum("ch,hij->cij", w_head, cot_ext, preferred_element_type=jnp.float32)
     ).astype(jnp.bfloat16)
     grad_hidden = jnp.einsum("co,oij->cij", w_point, trunk_gradient, preferred_element_type=jnp.float32)
-    conv_grad = (grad_hidden * silu_slope(conv_ext)).astype(jnp.bfloat16)
-    conv_grad_tile = conv_grad[:, step : step + rows, step : step + cols].astype(jnp.float32)
     trunk_grad_tile = trunk_gradient[:, step : step + rows, step : step + cols]
-
-    backward_pass = trunk_grad_tile.astype(jnp.float32)
-    kern_terms = []
-    for a in range(3):
-        for b in range(3):
-            backward_pass = backward_pass + depth_kernel[3 * a + b][:, None, None] * conv_grad[
-                :, step * (2 - a) : step * (2 - a) + rows, step * (2 - b) : step * (2 - b) + cols
-            ].astype(jnp.float32)
-            window = pair_ext[
-                :, step + step * a : step + step * a + rows, step + step * b : step + step * b + cols
-            ].astype(jnp.float32)
-            kern_terms.append(jnp.sum(conv_grad_tile * window, axis=(1, 2)))
-    kernel_part = jnp.stack(kern_terms)
+    hidden_state, backward_pass, kern_rows = depth_call(depth_kernel, pair_ext, grad_hidden, trunk_grad_tile)
+    mixed_out = jnp.einsum("co,cij->oij", w_point, hidden_state, preferred_element_type=jnp.float32)
+    pair_tile = pair_ext[:, halo : halo + rows, halo : halo + cols]
+    trunk_matrix = (pair_tile.astype(jnp.float32) + mixed_out).astype(jnp.bfloat16)
+    kernel_part = jnp.sum(kern_rows, axis=2).T
     left_part = jnp.sum(backward_pass, axis=2).T
     right_part = jnp.sum(backward_pass, axis=1).T
     point_part = jnp.einsum(

time: 182 us -> 248 us (1.36)
  local copies, waits for them, and re-layouts: 17.8 us -> 57 us
  Pallas kernels: 0 us -> 37.9 us
  other arithmetic: 31.3 us -> 15.8 us
  matrix products: 15.7 us -> 20.9 us
  starting transfers between devices: 68.7 us -> 64.3 us
  waiting for transfers between devices: 46.1 us -> 49.2 us
    pallas_call x0 -> x1, Pallas kernels: none -> 37.9 us  [depth_call(): pl.pallas_call(depth_kernel_body, grid=(chans,), in_specs=[pl.BlockSpec(m...]
    dot_general x0 -> x2, local copies, waits for them, and re-layouts: none -> 22.8 us  [the longest x1 11.4 us: body(): jnp.einsum('ch,hij->cij', w_head, cot_ext, preferred_element_type=jnp.flo...]
    add x1 -> x0, other arithmetic: 9.32 us -> none  [body(): conv_ext + depth_kernel[3 * a + b][:, None, None] * pair_ext[:, step * a:...]
    convert_element_type x0 -> x1, local copies, waits for them, and re-layouts: none -> 8.04 us  [body(): trunk_gradient = (grad_scale * jnp.einsum('ch,hij->cij', w_head, cot_ext,...]
    convert_element_type x1 -> x2, other arithmetic: 2.56 us -> 10.3 us  [the longest x1 6.14 us: body(): (pair_tile.astype(jnp.float32) + mixed_out).astype(jnp.bfloat16)]
    reduce_sum x1, other arithmetic: 7.48 us -> 0.14 us  [body(): kernel_part = jnp.sum(kern_rows, axis=2).T]
    slice x0 -> x2, local copies, waits for them, and re-layouts: none -> 6.63 us  [body(): trunk_grad_tile = trunk_gradient[:, step:step + rows, step:step + cols]]
    reduce_sum x1, other arithmetic: 6.95 us -> 1.15 us  [body(): right_part = jnp.sum(backward_pass, axis=1).T]
  transfers between devices with their start and end apart: 15 -> 15, of which waited for: 10 -> 12; matrix products, arithmetic and copies ran while one was open for 17% -> 4% of each run, Pallas kernels for 0% -> 0%
where the time goes in v3:
time: 248 us; the launch traced here: 246 us
  starting transfers between devices  64.3 us (26%)
  local copies, waits for them, and re-layouts  57 us (23%)
  waiting for transfers between devices  49.2 us (20%)
  Pallas kernels  37.9 us (15%)
  matrix products  20.9 us (8%)
  other arithmetic  15.8 us (6%)
    ppermute x9, waiting for transfers between devices, xor_round(): return lax.ppermute(flat, axis, [(i, i ^ bit) for i in range(count)])  42.5 us
    pallas_call x1, Pallas kernels, depth_call(): pl.pallas_call(depth_kernel_body, grid=(chans,), in_specs=[pl.BlockSpec(m...  37.9 us
    ppermute x9, starting transfers between devices, xor_round(): return lax.ppermute(flat, axis, [(i, i ^ bit) for i in range(count)])  33.8 us
    ppermute x4, starting transfers between devices, shifted(): return lax.ppermute(x, axis, pairs)  15.9 us
    dot_general x1, local copies, waits for them, and re-layouts, body(): jnp.einsum('ch,hij->cij', w_head, cot_ext, preferred_element_type=jnp.flo...  11.4 us
    dot_general x1, local copies, waits for them, and re-layouts, body(): jnp.einsum('co,oij->cij', w_point, trunk_gradient, preferred_element_type...  11.4 us
    convert_element_type x1, local copies, waits for them, and re-layouts, body(): trunk_gradient = (grad_scale * jnp.einsum('ch,hij->cij', w_head, cot_ext,...  8.04 us
    ppermute x1, starting transfers between devices, body(): right_ext = lax.ppermute(own_tile, ('row', 'col'), transpose_pairs())  7.43 us
  transfers between devices with their start and end apart: 15, of which 12 were waited for; matrix products, arithmetic and copies ran while one was open for 4% of the time, Pallas kernels for 0%

profile of v3, /device:TPU:6, one launch (start us, length us, event | category | flops | bytes accessed | tf_op | source)
XLA Modules:
  0.0 246.4 jit_solution(13043773238992406462)
XLA Ops:
  0.7 0.9 copy-done
  1.6 0.9 convolution_convert_fusion.1
  2.8 0.9 convolution_convert_fusion
  4.9 6.1 %collective-permute-start = (bf16[12800]{0:T(1024)(128)(2,1)S(1)}, bf16[12800]{0:T(1024)(128)(2,1)S(1)}, u32[]{:S(2)}, u32[]{:S(2)}) collective-permute-start(bf16[12800]{0:T(1024)(128)(2,1)S(1)} %pad_maximum_fusion.4), channel_id=1, source_target_pairs={{0,32},{32,64},{64,96},{96,128},{128,160},{160,192},{192,224},{224... | collective-permute-start | bytes 76808 | tf_op jit(solution)/shard_map/ppermute | solution.py:112
  11.3 7.0 %collective-permute-start.1 = (bf16[12800]{0:T(1024)(128)(2,1)S(1)}, bf16[12800]{0:T(1024)(128)(2,1)S(1)}, u32[]{:S(2)}, u32[]{:S(2)}) collective-permute-start(bf16[12800]{0:T(1024)(128)(2,1)S(1)} %pad_maximum_fusion.5), channel_id=1, source_target_pairs={{32,0},{64,32},{96,64},{128,96},{160,128},{192,160},{224,192},{256... | collective-permute-start | bytes 76808 | tf_op jit(solution)/shard_map/ppermute | solution.py:112
  18.5 2.2 copy.86
  21.8 7.4 %collective-permute-start.2 = (bf16[144,32]{0,1:T(8,128)(2,1)S(1)}, bf16[144,32]{0,1:T(8,128)(2,1)}, u32[]{:S(2)}, u32[]{:S(2)}) collective-permute-start(bf16[144,32]{0,1:T(8,128)(2,1)S(1)} %fusion.25), channel_id=1, source_target_pairs={{0,0},{1,1},{2,32},{3,33},{4,64},{5,65},{6,96},{7,97},{8,128},{9,1... | collective-permute-start | bytes 27656 | tf_op jit(solution)/shard_map/ppermute | solution.py:172
  30.7 1.3 collective-permute-start.3
  32.0 1.5 collective-permute-start.4
  33.6 0.9 collective-permute-done.2
  35.2 2.7 %select_convert_fusion.pair_ref = bf16[32,272,144]{2,1,0:T(8,128)(2,1)} fusion(f32[32,144]{1,0:T(8,128)S(1)} %convert_bitcast_fusion.1, f32[32,272]{1,0:T(8,128)S(1)} %convert_bitcast_fusion, pred[272,144]{1,0:T(8,128)(4,1)S(1)} %and_and_fusion), kind=kLoop, calls=%fused_computation | loop fusion | flops 3760128 | bytes 2599168 | tf_op jit(solution)/shard_map/convert_element_type | solution.py:178
  37.9 1.6 collective-permute-done.4
  39.6 4.3 %fusion.2 = f32[264,136,32]{0,2,1:T(8,128)} fusion(bf16[24,264,4]{1,0,2:T(8,128)(2,1)S(1)} %collective-permute-done.4, bf16[24,4,128]{1,0,2:T(8,128)(2,1)S(1)} %copy.87, bf16[24,256,128]{1,0,2:T(8,128)(2,1)S(1)} %copy.86, bf16[24,4,128]{1,0,2:T(8,128)(2,1)S(1)} %copy.85, bf16[24,264,4]{1,0,2:T(8,128)(2,1)S(1)} %collective-permute-done.3, ...), kind=kOutput, calls=%fused_computation.5 | convolution fusion | flops 63765504 | bytes 6320640 | tf_op jit(solution)/shard_map/ch,hij->cij/dot_general | solution.py:181
  43.8 11.4 %copy.88 = f32[264,136,32]{1,0,2:T(8,128)} copy(f32[264,136,32]{0,2,1:T(8,128)} %fusion.2) | data formatting | bytes 9191424 | tf_op jit(solution)/shard_map/ch,hij->cij/dot_general | solution.py:181
  55.2 4.2 %fusion = bf16[32,264,136]{2,1,0:T(8,128)(2,1)S(1)} fusion(f32[264,136,32]{1,0,2:T(8,128)} %copy.88), kind=kLoop, calls=%fused_computation.2 | loop fusion | flops 2297856 | bytes 6893568 | tf_op jit(solution)/shard_map/convert_element_type | solution.py:182
  59.4 2.0 copy-done.1
  61.4 3.6 %slice.273.gt_ref = bf16[32,256,128]{2,1,0:T(8,128)(2,1)} slice(bf16[32,264,136]{2,1,0:T(8,128)(2,1)S(1)} %fusion), slice={[0:32], [4:260], [4:132]} | slice | bytes 4194304 | tf_op jit(solution)/shard_map/slice | solution.py:184
  65.0 8.0 %copy.90 = bf16[32,264,136]{1,0,2:T(8,128)(2,1)} copy(bf16[32,264,136]{2,1,0:T(8,128)(2,1)} %copy-done.1) | data formatting | bytes 4595712 | tf_op jit(solution)/shard_map/convert_element_type | solution.py:182
  73.0 5.7 %fusion.28 = f32[264,136,32]{0,2,1:T(8,128)} fusion(bf16[32,264,136]{1,0,2:T(8,128)(2,1)} %copy.90, bf16[32,32]{1,0:T(8,128)(2,1)S(1)} %copy-done.10), kind=kOutput, calls=%fused_computation.52 | convolution fusion | flops 73531392 | bytes 6895616 | tf_op jit(solution)/shard_map/co,oij->cij/dot_general | solution.py:183
  78.8 11.4 %copy.91 = f32[264,136,32]{1,0,2:T(8,128)} copy(f32[264,136,32]{0,2,1:T(8,128)} %fusion.28) | data formatting | bytes 9191424 | tf_op jit(solution)/shard_map/co,oij->cij/dot_general | solution.py:183
  90.2 37.9 %shard_map.118 = (bf16[32,256,128]{2,1,0:T(8,128)(2,1)}, f32[32,256,128]{2,1,0:T(8,128)}, f32[32,9,128]{2,1,0:T(8,128)}) custom-call(f32[288]{0:T(512)} %reshape.280.taps_ref, bf16[32,272,144]{2,1,0:T(8,128)(2,1)} %select_convert_fusion.pair_ref, f32[32,264,136]{2,1,0:T(8,128)} %bitcast.48, bf16[32,256,128]{2,1,0:T(8,128)(2,1)} %slice.273.gt_ref), custom_call_target="tpu_custom_call" | custom-call | tf_op jit(solution)/shard_map/pallas_call | solution.py:82
  128.1 4.9 %fusion.14 = f32[256,128,32]{1,2,0:T(8,128)} fusion(bf16[32,256,128]{2,1,0:T(8,128)(2,1)} %get-tuple-element.11, bf16[32,32]{1,0:T(8,128)(2,1)S(1)} %copy-done.10), kind=kOutput, calls=%fused_computation.17 | convolution fusion | flops 67108864 | bytes 6293504 | tf_op jit(solution)/shard_map/co,cij->oij/dot_general | solution.py:186
  133.0 4.8 %copy.95 = bf16[32,256,128]{1,0,2:T(8,128)(2,1)} copy(bf16[32,256,128]{2,1,0:T(8,128)(2,1)} %get-tuple-element.11) | data formatting | bytes 4194304 | tf_op jit(solution)/shard_map/pallas_call | solution.py:82
  137.8 3.0 %copy.96 = bf16[32,256,128]{1,0,2:T(8,128)(2,1)} copy(bf16[32,256,128]{2,1,0:T(8,128)(2,1)S(1)} %copy-done.2) | data formatting | bytes 4194304 | tf_op jit(solution)/shard_map/slice | solution.py:184
  140.8 6.1 %fusion.1 = bf16[32,256,128]{2,1,0:T(8,128)(2,1)S(1)} fusion(f32[256,128,32]{1,2,0:T(8,128)} %fusion.14, bf16[32,272,144]{2,1,0:T(8,128)(2,1)} %select_convert_fusion.pair_ref), kind=kLoop, calls=%fused_computation.4 | loop fusion | flops 3145728 | bytes 8388608 | tf_op jit(solution)/shard_map/convert_element_type | solution.py:188
  147.0 2.1 fusion.18
  149.1 1.2 fusion.40
  150.3 7.2 %collective-permute-start.5 = (f32[128,32]{0,1:T(8,128)S(1)}, f32[128,32]{0,1:T(8,128)S(1)}, u32[]{:S(2)}, u32[]{:S(2)}) collective-permute-start(f32[128,32]{0,1:T(8,128)S(1)} %bitcast.55), channel_id=1, source_target_pairs={{0,0},{1,1},{2,32},{3,33},{4,64},{5,65},{6,96},{7,97},{8,128},{9,1... | collective-permute-start | bytes 49160 | tf_op jit(solution)/shard_map/ppermute | solution.py:198
  158.9 4.2 %collective-permute-done.5 = f32[128,32]{0,1:T(8,128)S(1)} collective-permute-done((f32[128,32]{0,1:T(8,128)S(1)}, f32[128,32]{0,1:T(8,128)S(1)}, u32[]{:S(2)}, u32[]{:S(2)}) %collective-permute-start.5) | collective-permute-done | bytes 16416 | tf_op jit(solution)/shard_map/ppermute | solution.py:198
  163.3 7.3 %collective-permute-start.6 = (f32[14368]{0:T(1024)S(1)}, f32[14368]{0:T(1024)S(1)}, u32[]{:S(2)}, u32[]{:S(2)}) collective-permute-start(f32[14368]{0:T(1024)S(1)} %concatenate.48), channel_id=1, source_target_pairs={{0,2},{1,3},{2,0},{3,1},{4,6},{5,7},{6,4},{7,5},{8,10},{9,11},{10,... | collective-permute-start | bytes 172424 | tf_op jit(solution)/shard_map/ppermute | solution.py:128
  170.7 2.2 collective-permute-done.6
  172.9 4.2 %collective-permute-start.7 = (f32[14368]{0:T(1024)S(1)}, f32[14368]{0:T(1024)S(1)}, u32[]{:S(2)}, u32[]{:S(2)}) collective-permute-start(f32[14368]{0:T(1024)S(1)} %add.94), channel_id=1, source_target_pairs={{0,4},{1,5},{2,6},{3,7},{4,0},{5,1},{6,2},{7,3},{8,12},{9,13},{10,... | collective-permute-start | bytes 172424 | tf_op jit(solution)/shard_map/ppermute | solution.py:128
  177.1 2.8 %collective-permute-done.7 = f32[14368]{0:T(1024)S(1)} collective-permute-done((f32[14368]{0:T(1024)S(1)}, f32[14368]{0:T(1024)S(1)}, u32[]{:S(2)}, u32[]{:S(2)}) %collective-permute-start.7) | collective-permute-done | bytes 57504 | tf_op jit(solution)/shard_map/ppermute | solution.py:128
  179.9 4.0 %collective-permute-start.8 = (f32[14368]{0:T(1024)S(1)}, f32[14368]{0:T(1024)S(1)}, u32[]{:S(2)}, u32[]{:S(2)}) collective-permute-start(f32[14368]{0:T(1024)S(1)} %add.95), channel_id=1, source_target_pairs={{0,8},{1,9},{2,10},{3,11},{4,12},{5,13},{6,14},{7,15},{8,0},{9,1},... | collective-permute-start | bytes 172424 | tf_op jit(solution)/shard_map/ppermute | solution.py:128
  183.9 6.1 %collective-permute-done.8 = f32[14368]{0:T(1024)S(1)} collective-permute-done((f32[14368]{0:T(1024)S(1)}, f32[14368]{0:T(1024)S(1)}, u32[]{:S(2)}, u32[]{:S(2)}) %collective-permute-start.8) | collective-permute-done | bytes 57504 | tf_op jit(solution)/shard_map/ppermute | solution.py:128
  190.0 2.9 %collective-permute-start.9 = (f32[14368]{0:T(1024)S(1)}, f32[14368]{0:T(1024)S(1)}, u32[]{:S(2)}, u32[]{:S(2)}) collective-permute-start(f32[14368]{0:T(1024)S(1)} %add.96), channel_id=1, source_target_pairs={{0,16},{1,17},{2,18},{3,19},{4,20},{5,21},{6,22},{7,23},{8,24},{9,... | collective-permute-start | bytes 172424 | tf_op jit(solution)/shard_map/ppermute | solution.py:128
  192.9 3.2 %collective-permute-done.9 = f32[14368]{0:T(1024)S(1)} collective-permute-done((f32[14368]{0:T(1024)S(1)}, f32[14368]{0:T(1024)S(1)}, u32[]{:S(2)}, u32[]{:S(2)}) %collective-permute-start.9) | collective-permute-done | bytes 57504 | tf_op jit(solution)/shard_map/ppermute | solution.py:128
  196.2 1.9 collective-permute-start.10
  198.1 1.2 collective-permute-done.10
  200.7 3.9 %collective-permute-start.11 = (f32[34848]{0:T(1024)S(1)}, f32[34848]{0:T(1024)S(1)}, u32[]{:S(2)}, u32[]{:S(2)}) collective-permute-start(f32[34848]{0:T(1024)S(1)} %pad_maximum_fusion), channel_id=1, source_target_pairs={{0,32},{32,0},{64,96},{96,64},{128,160},{160,128},{192,224},{224,1... | collective-permute-start | bytes 418184 | tf_op jit(solution)/shard_map/ppermute | solution.py:128
  204.6 7.8 %collective-permute-done.11 = f32[34848]{0:T(1024)S(1)} collective-permute-done((f32[34848]{0:T(1024)S(1)}, f32[34848]{0:T(1024)S(1)}, u32[]{:S(2)}, u32[]{:S(2)}) %collective-permute-start.11) | collective-permute-done | bytes 139424 | tf_op jit(solution)/shard_map/ppermute | solution.py:128
  212.4 5.5 %collective-permute-start.12 = (f32[34848]{0:T(1024)S(1)}, f32[34848]{0:T(1024)S(1)}, u32[]{:S(2)}, u32[]{:S(2)}) collective-permute-start(f32[34848]{0:T(1024)S(1)} %fusion.39), channel_id=1, source_target_pairs={{0,64},{32,96},{64,0},{96,32},{128,192},{160,224},{192,128},{224,1... | collective-permute-start | bytes 418184 | tf_op jit(solution)/shard_map/ppermute | solution.py:128
  217.8 8.4 %collective-permute-done.12 = f32[34848]{0:T(1024)S(1)} collective-permute-done((f32[34848]{0:T(1024)S(1)}, f32[34848]{0:T(1024)S(1)}, u32[]{:S(2)}, u32[]{:S(2)}) %collective-permute-start.12) | collective-permute-done | bytes 139424 | tf_op jit(solution)/shard_map/ppermute | solution.py:128
  226.3 1.9 collective-permute-start.13
  228.5 5.4 %collective-permute-done.13 = f32[34848]{0:T(1024)S(1)} collective-permute-done((f32[34848]{0:T(1024)S(1)}, f32[34848]{0:T(1024)S(1)}, u32[]{:S(2)}, u32[]{:S(2)}) %collective-permute-start.13) | collective-permute-done | bytes 139424 | tf_op jit(solution)/shard_map/ppermute | solution.py:128
  233.9 2.2 collective-permute-start.14
  236.1 0.9 fusion.17
  237.0 5.3 %collective-permute-done.14 = f32[34848]{0:T(1024)S(1)} collective-permute-done((f32[34848]{0:T(1024)S(1)}, f32[34848]{0:T(1024)S(1)}, u32[]{:S(2)}, u32[]{:S(2)}) %collective-permute-start.14) | collective-permute-done | bytes 139424 | tf_op jit(solution)/shard_map/ppermute | solution.py:128
  (109 shorter events, 12.6 us)
Async XLA Ops:
  0.6 1.0 copy-start
  0.6 20.0 %copy-start.11 = (f32[9,32]{1,0:T(8,128)S(1)}, f32[9,32]{1,0:T(8,128)}, u32[]{:S(2)}) copy-start(f32[9,32]{1,0:T(8,128)} %param.10) | copy-start | bytes 3460
  4.9 16.5 %collective-permute-start = (bf16[12800]{0:T(1024)(128)(2,1)S(1)}, bf16[12800]{0:T(1024)(128)(2,1)S(1)}, u32[]{:S(2)}, u32[]{:S(2)}) collective-permute-start(bf16[12800]{0:T(1024)(128)(2,1)S(1)} %pad_maximum_fusion.4), channel_id=1, source_target_pairs={{0,32},{32,64},{64,96},{96,128},{128,160},{160,192},{192,224},{224... | collective-permute-start | bytes 76808 | tf_op jit(solution)/shard_map/ppermute | solution.py:112
  11.3 10.2 %collective-permute-start.1 = (bf16[12800]{0:T(1024)(128)(2,1)S(1)}, bf16[12800]{0:T(1024)(128)(2,1)S(1)}, u32[]{:S(2)}, u32[]{:S(2)}) collective-permute-start(bf16[12800]{0:T(1024)(128)(2,1)S(1)} %pad_maximum_fusion.5), channel_id=1, source_target_pairs={{32,0},{64,32},{96,64},{128,96},{160,128},{192,160},{224,192},{256... | collective-permute-start | bytes 76808 | tf_op jit(solution)/shard_map/ppermute | solution.py:112
  21.8 12.7 %collective-permute-start.2 = (bf16[144,32]{0,1:T(8,128)(2,1)S(1)}, bf16[144,32]{0,1:T(8,128)(2,1)}, u32[]{:S(2)}, u32[]{:S(2)}) collective-permute-start(bf16[144,32]{0,1:T(8,128)(2,1)S(1)} %fusion.25), channel_id=1, source_target_pairs={{0,0},{1,1},{2,32},{3,33},{4,64},{5,65},{6,96},{7,97},{8,128},{9,1... | collective-permute-start | bytes 27656 | tf_op jit(solution)/shard_map/ppermute | solution.py:172
  30.6 9.0 %copy-start.12 = (bf16[32,24]{0,1:T(8,128)(2,1)S(1)}, bf16[32,24]{0,1:T(8,128)(2,1)}, u32[]{:S(2)}) copy-start(bf16[32,24]{0,1:T(8,128)(2,1)} %param.12) | copy-start | bytes 4612
  30.7 7.2 %collective-permute-start.3 = (bf16[24,264,4]{1,0,2:T(8,128)(2,1)S(1)}, bf16[24,264,4]{1,0,2:T(8,128)(2,1)S(1)}, u32[]{:S(2)}, u32[]{:S(2)}) collective-permute-start(bf16[24,264,4]{1,0,2:T(8,128)(2,1)S(1)} %get-tuple-element.32), channel_id=1, source_target_pairs={{0,1},{1,2},{2,3},{3,4},{4,5},{5,6},{6,7},{7,8},{8,9},{9,10},{10,1... | collective-permute-start | bytes 152072 | tf_op jit(solution)/shard_map/ppermute | solution.py:112
  32.0 7.5 %collective-permute-start.4 = (bf16[24,264,4]{1,0,2:T(8,128)(2,1)S(1)}, bf16[24,264,4]{1,0,2:T(8,128)(2,1)S(1)}, u32[]{:S(2)}, u32[]{:S(2)}) collective-permute-start(bf16[24,264,4]{1,0,2:T(8,128)(2,1)S(1)} %get-tuple-element.33), channel_id=1, source_target_pairs={{1,0},{2,1},{3,2},{4,3},{5,4},{6,5},{7,6},{8,7},{9,8},{10,9},{11,1... | collective-permute-start | bytes 152072 | tf_op jit(solution)/shard_map/ppermute | solution.py:112
  59.4 2.0 copy-start.1
  65.0 8.0 %copy-start.10 = (bf16[32,32]{1,0:T(8,128)(2,1)S(1)}, bf16[32,32]{1,0:T(8,128)(2,1)}, u32[]{:S(2)}) copy-start(bf16[32,32]{1,0:T(8,128)(2,1)} %param.11) | copy-start | bytes 6148
  133.0 4.8 %copy-start.2 = (bf16[32,256,128]{2,1,0:T(8,128)(2,1)S(1)}, bf16[32,256,128]{2,1,0:T(8,128)(2,1)}, u32[]{:S(2)}) copy-start(bf16[32,256,128]{2,1,0:T(8,128)(2,1)} %slice.273.gt_ref) | copy-start | bytes 6291460
  140.8 6.1 %copy-start.6 = (bf16[24,256,128]{2,1,0:T(8,128)(2,1)S(1)}, bf16[24,256,128]{2,1,0:T(8,128)(2,1)}, u32[]{:S(2)}) copy-start(bf16[24,256,128]{2,1,0:T(8,128)(2,1)} %param.13) | copy-start | bytes 4718596
  146.9 2.2 copy-start.5
  149.0 8.5 %copy-start.3 = (bf16[32,256,128]{1,0,2:T(8,128)(2,1)S(1)}, bf16[32,256,128]{1,0,2:T(8,128)(2,1)}, u32[]{:S(2)}) copy-start(bf16[32,256,128]{1,0,2:T(8,128)(2,1)} %copy.95) | copy-start | bytes 6291460
  149.0 8.5 %copy-start.4 = (bf16[32,256,128]{1,0,2:T(8,128)(2,1)S(1)}, bf16[32,256,128]{1,0,2:T(8,128)(2,1)}, u32[]{:S(2)}) copy-start(bf16[32,256,128]{1,0,2:T(8,128)(2,1)} %copy.96) | copy-start | bytes 6291460
  150.3 8.3 %copy-start.7 = (f32[32,9,128]{2,1,0:T(8,128)S(1)}, f32[32,9,128]{2,1,0:T(8,128)}, u32[]{:S(2)}) copy-start(f32[32,9,128]{2,1,0:T(8,128)} %get-tuple-element.10) | copy-start | bytes 442372
  150.3 12.8 %collective-permute-start.5 = (f32[128,32]{0,1:T(8,128)S(1)}, f32[128,32]{0,1:T(8,128)S(1)}, u32[]{:S(2)}, u32[]{:S(2)}) collective-permute-start(f32[128,32]{0,1:T(8,128)S(1)} %bitcast.55), channel_id=1, source_target_pairs={{0,0},{1,1},{2,32},{3,33},{4,64},{5,65},{6,96},{7,97},{8,128},{9,1... | collective-permute-start | bytes 49160 | tf_op jit(solution)/shard_map/ppermute | solution.py:198
  158.2 70.0 %copy-start.9 = (bf16[512,32]{0,1:T(8,128)(2,1)S(1)}, bf16[512,32]{0,1:T(8,128)(2,1)}, u32[]{:S(2)}) copy-start(bf16[512,32]{0,1:T(8,128)(2,1)} %param.9) | copy-start | bytes 98308
  158.2 77.9 %copy-start.8 = (bf16[512,32]{0,1:T(8,128)(2,1)S(1)}, bf16[512,32]{0,1:T(8,128)(2,1)}, u32[]{:S(2)}) copy-start(bf16[512,32]{0,1:T(8,128)(2,1)} %param.8) | copy-start | bytes 98308
  163.3 9.5 %collective-permute-start.6 = (f32[14368]{0:T(1024)S(1)}, f32[14368]{0:T(1024)S(1)}, u32[]{:S(2)}, u32[]{:S(2)}) collective-permute-start(f32[14368]{0:T(1024)S(1)} %concatenate.48), channel_id=1, source_target_pairs={{0,2},{1,3},{2,0},{3,1},{4,6},{5,7},{6,4},{7,5},{8,10},{9,11},{10,... | collective-permute-start | bytes 172424 | tf_op jit(solution)/shard_map/ppermute | solution.py:128
  172.9 7.0 %collective-permute-start.7 = (f32[14368]{0:T(1024)S(1)}, f32[14368]{0:T(1024)S(1)}, u32[]{:S(2)}, u32[]{:S(2)}) collective-permute-start(f32[14368]{0:T(1024)S(1)} %add.94), channel_id=1, source_target_pairs={{0,4},{1,5},{2,6},{3,7},{4,0},{5,1},{6,2},{7,3},{8,12},{9,13},{10,... | collective-permute-start | bytes 172424 | tf_op jit(solution)/shard_map/ppermute | solution.py:128
  179.9 10.1 %collective-permute-start.8 = (f32[14368]{0:T(1024)S(1)}, f32[14368]{0:T(1024)S(1)}, u32[]{:S(2)}, u32[]{:S(2)}) collective-permute-start(f32[14368]{0:T(1024)S(1)} %add.95), channel_id=1, source_target_pairs={{0,8},{1,9},{2,10},{3,11},{4,12},{5,13},{6,14},{7,15},{8,0},{9,1},... | collective-permute-start | bytes 172424 | tf_op jit(solution)/shard_map/ppermute | solution.py:128
  190.0 6.1 %collective-permute-start.9 = (f32[14368]{0:T(1024)S(1)}, f32[14368]{0:T(1024)S(1)}, u32[]{:S(2)}, u32[]{:S(2)}) collective-permute-start(f32[14368]{0:T(1024)S(1)} %add.96), channel_id=1, source_target_pairs={{0,16},{1,17},{2,18},{3,19},{4,20},{5,21},{6,22},{7,23},{8,24},{9,... | collective-permute-start | bytes 172424 | tf_op jit(solution)/shard_map/ppermute | solution.py:128
  196.2 3.1 %collective-permute-start.10 = (f32[14368]{0:T(1024)S(1)}, f32[14368]{0:T(1024)S(1)}, u32[]{:S(2)}, u32[]{:S(2)}) collective-permute-start(f32[14368]{0:T(1024)S(1)} %add.97), channel_id=1, source_target_pairs={{0,1},{1,0},{2,3},{3,2},{4,5},{5,4},{6,7},{7,6},{8,9},{9,8},{10,11... | collective-permute-start | bytes 172424 | tf_op jit(solution)/shard_map/ppermute | solution.py:128
  200.7 11.7 %collective-permute-start.11 = (f32[34848]{0:T(1024)S(1)}, f32[34848]{0:T(1024)S(1)}, u32[]{:S(2)}, u32[]{:S(2)}) collective-permute-start(f32[34848]{0:T(1024)S(1)} %pad_maximum_fusion), channel_id=1, source_target_pairs={{0,32},{32,0},{64,96},{96,64},{128,160},{160,128},{192,224},{224,1... | collective-permute-start | bytes 418184 | tf_op jit(solution)/shard_map/ppermute | solution.py:128
  212.4 13.9 %collective-permute-start.12 = (f32[34848]{0:T(1024)S(1)}, f32[34848]{0:T(1024)S(1)}, u32[]{:S(2)}, u32[]{:S(2)}) collective-permute-start(f32[34848]{0:T(1024)S(1)} %fusion.39), channel_id=1, source_target_pairs={{0,64},{32,96},{64,0},{96,32},{128,192},{160,224},{192,128},{224,1... | collective-permute-start | bytes 418184 | tf_op jit(solution)/shard_map/ppermute | solution.py:128
  226.3 7.6 %collective-permute-start.13 = (f32[34848]{0:T(1024)S(1)}, f32[34848]{0:T(1024)S(1)}, u32[]{:S(2)}, u32[]{:S(2)}) collective-permute-start(f32[34848]{0:T(1024)S(1)} %add.102), channel_id=1, source_target_pairs={{0,128},{32,160},{64,192},{96,224},{128,0},{160,32},{192,64},{224,... | collective-permute-start | bytes 418184 | tf_op jit(solution)/shard_map/ppermute | solution.py:128
  233.9 8.5 %collective-permute-start.14 = (f32[34848]{0:T(1024)S(1)}, f32[34848]{0:T(1024)S(1)}, u32[]{:S(2)}, u32[]{:S(2)}) collective-permute-start(f32[34848]{0:T(1024)S(1)} %add.103), channel_id=1, source_target_pairs={{0,256},{32,288},{64,320},{96,352},{128,384},{160,416},{192,448},{... | collective-permute-start | bytes 418184 | tf_op jit(solution)/shard_map/ppermute | solution.py:128

commit v4 on v2

--- a/solution.py
+++ b/solution.py
@@ -51,13 +51,12 @@
     left_proj = jnp.dot(bin_features, w_left, preferred_element_type=jnp.float32).astype(jnp.bfloat16)
     right_proj = jnp.dot(bin_features, w_right, preferred_element_type=jnp.float32).astype(jnp.bfloat16)
 
-    tail = (cotangent[:, rows - step :, :], left_proj[rows - halo :], right_proj[rows - halo :])
-    head = (cotangent[:, :step, :], left_proj[:halo], right_proj[:halo])
+    tail = (cotangent[:, rows - step :, :], left_proj[rows - halo :])
+    head = (cotangent[:, :step, :], left_proj[:halo])
     before = unpacked(shifted(packed(tail), "row", 1, row_count), tail)
     after = unpacked(shifted(packed(head), "row", -1, row_count), head)
     cot_rows = jnp.concatenate([before[0], cotangent, after[0]], axis=1)
     left_ext = jnp.concatenate([before[1], left_proj, after[1]], axis=0)
-    right_panel = jnp.concatenate([before[2], right_proj, after[2]], axis=0)
     cot_ext = jnp.concatenate(
         [
             shifted(cot_rows[:, :, cols - step :], "col", 1, col_count),
@@ -67,15 +66,24 @@
         axis=2,
     )
 
-    def transpose_pairs():
+    def transpose_pairs(shift=0):
         pairs = []
         for a in range(row_count):
             for b in range(col_count):
-                pairs.append((a * col_count + b, (b // ratio) * col_count + ratio * a + b % ratio))
+                tile = ratio * a + b % ratio + shift
+                if 0 <= tile < col_count:
+                    pairs.append((a * col_count + b, (b // ratio) * col_count + tile))
         return pairs
 
-    own_tile = lax.dynamic_slice_in_dim(right_panel, part * cols, cols + 2 * halo, 0)
-    right_ext = lax.ppermute(own_tile, ("row", "col"), transpose_pairs())
+    own_tile = lax.dynamic_slice_in_dim(right_proj, part * cols, cols, 0)
+    right_ext = jnp.concatenate(
+        [
+            lax.ppermute(own_tile[cols - halo :], ("row", "col"), transpose_pairs(1)),
+            lax.ppermute(own_tile, ("row", "col"), transpose_pairs()),
+            lax.ppermute(own_tile[:halo], ("row", "col"), transpose_pairs(-1)),
+        ],
+        axis=0,
+    )
 
     row_place = r * rows - halo + lax.broadcasted_iota(jnp.int32, (rows + 2 * halo, 1), 0)
     col_place = k * cols - halo + lax.broadcasted_iota(jnp.int32, (1, cols + 2 * halo), 1)

time: 182 us -> 195 us (1.071)
  starting transfers between devices: 68.7 us -> 75.7 us
  waiting for transfers between devices: 46.1 us -> 50.9 us
    ppermute x1 -> x3, starting transfers between devices: 6.47 us -> 21.9 us  [the longest x1 9.46 us: body(): lax.ppermute(own_tile, ('row', 'col'), transpose_pairs())]
    ppermute x4, starting transfers between devices: 18.1 us -> 11.7 us  [shifted(): return lax.ppermute(x, axis, pairs)]
    ppermute x9, waiting for transfers between devices: 40.6 us -> 43.4 us  [xor_round(): return lax.ppermute(flat, axis, [(i, i ^ bit) for i in range(count)])]
    reshape x8 -> x6, local copies, waits for them, and re-layouts: 0.71 us -> 3.3 us  [unpacked(): out.append(flat[at:at + like.size].reshape(like.shape))]
  transfers between devices with their start and end apart: 15 -> 17, of which waited for: 10 -> 11; matrix products, arithmetic and copies ran while one was open for 17% -> 15% of each run, Pallas kernels for 0% -> 0%
where the time goes in v4:
time: 195 us; the launch traced here: 193 us
  starting transfers between devices  75.7 us (39%)
  waiting for transfers between devices  50.9 us (26%)
  other arithmetic  30 us (15%)
  local copies, waits for them, and re-layouts  19 us (10%)
  matrix products  15.7 us (8%)
    ppermute x9, waiting for transfers between devices, xor_round(): return lax.ppermute(flat, axis, [(i, i ^ bit) for i in range(count)])  43.4 us
    ppermute x9, starting transfers between devices, xor_round(): return lax.ppermute(flat, axis, [(i, i ^ bit) for i in range(count)])  35.6 us
    ppermute x4, starting transfers between devices, shifted(): return lax.ppermute(x, axis, pairs)  11.7 us
    ppermute x1, starting transfers between devices, body(): lax.ppermute(own_tile, ('row', 'col'), transpose_pairs())  9.46 us
    add x1, other arithmetic, body(): conv_ext + depth_kernel[3 * a + b][:, None, None] * pair_ext[:, step * a:...  9.32 us
    ppermute x1, starting transfers between devices, body(): lax.ppermute(own_tile[:halo], ('row', 'col'), transpose_pairs(-1))  9.07 us
    unnamed x50, local copies, waits for them, and re-layouts  8.1 us
    reduce_sum x1, other arithmetic, body(): kern_terms.append(jnp.sum(conv_grad_tile * window, axis=(1, 2)))  7.48 us
  transfers between devices with their start and end apart: 17, of which 11 were waited for; matrix products, arithmetic and copies ran while one was open for 15% of the time, Pallas kernels for 0%

profile of v4, /device:TPU:6, one launch (start us, length us, event | category | flops | bytes accessed | tf_op | source)
XLA Modules:
  0.0 192.6 jit_solution(12658872903793408795)
XLA Ops:
  0.7 0.9 copy-done
  1.6 0.9 fusion.53
  2.5 9.5 %collective-permute-start.5 = (bf16[128,32]{0,1:T(8,128)(2,1)S(1)}, bf16[128,32]{0,1:T(8,128)(2,1)S(1)}, u32[]{:S(2)}, u32[]{:S(2)}) collective-permute-start(bf16[128,32]{0,1:T(8,128)(2,1)S(1)} %dynamic-slice_convert_fusion), channel_id=1, source_target_pairs={{0,0},{1,1},{2,32},{3,33},{4,64},{5,65},{6,96},{7,97},{8,128},{9,1... | collective-permute-start | bytes 24584 | tf_op jit(solution)/shard_map/ppermute | solution.py:82
  12.1 9.1 %collective-permute-start.6 = (bf16[8,32]{0,1:T(8,128)(2,1)S(1)}, bf16[8,32]{0,1:T(8,128)(2,1)S(1)}, u32[]{:S(2)}, u32[]{:S(2)}) collective-permute-start(bf16[8,32]{0,1:T(8,128)(2,1)S(1)} %get-tuple-element.49), channel_id=1, source_target_pairs={{1,0},{3,32},{5,64},{7,96},{9,128},{11,160},{13,192},{15,224},{17,... | collective-permute-start | bytes 1544 | tf_op jit(solution)/shard_map/ppermute | solution.py:83
  21.2 3.4 %collective-permute-start.4 = (bf16[8,32]{0,1:T(8,128)(2,1)S(1)}, bf16[8,32]{0,1:T(8,128)(2,1)S(1)}, u32[]{:S(2)}, u32[]{:S(2)}) collective-permute-start(bf16[8,32]{0,1:T(8,128)(2,1)S(1)} %get-tuple-element.48), channel_id=1, source_target_pairs={{0,1},{1,2},{2,33},{3,34},{4,65},{5,66},{6,97},{7,98},{8,129},{9,1... | collective-permute-start | bytes 1544 | tf_op jit(solution)/shard_map/ppermute | solution.py:81
  24.6 0.9 convolution_convert_fusion
  25.7 0.9 fusion.50
  26.6 4.9 %collective-permute-start.1 = (bf16[12544]{0:T(1024)(128)(2,1)S(1)}, bf16[12544]{0:T(1024)(128)(2,1)S(1)}, u32[]{:S(2)}, u32[]{:S(2)}) collective-permute-start(bf16[12544]{0:T(1024)(128)(2,1)S(1)} %pad_maximum_fusion.5), channel_id=1, source_target_pairs={{32,0},{64,32},{96,64},{128,96},{160,128},{192,160},{224,192},{256... | collective-permute-start | bytes 75272 | tf_op jit(solution)/shard_map/ppermute | solution.py:18
  31.7 1.9 collective-permute-start
  33.7 1.6 slice_bitcast_fusion.8
  35.4 2.1 %copy.36 = bf16[24,256,128]{1,0,2:T(8,128)(2,1)S(1)} copy(bf16[24,256,128]{2,1,0:T(8,128)(2,1)} %param.13) | data formatting | bytes 3145728 | tf_op args[6]
  38.6 1.8 collective-permute-done
  42.3 1.2 copy.35
  43.5 0.9 pad_maximum_fusion.3
  44.4 1.3 collective-permute-start.3
  45.7 3.7 %collective-permute-start.2 = (bf16[24,264,4]{1,0,2:T(8,128)(2,1)}, bf16[24,264,4]{1,0,2:T(8,128)(2,1)}, u32[]{:S(2)}, u32[]{:S(2)}) collective-permute-start(bf16[24,264,4]{1,0,2:T(8,128)(2,1)} %get-tuple-element.29), channel_id=1, source_target_pairs={{0,1},{1,2},{2,3},{3,4},{4,5},{5,6},{6,7},{7,8},{8,9},{9,10},{10,1... | collective-permute-start | bytes 152072 | tf_op jit(solution)/shard_map/ppermute | solution.py:18
  49.3 0.8 convert_bitcast_fusion
  50.1 1.4 select_convert_fusion
  51.6 9.3 %multiply_add_fusion = f32[32,264,136]{1,0,2:T(8,128)S(1)} fusion(bf16[32,272,144]{1,0,2:T(8,128)(2,1)S(1)} %select_convert_fusion, f32[32]{0:T(128)} %get-tuple-element.46, f32[32]{0:T(128)} %get-tuple-element.47, f32[32]{0:T(128)} %get-tuple-element.40, f32[32]{0:T(128)} %get-tuple-element.41, f32[32]{0:T(128)} %get-tuple-element.42, ...), kind=kLoop, calls=%fused_computation.13 | loop fusion | flops 29872128 | bytes 25277568 | tf_op jit(solution)/shard_map/add | solution.py:99
  60.9 2.8 %copy-done.3 = f32[32,264,136]{1,0,2:T(8,128)} copy-done((f32[32,264,136]{1,0,2:T(8,128)}, f32[32,264,136]{1,0,2:T(8,128)S(1)}, u32[]{:S(2)}) %copy-start.3) | copy-done | bytes 4595736
  63.7 2.6 %multiply_convert_fusion.1 = bf16[32,256,128]{1,0,2:T(8,128)(2,1)} fusion(f32[32,264,136]{1,0,2:T(8,128)S(1)} %multiply_add_fusion), kind=kLoop, calls=%fused_computation.31 | loop fusion | flops 5242880 | bytes 6291456 | tf_op jit(solution)/shard_map/convert_element_type | solution.py:103
  66.3 4.6 %fusion.30 = f32[32,24]{1,0:T(8,128)S(1)} fusion(bf16[24,256,128]{1,0,2:T(8,128)(2,1)S(1)} %copy.36, bf16[32,256,128]{1,0,2:T(8,128)(2,1)} %multiply_convert_fusion.1, bf16[32,272,144]{1,0,2:T(8,128)(2,1)} %copy-done.1, bf16[32,32]{1,0:T(8,128)(2,1)S(1)} %copy-done.19), kind=kOutput, calls=%fused_computation.50 | convolution fusion | flops 120586240 | bytes 5772288 | tf_op jit(solution)/shard_map/ydq,gdq->yg/dot_general | solution.py:133
  71.6 3.5 %fusion.16 = bf16[32,264,136]{1,0,2:T(8,128)(2,1)S(1)} fusion(bf16[24,264,4]{1,0,2:T(8,128)(2,1)} %collective-permute-done.3, bf16[24,4,128]{1,0,2:T(8,128)(2,1)S(1)} %copy.37, bf16[24,256,128]{1,0,2:T(8,128)(2,1)} %copy-done.4, bf16[24,4,128]{1,0,2:T(8,128)(2,1)} %copy-done.5, bf16[24,264,4]{1,0,2:T(8,128)(2,1)} %collective-permute-done.2, ...), kind=kOutput, calls=%fused_computation.32 | convolution fusion | flops 66063360 | bytes 4022784 | tf_op jit(solution)/shard_map/ch,hij->cij/dot_general | solution.py:109
  75.2 3.3 %fusion = bf16[32,264,136]{1,0,2:T(8,128)(2,1)S(1)} fusion(f32[32,264,136]{1,0,2:T(8,128)S(1)} %bitcast.82, bf16[32,264,136]{1,0,2:T(8,128)(2,1)S(1)} %fusion.16, bf16[32,32]{1,0:T(8,128)(2,1)S(1)} %copy-done.20), kind=kOutput, calls=%fused_computation.12 | convolution fusion | flops 83871744 | bytes 9193472 | tf_op jit(solution)/shard_map/co,oij->cij/dot_general | solution.py:111
  78.6 7.0 %fusion.49 = (f32[32,128]{0,1:T(8,128)S(1)}, f32[32,256]{1,0:T(8,128)S(1)}) fusion(bf16[32,264,136]{1,0,2:T(8,128)(2,1)S(1)} %fusion, f32[32]{0:T(128)S(1)} %copy-done.17, f32[32]{0:T(128)S(1)} %copy-done.18, f32[32]{0:T(128)S(1)} %copy-done.11, f32[32]{0:T(128)S(1)} %copy-done.12, f32[32]{0:T(128)S(1)} %copy-done.13, f32[32]{0:T(128)S(1)} %copy-done.14, ...), kind=kLoop, calls=%fused_computation.97 | loop fusion | flops 31444992 | bytes 21021824 | tf_op jit(solution)/shard_map/reduce_sum | solution.py:129
  85.6 7.5 %fusion.15 = (f32[32]{0:T(128)S(1)}, f32[32]{0:T(128)S(1)}, f32[32]{0:T(128)S(1)}, f32[32]{0:T(128)S(1)}, f32[32]{0:T(128)S(1)}, /*index=5*/f32[32]{0:T(128)S(1)}, f32[32]{0:T(128)S(1)}, f32[32]{0:T(128)S(1)}, f32[32]{0:T(128)S(1)}) fusion(bf16[32,272,144]{1,0,2:T(8,128)(2,1)S(1)} %copy-done.2, bf16[32,264,136]{1,0,2:T(8,128)(2,1)S(1)} %fusion), kind=kLoop, calls=%fused_computation.30 | loop fusion | flops 29359840 | bytes 20972672 | tf_op jit(solution)/shard_map/reduce_sum | solution.py:126
  93.1 6.4 %collective-permute-start.7 = (f32[128,32]{1,0:T(8,128)S(1)}, f32[128,32]{1,0:T(8,128)S(1)}, u32[]{:S(2)}, u32[]{:S(2)}) collective-permute-start(f32[128,32]{1,0:T(8,128)S(1)} %bitcast.88), channel_id=1, source_target_pairs={{0,0},{1,1},{2,32},{3,33},{4,64},{5,65},{6,96},{7,97},{8,128},{9,1... | collective-permute-start | bytes 49160 | tf_op jit(solution)/shard_map/ppermute | solution.py:136
  99.6 1.0 fusion.31
  101.0 5.7 %collective-permute-done.7 = f32[128,32]{1,0:T(8,128)S(1)} collective-permute-done((f32[128,32]{1,0:T(8,128)S(1)}, f32[128,32]{1,0:T(8,128)S(1)}, u32[]{:S(2)}, u32[]{:S(2)}) %collective-permute-start.7) | collective-permute-done | bytes 16416 | tf_op jit(solution)/shard_map/ppermute | solution.py:136
  106.9 6.1 %collective-permute-start.8 = (f32[14368]{0:T(1024)S(1)}, f32[14368]{0:T(1024)S(1)}, u32[]{:S(2)}, u32[]{:S(2)}) collective-permute-start(f32[14368]{0:T(1024)S(1)} %concatenate.48), channel_id=1, source_target_pairs={{0,2},{1,3},{2,0},{3,1},{4,6},{5,7},{6,4},{7,5},{8,10},{9,11},{10,... | collective-permute-start | bytes 172424 | tf_op jit(solution)/shard_map/ppermute | solution.py:34
  112.9 2.2 %collective-permute-done.8 = f32[14368]{0:T(1024)S(1)} collective-permute-done((f32[14368]{0:T(1024)S(1)}, f32[14368]{0:T(1024)S(1)}, u32[]{:S(2)}, u32[]{:S(2)}) %collective-permute-start.8) | collective-permute-done | bytes 57504 | tf_op jit(solution)/shard_map/ppermute | solution.py:34
  115.1 10.0 %collective-permute-start.9 = (f32[14368]{0:T(1024)S(1)}, f32[14368]{0:T(1024)S(1)}, u32[]{:S(2)}, u32[]{:S(2)}) collective-permute-start(f32[14368]{0:T(1024)S(1)} %add.175), channel_id=1, source_target_pairs={{0,4},{1,5},{2,6},{3,7},{4,0},{5,1},{6,2},{7,3},{8,12},{9,13},{10,... | collective-permute-start | bytes 172424 | tf_op jit(solution)/shard_map/ppermute | solution.py:34
  125.2 2.3 %collective-permute-done.9 = f32[14368]{0:T(1024)S(1)} collective-permute-done((f32[14368]{0:T(1024)S(1)}, f32[14368]{0:T(1024)S(1)}, u32[]{:S(2)}, u32[]{:S(2)}) %collective-permute-start.9) | collective-permute-done | bytes 57504 | tf_op jit(solution)/shard_map/ppermute | solution.py:34
  127.5 4.6 %collective-permute-start.10 = (f32[14368]{0:T(1024)S(1)}, f32[14368]{0:T(1024)S(1)}, u32[]{:S(2)}, u32[]{:S(2)}) collective-permute-start(f32[14368]{0:T(1024)S(1)} %add.176), channel_id=1, source_target_pairs={{0,8},{1,9},{2,10},{3,11},{4,12},{5,13},{6,14},{7,15},{8,0},{9,1},... | collective-permute-start | bytes 172424 | tf_op jit(solution)/shard_map/ppermute | solution.py:34
  132.1 5.8 %collective-permute-done.10 = f32[14368]{0:T(1024)S(1)} collective-permute-done((f32[14368]{0:T(1024)S(1)}, f32[14368]{0:T(1024)S(1)}, u32[]{:S(2)}, u32[]{:S(2)}) %collective-permute-start.10) | collective-permute-done | bytes 57504 | tf_op jit(solution)/shard_map/ppermute | solution.py:34
  138.0 1.9 collective-permute-start.11
  139.9 4.2 %collective-permute-done.11 = f32[14368]{0:T(1024)S(1)} collective-permute-done((f32[14368]{0:T(1024)S(1)}, f32[14368]{0:T(1024)S(1)}, u32[]{:S(2)}, u32[]{:S(2)}) %collective-permute-start.11) | collective-permute-done | bytes 57504 | tf_op jit(solution)/shard_map/ppermute | solution.py:34
  144.1 1.9 collective-permute-start.12
  146.0 1.2 collective-permute-done.12
  148.6 3.6 %collective-permute-start.13 = (f32[34848]{0:T(1024)S(1)}, f32[34848]{0:T(1024)S(1)}, u32[]{:S(2)}, u32[]{:S(2)}) collective-permute-start(f32[34848]{0:T(1024)S(1)} %pad_maximum_fusion), channel_id=1, source_target_pairs={{0,32},{32,0},{64,96},{96,64},{128,160},{160,128},{192,224},{224,1... | collective-permute-start | bytes 418184 | tf_op jit(solution)/shard_map/ppermute | solution.py:34
  152.2 7.5 %collective-permute-done.13 = f32[34848]{0:T(1024)S(1)} collective-permute-done((f32[34848]{0:T(1024)S(1)}, f32[34848]{0:T(1024)S(1)}, u32[]{:S(2)}, u32[]{:S(2)}) %collective-permute-start.13) | collective-permute-done | bytes 139424 | tf_op jit(solution)/shard_map/ppermute | solution.py:34
  159.7 3.5 %collective-permute-start.14 = (f32[34848]{0:T(1024)S(1)}, f32[34848]{0:T(1024)S(1)}, u32[]{:S(2)}, u32[]{:S(2)}) collective-permute-start(f32[34848]{0:T(1024)S(1)} %fusion.48), channel_id=1, source_target_pairs={{0,64},{32,96},{64,0},{96,32},{128,192},{160,224},{192,128},{224,1... | collective-permute-start | bytes 418184 | tf_op jit(solution)/shard_map/ppermute | solution.py:34
  163.2 9.3 %collective-permute-done.14 = f32[34848]{0:T(1024)S(1)} collective-permute-done((f32[34848]{0:T(1024)S(1)}, f32[34848]{0:T(1024)S(1)}, u32[]{:S(2)}, u32[]{:S(2)}) %collective-permute-start.14) | collective-permute-done | bytes 139424 | tf_op jit(solution)/shard_map/ppermute | solution.py:34
  172.5 1.9 collective-permute-start.15
  174.7 5.4 %collective-permute-done.15 = f32[34848]{0:T(1024)S(1)} collective-permute-done((f32[34848]{0:T(1024)S(1)}, f32[34848]{0:T(1024)S(1)}, u32[]{:S(2)}, u32[]{:S(2)}) %collective-permute-start.15) | collective-permute-done | bytes 139424 | tf_op jit(solution)/shard_map/ppermute | solution.py:34
  180.1 2.1 %collective-permute-start.16 = (f32[34848]{0:T(1024)S(1)}, f32[34848]{0:T(1024)S(1)}, u32[]{:S(2)}, u32[]{:S(2)}) collective-permute-start(f32[34848]{0:T(1024)S(1)} %add.184), channel_id=1, source_target_pairs={{0,256},{32,288},{64,320},{96,352},{128,384},{160,416},{192,448},{... | collective-permute-start | bytes 418184 | tf_op jit(solution)/shard_map/ppermute | solution.py:34
  182.2 0.9 fusion.29
  183.1 5.5 %collective-permute-done.16 = f32[34848]{0:T(1024)S(1)} collective-permute-done((f32[34848]{0:T(1024)S(1)}, f32[34848]{0:T(1024)S(1)}, u32[]{:S(2)}, u32[]{:S(2)}) %collective-permute-start.16) | collective-permute-done | bytes 139424 | tf_op jit(solution)/shard_map/ppermute | solution.py:34
  (118 shorter events, 10.6 us)
Async XLA Ops:
  0.6 1.0 copy-start
  2.5 35.0 %collective-permute-start.5 = (bf16[128,32]{0,1:T(8,128)(2,1)S(1)}, bf16[128,32]{0,1:T(8,128)(2,1)S(1)}, u32[]{:S(2)}, u32[]{:S(2)}) collective-permute-start(bf16[128,32]{0,1:T(8,128)(2,1)S(1)} %dynamic-slice_convert_fusion), channel_id=1, source_target_pairs={{0,0},{1,1},{2,32},{3,33},{4,64},{5,65},{6,96},{7,97},{8,128},{9,1... | collective-permute-start | bytes 24584 | tf_op jit(solution)/shard_map/ppermute | solution.py:82
  12.1 25.5 %collective-permute-start.6 = (bf16[8,32]{0,1:T(8,128)(2,1)S(1)}, bf16[8,32]{0,1:T(8,128)(2,1)S(1)}, u32[]{:S(2)}, u32[]{:S(2)}) collective-permute-start(bf16[8,32]{0,1:T(8,128)(2,1)S(1)} %get-tuple-element.49), channel_id=1, source_target_pairs={{1,0},{3,32},{5,64},{7,96},{9,128},{11,160},{13,192},{15,224},{17,... | collective-permute-start | bytes 1544 | tf_op jit(solution)/shard_map/ppermute | solution.py:83
  21.2 16.4 %collective-permute-start.4 = (bf16[8,32]{0,1:T(8,128)(2,1)S(1)}, bf16[8,32]{0,1:T(8,128)(2,1)S(1)}, u32[]{:S(2)}, u32[]{:S(2)}) collective-permute-start(bf16[8,32]{0,1:T(8,128)(2,1)S(1)} %get-tuple-element.48), channel_id=1, source_target_pairs={{0,1},{1,2},{2,33},{3,34},{4,65},{5,66},{6,97},{7,98},{8,129},{9,1... | collective-permute-start | bytes 1544 | tf_op jit(solution)/shard_map/ppermute | solution.py:81
  26.6 11.1 %collective-permute-start.1 = (bf16[12544]{0:T(1024)(128)(2,1)S(1)}, bf16[12544]{0:T(1024)(128)(2,1)S(1)}, u32[]{:S(2)}, u32[]{:S(2)}) collective-permute-start(bf16[12544]{0:T(1024)(128)(2,1)S(1)} %pad_maximum_fusion.5), channel_id=1, source_target_pairs={{32,0},{64,32},{96,64},{128,96},{160,128},{192,160},{224,192},{256... | collective-permute-start | bytes 75272 | tf_op jit(solution)/shard_map/ppermute | solution.py:18
  31.7 8.7 %collective-permute-start = (bf16[12544]{0:T(1024)(128)(2,1)S(1)}, bf16[12544]{0:T(1024)(128)(2,1)S(1)}, u32[]{:S(2)}, u32[]{:S(2)}) collective-permute-start(bf16[12544]{0:T(1024)(128)(2,1)S(1)} %pad_maximum_fusion.4), channel_id=1, source_target_pairs={{0,32},{32,64},{64,96},{96,128},{128,160},{160,192},{192,224},{224... | collective-permute-start | bytes 75272 | tf_op jit(solution)/shard_map/ppermute | solution.py:18
  37.5 28.8 %copy-start.4 = (bf16[24,256,128]{1,0,2:T(8,128)(2,1)}, bf16[24,256,128]{1,0,2:T(8,128)(2,1)S(1)}, u32[]{:S(2)}) copy-start(bf16[24,256,128]{1,0,2:T(8,128)(2,1)S(1)} %copy.36) | copy-start | bytes 4718596
  43.5 17.4 %copy-start.5 = (bf16[24,4,128]{1,0,2:T(8,128)(2,1)}, bf16[24,4,128]{1,0,2:T(8,128)(2,1)S(1)}, u32[]{:S(2)}) copy-start(bf16[24,4,128]{1,0,2:T(8,128)(2,1)S(1)} %copy.35) | copy-start | bytes 73732
  44.4 27.2 %collective-permute-start.3 = (bf16[24,264,4]{1,0,2:T(8,128)(2,1)}, bf16[24,264,4]{1,0,2:T(8,128)(2,1)}, u32[]{:S(2)}, u32[]{:S(2)}) collective-permute-start(bf16[24,264,4]{1,0,2:T(8,128)(2,1)} %get-tuple-element.30), channel_id=1, source_target_pairs={{1,0},{2,1},{3,2},{4,3},{5,4},{6,5},{7,6},{8,7},{9,8},{10,9},{11,1... | collective-permute-start | bytes 152072 | tf_op jit(solution)/shard_map/ppermute | solution.py:18
  45.7 25.9 %collective-permute-start.2 = (bf16[24,264,4]{1,0,2:T(8,128)(2,1)}, bf16[24,264,4]{1,0,2:T(8,128)(2,1)}, u32[]{:S(2)}, u32[]{:S(2)}) collective-permute-start(bf16[24,264,4]{1,0,2:T(8,128)(2,1)} %get-tuple-element.29), channel_id=1, source_target_pairs={{0,1},{1,2},{2,3},{3,4},{4,5},{5,6},{6,7},{7,8},{8,9},{9,10},{10,1... | collective-permute-start | bytes 152072 | tf_op jit(solution)/shard_map/ppermute | solution.py:18
  51.6 9.3 %copy-start.1 = (bf16[32,272,144]{1,0,2:T(8,128)(2,1)}, bf16[32,272,144]{1,0,2:T(8,128)(2,1)S(1)}, u32[]{:S(2)}) copy-start(bf16[32,272,144]{1,0,2:T(8,128)(2,1)S(1)} %select_convert_fusion) | copy-start | bytes 7520260
  60.9 2.8 %copy-start.3 = (f32[32,264,136]{1,0,2:T(8,128)}, f32[32,264,136]{1,0,2:T(8,128)S(1)}, u32[]{:S(2)}) copy-start(f32[32,264,136]{1,0,2:T(8,128)S(1)} %multiply_add_fusion) | copy-start | bytes 13787140
  63.7 2.6 %copy-start.19 = (bf16[32,32]{1,0:T(8,128)(2,1)S(1)}, bf16[32,32]{1,0:T(8,128)(2,1)}, u32[]{:S(2)}) copy-start(bf16[32,32]{1,0:T(8,128)(2,1)} %param.11) | copy-start | bytes 6148
  70.9 4.2 %slice-start = ((s8[6684672]{0:T(1024)(128)(4,1)}), s8[2490368]{0:T(1024)(128)(4,1)S(1)}, s32[]{:S(2)}) async-start(s8[6684672]{0:T(1024)(128)(4,1)} %bitcast.81), calls=%async_computation | async-start | bytes 4980736
  71.6 3.5 %slice-start.1 = ((s8[6684672]{0:T(1024)(128)(4,1)}), s8[4194304]{0:T(1024)(128)(4,1)S(1)}, s32[]{:S(2)}) async-start(s8[6684672]{0:T(1024)(128)(4,1)} %bitcast.81), calls=%async_computation.1 | async-start | bytes 8388608
  71.6 3.6 %copy-start.20 = (bf16[32,32]{1,0:T(8,128)(2,1)S(1)}, bf16[32,32]{1,0:T(8,128)(2,1)}, u32[]{:S(2)}) copy-start(bf16[32,32]{1,0:T(8,128)(2,1)} %param.11) | copy-start | bytes 6148
  75.1 3.4 %copy-start.10 = (f32[32]{0:T(128)S(1)}, f32[32]{0:T(128)}, u32[]{:S(2)}) copy-start(f32[32]{0:T(128)} %get-tuple-element.39) | copy-start | bytes 388
  75.2 3.4 %copy-start.11 = (f32[32]{0:T(128)S(1)}, f32[32]{0:T(128)}, u32[]{:S(2)}) copy-start(f32[32]{0:T(128)} %get-tuple-element.40) | copy-start | bytes 388
  75.2 3.4 %copy-start.12 = (f32[32]{0:T(128)S(1)}, f32[32]{0:T(128)}, u32[]{:S(2)}) copy-start(f32[32]{0:T(128)} %get-tuple-element.41) | copy-start | bytes 388
  75.2 3.4 %copy-start.13 = (f32[32]{0:T(128)S(1)}, f32[32]{0:T(128)}, u32[]{:S(2)}) copy-start(f32[32]{0:T(128)} %get-tuple-element.42) | copy-start | bytes 388
  75.2 3.4 %copy-start.14 = (f32[32]{0:T(128)S(1)}, f32[32]{0:T(128)}, u32[]{:S(2)}) copy-start(f32[32]{0:T(128)} %get-tuple-element.43) | copy-start | bytes 388
  75.2 3.4 %copy-start.15 = (f32[32]{0:T(128)S(1)}, f32[32]{0:T(128)}, u32[]{:S(2)}) copy-start(f32[32]{0:T(128)} %get-tuple-element.44) | copy-start | bytes 388
  75.2 3.4 %copy-start.16 = (f32[32]{0:T(128)S(1)}, f32[32]{0:T(128)}, u32[]{:S(2)}) copy-start(f32[32]{0:T(128)} %get-tuple-element.45) | copy-start | bytes 388
  75.2 3.4 %copy-start.17 = (f32[32]{0:T(128)S(1)}, f32[32]{0:T(128)}, u32[]{:S(2)}) copy-start(f32[32]{0:T(128)} %get-tuple-element.46) | copy-start | bytes 388
  75.2 3.4 %copy-start.18 = (f32[32]{0:T(128)S(1)}, f32[32]{0:T(128)}, u32[]{:S(2)}) copy-start(f32[32]{0:T(128)} %get-tuple-element.47) | copy-start | bytes 388
  78.6 7.0 %copy-start.2 = (bf16[32,272,144]{1,0,2:T(8,128)(2,1)S(1)}, bf16[32,272,144]{1,0,2:T(8,128)(2,1)}, u32[]{:S(2)}) copy-start(bf16[32,272,144]{1,0,2:T(8,128)(2,1)} %copy-done.1) | copy-start | bytes 7520260
  85.6 13.9 %copy-start.6 = (bf16[32,256,128]{1,0,2:T(8,128)(2,1)S(1)}, bf16[32,256,128]{1,0,2:T(8,128)(2,1)}, u32[]{:S(2)}) copy-start(bf16[32,256,128]{1,0,2:T(8,128)(2,1)} %multiply_convert_fusion.1) | copy-start | bytes 6291460
  93.1 13.7 %copy-start.9 = (f32[768]{0:T(1024)S(1)}, f32[768]{0:T(1024)}, u32[]{:S(2)}) copy-start(f32[768]{0:T(1024)} %reshape.258) | copy-start | bytes 9220
  93.1 81.3 %copy-start.8 = (bf16[512,32]{0,1:T(8,128)(2,1)S(1)}, bf16[512,32]{0,1:T(8,128)(2,1)}, u32[]{:S(2)}) copy-start(bf16[512,32]{0,1:T(8,128)(2,1)} %param.9) | copy-start | bytes 98308
  93.1 89.1 %copy-start.7 = (bf16[512,32]{0,1:T(8,128)(2,1)S(1)}, bf16[512,32]{0,1:T(8,128)(2,1)}, u32[]{:S(2)}) copy-start(bf16[512,32]{0,1:T(8,128)(2,1)} %param.8) | copy-start | bytes 98308
  93.1 13.6 %collective-permute-start.7 = (f32[128,32]{1,0:T(8,128)S(1)}, f32[128,32]{1,0:T(8,128)S(1)}, u32[]{:S(2)}, u32[]{:S(2)}) collective-permute-start(f32[128,32]{1,0:T(8,128)S(1)} %bitcast.88), channel_id=1, source_target_pairs={{0,0},{1,1},{2,32},{3,33},{4,64},{5,65},{6,96},{7,97},{8,128},{9,1... | collective-permute-start | bytes 49160 | tf_op jit(solution)/shard_map/ppermute | solution.py:136
  106.9 8.2 %collective-permute-start.8 = (f32[14368]{0:T(1024)S(1)}, f32[14368]{0:T(1024)S(1)}, u32[]{:S(2)}, u32[]{:S(2)}) collective-permute-start(f32[14368]{0:T(1024)S(1)} %concatenate.48), channel_id=1, source_target_pairs={{0,2},{1,3},{2,0},{3,1},{4,6},{5,7},{6,4},{7,5},{8,10},{9,11},{10,... | collective-permute-start | bytes 172424 | tf_op jit(solution)/shard_map/ppermute | solution.py:34
  115.1 12.3 %collective-permute-start.9 = (f32[14368]{0:T(1024)S(1)}, f32[14368]{0:T(1024)S(1)}, u32[]{:S(2)}, u32[]{:S(2)}) collective-permute-start(f32[14368]{0:T(1024)S(1)} %add.175), channel_id=1, source_target_pairs={{0,4},{1,5},{2,6},{3,7},{4,0},{5,1},{6,2},{7,3},{8,12},{9,13},{10,... | collective-permute-start | bytes 172424 | tf_op jit(solution)/shard_map/ppermute | solution.py:34
  127.5 10.5 %collective-permute-start.10 = (f32[14368]{0:T(1024)S(1)}, f32[14368]{0:T(1024)S(1)}, u32[]{:S(2)}, u32[]{:S(2)}) collective-permute-start(f32[14368]{0:T(1024)S(1)} %add.176), channel_id=1, source_target_pairs={{0,8},{1,9},{2,10},{3,11},{4,12},{5,13},{6,14},{7,15},{8,0},{9,1},... | collective-permute-start | bytes 172424 | tf_op jit(solution)/shard_map/ppermute | solution.py:34
  138.0 6.1 %collective-permute-start.11 = (f32[14368]{0:T(1024)S(1)}, f32[14368]{0:T(1024)S(1)}, u32[]{:S(2)}, u32[]{:S(2)}) collective-permute-start(f32[14368]{0:T(1024)S(1)} %add.177), channel_id=1, source_target_pairs={{0,16},{1,17},{2,18},{3,19},{4,20},{5,21},{6,22},{7,23},{8,24},{9,... | collective-permute-start | bytes 172424 | tf_op jit(solution)/shard_map/ppermute | solution.py:34
  144.1 3.1 %collective-permute-start.12 = (f32[14368]{0:T(1024)S(1)}, f32[14368]{0:T(1024)S(1)}, u32[]{:S(2)}, u32[]{:S(2)}) collective-permute-start(f32[14368]{0:T(1024)S(1)} %add.178), channel_id=1, source_target_pairs={{0,1},{1,0},{2,3},{3,2},{4,5},{5,4},{6,7},{7,6},{8,9},{9,8},{10,11... | collective-permute-start | bytes 172424 | tf_op jit(solution)/shard_map/ppermute | solution.py:34
  148.6 11.1 %collective-permute-start.13 = (f32[34848]{0:T(1024)S(1)}, f32[34848]{0:T(1024)S(1)}, u32[]{:S(2)}, u32[]{:S(2)}) collective-permute-start(f32[34848]{0:T(1024)S(1)} %pad_maximum_fusion), channel_id=1, source_target_pairs={{0,32},{32,0},{64,96},{96,64},{128,160},{160,128},{192,224},{224,1... | collective-permute-start | bytes 418184 | tf_op jit(solution)/shard_map/ppermute | solution.py:34
  159.7 12.7 %collective-permute-start.14 = (f32[34848]{0:T(1024)S(1)}, f32[34848]{0:T(1024)S(1)}, u32[]{:S(2)}, u32[]{:S(2)}) collective-permute-start(f32[34848]{0:T(1024)S(1)} %fusion.48), channel_id=1, source_target_pairs={{0,64},{32,96},{64,0},{96,32},{128,192},{160,224},{192,128},{224,1... | collective-permute-start | bytes 418184 | tf_op jit(solution)/shard_map/ppermute | solution.py:34
  172.5 7.6 %collective-permute-start.15 = (f32[34848]{0:T(1024)S(1)}, f32[34848]{0:T(1024)S(1)}, u32[]{:S(2)}, u32[]{:S(2)}) collective-permute-start(f32[34848]{0:T(1024)S(1)} %add.183), channel_id=1, source_target_pairs={{0,128},{32,160},{64,192},{96,224},{128,0},{160,32},{192,64},{224,... | collective-permute-start | bytes 418184 | tf_op jit(solution)/shard_map/ppermute | solution.py:34
  180.1 8.5 %collective-permute-start.16 = (f32[34848]{0:T(1024)S(1)}, f32[34848]{0:T(1024)S(1)}, u32[]{:S(2)}, u32[]{:S(2)}) collective-permute-start(f32[34848]{0:T(1024)S(1)} %add.184), channel_id=1, source_target_pairs={{0,256},{32,288},{64,320},{96,352},{128,384},{160,416},{192,448},{... | collective-permute-start | bytes 418184 | tf_op jit(solution)/shard_map/ppermute | solution.py:34

commit v5 on v2

--- a/solution.py
+++ b/solution.py
@@ -58,13 +58,10 @@
     cot_rows = jnp.concatenate([before[0], cotangent, after[0]], axis=1)
     left_ext = jnp.concatenate([before[1], left_proj, after[1]], axis=0)
     right_panel = jnp.concatenate([before[2], right_proj, after[2]], axis=0)
-    cot_ext = jnp.concatenate(
-        [
-            shifted(cot_rows[:, :, cols - step :], "col", 1, col_count),
-            cot_rows,
-            shifted(cot_rows[:, :, :step], "col", -1, col_count),
-        ],
-        axis=2,
+    cot_strips = (
+        shifted(cot_rows[:, :, cols - step :], "col", 1, col_count),
+        cot_rows,
+        shifted(cot_rows[:, :, :step], "col", -1, col_count),
     )
 
     def transpose_pairs():
@@ -97,10 +94,20 @@
     pair_tile = pair_ext[:, halo : halo + rows, halo : halo + cols]
     trunk_matrix = (pair_tile.astype(jnp.float32) + mixed_out).astype(jnp.bfloat16)
 
-    trunk_gradient = (
-        grad_scale * jnp.einsum("ch,hij->cij", w_head, cot_ext, preferred_element_type=jnp.float32)
-    ).astype(jnp.bfloat16)
-    grad_hidden = jnp.einsum("co,oij->cij", w_point, trunk_gradient, preferred_element_type=jnp.float32)
+    trunk_strips = [
+        (
+            grad_scale * jnp.einsum("ch,hij->cij", w_head, strip, preferred_element_type=jnp.float32)
+        ).astype(jnp.bfloat16)
+        for strip in cot_strips
+    ]
+    trunk_gradient = jnp.concatenate(trunk_strips, axis=2)
+    grad_hidden = jnp.concatenate(
+        [
+            jnp.einsum("co,oij->cij", w_point, strip, preferred_element_type=jnp.float32)
+            for strip in trunk_strips
+        ],
+        axis=2,
+    )
     conv_grad = (grad_hidden * silu_slope(conv_ext)).astype(jnp.bfloat16)
     conv_grad_tile = conv_grad[:, step : step + rows, step : step + cols].astype(jnp.float32)
     trunk_grad_tile = trunk_gradient[:, step : step + rows, step : step + cols]

time: 182 us -> 214 us (1.18)
  other arithmetic: 31.3 us -> 54.2 us
  local copies, waits for them, and re-layouts: 17.8 us -> 29.4 us
  waiting for transfers between devices: 46.1 us -> 43.2 us
    convert_element_type x0 -> x1, other arithmetic: none -> 29.5 us  [body(): conv_grad = (grad_hidden * silu_slope(conv_ext)).astype(jnp.bfloat16)]
    slice x0 -> x3, local copies, waits for them, and re-layouts: none -> 9.71 us  [the longest x2 6.05 us: body(): cot_rows[:, :, cols - step:]]
    add x1 -> x0, other arithmetic: 9.32 us -> none  [body(): conv_ext + depth_kernel[3 * a + b][:, None, None] * pair_ext[:, step * a:...]
    dot_general x0 -> x2, local copies, waits for them, and re-layouts: none -> 7.3 us  [body(): jnp.einsum('co,oij->cij', w_point, strip, preferred_element_type=jnp.floa...]
    ppermute x1, waiting for transfers between devices: 5.48 us -> 0.01 us  [body(): right_moved = lax.ppermute(right_part, ('row', 'col'), transpose_pairs())]
    ppermute x4, waiting for transfers between devices: 0.01 us -> 5.35 us  [shifted(): return lax.ppermute(x, axis, pairs)]
    ppermute x1, starting transfers between devices: 6.47 us -> 1.92 us  [body(): right_ext = lax.ppermute(own_tile, ('row', 'col'), transpose_pairs())]
    ppermute x1, starting transfers between devices: 6.99 us -> 11 us  [body(): right_moved = lax.ppermute(right_part, ('row', 'col'), transpose_pairs())]
  transfers between devices with their start and end apart: 15 -> 15, of which waited for: 10 -> 10; matrix products, arithmetic and copies ran while one was open for 17% -> 14% of each run, Pallas kernels for 0% -> 0%
where the time goes in v5:
time: 214 us; the launch traced here: 213 us
  starting transfers between devices  70 us (33%)
  other arithmetic  54.2 us (25%)
  waiting for transfers between devices  43.2 us (20%)
  local copies, waits for them, and re-layouts  29.4 us (14%)
  matrix products  14.7 us (7%)
    ppermute x9, starting transfers between devices, xor_round(): return lax.ppermute(flat, axis, [(i, i ^ bit) for i in range(count)])  39.7 us
    ppermute x9, waiting for transfers between devices, xor_round(): return lax.ppermute(flat, axis, [(i, i ^ bit) for i in range(count)])  37.9 us
    convert_element_type x1, other arithmetic, body(): conv_grad = (grad_hidden * silu_slope(conv_ext)).astype(jnp.bfloat16)  29.5 us
    ppermute x4, starting transfers between devices, shifted(): return lax.ppermute(x, axis, pairs)  17.4 us
    ppermute x1, starting transfers between devices, body(): right_moved = lax.ppermute(right_part, ('row', 'col'), transpose_pairs())  11 us
    reduce_sum x1, other arithmetic, body(): kern_terms.append(jnp.sum(conv_grad_tile * window, axis=(1, 2)))  7.34 us
    dot_general x2, local copies, waits for them, and re-layouts, body(): jnp.einsum('co,oij->cij', w_point, strip, preferred_element_type=jnp.floa...  7.3 us
    reduce_sum x1, other arithmetic, body(): right_part = jnp.sum(backward_pass, axis=1).T  7.14 us
  transfers between devices with their start and end apart: 15, of which 10 were waited for; matrix products, arithmetic and copies ran while one was open for 14% of the time, Pallas kernels for 0%

profile of v5, /device:TPU:6, one launch (start us, length us, event | category | flops | bytes accessed | tf_op | source)
XLA Modules:
  0.0 212.7 jit_solution(13617813261133027230)
XLA Ops:
  0.6 0.9 copy-done
  1.6 0.9 convolution_convert_fusion.1
  2.5 0.9 convolution_convert_fusion
  4.0 0.9 fusion.62
  4.8 11.2 %collective-permute-start.1 = (bf16[12800]{0:T(1024)(128)(2,1)S(1)}, bf16[12800]{0:T(1024)(128)(2,1)S(1)}, u32[]{:S(2)}, u32[]{:S(2)}) collective-permute-start(bf16[12800]{0:T(1024)(128)(2,1)S(1)} %pad_maximum_fusion.2), channel_id=1, source_target_pairs={{32,0},{64,32},{96,64},{128,96},{160,128},{192,160},{224,192},{256... | collective-permute-start | bytes 76808 | tf_op jit(solution)/shard_map/ppermute | solution.py:18
  16.4 1.9 collective-permute-start
  18.5 1.0 slice_bitcast_fusion.8
  19.8 5.3 %collective-permute-done = bf16[12800]{0:T(1024)(128)(2,1)S(1)} collective-permute-done((bf16[12800]{0:T(1024)(128)(2,1)S(1)}, bf16[12800]{0:T(1024)(128)(2,1)S(1)}, u32[]{:S(2)}, u32[]{:S(2)}) %collective-permute-start) | collective-permute-done | bytes 25632 | tf_op jit(solution)/shard_map/ppermute | solution.py:18
  25.7 1.9 collective-permute-start.4
  27.6 2.5 %copy_dynamic-update-slice_fusion = bf16[24,264,128]{2,0,1:T(8,128)(2,1)S(1)} fusion(bf16[24,264,128]{2,0,1:T(8,128)(2,1)S(1)} %copy_dynamic-update-slice_fusion.2, bf16[24,256,128]{2,1,0:T(8,128)(2,1)} %param.13), kind=kLoop, calls=%fused_computation.38 | loop fusion | bytes 3145728
  30.2 2.4 %fusion.61 = (bf16[24,264,4]{2,0,1:T(8,128)(2,1)}, bf16[24,264,4]{2,0,1:T(8,128)(2,1)}) fusion(bf16[24,264,128]{2,0,1:T(8,128)(2,1)S(1)} %copy_dynamic-update-slice_fusion.1), kind=kLoop, calls=%fused_computation.111 | loop fusion | bytes 202752 | tf_op jit(solution)/shard_map/slice | solution.py:62
  32.6 0.8 fusion.18
  33.4 3.7 %copy.50 = bf16[24,264,4]{1,0,2:T(8,128)(2,1)S(1)} copy(bf16[24,264,4]{2,0,1:T(8,128)(2,1)} %get-tuple-element.31) | data formatting | bytes 101376 | tf_op jit(solution)/shard_map/slice | solution.py:62
  37.0 3.7 %copy.52 = bf16[24,264,4]{1,0,2:T(8,128)(2,1)S(1)} copy(bf16[24,264,4]{2,0,1:T(8,128)(2,1)} %get-tuple-element.32) | data formatting | bytes 101376 | tf_op jit(solution)/shard_map/slice | solution.py:64
  40.7 1.3 collective-permute-start.3
  42.0 3.0 %collective-permute-start.2 = (bf16[24,264,4]{1,0,2:T(8,128)(2,1)S(1)}, bf16[24,264,4]{1,0,2:T(8,128)(2,1)S(1)}, u32[]{:S(2)}, u32[]{:S(2)}) collective-permute-start(bf16[24,264,4]{1,0,2:T(8,128)(2,1)S(1)} %copy.50), channel_id=1, source_target_pairs={{0,1},{1,2},{2,3},{3,4},{4,5},{5,6},{6,7},{7,8},{8,9},{9,10},{10,1... | collective-permute-start | bytes 152072 | tf_op jit(solution)/shard_map/ppermute | solution.py:18
  45.0 2.7 %convolution_bitcast_fusion = f32[32,264,128]{2,0,1:T(8,128)} fusion(bf16[32,264,128]{2,0,1:T(8,128)(2,1)S(1)} %fusion.18, bf16[32,32]{1,0:T(8,128)(2,1)S(1)} %copy-done.3), kind=kOutput, calls=%fused_computation.32 | convolution fusion | flops 69206016 | bytes 6490112 | tf_op jit(solution)/shard_map/co,oij->cij/dot_general | solution.py:106
  47.9 3.7 %select_convert_fusion = bf16[32,272,144]{2,0,1:T(8,128)(2,1)} fusion(f32[32,144]{1,0:T(8,128)S(1)} %convert_bitcast_fusion.1, f32[32,272]{0,1:T(8,128)S(1)} %copy.56, pred[272,144]{1,0:T(8,128)(4,1)S(1)} %and_and_fusion), kind=kLoop, calls=%fused_computation.10 | loop fusion | flops 3760128 | bytes 2599168 | tf_op jit(solution)/shard_map/convert_element_type | solution.py:81
  51.9 3.7 %copy.53 = f32[264,4,32]{1,2,0:T(8,128)} copy(f32[264,4,32]{0,2,1:T(8,128)S(1)} %fusion.27) | data formatting | bytes 270336 | tf_op jit(solution)/shard_map/co,oij->cij/dot_general | solution.py:106
  56.0 3.6 %copy.51 = f32[264,4,32]{1,2,0:T(8,128)} copy(f32[264,4,32]{0,2,1:T(8,128)S(1)} %fusion.26) | data formatting | bytes 270336 | tf_op jit(solution)/shard_map/co,oij->cij/dot_general | solution.py:106
  59.6 29.5 %fusion = (bf16[32,264,136]{2,0,1:T(8,128)(2,1)S(1)}, f32[32,264,136]{2,0,1:T(8,128)}) fusion(f32[32,264,4]{2,0,1:T(8,128)} %bitcast.103, f32[32,264,128]{2,0,1:T(8,128)} %convolution_bitcast_fusion, f32[32,264,4]{2,0,1:T(8,128)} %bitcast.104, bf16[32,272,144]{2,0,1:T(8,128)(2,1)} %select_convert_fusion, f32[32]{0:T(128)S(1)} %get-tuple-element.54, ...), kind=kLoop, calls=%fused_computation.12 | loop fusion | flops 42510336 | bytes 32171136 | tf_op jit(solution)/shard_map/convert_element_type | solution.py:111
  89.2 7.3 %fusion.15 = (f32[32]{0:T(128)S(1)}, f32[32]{0:T(128)S(1)}, f32[32]{0:T(128)S(1)}, f32[32]{0:T(128)S(1)}, f32[32]{0:T(128)S(1)}, /*index=5*/f32[32]{0:T(128)S(1)}, f32[32]{0:T(128)S(1)}, f32[32]{0:T(128)S(1)}, f32[32]{0:T(128)S(1)}) fusion(bf16[32,272,144]{2,0,1:T(8,128)(2,1)S(1)} %bitcast.102, bf16[32,264,136]{2,0,1:T(8,128)(2,1)S(1)} %get-tuple-element.29), kind=kLoop, calls=%fused_computation.30 | loop fusion | flops 29359840 | bytes 20972672 | tf_op jit(solution)/shard_map/reduce_sum | solution.py:125
  96.5 7.1 %fusion.60 = (f32[32,128]{1,0:T(8,128)S(1)}, f32[32,256]{0,1:T(8,128)S(1)}) fusion(bf16[32,264,136]{2,0,1:T(8,128)(2,1)S(1)} %get-tuple-element.29, f32[32]{0:T(128)S(1)} %get-tuple-element.54, f32[32]{0:T(128)S(1)} %get-tuple-element.55, f32[32]{0:T(128)S(1)} %get-tuple-element.48, f32[32]{0:T(128)S(1)} %get-tuple-element.49, f32[32]{0:T(128)S(1)} %get-tuple-element.50, ...), kind=kLoop, calls=%fused_computation.110 | loop fusion | flops 31444992 | bytes 21021824 | tf_op jit(solution)/shard_map/reduce_sum | solution.py:128
  103.6 5.9 %multiply_convert_fusion.1 = bf16[32,256,128]{2,0,1:T(8,128)(2,1)} fusion(f32[32,264,136]{2,0,1:T(8,128)} %get-tuple-element.30), kind=kLoop, calls=%fused_computation.31 | loop fusion | flops 5242880 | bytes 6291456 | tf_op jit(solution)/shard_map/convert_element_type | solution.py:92
  109.5 5.0 %fusion.28 = f32[32,24]{1,0:T(8,128)S(1)} fusion(bf16[24,256,128]{2,1,0:T(8,128)(2,1)} %param.13, bf16[32,256,128]{2,0,1:T(8,128)(2,1)} %multiply_convert_fusion.1, bf16[32,272,144]{2,0,1:T(8,128)(2,1)} %select_convert_fusion, bf16[32,32]{1,0:T(8,128)(2,1)S(1)} %copy-done.3), kind=kOutput, calls=%fused_computation.53 | convolution fusion | flops 120586240 | bytes 5772288 | tf_op jit(solution)/shard_map/ydq,gdq->yg/dot_general | solution.py:132
  114.5 11.0 %collective-permute-start.5 = (f32[128,32]{0,1:T(8,128)S(1)}, f32[128,32]{0,1:T(8,128)S(1)}, u32[]{:S(2)}, u32[]{:S(2)}) collective-permute-start(f32[128,32]{0,1:T(8,128)S(1)} %bitcast.110), channel_id=1, source_target_pairs={{0,0},{1,1},{2,32},{3,33},{4,64},{5,65},{6,96},{7,97},{8,128},{9,1... | collective-permute-start | bytes 49160 | tf_op jit(solution)/shard_map/ppermute | solution.py:135
  125.5 2.3 %fusion.31 = f32[32,32]{1,0:T(8,128)S(1)} fusion(bf16[32,256,128]{2,0,1:T(8,128)(2,1)} %multiply_convert_fusion.1, bf16[32,264,128]{2,0,1:T(8,128)(2,1)S(1)} %fusion.18), kind=kOutput, calls=%fused_computation.54 | convolution fusion | flops 67108864 | bytes 4198400 | tf_op jit(solution)/shard_map/fsk,gsk->fg/dot_general | solution.py:129
  128.4 4.4 %collective-permute-start.6 = (f32[14368]{0:T(1024)S(1)}, f32[14368]{0:T(1024)S(1)}, u32[]{:S(2)}, u32[]{:S(2)}) collective-permute-start(f32[14368]{0:T(1024)S(1)} %concatenate.48), channel_id=1, source_target_pairs={{0,2},{1,3},{2,0},{3,1},{4,6},{5,7},{6,4},{7,5},{8,10},{9,11},{10,... | collective-permute-start | bytes 172424 | tf_op jit(solution)/shard_map/ppermute | solution.py:34
  132.8 2.3 %collective-permute-done.6 = f32[14368]{0:T(1024)S(1)} collective-permute-done((f32[14368]{0:T(1024)S(1)}, f32[14368]{0:T(1024)S(1)}, u32[]{:S(2)}, u32[]{:S(2)}) %collective-permute-start.6) | collective-permute-done | bytes 57504 | tf_op jit(solution)/shard_map/ppermute | solution.py:34
  135.1 6.4 %collective-permute-start.7 = (f32[14368]{0:T(1024)S(1)}, f32[14368]{0:T(1024)S(1)}, u32[]{:S(2)}, u32[]{:S(2)}) collective-permute-start(f32[14368]{0:T(1024)S(1)} %add.175), channel_id=1, source_target_pairs={{0,4},{1,5},{2,6},{3,7},{4,0},{5,1},{6,2},{7,3},{8,12},{9,13},{10,... | collective-permute-start | bytes 172424 | tf_op jit(solution)/shard_map/ppermute | solution.py:34
  141.5 2.8 %collective-permute-done.7 = f32[14368]{0:T(1024)S(1)} collective-permute-done((f32[14368]{0:T(1024)S(1)}, f32[14368]{0:T(1024)S(1)}, u32[]{:S(2)}, u32[]{:S(2)}) %collective-permute-start.7) | collective-permute-done | bytes 57504 | tf_op jit(solution)/shard_map/ppermute | solution.py:34
  144.4 5.6 %collective-permute-start.8 = (f32[14368]{0:T(1024)S(1)}, f32[14368]{0:T(1024)S(1)}, u32[]{:S(2)}, u32[]{:S(2)}) collective-permute-start(f32[14368]{0:T(1024)S(1)} %add.176), channel_id=1, source_target_pairs={{0,8},{1,9},{2,10},{3,11},{4,12},{5,13},{6,14},{7,15},{8,0},{9,1},... | collective-permute-start | bytes 172424 | tf_op jit(solution)/shard_map/ppermute | solution.py:34
  150.0 4.5 %collective-permute-done.8 = f32[14368]{0:T(1024)S(1)} collective-permute-done((f32[14368]{0:T(1024)S(1)}, f32[14368]{0:T(1024)S(1)}, u32[]{:S(2)}, u32[]{:S(2)}) %collective-permute-start.8) | collective-permute-done | bytes 57504 | tf_op jit(solution)/shard_map/ppermute | solution.py:34
  154.5 4.3 %collective-permute-start.9 = (f32[14368]{0:T(1024)S(1)}, f32[14368]{0:T(1024)S(1)}, u32[]{:S(2)}, u32[]{:S(2)}) collective-permute-start(f32[14368]{0:T(1024)S(1)} %add.177), channel_id=1, source_target_pairs={{0,16},{1,17},{2,18},{3,19},{4,20},{5,21},{6,22},{7,23},{8,24},{9,... | collective-permute-start | bytes 172424 | tf_op jit(solution)/shard_map/ppermute | solution.py:34
  158.8 2.2 %collective-permute-done.9 = f32[14368]{0:T(1024)S(1)} collective-permute-done((f32[14368]{0:T(1024)S(1)}, f32[14368]{0:T(1024)S(1)}, u32[]{:S(2)}, u32[]{:S(2)}) %collective-permute-start.9) | collective-permute-done | bytes 57504 | tf_op jit(solution)/shard_map/ppermute | solution.py:34
  161.0 1.9 collective-permute-start.10
  162.9 1.2 collective-permute-done.10
  165.5 5.1 %collective-permute-start.11 = (f32[34848]{0:T(1024)S(1)}, f32[34848]{0:T(1024)S(1)}, u32[]{:S(2)}, u32[]{:S(2)}) collective-permute-start(f32[34848]{0:T(1024)S(1)} %pad_maximum_fusion), channel_id=1, source_target_pairs={{0,32},{32,0},{64,96},{96,64},{128,160},{160,128},{192,224},{224,1... | collective-permute-start | bytes 418184 | tf_op jit(solution)/shard_map/ppermute | solution.py:34
  170.6 7.1 %collective-permute-done.11 = f32[34848]{0:T(1024)S(1)} collective-permute-done((f32[34848]{0:T(1024)S(1)}, f32[34848]{0:T(1024)S(1)}, u32[]{:S(2)}, u32[]{:S(2)}) %collective-permute-start.11) | collective-permute-done | bytes 139424 | tf_op jit(solution)/shard_map/ppermute | solution.py:34
  177.8 8.1 %collective-permute-start.12 = (f32[34848]{0:T(1024)S(1)}, f32[34848]{0:T(1024)S(1)}, u32[]{:S(2)}, u32[]{:S(2)}) collective-permute-start(f32[34848]{0:T(1024)S(1)} %fusion.59), channel_id=1, source_target_pairs={{0,64},{32,96},{64,0},{96,32},{128,192},{160,224},{192,128},{224,1... | collective-permute-start | bytes 418184 | tf_op jit(solution)/shard_map/ppermute | solution.py:34
  185.9 6.1 %collective-permute-done.12 = f32[34848]{0:T(1024)S(1)} collective-permute-done((f32[34848]{0:T(1024)S(1)}, f32[34848]{0:T(1024)S(1)}, u32[]{:S(2)}, u32[]{:S(2)}) %collective-permute-start.12) | collective-permute-done | bytes 139424 | tf_op jit(solution)/shard_map/ppermute | solution.py:34
  192.0 1.9 collective-permute-start.13
  194.2 5.9 %collective-permute-done.13 = f32[34848]{0:T(1024)S(1)} collective-permute-done((f32[34848]{0:T(1024)S(1)}, f32[34848]{0:T(1024)S(1)}, u32[]{:S(2)}, u32[]{:S(2)}) %collective-permute-start.13) | collective-permute-done | bytes 139424 | tf_op jit(solution)/shard_map/ppermute | solution.py:34
  200.2 1.9 collective-permute-start.14
  202.1 0.9 fusion.21
  203.0 5.7 %collective-permute-done.14 = f32[34848]{0:T(1024)S(1)} collective-permute-done((f32[34848]{0:T(1024)S(1)}, f32[34848]{0:T(1024)S(1)}, u32[]{:S(2)}, u32[]{:S(2)}) %collective-permute-start.14) | collective-permute-done | bytes 139424 | tf_op jit(solution)/shard_map/ppermute | solution.py:34
  211.1 0.7 copy.68
  212.0 0.7 copy.67
  (96 shorter events, 7.5 us)
Async XLA Ops:
  0.6 1.0 copy-start
  4.8 14.6 %collective-permute-start.1 = (bf16[12800]{0:T(1024)(128)(2,1)S(1)}, bf16[12800]{0:T(1024)(128)(2,1)S(1)}, u32[]{:S(2)}, u32[]{:S(2)}) collective-permute-start(bf16[12800]{0:T(1024)(128)(2,1)S(1)} %pad_maximum_fusion.2), channel_id=1, source_target_pairs={{32,0},{64,32},{96,64},{128,96},{160,128},{192,160},{224,192},{256... | collective-permute-start | bytes 76808 | tf_op jit(solution)/shard_map/ppermute | solution.py:18
  16.4 8.8 %collective-permute-start = (bf16[12800]{0:T(1024)(128)(2,1)S(1)}, bf16[12800]{0:T(1024)(128)(2,1)S(1)}, u32[]{:S(2)}, u32[]{:S(2)}) collective-permute-start(bf16[12800]{0:T(1024)(128)(2,1)S(1)} %pad_maximum_fusion.1), channel_id=1, source_target_pairs={{0,32},{32,64},{64,96},{96,128},{128,160},{160,192},{192,224},{224... | collective-permute-start | bytes 76808 | tf_op jit(solution)/shard_map/ppermute | solution.py:18
  25.7 22.2 %collective-permute-start.4 = (bf16[144,32]{0,1:T(8,128)(2,1)S(1)}, bf16[144,32]{0,1:T(8,128)(2,1)S(1)}, u32[]{:S(2)}, u32[]{:S(2)}) collective-permute-start(bf16[144,32]{0,1:T(8,128)(2,1)S(1)} %fusion.38), channel_id=1, source_target_pairs={{0,0},{1,1},{2,32},{3,33},{4,64},{5,65},{6,96},{7,97},{8,128},{9,1... | collective-permute-start | bytes 27656 | tf_op jit(solution)/shard_map/ppermute | solution.py:75
  27.6 5.0 %copy-start.4 = (bf16[32,24]{0,1:T(8,128)(2,1)S(1)}, bf16[32,24]{0,1:T(8,128)(2,1)}, u32[]{:S(2)}) copy-start(bf16[32,24]{0,1:T(8,128)(2,1)} %param.12) | copy-start | bytes 4612
  32.6 12.5 %copy-start.3 = (bf16[32,32]{1,0:T(8,128)(2,1)S(1)}, bf16[32,32]{1,0:T(8,128)(2,1)}, u32[]{:S(2)}) copy-start(bf16[32,32]{1,0:T(8,128)(2,1)} %param.11) | copy-start | bytes 6148
  40.7 10.9 %collective-permute-start.3 = (bf16[24,264,4]{1,0,2:T(8,128)(2,1)S(1)}, bf16[24,264,4]{1,0,2:T(8,128)(2,1)S(1)}, u32[]{:S(2)}, u32[]{:S(2)}) collective-permute-start(bf16[24,264,4]{1,0,2:T(8,128)(2,1)S(1)} %copy.52), channel_id=1, source_target_pairs={{1,0},{2,1},{3,2},{4,3},{5,4},{6,5},{7,6},{8,7},{9,8},{10,9},{11,1... | collective-permute-start | bytes 152072 | tf_op jit(solution)/shard_map/ppermute | solution.py:18
  42.0 13.6 %collective-permute-start.2 = (bf16[24,264,4]{1,0,2:T(8,128)(2,1)S(1)}, bf16[24,264,4]{1,0,2:T(8,128)(2,1)S(1)}, u32[]{:S(2)}, u32[]{:S(2)}) collective-permute-start(bf16[24,264,4]{1,0,2:T(8,128)(2,1)S(1)} %copy.50), channel_id=1, source_target_pairs={{0,1},{1,2},{2,3},{3,4},{4,5},{5,6},{6,7},{7,8},{8,9},{9,10},{10,1... | collective-permute-start | bytes 152072 | tf_op jit(solution)/shard_map/ppermute | solution.py:18
  55.9 33.2 %slice-start = ((s8[4456448]{0:T(1024)(128)(4,1)}), s8[262144]{0:T(1024)(128)(4,1)S(1)}, s32[]{:S(2)}) async-start(s8[4456448]{0:T(1024)(128)(4,1)} %bitcast.101), calls=%async_computation | async-start | bytes 524288
  59.6 29.5 %slice-start.1 = ((s8[4456448]{0:T(1024)(128)(4,1)}), s8[4194304]{0:T(1024)(128)(4,1)S(1)}, s32[]{:S(2)}) async-start(s8[4456448]{0:T(1024)(128)(4,1)} %bitcast.101), calls=%async_computation.1 | async-start | bytes 8388608
  114.5 79.5 %copy-start.2 = (bf16[512,32]{0,1:T(8,128)(2,1)S(1)}, bf16[512,32]{0,1:T(8,128)(2,1)}, u32[]{:S(2)}) copy-start(bf16[512,32]{0,1:T(8,128)(2,1)} %param.9) | copy-start | bytes 98308
  114.5 87.6 %copy-start.1 = (bf16[512,32]{0,1:T(8,128)(2,1)S(1)}, bf16[512,32]{0,1:T(8,128)(2,1)}, u32[]{:S(2)}) copy-start(bf16[512,32]{0,1:T(8,128)(2,1)} %param.8) | copy-start | bytes 98308
  114.5 13.6 %collective-permute-start.5 = (f32[128,32]{0,1:T(8,128)S(1)}, f32[128,32]{0,1:T(8,128)S(1)}, u32[]{:S(2)}, u32[]{:S(2)}) collective-permute-start(f32[128,32]{0,1:T(8,128)S(1)} %bitcast.110), channel_id=1, source_target_pairs={{0,0},{1,1},{2,32},{3,33},{4,64},{5,65},{6,96},{7,97},{8,128},{9,1... | collective-permute-start | bytes 49160 | tf_op jit(solution)/shard_map/ppermute | solution.py:135
  128.4 6.7 %collective-permute-start.6 = (f32[14368]{0:T(1024)S(1)}, f32[14368]{0:T(1024)S(1)}, u32[]{:S(2)}, u32[]{:S(2)}) collective-permute-start(f32[14368]{0:T(1024)S(1)} %concatenate.48), channel_id=1, source_target_pairs={{0,2},{1,3},{2,0},{3,1},{4,6},{5,7},{6,4},{7,5},{8,10},{9,11},{10,... | collective-permute-start | bytes 172424 | tf_op jit(solution)/shard_map/ppermute | solution.py:34
  135.1 9.3 %collective-permute-start.7 = (f32[14368]{0:T(1024)S(1)}, f32[14368]{0:T(1024)S(1)}, u32[]{:S(2)}, u32[]{:S(2)}) collective-permute-start(f32[14368]{0:T(1024)S(1)} %add.175), channel_id=1, source_target_pairs={{0,4},{1,5},{2,6},{3,7},{4,0},{5,1},{6,2},{7,3},{8,12},{9,13},{10,... | collective-permute-start | bytes 172424 | tf_op jit(solution)/shard_map/ppermute | solution.py:34
  144.4 10.1 %collective-permute-start.8 = (f32[14368]{0:T(1024)S(1)}, f32[14368]{0:T(1024)S(1)}, u32[]{:S(2)}, u32[]{:S(2)}) collective-permute-start(f32[14368]{0:T(1024)S(1)} %add.176), channel_id=1, source_target_pairs={{0,8},{1,9},{2,10},{3,11},{4,12},{5,13},{6,14},{7,15},{8,0},{9,1},... | collective-permute-start | bytes 172424 | tf_op jit(solution)/shard_map/ppermute | solution.py:34
  154.5 6.5 %collective-permute-start.9 = (f32[14368]{0:T(1024)S(1)}, f32[14368]{0:T(1024)S(1)}, u32[]{:S(2)}, u32[]{:S(2)}) collective-permute-start(f32[14368]{0:T(1024)S(1)} %add.177), channel_id=1, source_target_pairs={{0,16},{1,17},{2,18},{3,19},{4,20},{5,21},{6,22},{7,23},{8,24},{9,... | collective-permute-start | bytes 172424 | tf_op jit(solution)/shard_map/ppermute | solution.py:34
  161.0 3.1 %collective-permute-start.10 = (f32[14368]{0:T(1024)S(1)}, f32[14368]{0:T(1024)S(1)}, u32[]{:S(2)}, u32[]{:S(2)}) collective-permute-start(f32[14368]{0:T(1024)S(1)} %add.178), channel_id=1, source_target_pairs={{0,1},{1,0},{2,3},{3,2},{4,5},{5,4},{6,7},{7,6},{8,9},{9,8},{10,11... | collective-permute-start | bytes 172424 | tf_op jit(solution)/shard_map/ppermute | solution.py:34
  165.5 12.3 %collective-permute-start.11 = (f32[34848]{0:T(1024)S(1)}, f32[34848]{0:T(1024)S(1)}, u32[]{:S(2)}, u32[]{:S(2)}) collective-permute-start(f32[34848]{0:T(1024)S(1)} %pad_maximum_fusion), channel_id=1, source_target_pairs={{0,32},{32,0},{64,96},{96,64},{128,160},{160,128},{192,224},{224,1... | collective-permute-start | bytes 418184 | tf_op jit(solution)/shard_map/ppermute | solution.py:34
  177.8 14.2 %collective-permute-start.12 = (f32[34848]{0:T(1024)S(1)}, f32[34848]{0:T(1024)S(1)}, u32[]{:S(2)}, u32[]{:S(2)}) collective-permute-start(f32[34848]{0:T(1024)S(1)} %fusion.59), channel_id=1, source_target_pairs={{0,64},{32,96},{64,0},{96,32},{128,192},{160,224},{192,128},{224,1... | collective-permute-start | bytes 418184 | tf_op jit(solution)/shard_map/ppermute | solution.py:34
  192.0 8.1 %collective-permute-start.13 = (f32[34848]{0:T(1024)S(1)}, f32[34848]{0:T(1024)S(1)}, u32[]{:S(2)}, u32[]{:S(2)}) collective-permute-start(f32[34848]{0:T(1024)S(1)} %add.183), channel_id=1, source_target_pairs={{0,128},{32,160},{64,192},{96,224},{128,0},{160,32},{192,64},{224,... | collective-permute-start | bytes 418184 | tf_op jit(solution)/shard_map/ppermute | solution.py:34
  200.2 8.5 %collective-permute-start.14 = (f32[34848]{0:T(1024)S(1)}, f32[34848]{0:T(1024)S(1)}, u32[]{:S(2)}, u32[]{:S(2)}) collective-permute-start(f32[34848]{0:T(1024)S(1)} %add.184), channel_id=1, source_target_pairs={{0,256},{32,288},{64,320},{96,352},{128,384},{160,416},{192,448},{... | collective-permute-start | bytes 418184 | tf_op jit(solution)/shard_map/ppermute | solution.py:34

commit v6 on v2

--- a/solution.py
+++ b/solution.py
@@ -80,8 +80,13 @@
     row_place = r * rows - halo + lax.broadcasted_iota(jnp.int32, (rows + 2 * halo, 1), 0)
     col_place = k * cols - halo + lax.broadcasted_iota(jnp.int32, (1, cols + 2 * halo), 1)
     valid = (row_place >= 0) & (row_place < bins) & (col_place >= 0) & (col_place < bins)
-    pair_sum = left_ext.astype(jnp.float32).T[:, :, None] + right_ext.astype(jnp.float32).T[:, None, :]
-    pair_ext = jnp.where(valid[None], pair_sum, 0.0).astype(jnp.bfloat16)
+    pair_sum = right_ext.astype(jnp.float32).T[:, :, None] + left_ext.astype(jnp.float32).T[:, None, :]
+    pair_ext = jnp.where(valid.T[None], pair_sum, 0.0).astype(jnp.bfloat16)
+    cot_ext = cot_ext.transpose(0, 2, 1)
+    cotangent = cotangent.transpose(0, 2, 1)
+    taps_by_col = depth_kernel.reshape(3, 3, -1).transpose(1, 0, 2).reshape(depth_kernel.shape)
+    depth_kernel = taps_by_col
+    rows, cols = cols, rows
 
     ext_rows = rows + 2 * step
     ext_cols = cols + 2 * step
@@ -117,8 +122,10 @@
             ].astype(jnp.float32)
             kern_terms.append(jnp.sum(conv_grad_tile * window, axis=(1, 2)))
     kernel_part = jnp.stack(kern_terms)
-    left_part = jnp.sum(backward_pass, axis=2).T
-    right_part = jnp.sum(backward_pass, axis=1).T
+    kernel_part = kernel_part.reshape(3, 3, -1).transpose(1, 0, 2).reshape(kernel_part.shape)
+    left_part = jnp.sum(backward_pass, axis=1).T
+    right_part = jnp.sum(backward_pass, axis=2).T
+    rows, cols = cols, rows
     point_part = jnp.einsum(
         "fsk,gsk->fg", hidden_state, trunk_grad_tile, preferred_element_type=jnp.float32
     )

time: 182 us -> 190 us (1.044)
  local copies, waits for them, and re-layouts: 17.8 us -> 22.4 us
    ppermute x1, waiting for transfers between devices: 5.48 us -> 1.71 us  [body(): right_moved = lax.ppermute(right_part, ('row', 'col'), transpose_pairs())]
    ppermute x1, starting transfers between devices: 6.99 us -> 10.7 us  [body(): right_moved = lax.ppermute(right_part, ('row', 'col'), transpose_pairs())]
    slice x6, local copies, waits for them, and re-layouts: 0.94 us -> 3.91 us  [unpacked(): out.append(flat[at:at + like.size].reshape(like.shape))]
    ppermute x9, waiting for transfers between devices: 40.6 us -> 43.3 us  [xor_round(): return lax.ppermute(flat, axis, [(i, i ^ bit) for i in range(count)])]
    ppermute x1, starting transfers between devices: 6.47 us -> 4.15 us  [body(): right_ext = lax.ppermute(own_tile, ('row', 'col'), transpose_pairs())]
    unnamed x50 -> x56, local copies, waits for them, and re-layouts: 8.12 us -> 8.14 us
  transfers between devices with their start and end apart: 15 -> 15, of which waited for: 10 -> 11; matrix products, arithmetic and copies ran while one was open for 17% -> 19% of each run, Pallas kernels for 0% -> 0%
where the time goes in v6:
time: 190 us; the launch traced here: 188 us
  starting transfers between devices  70.6 us (37%)
  waiting for transfers between devices  45.8 us (24%)
  other arithmetic  32 us (17%)
  local copies, waits for them, and re-layouts  22.4 us (12%)
  matrix products  16.2 us (9%)
    ppermute x9, waiting for transfers between devices, xor_round(): return lax.ppermute(flat, axis, [(i, i ^ bit) for i in range(count)])  43.3 us
    ppermute x9, starting transfers between devices, xor_round(): return lax.ppermute(flat, axis, [(i, i ^ bit) for i in range(count)])  37.7 us
    ppermute x4, starting transfers between devices, shifted(): return lax.ppermute(x, axis, pairs)  18.1 us
    ppermute x1, starting transfers between devices, body(): right_moved = lax.ppermute(right_part, ('row', 'col'), transpose_pairs())  10.7 us
    add x1, other arithmetic, body(): conv_ext + depth_kernel[3 * a + b][:, None, None] * pair_ext[:, step * a:...  9.35 us
    unnamed x56, local copies, waits for them, and re-layouts  8.14 us
    reduce_sum x1, other arithmetic, body(): kern_terms.append(jnp.sum(conv_grad_tile * window, axis=(1, 2)))  7.43 us
    reduce_sum x1, other arithmetic, body(): right_part = jnp.sum(backward_pass, axis=2).T  6.97 us
  transfers between devices with their start and end apart: 15, of which 11 were waited for; matrix products, arithmetic and copies ran while one was open for 19% of the time, Pallas kernels for 0%

profile of v6, /device:TPU:6, one launch (start us, length us, event | category | flops | bytes accessed | tf_op | source)
XLA Modules:
  0.0 188.4 jit_solution(7769351590748237634)
XLA Ops:
  0.7 0.9 copy-done
  1.6 0.9 convolution_convert_fusion
  2.8 0.9 convolution_convert_fusion.1
  4.0 0.9 fusion.51
  4.8 11.2 %collective-permute-start.1 = (bf16[12800]{0:T(1024)(128)(2,1)S(1)}, bf16[12800]{0:T(1024)(128)(2,1)}, u32[]{:S(2)}, u32[]{:S(2)}) collective-permute-start(bf16[12800]{0:T(1024)(128)(2,1)S(1)} %pad_maximum_fusion.5), channel_id=1, source_target_pairs={{32,0},{64,32},{96,64},{128,96},{160,128},{192,160},{224,192},{256... | collective-permute-start | bytes 76808 | tf_op jit(solution)/shard_map/ppermute | solution.py:18
  17.0 1.9 %collective-permute-start = (bf16[12800]{0:T(1024)(128)(2,1)}, bf16[12800]{0:T(1024)(128)(2,1)}, u32[]{:S(2)}, u32[]{:S(2)}) collective-permute-start(bf16[12800]{0:T(1024)(128)(2,1)} %pad_maximum_fusion.4), channel_id=1, source_target_pairs={{0,32},{32,64},{64,96},{96,128},{128,160},{160,192},{192,224},{224... | collective-permute-start | bytes 76808 | tf_op jit(solution)/shard_map/ppermute | solution.py:18
  20.4 2.1 %copy.47 = bf16[24,256,128]{1,0,2:T(8,128)(2,1)S(1)} copy(bf16[24,256,128]{2,1,0:T(8,128)(2,1)} %param.13) | data formatting | bytes 3145728 | tf_op args[6]
  22.6 1.8 copy.58
  25.3 0.8 collective-permute-done
  26.1 0.8 fusion.53
  27.5 4.2 %collective-permute-start.4 = (bf16[144,32]{0,1:T(8,128)(2,1)S(1)}, bf16[144,32]{0,1:T(8,128)(2,1)S(1)}, u32[]{:S(2)}, u32[]{:S(2)}) collective-permute-start(bf16[144,32]{0,1:T(8,128)(2,1)S(1)} %fusion.35), channel_id=1, source_target_pairs={{0,0},{1,1},{2,32},{3,33},{4,64},{5,65},{6,96},{7,97},{8,128},{9,1... | collective-permute-start | bytes 27656 | tf_op jit(solution)/shard_map/ppermute | solution.py:78
  31.7 0.7 slice.423
  32.9 0.8 slice.420
  34.1 0.9 pad_maximum_fusion.3
  35.1 1.3 collective-permute-start.3
  36.4 3.7 %collective-permute-start.2 = (bf16[24,264,4]{1,0,2:T(8,128)(2,1)}, bf16[24,264,4]{1,0,2:T(8,128)(2,1)}, u32[]{:S(2)}, u32[]{:S(2)}) collective-permute-start(bf16[24,264,4]{1,0,2:T(8,128)(2,1)} %get-tuple-element.29), channel_id=1, source_target_pairs={{0,1},{1,2},{2,3},{3,4},{4,5},{5,6},{6,7},{7,8},{8,9},{9,10},{10,1... | collective-permute-start | bytes 152072 | tf_op jit(solution)/shard_map/ppermute | solution.py:18
  41.4 0.9 copy.52
  42.2 2.2 %select_convert_fusion = bf16[32,144,272]{2,0,1:T(8,128)(2,1)S(1)} fusion(f32[32,272]{1,0:T(8,128)} %convert_bitcast_fusion, f32[32,144]{0,1:T(8,128)S(1)} %copy.52, pred[144,272]{1,0:T(8,128)(4,1)S(1)} %and_and_fusion), kind=kLoop, calls=%fused_computation.10 | loop fusion | flops 3760128 | bytes 2599168 | tf_op jit(solution)/shard_map/convert_element_type | solution.py:84
  44.5 9.3 %multiply_add_fusion = f32[32,136,264]{2,0,1:T(8,128)S(1)} fusion(bf16[32,144,272]{2,0,1:T(8,128)(2,1)S(1)} %select_convert_fusion, f32[32]{0:T(128)} %get-tuple-element.46, f32[32]{0:T(128)} %get-tuple-element.47, f32[32]{0:T(128)} %get-tuple-element.48, f32[32]{0:T(128)} %get-tuple-element.49, f32[32]{0:T(128)} %get-tuple-element.50, ...), kind=kLoop, calls=%fused_computation.13 | loop fusion | flops 29872128 | bytes 25277568 | tf_op jit(solution)/shard_map/add | solution.py:96
  53.9 2.8 %copy-done.3 = f32[32,136,264]{2,0,1:T(8,128)} copy-done((f32[32,136,264]{2,0,1:T(8,128)}, f32[32,136,264]{2,0,1:T(8,128)S(1)}, u32[]{:S(2)}) %copy-start.3) | copy-done | bytes 4595736
  56.7 2.6 %multiply_convert_fusion.1 = bf16[32,128,256]{2,0,1:T(8,128)(2,1)} fusion(f32[32,136,264]{2,0,1:T(8,128)S(1)} %multiply_add_fusion), kind=kLoop, calls=%fused_computation.31 | loop fusion | flops 5242880 | bytes 6291456 | tf_op jit(solution)/shard_map/convert_element_type | solution.py:100
  59.2 5.1 %fusion.29 = f32[32,24]{1,0:T(8,128)S(1)} fusion(bf16[24,128,256]{2,0,1:T(8,128)(2,1)} %copy.58, bf16[32,128,256]{2,0,1:T(8,128)(2,1)} %multiply_convert_fusion.1, bf16[32,144,272]{2,0,1:T(8,128)(2,1)} %copy-done.1, bf16[32,32]{1,0:T(8,128)(2,1)S(1)} %copy-done.22), kind=kOutput, calls=%fused_computation.51 | convolution fusion | flops 120586240 | bytes 5772288 | tf_op jit(solution)/shard_map/ydq,gdq->yg/dot_general | solution.py:132
  65.1 3.5 %fusion.16 = bf16[32,136,264]{2,0,1:T(8,128)(2,1)S(1)} fusion(bf16[24,264,4]{1,0,2:T(8,128)(2,1)} %collective-permute-done.3, bf16[24,4,128]{1,0,2:T(8,128)(2,1)S(1)} %copy-done.7, bf16[24,256,128]{1,0,2:T(8,128)(2,1)} %copy-done.5, bf16[24,4,128]{1,0,2:T(8,128)(2,1)} %copy-done.8, bf16[24,264,4]{1,0,2:T(8,128)(2,1)} %collective-permute-done.2, ...), kind=kOutput, calls=%fused_computation.32 | convolution fusion | flops 66063360 | bytes 4022784 | tf_op jit(solution)/shard_map/ch,hij->cij/dot_general | solution.py:106
  68.7 3.3 %fusion = bf16[32,136,264]{2,0,1:T(8,128)(2,1)S(1)} fusion(f32[32,136,264]{2,0,1:T(8,128)S(1)} %bitcast.90, bf16[32,136,264]{2,0,1:T(8,128)(2,1)S(1)} %fusion.16, bf16[32,32]{1,0:T(8,128)(2,1)S(1)} %copy-done.23), kind=kOutput, calls=%fused_computation.12 | convolution fusion | flops 83871744 | bytes 9193472 | tf_op jit(solution)/shard_map/co,oij->cij/dot_general | solution.py:108
  72.1 7.0 %fusion.50 = (f32[32,128]{0,1:T(8,128)S(1)}, f32[32,256]{1,0:T(8,128)S(1)}) fusion(bf16[32,136,264]{2,0,1:T(8,128)(2,1)S(1)} %fusion, f32[32]{0:T(128)S(1)} %copy-done.14, f32[32]{0:T(128)S(1)} %copy-done.15, f32[32]{0:T(128)S(1)} %copy-done.16, f32[32]{0:T(128)S(1)} %copy-done.17, f32[32]{0:T(128)S(1)} %copy-done.18, f32[32]{0:T(128)S(1)} %copy-done.19, ...), kind=kLoop, calls=%fused_computation.103 | loop fusion | flops 31444992 | bytes 21021824 | tf_op jit(solution)/shard_map/reduce_sum | solution.py:127
  79.1 7.4 %fusion.15 = (f32[32]{0:T(128)S(1)}, f32[32]{0:T(128)S(1)}, f32[32]{0:T(128)S(1)}, f32[32]{0:T(128)S(1)}, f32[32]{0:T(128)S(1)}, /*index=5*/f32[32]{0:T(128)S(1)}, f32[32]{0:T(128)S(1)}, f32[32]{0:T(128)S(1)}, f32[32]{0:T(128)S(1)}) fusion(bf16[32,144,272]{2,0,1:T(8,128)(2,1)S(1)} %copy-done.2, bf16[32,136,264]{2,0,1:T(8,128)(2,1)S(1)} %fusion), kind=kLoop, calls=%fused_computation.30 | loop fusion | flops 29359840 | bytes 20972672 | tf_op jit(solution)/shard_map/reduce_sum | solution.py:123
  86.6 10.7 %collective-permute-start.5 = (f32[128,32]{1,0:T(8,128)S(1)}, f32[128,32]{1,0:T(8,128)S(1)}, u32[]{:S(2)}, u32[]{:S(2)}) collective-permute-start(f32[128,32]{1,0:T(8,128)S(1)} %bitcast.97), channel_id=1, source_target_pairs={{0,0},{1,1},{2,32},{3,33},{4,64},{5,65},{6,96},{7,97},{8,128},{9,1... | collective-permute-start | bytes 49160 | tf_op jit(solution)/shard_map/ppermute | solution.py:135
  97.3 1.0 fusion.30
  98.8 1.7 collective-permute-done.5
  100.6 5.7 %collective-permute-start.6 = (f32[14368]{0:T(1024)S(1)}, f32[14368]{0:T(1024)S(1)}, u32[]{:S(2)}, u32[]{:S(2)}) collective-permute-start(f32[14368]{0:T(1024)S(1)} %concatenate.48), channel_id=1, source_target_pairs={{0,2},{1,3},{2,0},{3,1},{4,6},{5,7},{6,4},{7,5},{8,10},{9,11},{10,... | collective-permute-start | bytes 172424 | tf_op jit(solution)/shard_map/ppermute | solution.py:34
  106.4 2.5 %collective-permute-done.6 = f32[14368]{0:T(1024)S(1)} collective-permute-done((f32[14368]{0:T(1024)S(1)}, f32[14368]{0:T(1024)S(1)}, u32[]{:S(2)}, u32[]{:S(2)}) %collective-permute-start.6) | collective-permute-done | bytes 57504 | tf_op jit(solution)/shard_map/ppermute | solution.py:34
  108.9 6.7 %collective-permute-start.7 = (f32[14368]{0:T(1024)S(1)}, f32[14368]{0:T(1024)S(1)}, u32[]{:S(2)}, u32[]{:S(2)}) collective-permute-start(f32[14368]{0:T(1024)S(1)} %add.175), channel_id=1, source_target_pairs={{0,4},{1,5},{2,6},{3,7},{4,0},{5,1},{6,2},{7,3},{8,12},{9,13},{10,... | collective-permute-start | bytes 172424 | tf_op jit(solution)/shard_map/ppermute | solution.py:34
  115.6 4.1 %collective-permute-done.7 = f32[14368]{0:T(1024)S(1)} collective-permute-done((f32[14368]{0:T(1024)S(1)}, f32[14368]{0:T(1024)S(1)}, u32[]{:S(2)}, u32[]{:S(2)}) %collective-permute-start.7) | collective-permute-done | bytes 57504 | tf_op jit(solution)/shard_map/ppermute | solution.py:34
  119.7 3.0 %collective-permute-start.8 = (f32[14368]{0:T(1024)S(1)}, f32[14368]{0:T(1024)S(1)}, u32[]{:S(2)}, u32[]{:S(2)}) collective-permute-start(f32[14368]{0:T(1024)S(1)} %add.176), channel_id=1, source_target_pairs={{0,8},{1,9},{2,10},{3,11},{4,12},{5,13},{6,14},{7,15},{8,0},{9,1},... | collective-permute-start | bytes 172424 | tf_op jit(solution)/shard_map/ppermute | solution.py:34
  122.7 7.0 %collective-permute-done.8 = f32[14368]{0:T(1024)S(1)} collective-permute-done((f32[14368]{0:T(1024)S(1)}, f32[14368]{0:T(1024)S(1)}, u32[]{:S(2)}, u32[]{:S(2)}) %collective-permute-start.8) | collective-permute-done | bytes 57504 | tf_op jit(solution)/shard_map/ppermute | solution.py:34
  129.7 4.8 %collective-permute-start.9 = (f32[14368]{0:T(1024)S(1)}, f32[14368]{0:T(1024)S(1)}, u32[]{:S(2)}, u32[]{:S(2)}) collective-permute-start(f32[14368]{0:T(1024)S(1)} %add.177), channel_id=1, source_target_pairs={{0,16},{1,17},{2,18},{3,19},{4,20},{5,21},{6,22},{7,23},{8,24},{9,... | collective-permute-start | bytes 172424 | tf_op jit(solution)/shard_map/ppermute | solution.py:34
  134.5 2.2 %collective-permute-done.9 = f32[14368]{0:T(1024)S(1)} collective-permute-done((f32[14368]{0:T(1024)S(1)}, f32[14368]{0:T(1024)S(1)}, u32[]{:S(2)}, u32[]{:S(2)}) %collective-permute-start.9) | collective-permute-done | bytes 57504 | tf_op jit(solution)/shard_map/ppermute | solution.py:34
  136.7 1.9 %collective-permute-start.10 = (f32[14368]{0:T(1024)S(1)}, f32[14368]{0:T(1024)S(1)}, u32[]{:S(2)}, u32[]{:S(2)}) collective-permute-start(f32[14368]{0:T(1024)S(1)} %add.178), channel_id=1, source_target_pairs={{0,1},{1,0},{2,3},{3,2},{4,5},{5,4},{6,7},{7,6},{8,9},{9,8},{10,11... | collective-permute-start | bytes 172424 | tf_op jit(solution)/shard_map/ppermute | solution.py:34
  138.7 1.2 collective-permute-done.10
  141.2 5.7 %collective-permute-start.11 = (f32[34848]{0:T(1024)S(1)}, f32[34848]{0:T(1024)S(1)}, u32[]{:S(2)}, u32[]{:S(2)}) collective-permute-start(f32[34848]{0:T(1024)S(1)} %pad_maximum_fusion), channel_id=1, source_target_pairs={{0,32},{32,0},{64,96},{96,64},{128,160},{160,128},{192,224},{224,1... | collective-permute-start | bytes 418184 | tf_op jit(solution)/shard_map/ppermute | solution.py:34
  147.0 7.1 %collective-permute-done.11 = f32[34848]{0:T(1024)S(1)} collective-permute-done((f32[34848]{0:T(1024)S(1)}, f32[34848]{0:T(1024)S(1)}, u32[]{:S(2)}, u32[]{:S(2)}) %collective-permute-start.11) | collective-permute-done | bytes 139424 | tf_op jit(solution)/shard_map/ppermute | solution.py:34
  154.1 6.0 %collective-permute-start.12 = (f32[34848]{0:T(1024)S(1)}, f32[34848]{0:T(1024)S(1)}, u32[]{:S(2)}, u32[]{:S(2)}) collective-permute-start(f32[34848]{0:T(1024)S(1)} %fusion.49), channel_id=1, source_target_pairs={{0,64},{32,96},{64,0},{96,32},{128,192},{160,224},{192,128},{224,1... | collective-permute-start | bytes 418184 | tf_op jit(solution)/shard_map/ppermute | solution.py:34
  160.2 8.3 %collective-permute-done.12 = f32[34848]{0:T(1024)S(1)} collective-permute-done((f32[34848]{0:T(1024)S(1)}, f32[34848]{0:T(1024)S(1)}, u32[]{:S(2)}, u32[]{:S(2)}) %collective-permute-start.12) | collective-permute-done | bytes 139424 | tf_op jit(solution)/shard_map/ppermute | solution.py:34
  168.4 1.9 %collective-permute-start.13 = (f32[34848]{0:T(1024)S(1)}, f32[34848]{0:T(1024)S(1)}, u32[]{:S(2)}, u32[]{:S(2)}) collective-permute-start(f32[34848]{0:T(1024)S(1)} %add.183), channel_id=1, source_target_pairs={{0,128},{32,160},{64,192},{96,224},{128,0},{160,32},{192,64},{224,... | collective-permute-start | bytes 418184 | tf_op jit(solution)/shard_map/ppermute | solution.py:34
  170.6 5.2 %collective-permute-done.13 = f32[34848]{0:T(1024)S(1)} collective-permute-done((f32[34848]{0:T(1024)S(1)}, f32[34848]{0:T(1024)S(1)}, u32[]{:S(2)}, u32[]{:S(2)}) %collective-permute-start.13) | collective-permute-done | bytes 139424 | tf_op jit(solution)/shard_map/ppermute | solution.py:34
  175.9 1.9 %collective-permute-start.14 = (f32[34848]{0:T(1024)S(1)}, f32[34848]{0:T(1024)S(1)}, u32[]{:S(2)}, u32[]{:S(2)}) collective-permute-start(f32[34848]{0:T(1024)S(1)} %add.184), channel_id=1, source_target_pairs={{0,256},{32,288},{64,320},{96,352},{128,384},{160,416},{192,448},{... | collective-permute-start | bytes 418184 | tf_op jit(solution)/shard_map/ppermute | solution.py:34
  177.8 0.9 fusion.28
  178.7 5.7 %collective-permute-done.14 = f32[34848]{0:T(1024)S(1)} collective-permute-done((f32[34848]{0:T(1024)S(1)}, f32[34848]{0:T(1024)S(1)}, u32[]{:S(2)}, u32[]{:S(2)}) %collective-permute-start.14) | collective-permute-done | bytes 139424 | tf_op jit(solution)/shard_map/ppermute | solution.py:34
  (134 shorter events, 13.8 us)
Async XLA Ops:
  0.6 1.0 copy-start
  0.6 22.0 %copy-start.4 = (bf16[24,256,128]{2,1,0:T(8,128)(2,1)S(1)}, bf16[24,256,128]{2,1,0:T(8,128)(2,1)}, u32[]{:S(2)}) copy-start(bf16[24,256,128]{2,1,0:T(8,128)(2,1)} %param.13) | copy-start | bytes 4718596
  4.8 19.6 %collective-permute-start.1 = (bf16[12800]{0:T(1024)(128)(2,1)S(1)}, bf16[12800]{0:T(1024)(128)(2,1)}, u32[]{:S(2)}, u32[]{:S(2)}) collective-permute-start(bf16[12800]{0:T(1024)(128)(2,1)S(1)} %pad_maximum_fusion.5), channel_id=1, source_target_pairs={{32,0},{64,32},{96,64},{128,96},{160,128},{192,160},{224,192},{256... | collective-permute-start | bytes 76808 | tf_op jit(solution)/shard_map/ppermute | solution.py:18
  17.0 9.1 %collective-permute-start = (bf16[12800]{0:T(1024)(128)(2,1)}, bf16[12800]{0:T(1024)(128)(2,1)}, u32[]{:S(2)}, u32[]{:S(2)}) collective-permute-start(bf16[12800]{0:T(1024)(128)(2,1)} %pad_maximum_fusion.4), channel_id=1, source_target_pairs={{0,32},{32,64},{64,96},{96,128},{128,160},{160,192},{192,224},{224... | collective-permute-start | bytes 76808 | tf_op jit(solution)/shard_map/ppermute | solution.py:18
  22.6 18.8 %copy-start.5 = (bf16[24,256,128]{1,0,2:T(8,128)(2,1)}, bf16[24,256,128]{1,0,2:T(8,128)(2,1)S(1)}, u32[]{:S(2)}) copy-start(bf16[24,256,128]{1,0,2:T(8,128)(2,1)S(1)} %copy.47) | copy-start | bytes 4718596
  27.5 13.2 %collective-permute-start.4 = (bf16[144,32]{0,1:T(8,128)(2,1)S(1)}, bf16[144,32]{0,1:T(8,128)(2,1)S(1)}, u32[]{:S(2)}, u32[]{:S(2)}) collective-permute-start(bf16[144,32]{0,1:T(8,128)(2,1)S(1)} %fusion.35), channel_id=1, source_target_pairs={{0,0},{1,1},{2,32},{3,33},{4,64},{5,65},{6,96},{7,97},{8,128},{9,1... | collective-permute-start | bytes 27656 | tf_op jit(solution)/shard_map/ppermute | solution.py:78
  32.9 20.9 %copy-start.6 = (bf16[24,4,128]{1,0,2:T(8,128)(2,1)}, bf16[24,4,128]{1,0,2:T(8,128)(2,1)S(1)}, u32[]{:S(2)}) copy-start(bf16[24,4,128]{1,0,2:T(8,128)(2,1)S(1)} %copy.48) | copy-start | bytes 73732
  34.1 19.7 %copy-start.8 = (bf16[24,4,128]{1,0,2:T(8,128)(2,1)}, bf16[24,4,128]{1,0,2:T(8,128)(2,1)S(1)}, u32[]{:S(2)}) copy-start(bf16[24,4,128]{1,0,2:T(8,128)(2,1)S(1)} %copy.46) | copy-start | bytes 73732
  35.1 30.0 %collective-permute-start.3 = (bf16[24,264,4]{1,0,2:T(8,128)(2,1)}, bf16[24,264,4]{1,0,2:T(8,128)(2,1)}, u32[]{:S(2)}, u32[]{:S(2)}) collective-permute-start(bf16[24,264,4]{1,0,2:T(8,128)(2,1)} %get-tuple-element.30), channel_id=1, source_target_pairs={{1,0},{2,1},{3,2},{4,3},{5,4},{6,5},{7,6},{8,7},{9,8},{10,9},{11,1... | collective-permute-start | bytes 152072 | tf_op jit(solution)/shard_map/ppermute | solution.py:18
  36.4 28.7 %collective-permute-start.2 = (bf16[24,264,4]{1,0,2:T(8,128)(2,1)}, bf16[24,264,4]{1,0,2:T(8,128)(2,1)}, u32[]{:S(2)}, u32[]{:S(2)}) collective-permute-start(bf16[24,264,4]{1,0,2:T(8,128)(2,1)} %get-tuple-element.29), channel_id=1, source_target_pairs={{0,1},{1,2},{2,3},{3,4},{4,5},{5,6},{6,7},{7,8},{8,9},{9,10},{10,1... | collective-permute-start | bytes 152072 | tf_op jit(solution)/shard_map/ppermute | solution.py:18
  44.5 9.4 %copy-start.1 = (bf16[32,144,272]{2,0,1:T(8,128)(2,1)}, bf16[32,144,272]{2,0,1:T(8,128)(2,1)S(1)}, u32[]{:S(2)}) copy-start(bf16[32,144,272]{2,0,1:T(8,128)(2,1)S(1)} %select_convert_fusion) | copy-start | bytes 7520260
  53.9 2.8 %copy-start.3 = (f32[32,136,264]{2,0,1:T(8,128)}, f32[32,136,264]{2,0,1:T(8,128)S(1)}, u32[]{:S(2)}) copy-start(f32[32,136,264]{2,0,1:T(8,128)S(1)} %multiply_add_fusion) | copy-start | bytes 13787140
  56.7 2.6 %copy-start.22 = (bf16[32,32]{1,0:T(8,128)(2,1)S(1)}, bf16[32,32]{1,0:T(8,128)(2,1)}, u32[]{:S(2)}) copy-start(bf16[32,32]{1,0:T(8,128)(2,1)} %param.11) | copy-start | bytes 6148
  59.2 5.8 %copy-start.7 = (bf16[24,4,128]{1,0,2:T(8,128)(2,1)S(1)}, bf16[24,4,128]{1,0,2:T(8,128)(2,1)}, u32[]{:S(2)}) copy-start(bf16[24,4,128]{1,0,2:T(8,128)(2,1)} %copy-done.6) | copy-start | bytes 73732
  64.4 4.3 %slice-start = ((s8[6684672]{0:T(1024)(128)(4,1)}), s8[2490368]{0:T(1024)(128)(4,1)S(1)}, s32[]{:S(2)}) async-start(s8[6684672]{0:T(1024)(128)(4,1)} %bitcast.89), calls=%async_computation | async-start | bytes 4980736
  65.1 3.6 %slice-start.1 = ((s8[6684672]{0:T(1024)(128)(4,1)}), s8[4194304]{0:T(1024)(128)(4,1)S(1)}, s32[]{:S(2)}) async-start(s8[6684672]{0:T(1024)(128)(4,1)} %bitcast.89), calls=%async_computation.1 | async-start | bytes 8388608
  65.1 3.6 %copy-start.23 = (bf16[32,32]{1,0:T(8,128)(2,1)S(1)}, bf16[32,32]{1,0:T(8,128)(2,1)}, u32[]{:S(2)}) copy-start(bf16[32,32]{1,0:T(8,128)(2,1)} %param.11) | copy-start | bytes 6148
  68.6 3.4 %copy-start.13 = (f32[32]{0:T(128)S(1)}, f32[32]{0:T(128)}, u32[]{:S(2)}) copy-start(f32[32]{0:T(128)} %get-tuple-element.45) | copy-start | bytes 388
  68.7 3.4 %copy-start.14 = (f32[32]{0:T(128)S(1)}, f32[32]{0:T(128)}, u32[]{:S(2)}) copy-start(f32[32]{0:T(128)} %get-tuple-element.46) | copy-start | bytes 388
  68.7 3.4 %copy-start.15 = (f32[32]{0:T(128)S(1)}, f32[32]{0:T(128)}, u32[]{:S(2)}) copy-start(f32[32]{0:T(128)} %get-tuple-element.47) | copy-start | bytes 388
  68.7 3.4 %copy-start.16 = (f32[32]{0:T(128)S(1)}, f32[32]{0:T(128)}, u32[]{:S(2)}) copy-start(f32[32]{0:T(128)} %get-tuple-element.48) | copy-start | bytes 388
  68.7 3.4 %copy-start.17 = (f32[32]{0:T(128)S(1)}, f32[32]{0:T(128)}, u32[]{:S(2)}) copy-start(f32[32]{0:T(128)} %get-tuple-element.49) | copy-start | bytes 388
  68.7 3.4 %copy-start.18 = (f32[32]{0:T(128)S(1)}, f32[32]{0:T(128)}, u32[]{:S(2)}) copy-start(f32[32]{0:T(128)} %get-tuple-element.50) | copy-start | bytes 388
  68.7 3.4 %copy-start.19 = (f32[32]{0:T(128)S(1)}, f32[32]{0:T(128)}, u32[]{:S(2)}) copy-start(f32[32]{0:T(128)} %get-tuple-element.51) | copy-start | bytes 388
  68.7 3.4 %copy-start.20 = (f32[32]{0:T(128)S(1)}, f32[32]{0:T(128)}, u32[]{:S(2)}) copy-start(f32[32]{0:T(128)} %get-tuple-element.52) | copy-start | bytes 388
  68.7 3.4 %copy-start.21 = (f32[32]{0:T(128)S(1)}, f32[32]{0:T(128)}, u32[]{:S(2)}) copy-start(f32[32]{0:T(128)} %get-tuple-element.53) | copy-start | bytes 388
  72.1 7.0 %copy-start.2 = (bf16[32,144,272]{2,0,1:T(8,128)(2,1)S(1)}, bf16[32,144,272]{2,0,1:T(8,128)(2,1)}, u32[]{:S(2)}) copy-start(bf16[32,144,272]{2,0,1:T(8,128)(2,1)} %copy-done.1) | copy-start | bytes 7520260
  79.1 18.2 %copy-start.9 = (bf16[32,128,256]{2,0,1:T(8,128)(2,1)S(1)}, bf16[32,128,256]{2,0,1:T(8,128)(2,1)}, u32[]{:S(2)}) copy-start(bf16[32,128,256]{2,0,1:T(8,128)(2,1)} %multiply_convert_fusion.1) | copy-start | bytes 6291460
  86.6 14.0 %copy-start.12 = (f32[768]{0:T(1024)S(1)}, f32[768]{0:T(1024)}, u32[]{:S(2)}) copy-start(f32[768]{0:T(1024)} %reshape.304) | copy-start | bytes 9220
  86.6 83.8 %copy-start.11 = (bf16[512,32]{0,1:T(8,128)(2,1)S(1)}, bf16[512,32]{0,1:T(8,128)(2,1)}, u32[]{:S(2)}) copy-start(bf16[512,32]{0,1:T(8,128)(2,1)} %param.9) | copy-start | bytes 98308
  86.6 91.2 %copy-start.10 = (bf16[512,32]{0,1:T(8,128)(2,1)S(1)}, bf16[512,32]{0,1:T(8,128)(2,1)}, u32[]{:S(2)}) copy-start(bf16[512,32]{0,1:T(8,128)(2,1)} %param.8) | copy-start | bytes 98308
  86.6 13.9 %collective-permute-start.5 = (f32[128,32]{1,0:T(8,128)S(1)}, f32[128,32]{1,0:T(8,128)S(1)}, u32[]{:S(2)}, u32[]{:S(2)}) collective-permute-start(f32[128,32]{1,0:T(8,128)S(1)} %bitcast.97), channel_id=1, source_target_pairs={{0,0},{1,1},{2,32},{3,33},{4,64},{5,65},{6,96},{7,97},{8,128},{9,1... | collective-permute-start | bytes 49160 | tf_op jit(solution)/shard_map/ppermute | solution.py:135
  100.6 8.2 %collective-permute-start.6 = (f32[14368]{0:T(1024)S(1)}, f32[14368]{0:T(1024)S(1)}, u32[]{:S(2)}, u32[]{:S(2)}) collective-permute-start(f32[14368]{0:T(1024)S(1)} %concatenate.48), channel_id=1, source_target_pairs={{0,2},{1,3},{2,0},{3,1},{4,6},{5,7},{6,4},{7,5},{8,10},{9,11},{10,... | collective-permute-start | bytes 172424 | tf_op jit(solution)/shard_map/ppermute | solution.py:34
  108.9 10.8 %collective-permute-start.7 = (f32[14368]{0:T(1024)S(1)}, f32[14368]{0:T(1024)S(1)}, u32[]{:S(2)}, u32[]{:S(2)}) collective-permute-start(f32[14368]{0:T(1024)S(1)} %add.175), channel_id=1, source_target_pairs={{0,4},{1,5},{2,6},{3,7},{4,0},{5,1},{6,2},{7,3},{8,12},{9,13},{10,... | collective-permute-start | bytes 172424 | tf_op jit(solution)/shard_map/ppermute | solution.py:34
  119.7 10.0 %collective-permute-start.8 = (f32[14368]{0:T(1024)S(1)}, f32[14368]{0:T(1024)S(1)}, u32[]{:S(2)}, u32[]{:S(2)}) collective-permute-start(f32[14368]{0:T(1024)S(1)} %add.176), channel_id=1, source_target_pairs={{0,8},{1,9},{2,10},{3,11},{4,12},{5,13},{6,14},{7,15},{8,0},{9,1},... | collective-permute-start | bytes 172424 | tf_op jit(solution)/shard_map/ppermute | solution.py:34
  129.7 7.0 %collective-permute-start.9 = (f32[14368]{0:T(1024)S(1)}, f32[14368]{0:T(1024)S(1)}, u32[]{:S(2)}, u32[]{:S(2)}) collective-permute-start(f32[14368]{0:T(1024)S(1)} %add.177), channel_id=1, source_target_pairs={{0,16},{1,17},{2,18},{3,19},{4,20},{5,21},{6,22},{7,23},{8,24},{9,... | collective-permute-start | bytes 172424 | tf_op jit(solution)/shard_map/ppermute | solution.py:34
  136.7 3.1 %collective-permute-start.10 = (f32[14368]{0:T(1024)S(1)}, f32[14368]{0:T(1024)S(1)}, u32[]{:S(2)}, u32[]{:S(2)}) collective-permute-start(f32[14368]{0:T(1024)S(1)} %add.178), channel_id=1, source_target_pairs={{0,1},{1,0},{2,3},{3,2},{4,5},{5,4},{6,7},{7,6},{8,9},{9,8},{10,11... | collective-permute-start | bytes 172424 | tf_op jit(solution)/shard_map/ppermute | solution.py:34
  141.2 12.9 %collective-permute-start.11 = (f32[34848]{0:T(1024)S(1)}, f32[34848]{0:T(1024)S(1)}, u32[]{:S(2)}, u32[]{:S(2)}) collective-permute-start(f32[34848]{0:T(1024)S(1)} %pad_maximum_fusion), channel_id=1, source_target_pairs={{0,32},{32,0},{64,96},{96,64},{128,160},{160,128},{192,224},{224,1... | collective-permute-start | bytes 418184 | tf_op jit(solution)/shard_map/ppermute | solution.py:34
  154.1 14.3 %collective-permute-start.12 = (f32[34848]{0:T(1024)S(1)}, f32[34848]{0:T(1024)S(1)}, u32[]{:S(2)}, u32[]{:S(2)}) collective-permute-start(f32[34848]{0:T(1024)S(1)} %fusion.49), channel_id=1, source_target_pairs={{0,64},{32,96},{64,0},{96,32},{128,192},{160,224},{192,128},{224,1... | collective-permute-start | bytes 418184 | tf_op jit(solution)/shard_map/ppermute | solution.py:34
  168.4 7.4 %collective-permute-start.13 = (f32[34848]{0:T(1024)S(1)}, f32[34848]{0:T(1024)S(1)}, u32[]{:S(2)}, u32[]{:S(2)}) collective-permute-start(f32[34848]{0:T(1024)S(1)} %add.183), channel_id=1, source_target_pairs={{0,128},{32,160},{64,192},{96,224},{128,0},{160,32},{192,64},{224,... | collective-permute-start | bytes 418184 | tf_op jit(solution)/shard_map/ppermute | solution.py:34
  175.9 8.5 %collective-permute-start.14 = (f32[34848]{0:T(1024)S(1)}, f32[34848]{0:T(1024)S(1)}, u32[]{:S(2)}, u32[]{:S(2)}) collective-permute-start(f32[34848]{0:T(1024)S(1)} %add.184), channel_id=1, source_target_pairs={{0,256},{32,288},{64,320},{96,352},{128,384},{160,416},{192,448},{... | collective-permute-start | bytes 418184 | tf_op jit(solution)/shard_map/ppermute | solution.py:34

commit v7 on v2

--- a/solution.py
+++ b/solution.py
@@ -158,8 +158,10 @@
     bit = 1
     while bit < row_count:
         likes = (wleft_part, wright_part, small)
-        flat = packed(likes)
-        wleft_part, wright_part, small = unpacked(flat + xor_round(flat, "row", row_count, bit), likes)
+        flat = packed(likes).astype(jnp.bfloat16)
+        got = xor_round(flat, "row", row_count, bit)
+        total = flat.astype(jnp.float32) + got.astype(jnp.float32)
+        wleft_part, wright_part, small = unpacked(total, likes)
         bit *= 2
 
     kernel_sum, point_sum, head_sum = unpacked(small, (kernel_part, point_part, head_part))

time: 182 us -> 175 us (0.962)
  waiting for transfers between devices: 46.1 us -> 38.7 us
    ppermute x9, waiting for transfers between devices: 40.6 us -> 33.2 us  [xor_round(): return lax.ppermute(flat, axis, [(i, i ^ bit) for i in range(count)])]
  transfers between devices with their start and end apart: 15 -> 15, of which waited for: 10 -> 10; matrix products, arithmetic and copies ran while one was open for 17% -> 18% of each run, Pallas kernels for 0% -> 0%
where the time goes in v7:
time: 175 us; the launch traced here: 173 us
  starting transfers between devices  68.5 us (39%)
  waiting for transfers between devices  38.7 us (22%)
  other arithmetic  31.4 us (18%)
  local copies, waits for them, and re-layouts  17.8 us (10%)
  matrix products  15.7 us (9%)
    ppermute x9, starting transfers between devices, xor_round(): return lax.ppermute(flat, axis, [(i, i ^ bit) for i in range(count)])  36.9 us
    ppermute x9, waiting for transfers between devices, xor_round(): return lax.ppermute(flat, axis, [(i, i ^ bit) for i in range(count)])  33.2 us
    ppermute x4, starting transfers between devices, shifted(): return lax.ppermute(x, axis, pairs)  18.1 us
    add x1, other arithmetic, body(): conv_ext + depth_kernel[3 * a + b][:, None, None] * pair_ext[:, step * a:...  9.32 us
    unnamed x50, local copies, waits for them, and re-layouts  8.12 us
    reduce_sum x1, other arithmetic, body(): kern_terms.append(jnp.sum(conv_grad_tile * window, axis=(1, 2)))  7.48 us
    ppermute x1, starting transfers between devices, body(): right_moved = lax.ppermute(right_part, ('row', 'col'), transpose_pairs())  6.99 us
    reduce_sum x1, other arithmetic, body(): right_part = jnp.sum(backward_pass, axis=1).T  6.95 us
  transfers between devices with their start and end apart: 15, of which 10 were waited for; matrix products, arithmetic and copies ran while one was open for 18% of the time, Pallas kernels for 0%

profile of v7, /device:TPU:6, one launch (start us, length us, event | category | flops | bytes accessed | tf_op | source)
XLA Modules:
  0.0 173.4 jit_solution(10558691439072655925)
XLA Ops:
  0.6 0.9 copy-done
  1.6 0.9 convolution_convert_fusion.2
  2.8 0.9 convolution_convert_fusion.3
  4.0 0.9 fusion.54
  4.9 6.1 %collective-permute-start = (bf16[12800]{0:T(1024)(128)(2,1)S(1)}, bf16[12800]{0:T(1024)(128)(2,1)S(1)}, u32[]{:S(2)}, u32[]{:S(2)}) collective-permute-start(bf16[12800]{0:T(1024)(128)(2,1)S(1)} %pad_maximum_fusion.4), channel_id=1, source_target_pairs={{0,32},{32,64},{64,96},{96,128},{128,160},{160,192},{192,224},{224... | collective-permute-start | bytes 76808 | tf_op jit(solution)/shard_map/ppermute | solution.py:18
  11.3 7.0 %collective-permute-start.1 = (bf16[12800]{0:T(1024)(128)(2,1)S(1)}, bf16[12800]{0:T(1024)(128)(2,1)S(1)}, u32[]{:S(2)}, u32[]{:S(2)}) collective-permute-start(bf16[12800]{0:T(1024)(128)(2,1)S(1)} %pad_maximum_fusion.5), channel_id=1, source_target_pairs={{32,0},{64,32},{96,64},{128,96},{160,128},{192,160},{224,192},{256... | collective-permute-start | bytes 76808 | tf_op jit(solution)/shard_map/ppermute | solution.py:18
  18.5 1.6 slice_bitcast_fusion.8
  20.1 2.1 %copy.42 = bf16[24,256,128]{1,0,2:T(8,128)(2,1)S(1)} copy(bf16[24,256,128]{2,1,0:T(8,128)(2,1)} %param.13) | data formatting | bytes 3145728 | tf_op args[6]
  22.8 6.5 %collective-permute-start.4 = (bf16[144,32]{0,1:T(8,128)(2,1)S(1)}, bf16[144,32]{0,1:T(8,128)(2,1)S(1)}, u32[]{:S(2)}, u32[]{:S(2)}) collective-permute-start(bf16[144,32]{0,1:T(8,128)(2,1)S(1)} %fusion.38), channel_id=1, source_target_pairs={{0,0},{1,1},{2,32},{3,33},{4,64},{5,65},{6,96},{7,97},{8,128},{9,1... | collective-permute-start | bytes 27656 | tf_op jit(solution)/shard_map/ppermute | solution.py:78
  30.6 0.9 pad_maximum_fusion.2
  31.5 1.3 collective-permute-start.3
  32.8 3.7 %collective-permute-start.2 = (bf16[24,264,4]{1,0,2:T(8,128)(2,1)}, bf16[24,264,4]{1,0,2:T(8,128)(2,1)}, u32[]{:S(2)}, u32[]{:S(2)}) collective-permute-start(bf16[24,264,4]{1,0,2:T(8,128)(2,1)} %get-tuple-element.29), channel_id=1, source_target_pairs={{0,1},{1,2},{2,3},{3,4},{4,5},{5,6},{6,7},{7,8},{8,9},{9,10},{10,1... | collective-permute-start | bytes 152072 | tf_op jit(solution)/shard_map/ppermute | solution.py:18
  36.5 0.7 convert_bitcast_fusion
  37.8 0.9 copy.48
  38.6 2.2 %select_convert_fusion = bf16[32,272,144]{1,0,2:T(8,128)(2,1)S(1)} fusion(f32[32,144]{0,1:T(8,128)S(1)} %copy.48, f32[32,272]{1,0:T(8,128)} %convert_bitcast_fusion, pred[272,144]{0,1:T(8,128)(4,1)S(1)} %and_and_fusion), kind=kLoop, calls=%fused_computation.10 | loop fusion | flops 3760128 | bytes 2599168 | tf_op jit(solution)/shard_map/convert_element_type | solution.py:84
  40.9 9.3 %multiply_add_fusion = f32[32,264,136]{1,0,2:T(8,128)S(1)} fusion(bf16[32,272,144]{1,0,2:T(8,128)(2,1)S(1)} %select_convert_fusion, f32[32]{0:T(128)} %get-tuple-element.52, f32[32]{0:T(128)} %get-tuple-element.53, f32[32]{0:T(128)} %get-tuple-element.46, f32[32]{0:T(128)} %get-tuple-element.47, f32[32]{0:T(128)} %get-tuple-element.48, ...), kind=kLoop, calls=%fused_computation.13 | loop fusion | flops 29872128 | bytes 25277568 | tf_op jit(solution)/shard_map/add | solution.py:91
  50.2 2.8 %copy-done.3 = f32[32,264,136]{1,0,2:T(8,128)} copy-done((f32[32,264,136]{1,0,2:T(8,128)}, f32[32,264,136]{1,0,2:T(8,128)S(1)}, u32[]{:S(2)}) %copy-start.3) | copy-done | bytes 4595736
  53.0 2.6 %multiply_convert_fusion.1 = bf16[32,256,128]{1,0,2:T(8,128)(2,1)} fusion(f32[32,264,136]{1,0,2:T(8,128)S(1)} %multiply_add_fusion), kind=kLoop, calls=%fused_computation.31 | loop fusion | flops 5242880 | bytes 6291456 | tf_op jit(solution)/shard_map/convert_element_type | solution.py:95
  55.6 4.6 %fusion.32 = f32[32,24]{1,0:T(8,128)S(1)} fusion(bf16[24,256,128]{1,0,2:T(8,128)(2,1)S(1)} %copy.42, bf16[32,256,128]{1,0,2:T(8,128)(2,1)} %multiply_convert_fusion.1, bf16[32,272,144]{1,0,2:T(8,128)(2,1)} %copy-done.1, bf16[32,32]{1,0:T(8,128)(2,1)S(1)} %copy-done.19), kind=kOutput, calls=%fused_computation.53 | convolution fusion | flops 120586240 | bytes 5772288 | tf_op jit(solution)/shard_map/ydq,gdq->yg/dot_general | solution.py:125
  60.2 0.7 reshape.302
  60.9 3.5 %fusion.16 = bf16[32,264,136]{1,0,2:T(8,128)(2,1)S(1)} fusion(bf16[24,264,4]{1,0,2:T(8,128)(2,1)} %collective-permute-done.3, bf16[24,4,128]{1,0,2:T(8,128)(2,1)S(1)} %copy.43, bf16[24,256,128]{1,0,2:T(8,128)(2,1)} %copy-done.4, bf16[24,4,128]{1,0,2:T(8,128)(2,1)} %copy-done.5, bf16[24,264,4]{1,0,2:T(8,128)(2,1)} %collective-permute-done.2, ...), kind=kOutput, calls=%fused_computation.32 | convolution fusion | flops 66063360 | bytes 4022784 | tf_op jit(solution)/shard_map/ch,hij->cij/dot_general | solution.py:101
  64.5 3.3 %fusion = bf16[32,264,136]{1,0,2:T(8,128)(2,1)S(1)} fusion(f32[32,264,136]{1,0,2:T(8,128)S(1)} %bitcast.82, bf16[32,264,136]{1,0,2:T(8,128)(2,1)S(1)} %fusion.16, bf16[32,32]{1,0:T(8,128)(2,1)S(1)} %copy-done.20), kind=kOutput, calls=%fused_computation.12 | convolution fusion | flops 83871744 | bytes 9193472 | tf_op jit(solution)/shard_map/co,oij->cij/dot_general | solution.py:103
  68.0 7.0 %fusion.53 = (f32[32,128]{0,1:T(8,128)S(1)}, f32[32,256]{1,0:T(8,128)S(1)}) fusion(bf16[32,264,136]{1,0,2:T(8,128)(2,1)S(1)} %fusion, f32[32]{0:T(128)S(1)} %copy-done.17, f32[32]{0:T(128)S(1)} %copy-done.18, f32[32]{0:T(128)S(1)} %copy-done.11, f32[32]{0:T(128)S(1)} %copy-done.12, f32[32]{0:T(128)S(1)} %copy-done.13, f32[32]{0:T(128)S(1)} %copy-done.14, ...), kind=kLoop, calls=%fused_computation.108 | loop fusion | flops 31444992 | bytes 21021824 | tf_op jit(solution)/shard_map/reduce_sum | solution.py:121
  74.9 7.5 %fusion.15 = (f32[32]{0:T(128)S(1)}, f32[32]{0:T(128)S(1)}, f32[32]{0:T(128)S(1)}, f32[32]{0:T(128)S(1)}, f32[32]{0:T(128)S(1)}, /*index=5*/f32[32]{0:T(128)S(1)}, f32[32]{0:T(128)S(1)}, f32[32]{0:T(128)S(1)}, f32[32]{0:T(128)S(1)}) fusion(bf16[32,272,144]{1,0,2:T(8,128)(2,1)S(1)} %copy-done.2, bf16[32,264,136]{1,0,2:T(8,128)(2,1)S(1)} %fusion), kind=kLoop, calls=%fused_computation.30 | loop fusion | flops 29359840 | bytes 20972672 | tf_op jit(solution)/shard_map/reduce_sum | solution.py:118
  82.4 7.0 %collective-permute-start.5 = (f32[128,32]{1,0:T(8,128)S(1)}, f32[128,32]{1,0:T(8,128)S(1)}, u32[]{:S(2)}, u32[]{:S(2)}) collective-permute-start(f32[128,32]{1,0:T(8,128)S(1)} %bitcast.88), channel_id=1, source_target_pairs={{0,0},{1,1},{2,32},{3,33},{4,64},{5,65},{6,96},{7,97},{8,128},{9,1... | collective-permute-start | bytes 49160 | tf_op jit(solution)/shard_map/ppermute | solution.py:128
  89.5 1.0 fusion.33
  90.9 5.5 %collective-permute-done.5 = f32[128,32]{1,0:T(8,128)S(1)} collective-permute-done((f32[128,32]{1,0:T(8,128)S(1)}, f32[128,32]{1,0:T(8,128)S(1)}, u32[]{:S(2)}, u32[]{:S(2)}) %collective-permute-start.5) | collective-permute-done | bytes 16416 | tf_op jit(solution)/shard_map/ppermute | solution.py:128
  96.5 7.0 %collective-permute-start.6 = (f32[14368]{0:T(1024)S(1)}, f32[14368]{0:T(1024)S(1)}, u32[]{:S(2)}, u32[]{:S(2)}) collective-permute-start(f32[14368]{0:T(1024)S(1)} %concatenate.49), channel_id=1, source_target_pairs={{0,2},{1,3},{2,0},{3,1},{4,6},{5,7},{6,4},{7,5},{8,10},{9,11},{10,... | collective-permute-start | bytes 172424 | tf_op jit(solution)/shard_map/ppermute | solution.py:34
  103.6 2.3 %collective-permute-done.6 = f32[14368]{0:T(1024)S(1)} collective-permute-done((f32[14368]{0:T(1024)S(1)}, f32[14368]{0:T(1024)S(1)}, u32[]{:S(2)}, u32[]{:S(2)}) %collective-permute-start.6) | collective-permute-done | bytes 57504 | tf_op jit(solution)/shard_map/ppermute | solution.py:34
  105.9 5.7 %collective-permute-start.7 = (f32[14368]{0:T(1024)S(1)}, f32[14368]{0:T(1024)S(1)}, u32[]{:S(2)}, u32[]{:S(2)}) collective-permute-start(f32[14368]{0:T(1024)S(1)} %add.175), channel_id=1, source_target_pairs={{0,4},{1,5},{2,6},{3,7},{4,0},{5,1},{6,2},{7,3},{8,12},{9,13},{10,... | collective-permute-start | bytes 172424 | tf_op jit(solution)/shard_map/ppermute | solution.py:34
  111.6 2.8 %collective-permute-done.7 = f32[14368]{0:T(1024)S(1)} collective-permute-done((f32[14368]{0:T(1024)S(1)}, f32[14368]{0:T(1024)S(1)}, u32[]{:S(2)}, u32[]{:S(2)}) %collective-permute-start.7) | collective-permute-done | bytes 57504 | tf_op jit(solution)/shard_map/ppermute | solution.py:34
  114.5 5.7 %collective-permute-start.8 = (f32[14368]{0:T(1024)S(1)}, f32[14368]{0:T(1024)S(1)}, u32[]{:S(2)}, u32[]{:S(2)}) collective-permute-start(f32[14368]{0:T(1024)S(1)} %add.176), channel_id=1, source_target_pairs={{0,8},{1,9},{2,10},{3,11},{4,12},{5,13},{6,14},{7,15},{8,0},{9,1},... | collective-permute-start | bytes 172424 | tf_op jit(solution)/shard_map/ppermute | solution.py:34
  120.2 4.9 %collective-permute-done.8 = f32[14368]{0:T(1024)S(1)} collective-permute-done((f32[14368]{0:T(1024)S(1)}, f32[14368]{0:T(1024)S(1)}, u32[]{:S(2)}, u32[]{:S(2)}) %collective-permute-start.8) | collective-permute-done | bytes 57504 | tf_op jit(solution)/shard_map/ppermute | solution.py:34
  125.2 3.0 %collective-permute-start.9 = (f32[14368]{0:T(1024)S(1)}, f32[14368]{0:T(1024)S(1)}, u32[]{:S(2)}, u32[]{:S(2)}) collective-permute-start(f32[14368]{0:T(1024)S(1)} %add.177), channel_id=1, source_target_pairs={{0,16},{1,17},{2,18},{3,19},{4,20},{5,21},{6,22},{7,23},{8,24},{9,... | collective-permute-start | bytes 172424 | tf_op jit(solution)/shard_map/ppermute | solution.py:34
  128.2 3.1 %collective-permute-done.9 = f32[14368]{0:T(1024)S(1)} collective-permute-done((f32[14368]{0:T(1024)S(1)}, f32[14368]{0:T(1024)S(1)}, u32[]{:S(2)}, u32[]{:S(2)}) %collective-permute-start.9) | collective-permute-done | bytes 57504 | tf_op jit(solution)/shard_map/ppermute | solution.py:34
  131.3 1.9 %collective-permute-start.10 = (f32[14368]{0:T(1024)S(1)}, f32[14368]{0:T(1024)S(1)}, u32[]{:S(2)}, u32[]{:S(2)}) collective-permute-start(f32[14368]{0:T(1024)S(1)} %add.178), channel_id=1, source_target_pairs={{0,1},{1,0},{2,3},{3,2},{4,5},{5,4},{6,7},{7,6},{8,9},{9,8},{10,11... | collective-permute-start | bytes 172424 | tf_op jit(solution)/shard_map/ppermute | solution.py:34
  133.2 1.2 collective-permute-done.10
  135.8 3.1 %collective-permute-start.11 = (bf16[34848]{0:T(1024)(128)(2,1)S(1)}, bf16[34848]{0:T(1024)(128)(2,1)S(1)}, u32[]{:S(2)}, u32[]{:S(2)}) collective-permute-start(bf16[34848]{0:T(1024)(128)(2,1)S(1)} %pad_maximum_fusion.3), channel_id=1, source_target_pairs={{0,32},{32,0},{64,96},{96,64},{128,160},{160,128},{192,224},{224,1... | collective-permute-start | bytes 209096 | tf_op jit(solution)/shard_map/ppermute | solution.py:34
  139.0 5.5 %collective-permute-done.11 = bf16[34848]{0:T(1024)(128)(2,1)S(1)} collective-permute-done((bf16[34848]{0:T(1024)(128)(2,1)S(1)}, bf16[34848]{0:T(1024)(128)(2,1)S(1)}, u32[]{:S(2)}, u32[]{:S(2)}) %collective-permute-start.11) | collective-permute-done | bytes 69728 | tf_op jit(solution)/shard_map/ppermute | solution.py:34
  144.4 6.2 %collective-permute-start.12 = (bf16[34848]{0:T(1024)(128)(2,1)S(1)}, bf16[34848]{0:T(1024)(128)(2,1)S(1)}, u32[]{:S(2)}, u32[]{:S(2)}) collective-permute-start(bf16[34848]{0:T(1024)(128)(2,1)S(1)} %add_convert_fusion.2), channel_id=1, source_target_pairs={{0,64},{32,96},{64,0},{96,32},{128,192},{160,224},{192,128},{224,1... | collective-permute-start | bytes 209096 | tf_op jit(solution)/shard_map/ppermute | solution.py:34
  150.7 4.7 %collective-permute-done.12 = bf16[34848]{0:T(1024)(128)(2,1)S(1)} collective-permute-done((bf16[34848]{0:T(1024)(128)(2,1)S(1)}, bf16[34848]{0:T(1024)(128)(2,1)S(1)}, u32[]{:S(2)}, u32[]{:S(2)}) %collective-permute-start.12) | collective-permute-done | bytes 69728 | tf_op jit(solution)/shard_map/ppermute | solution.py:34
  155.4 1.9 %collective-permute-start.13 = (bf16[34848]{0:T(1024)(128)(2,1)S(1)}, bf16[34848]{0:T(1024)(128)(2,1)S(1)}, u32[]{:S(2)}, u32[]{:S(2)}) collective-permute-start(bf16[34848]{0:T(1024)(128)(2,1)S(1)} %add_convert_fusion.1), channel_id=1, source_target_pairs={{0,128},{32,160},{64,192},{96,224},{128,0},{160,32},{192,64},{224,... | collective-permute-start | bytes 209096 | tf_op jit(solution)/shard_map/ppermute | solution.py:34
  157.6 4.0 %collective-permute-done.13 = bf16[34848]{0:T(1024)(128)(2,1)S(1)} collective-permute-done((bf16[34848]{0:T(1024)(128)(2,1)S(1)}, bf16[34848]{0:T(1024)(128)(2,1)S(1)}, u32[]{:S(2)}, u32[]{:S(2)}) %collective-permute-start.13) | collective-permute-done | bytes 69728 | tf_op jit(solution)/shard_map/ppermute | solution.py:34
  161.6 2.2 %collective-permute-start.14 = (bf16[34848]{0:T(1024)(128)(2,1)S(1)}, bf16[34848]{0:T(1024)(128)(2,1)S(1)}, u32[]{:S(2)}, u32[]{:S(2)}) collective-permute-start(bf16[34848]{0:T(1024)(128)(2,1)S(1)} %add_convert_fusion), channel_id=1, source_target_pairs={{0,256},{32,288},{64,320},{96,352},{128,384},{160,416},{192,448},{... | collective-permute-start | bytes 209096 | tf_op jit(solution)/shard_map/ppermute | solution.py:34
  163.8 0.9 fusion.29
  164.7 4.7 %collective-permute-done.14 = bf16[34848]{0:T(1024)(128)(2,1)S(1)} collective-permute-done((bf16[34848]{0:T(1024)(128)(2,1)S(1)}, bf16[34848]{0:T(1024)(128)(2,1)S(1)}, u32[]{:S(2)}, u32[]{:S(2)}) %collective-permute-start.14) | collective-permute-done | bytes 69728 | tf_op jit(solution)/shard_map/ppermute | solution.py:34
  169.7 0.7 copy.57
  170.6 0.7 copy.58
  (122 shorter events, 8.2 us)
Async XLA Ops:
  0.6 1.0 copy-start
  4.9 17.4 %collective-permute-start = (bf16[12800]{0:T(1024)(128)(2,1)S(1)}, bf16[12800]{0:T(1024)(128)(2,1)S(1)}, u32[]{:S(2)}, u32[]{:S(2)}) collective-permute-start(bf16[12800]{0:T(1024)(128)(2,1)S(1)} %pad_maximum_fusion.4), channel_id=1, source_target_pairs={{0,32},{32,64},{64,96},{96,128},{128,160},{160,192},{192,224},{224... | collective-permute-start | bytes 76808 | tf_op jit(solution)/shard_map/ppermute | solution.py:18
  11.3 11.2 %collective-permute-start.1 = (bf16[12800]{0:T(1024)(128)(2,1)S(1)}, bf16[12800]{0:T(1024)(128)(2,1)S(1)}, u32[]{:S(2)}, u32[]{:S(2)}) collective-permute-start(bf16[12800]{0:T(1024)(128)(2,1)S(1)} %pad_maximum_fusion.5), channel_id=1, source_target_pairs={{32,0},{64,32},{96,64},{128,96},{160,128},{192,160},{224,192},{256... | collective-permute-start | bytes 76808 | tf_op jit(solution)/shard_map/ppermute | solution.py:18
  22.3 33.3 %copy-start.4 = (bf16[24,256,128]{1,0,2:T(8,128)(2,1)}, bf16[24,256,128]{1,0,2:T(8,128)(2,1)S(1)}, u32[]{:S(2)}) copy-start(bf16[24,256,128]{1,0,2:T(8,128)(2,1)S(1)} %copy.42) | copy-start | bytes 4718596
  22.8 14.4 %collective-permute-start.4 = (bf16[144,32]{0,1:T(8,128)(2,1)S(1)}, bf16[144,32]{0,1:T(8,128)(2,1)S(1)}, u32[]{:S(2)}, u32[]{:S(2)}) collective-permute-start(bf16[144,32]{0,1:T(8,128)(2,1)S(1)} %fusion.38), channel_id=1, source_target_pairs={{0,0},{1,1},{2,32},{3,33},{4,64},{5,65},{6,96},{7,97},{8,128},{9,1... | collective-permute-start | bytes 27656 | tf_op jit(solution)/shard_map/ppermute | solution.py:78
  30.6 19.6 %copy-start.5 = (bf16[24,4,128]{1,0,2:T(8,128)(2,1)}, bf16[24,4,128]{1,0,2:T(8,128)(2,1)S(1)}, u32[]{:S(2)}) copy-start(bf16[24,4,128]{1,0,2:T(8,128)(2,1)S(1)} %copy.41) | copy-start | bytes 73732
  31.5 29.4 %collective-permute-start.3 = (bf16[24,264,4]{1,0,2:T(8,128)(2,1)}, bf16[24,264,4]{1,0,2:T(8,128)(2,1)}, u32[]{:S(2)}, u32[]{:S(2)}) collective-permute-start(bf16[24,264,4]{1,0,2:T(8,128)(2,1)} %get-tuple-element.30), channel_id=1, source_target_pairs={{1,0},{2,1},{3,2},{4,3},{5,4},{6,5},{7,6},{8,7},{9,8},{10,9},{11,1... | collective-permute-start | bytes 152072 | tf_op jit(solution)/shard_map/ppermute | solution.py:18
  32.8 28.1 %collective-permute-start.2 = (bf16[24,264,4]{1,0,2:T(8,128)(2,1)}, bf16[24,264,4]{1,0,2:T(8,128)(2,1)}, u32[]{:S(2)}, u32[]{:S(2)}) collective-permute-start(bf16[24,264,4]{1,0,2:T(8,128)(2,1)} %get-tuple-element.29), channel_id=1, source_target_pairs={{0,1},{1,2},{2,3},{3,4},{4,5},{5,6},{6,7},{7,8},{8,9},{9,10},{10,1... | collective-permute-start | bytes 152072 | tf_op jit(solution)/shard_map/ppermute | solution.py:18
  40.9 9.3 %copy-start.1 = (bf16[32,272,144]{1,0,2:T(8,128)(2,1)}, bf16[32,272,144]{1,0,2:T(8,128)(2,1)S(1)}, u32[]{:S(2)}) copy-start(bf16[32,272,144]{1,0,2:T(8,128)(2,1)S(1)} %select_convert_fusion) | copy-start | bytes 7520260
  50.2 2.8 %copy-start.3 = (f32[32,264,136]{1,0,2:T(8,128)}, f32[32,264,136]{1,0,2:T(8,128)S(1)}, u32[]{:S(2)}) copy-start(f32[32,264,136]{1,0,2:T(8,128)S(1)} %multiply_add_fusion) | copy-start | bytes 13787140
  53.0 2.6 %copy-start.19 = (bf16[32,32]{1,0:T(8,128)(2,1)S(1)}, bf16[32,32]{1,0:T(8,128)(2,1)}, u32[]{:S(2)}) copy-start(bf16[32,32]{1,0:T(8,128)(2,1)} %param.11) | copy-start | bytes 6148
  60.2 4.2 %slice-start = ((s8[6684672]{0:T(1024)(128)(4,1)}), s8[2490368]{0:T(1024)(128)(4,1)S(1)}, s32[]{:S(2)}) async-start(s8[6684672]{0:T(1024)(128)(4,1)} %bitcast.81), calls=%async_computation | async-start | bytes 4980736
  60.9 3.5 %slice-start.1 = ((s8[6684672]{0:T(1024)(128)(4,1)}), s8[4194304]{0:T(1024)(128)(4,1)S(1)}, s32[]{:S(2)}) async-start(s8[6684672]{0:T(1024)(128)(4,1)} %bitcast.81), calls=%async_computation.1 | async-start | bytes 8388608
  60.9 3.6 %copy-start.20 = (bf16[32,32]{1,0:T(8,128)(2,1)S(1)}, bf16[32,32]{1,0:T(8,128)(2,1)}, u32[]{:S(2)}) copy-start(bf16[32,32]{1,0:T(8,128)(2,1)} %param.11) | copy-start | bytes 6148
  64.4 3.4 %copy-start.10 = (f32[32]{0:T(128)S(1)}, f32[32]{0:T(128)}, u32[]{:S(2)}) copy-start(f32[32]{0:T(128)} %get-tuple-element.45) | copy-start | bytes 388
  64.5 3.4 %copy-start.11 = (f32[32]{0:T(128)S(1)}, f32[32]{0:T(128)}, u32[]{:S(2)}) copy-start(f32[32]{0:T(128)} %get-tuple-element.46) | copy-start | bytes 388
  64.5 3.4 %copy-start.12 = (f32[32]{0:T(128)S(1)}, f32[32]{0:T(128)}, u32[]{:S(2)}) copy-start(f32[32]{0:T(128)} %get-tuple-element.47) | copy-start | bytes 388
  64.5 3.4 %copy-start.13 = (f32[32]{0:T(128)S(1)}, f32[32]{0:T(128)}, u32[]{:S(2)}) copy-start(f32[32]{0:T(128)} %get-tuple-element.48) | copy-start | bytes 388
  64.5 3.4 %copy-start.14 = (f32[32]{0:T(128)S(1)}, f32[32]{0:T(128)}, u32[]{:S(2)}) copy-start(f32[32]{0:T(128)} %get-tuple-element.49) | copy-start | bytes 388
  64.5 3.4 %copy-start.15 = (f32[32]{0:T(128)S(1)}, f32[32]{0:T(128)}, u32[]{:S(2)}) copy-start(f32[32]{0:T(128)} %get-tuple-element.50) | copy-start | bytes 388
  64.5 3.4 %copy-start.16 = (f32[32]{0:T(128)S(1)}, f32[32]{0:T(128)}, u32[]{:S(2)}) copy-start(f32[32]{0:T(128)} %get-tuple-element.51) | copy-start | bytes 388
  64.5 3.4 %copy-start.17 = (f32[32]{0:T(128)S(1)}, f32[32]{0:T(128)}, u32[]{:S(2)}) copy-start(f32[32]{0:T(128)} %get-tuple-element.52) | copy-start | bytes 388
  64.5 3.4 %copy-start.18 = (f32[32]{0:T(128)S(1)}, f32[32]{0:T(128)}, u32[]{:S(2)}) copy-start(f32[32]{0:T(128)} %get-tuple-element.53) | copy-start | bytes 388
  67.9 7.0 %copy-start.2 = (bf16[32,272,144]{1,0,2:T(8,128)(2,1)S(1)}, bf16[32,272,144]{1,0,2:T(8,128)(2,1)}, u32[]{:S(2)}) copy-start(bf16[32,272,144]{1,0,2:T(8,128)(2,1)} %copy-done.1) | copy-start | bytes 7520260
  74.9 14.5 %copy-start.6 = (bf16[32,256,128]{1,0,2:T(8,128)(2,1)S(1)}, bf16[32,256,128]{1,0,2:T(8,128)(2,1)}, u32[]{:S(2)}) copy-start(bf16[32,256,128]{1,0,2:T(8,128)(2,1)} %multiply_convert_fusion.1) | copy-start | bytes 6291460
  82.4 14.0 %copy-start.9 = (f32[768]{0:T(1024)S(1)}, f32[768]{0:T(1024)}, u32[]{:S(2)}) copy-start(f32[768]{0:T(1024)} %reshape.302) | copy-start | bytes 9220
  82.4 74.9 %copy-start.8 = (bf16[512,32]{0,1:T(8,128)(2,1)S(1)}, bf16[512,32]{0,1:T(8,128)(2,1)}, u32[]{:S(2)}) copy-start(bf16[512,32]{0,1:T(8,128)(2,1)} %param.9) | copy-start | bytes 98308
  82.4 81.4 %copy-start.7 = (bf16[512,32]{0,1:T(8,128)(2,1)S(1)}, bf16[512,32]{0,1:T(8,128)(2,1)}, u32[]{:S(2)}) copy-start(bf16[512,32]{0,1:T(8,128)(2,1)} %param.8) | copy-start | bytes 98308
  82.4 13.9 %collective-permute-start.5 = (f32[128,32]{1,0:T(8,128)S(1)}, f32[128,32]{1,0:T(8,128)S(1)}, u32[]{:S(2)}, u32[]{:S(2)}) collective-permute-start(f32[128,32]{1,0:T(8,128)S(1)} %bitcast.88), channel_id=1, source_target_pairs={{0,0},{1,1},{2,32},{3,33},{4,64},{5,65},{6,96},{7,97},{8,128},{9,1... | collective-permute-start | bytes 49160 | tf_op jit(solution)/shard_map/ppermute | solution.py:128
  96.5 9.3 %collective-permute-start.6 = (f32[14368]{0:T(1024)S(1)}, f32[14368]{0:T(1024)S(1)}, u32[]{:S(2)}, u32[]{:S(2)}) collective-permute-start(f32[14368]{0:T(1024)S(1)} %concatenate.49), channel_id=1, source_target_pairs={{0,2},{1,3},{2,0},{3,1},{4,6},{5,7},{6,4},{7,5},{8,10},{9,11},{10,... | collective-permute-start | bytes 172424 | tf_op jit(solution)/shard_map/ppermute | solution.py:34
  105.9 8.6 %collective-permute-start.7 = (f32[14368]{0:T(1024)S(1)}, f32[14368]{0:T(1024)S(1)}, u32[]{:S(2)}, u32[]{:S(2)}) collective-permute-start(f32[14368]{0:T(1024)S(1)} %add.175), channel_id=1, source_target_pairs={{0,4},{1,5},{2,6},{3,7},{4,0},{5,1},{6,2},{7,3},{8,12},{9,13},{10,... | collective-permute-start | bytes 172424 | tf_op jit(solution)/shard_map/ppermute | solution.py:34
  114.5 10.7 %collective-permute-start.8 = (f32[14368]{0:T(1024)S(1)}, f32[14368]{0:T(1024)S(1)}, u32[]{:S(2)}, u32[]{:S(2)}) collective-permute-start(f32[14368]{0:T(1024)S(1)} %add.176), channel_id=1, source_target_pairs={{0,8},{1,9},{2,10},{3,11},{4,12},{5,13},{6,14},{7,15},{8,0},{9,1},... | collective-permute-start | bytes 172424 | tf_op jit(solution)/shard_map/ppermute | solution.py:34
  125.2 6.1 %collective-permute-start.9 = (f32[14368]{0:T(1024)S(1)}, f32[14368]{0:T(1024)S(1)}, u32[]{:S(2)}, u32[]{:S(2)}) collective-permute-start(f32[14368]{0:T(1024)S(1)} %add.177), channel_id=1, source_target_pairs={{0,16},{1,17},{2,18},{3,19},{4,20},{5,21},{6,22},{7,23},{8,24},{9,... | collective-permute-start | bytes 172424 | tf_op jit(solution)/shard_map/ppermute | solution.py:34
  131.3 3.1 %collective-permute-start.10 = (f32[14368]{0:T(1024)S(1)}, f32[14368]{0:T(1024)S(1)}, u32[]{:S(2)}, u32[]{:S(2)}) collective-permute-start(f32[14368]{0:T(1024)S(1)} %add.178), channel_id=1, source_target_pairs={{0,1},{1,0},{2,3},{3,2},{4,5},{5,4},{6,7},{7,6},{8,9},{9,8},{10,11... | collective-permute-start | bytes 172424 | tf_op jit(solution)/shard_map/ppermute | solution.py:34
  135.8 8.6 %collective-permute-start.11 = (bf16[34848]{0:T(1024)(128)(2,1)S(1)}, bf16[34848]{0:T(1024)(128)(2,1)S(1)}, u32[]{:S(2)}, u32[]{:S(2)}) collective-permute-start(bf16[34848]{0:T(1024)(128)(2,1)S(1)} %pad_maximum_fusion.3), channel_id=1, source_target_pairs={{0,32},{32,0},{64,96},{96,64},{128,160},{160,128},{192,224},{224,1... | collective-permute-start | bytes 209096 | tf_op jit(solution)/shard_map/ppermute | solution.py:34
  144.4 10.9 %collective-permute-start.12 = (bf16[34848]{0:T(1024)(128)(2,1)S(1)}, bf16[34848]{0:T(1024)(128)(2,1)S(1)}, u32[]{:S(2)}, u32[]{:S(2)}) collective-permute-start(bf16[34848]{0:T(1024)(128)(2,1)S(1)} %add_convert_fusion.2), channel_id=1, source_target_pairs={{0,64},{32,96},{64,0},{96,32},{128,192},{160,224},{192,128},{224,1... | collective-permute-start | bytes 209096 | tf_op jit(solution)/shard_map/ppermute | solution.py:34
  155.4 6.2 %collective-permute-start.13 = (bf16[34848]{0:T(1024)(128)(2,1)S(1)}, bf16[34848]{0:T(1024)(128)(2,1)S(1)}, u32[]{:S(2)}, u32[]{:S(2)}) collective-permute-start(bf16[34848]{0:T(1024)(128)(2,1)S(1)} %add_convert_fusion.1), channel_id=1, source_target_pairs={{0,128},{32,160},{64,192},{96,224},{128,0},{160,32},{192,64},{224,... | collective-permute-start | bytes 209096 | tf_op jit(solution)/shard_map/ppermute | solution.py:34
  161.6 7.7 %collective-permute-start.14 = (bf16[34848]{0:T(1024)(128)(2,1)S(1)}, bf16[34848]{0:T(1024)(128)(2,1)S(1)}, u32[]{:S(2)}, u32[]{:S(2)}) collective-permute-start(bf16[34848]{0:T(1024)(128)(2,1)S(1)} %add_convert_fusion), channel_id=1, source_target_pairs={{0,256},{32,288},{64,320},{96,352},{128,384},{160,416},{192,448},{... | collective-permute-start | bytes 209096 | tf_op jit(solution)/shard_map/ppermute | solution.py:34

commit v8 on v7

--- a/solution.py
+++ b/solution.py
@@ -129,15 +129,18 @@
     bit = ratio
     while bit < col_count:
         likes = (left_part, right_moved, small)
-        flat = packed(likes)
-        left_part, right_moved, small = unpacked(flat + xor_round(flat, "col", col_count, bit), likes)
+        flat = packed(likes).astype(jnp.bfloat16)
+        got = xor_round(flat, "col", col_count, bit)
+        total = flat.astype(jnp.float32) + got.astype(jnp.float32)
+        left_part, right_moved, small = unpacked(total, likes)
         bit *= 2
     right_block = right_moved
     bit = 1
     while bit < ratio:
         likes = (left_part, right_block, small)
-        flat = packed(likes)
-        got = unpacked(xor_round(flat, "col", col_count, bit), likes)
+        flat = packed(likes).astype(jnp.bfloat16)
+        got = unpacked(xor_round(flat, "col", col_count, bit).astype(jnp.float32), likes)
+        left_part, right_block, small = unpacked(flat.astype(jnp.float32), likes)
         left_part = left_part + got[0]
         small = small + got[2]
         upper = (k & bit) != 0

time: 175 us -> 169 us (0.966)
  waiting for transfers between devices: 38.7 us -> 35.4 us
    ppermute x9, waiting for transfers between devices: 33.2 us -> 30.9 us  [xor_round(): return lax.ppermute(flat, axis, [(i, i ^ bit) for i in range(count)])]
    unnamed x50 -> x48, local copies, waits for them, and re-layouts: 8.12 us -> 8.19 us
where the time goes in v8:
time: 169 us; the launch traced here: 168 us
  starting transfers between devices  67 us (40%)
  waiting for transfers between devices  35.4 us (21%)
  other arithmetic  31.4 us (19%)
  local copies, waits for them, and re-layouts  17.5 us (10%)
  matrix products  15.7 us (9%)
    ppermute x9, starting transfers between devices, xor_round(): return lax.ppermute(flat, axis, [(i, i ^ bit) for i in range(count)])  35.5 us
    ppermute x9, waiting for transfers between devices, xor_round(): return lax.ppermute(flat, axis, [(i, i ^ bit) for i in range(count)])  30.9 us
    ppermute x4, starting transfers between devices, shifted(): return lax.ppermute(x, axis, pairs)  18.1 us
    add x1, other arithmetic, body(): conv_ext + depth_kernel[3 * a + b][:, None, None] * pair_ext[:, step * a:...  9.35 us
    unnamed x48, local copies, waits for them, and re-layouts  8.19 us
    reduce_sum x1, other arithmetic, body(): kern_terms.append(jnp.sum(conv_grad_tile * window, axis=(1, 2)))  7.48 us
    ppermute x1, starting transfers between devices, body(): right_moved = lax.ppermute(right_part, ('row', 'col'), transpose_pairs())  6.98 us
    reduce_sum x1, other arithmetic, body(): right_part = jnp.sum(backward_pass, axis=1).T  6.96 us
  transfers between devices with their start and end apart: 15, of which 10 were waited for; matrix products, arithmetic and copies ran while one was open for 18% of the time, Pallas kernels for 0%

profile of v8, /device:TPU:6, one launch (start us, length us, event | category | flops | bytes accessed | tf_op | source)
XLA Modules:
  0.0 168.4 jit_solution(5036428018382067177)
XLA Ops:
  0.6 0.9 copy-done
  1.6 0.9 convolution_convert_fusion.2
  2.8 0.9 convolution_convert_fusion.3
  4.0 0.9 fusion.58
  4.9 6.1 %collective-permute-start = (bf16[12800]{0:T(1024)(128)(2,1)S(1)}, bf16[12800]{0:T(1024)(128)(2,1)S(1)}, u32[]{:S(2)}, u32[]{:S(2)}) collective-permute-start(bf16[12800]{0:T(1024)(128)(2,1)S(1)} %pad_maximum_fusion.4), channel_id=1, source_target_pairs={{0,32},{32,64},{64,96},{96,128},{128,160},{160,192},{192,224},{224... | collective-permute-start | bytes 76808 | tf_op jit(solution)/shard_map/ppermute | solution.py:18
  11.3 7.0 %collective-permute-start.1 = (bf16[12800]{0:T(1024)(128)(2,1)S(1)}, bf16[12800]{0:T(1024)(128)(2,1)S(1)}, u32[]{:S(2)}, u32[]{:S(2)}) collective-permute-start(bf16[12800]{0:T(1024)(128)(2,1)S(1)} %pad_maximum_fusion.5), channel_id=1, source_target_pairs={{32,0},{64,32},{96,64},{128,96},{160,128},{192,160},{224,192},{256... | collective-permute-start | bytes 76808 | tf_op jit(solution)/shard_map/ppermute | solution.py:18
  18.5 1.6 slice_bitcast_fusion.8
  20.1 2.2 %copy.42 = bf16[24,256,128]{1,0,2:T(8,128)(2,1)S(1)} copy(bf16[24,256,128]{2,1,0:T(8,128)(2,1)} %param.13) | data formatting | bytes 3145728 | tf_op args[6]
  22.8 6.5 %collective-permute-start.4 = (bf16[144,32]{0,1:T(8,128)(2,1)S(1)}, bf16[144,32]{0,1:T(8,128)(2,1)S(1)}, u32[]{:S(2)}, u32[]{:S(2)}) collective-permute-start(bf16[144,32]{0,1:T(8,128)(2,1)S(1)} %fusion.42), channel_id=1, source_target_pairs={{0,0},{1,1},{2,32},{3,33},{4,64},{5,65},{6,96},{7,97},{8,128},{9,1... | collective-permute-start | bytes 27656 | tf_op jit(solution)/shard_map/ppermute | solution.py:78
  30.6 0.9 pad_maximum_fusion.2
  31.5 1.3 collective-permute-start.3
  32.8 3.7 %collective-permute-start.2 = (bf16[24,264,4]{1,0,2:T(8,128)(2,1)}, bf16[24,264,4]{1,0,2:T(8,128)(2,1)}, u32[]{:S(2)}, u32[]{:S(2)}) collective-permute-start(bf16[24,264,4]{1,0,2:T(8,128)(2,1)} %get-tuple-element.31), channel_id=1, source_target_pairs={{0,1},{1,2},{2,3},{3,4},{4,5},{5,6},{6,7},{7,8},{8,9},{9,10},{10,1... | collective-permute-start | bytes 152072 | tf_op jit(solution)/shard_map/ppermute | solution.py:18
  36.5 0.7 convert_bitcast_fusion
  37.8 0.9 copy.48
  38.6 2.2 %select_convert_fusion = bf16[32,272,144]{1,0,2:T(8,128)(2,1)S(1)} fusion(f32[32,144]{0,1:T(8,128)S(1)} %copy.48, f32[32,272]{1,0:T(8,128)} %convert_bitcast_fusion, pred[272,144]{0,1:T(8,128)(4,1)S(1)} %and_and_fusion), kind=kLoop, calls=%fused_computation.10 | loop fusion | flops 3760128 | bytes 2599168 | tf_op jit(solution)/shard_map/convert_element_type | solution.py:84
  40.9 9.4 %multiply_add_fusion = f32[32,264,136]{1,0,2:T(8,128)S(1)} fusion(bf16[32,272,144]{1,0,2:T(8,128)(2,1)S(1)} %select_convert_fusion, f32[32]{0:T(128)} %get-tuple-element.54, f32[32]{0:T(128)} %get-tuple-element.55, f32[32]{0:T(128)} %get-tuple-element.48, f32[32]{0:T(128)} %get-tuple-element.49, f32[32]{0:T(128)} %get-tuple-element.50, ...), kind=kLoop, calls=%fused_computation.13 | loop fusion | flops 29872128 | bytes 25277568 | tf_op jit(solution)/shard_map/add | solution.py:91
  50.3 2.8 %copy-done.3 = f32[32,264,136]{1,0,2:T(8,128)} copy-done((f32[32,264,136]{1,0,2:T(8,128)}, f32[32,264,136]{1,0,2:T(8,128)S(1)}, u32[]{:S(2)}) %copy-start.3) | copy-done | bytes 4595736
  53.1 2.6 %multiply_convert_fusion.1 = bf16[32,256,128]{1,0,2:T(8,128)(2,1)} fusion(f32[32,264,136]{1,0,2:T(8,128)S(1)} %multiply_add_fusion), kind=kLoop, calls=%fused_computation.31 | loop fusion | flops 5242880 | bytes 6291456 | tf_op jit(solution)/shard_map/convert_element_type | solution.py:95
  55.6 4.6 %fusion.39 = bf16[32,24]{0,1:T(8,128)(2,1)S(1)} fusion(bf16[24,256,128]{1,0,2:T(8,128)(2,1)S(1)} %copy.42, bf16[32,256,128]{1,0,2:T(8,128)(2,1)} %multiply_convert_fusion.1, bf16[32,272,144]{1,0,2:T(8,128)(2,1)} %copy-done.1, bf16[32,32]{1,0:T(8,128)(2,1)S(1)} %copy-done.18), kind=kOutput, calls=%fused_computation.56 | convolution fusion | flops 120587008 | bytes 5770752 | tf_op jit(solution)/shard_map/ydq,gdq->yg/dot_general | solution.py:125
  60.5 3.5 %fusion.16 = bf16[32,264,136]{1,0,2:T(8,128)(2,1)S(1)} fusion(bf16[24,264,4]{1,0,2:T(8,128)(2,1)} %collective-permute-done.3, bf16[24,4,128]{1,0,2:T(8,128)(2,1)S(1)} %copy.43, bf16[24,256,128]{1,0,2:T(8,128)(2,1)} %copy-done.4, bf16[24,4,128]{1,0,2:T(8,128)(2,1)} %copy-done.5, bf16[24,264,4]{1,0,2:T(8,128)(2,1)} %collective-permute-done.2, ...), kind=kOutput, calls=%fused_computation.32 | convolution fusion | flops 66063360 | bytes 4022784 | tf_op jit(solution)/shard_map/ch,hij->cij/dot_general | solution.py:101
  64.2 3.3 %fusion = bf16[32,264,136]{1,0,2:T(8,128)(2,1)S(1)} fusion(f32[32,264,136]{1,0,2:T(8,128)S(1)} %bitcast.108, bf16[32,264,136]{1,0,2:T(8,128)(2,1)S(1)} %fusion.16, bf16[32,32]{1,0:T(8,128)(2,1)S(1)} %copy-done.19), kind=kOutput, calls=%fused_computation.12 | convolution fusion | flops 83871744 | bytes 9193472 | tf_op jit(solution)/shard_map/co,oij->cij/dot_general | solution.py:103
  67.6 7.0 %fusion.56 = (bf16[32,128]{0,1:T(8,128)(2,1)S(1)}, bf16[32,256]{1,0:T(8,128)(2,1)S(1)}) fusion(bf16[32,264,136]{1,0,2:T(8,128)(2,1)S(1)} %fusion, f32[32]{0:T(128)S(1)} %copy-done.16, f32[32]{0:T(128)S(1)} %copy-done.17, f32[32]{0:T(128)S(1)} %copy-done.10, f32[32]{0:T(128)S(1)} %copy-done.11, f32[32]{0:T(128)S(1)} %copy-done.12, f32[32]{0:T(128)S(1)} %copy-done.13, ...), kind=kLoop, calls=%fused_computation.123 | loop fusion | flops 31444992 | bytes 20997248 | tf_op jit(solution)/shard_map/reduce_sum | solution.py:121
  74.6 7.5 %fusion.15 = (bf16[32]{0:T(256)(128)(2,1)S(1)}, bf16[32]{0:T(256)(128)(2,1)S(1)}, bf16[32]{0:T(256)(128)(2,1)S(1)}, bf16[32]{0:T(256)(128)(2,1)S(1)}, bf16[32]{0...) fusion(bf16[32,272,144]{1,0,2:T(8,128)(2,1)S(1)} %copy-done.2, ...), kind=kLoop, calls=%fused_computation.30 | loop fusion | flops 29359840 | bytes 20972096 | tf_op jit(solution)/shard_map/reduce_sum | solution.py:118
  82.1 7.0 %collective-permute-start.5 = (bf16[128,32]{1,0:T(8,128)(2,1)S(1)}, bf16[128,32]{1,0:T(8,128)(2,1)S(1)}, u32[]{:S(2)}, u32[]{:S(2)}) collective-permute-start(bf16[128,32]{1,0:T(8,128)(2,1)S(1)} %bitcast.114), channel_id=1, source_target_pairs={{0,0},{1,1},{2,32},{3,33},{4,64},{5,65},{6,96},{7,97},{8,128},{9,1... | collective-permute-start | bytes 24584 | tf_op jit(solution)/shard_map/ppermute | solution.py:128
  89.1 1.0 fusion.35
  90.6 4.5 %collective-permute-done.5 = bf16[128,32]{1,0:T(8,128)(2,1)S(1)} collective-permute-done((bf16[128,32]{1,0:T(8,128)(2,1)S(1)}, bf16[128,32]{1,0:T(8,128)(2,1)S(1)}, u32[]{:S(2)}, u32[]{:S(2)}) %collective-permute-start.5) | collective-permute-done | bytes 8224 | tf_op jit(solution)/shard_map/ppermute | solution.py:128
  95.2 7.0 %collective-permute-start.6 = (bf16[14368]{0:T(1024)(128)(2,1)S(1)}, bf16[14368]{0:T(1024)(128)(2,1)S(1)}, u32[]{:S(2)}, u32[]{:S(2)}) collective-permute-start(bf16[14368]{0:T(1024)(128)(2,1)S(1)} %concatenate.52), channel_id=1, source_target_pairs={{0,2},{1,3},{2,0},{3,1},{4,6},{5,7},{6,4},{7,5},{8,10},{9,11},{10,... | collective-permute-start | bytes 86216 | tf_op jit(solution)/shard_map/ppermute | solution.py:34
  102.2 1.9 %collective-permute-done.6 = bf16[14368]{0:T(1024)(128)(2,1)S(1)} collective-permute-done((bf16[14368]{0:T(1024)(128)(2,1)S(1)}, bf16[14368]{0:T(1024)(128)(2,1)S(1)}, u32[]{:S(2)}, u32[]{:S(2)}) %collective-permute-start.6) | collective-permute-done | bytes 28768 | tf_op jit(solution)/shard_map/ppermute | solution.py:34
  104.1 4.8 %collective-permute-start.7 = (bf16[14368]{0:T(1024)(128)(2,1)S(1)}, bf16[14368]{0:T(1024)(128)(2,1)S(1)}, u32[]{:S(2)}, u32[]{:S(2)}) collective-permute-start(bf16[14368]{0:T(1024)(128)(2,1)S(1)} %add_convert_fusion.6), channel_id=1, source_target_pairs={{0,4},{1,5},{2,6},{3,7},{4,0},{5,1},{6,2},{7,3},{8,12},{9,13},{10,... | collective-permute-start | bytes 86216 | tf_op jit(solution)/shard_map/ppermute | solution.py:34
  108.9 1.9 %collective-permute-done.7 = bf16[14368]{0:T(1024)(128)(2,1)S(1)} collective-permute-done((bf16[14368]{0:T(1024)(128)(2,1)S(1)}, bf16[14368]{0:T(1024)(128)(2,1)S(1)}, u32[]{:S(2)}, u32[]{:S(2)}) %collective-permute-start.7) | collective-permute-done | bytes 28768 | tf_op jit(solution)/shard_map/ppermute | solution.py:34
  110.8 4.8 %collective-permute-start.8 = (bf16[14368]{0:T(1024)(128)(2,1)S(1)}, bf16[14368]{0:T(1024)(128)(2,1)S(1)}, u32[]{:S(2)}, u32[]{:S(2)}) collective-permute-start(bf16[14368]{0:T(1024)(128)(2,1)S(1)} %add_convert_fusion.5), channel_id=1, source_target_pairs={{0,8},{1,9},{2,10},{3,11},{4,12},{5,13},{6,14},{7,15},{8,0},{9,1},... | collective-permute-start | bytes 86216 | tf_op jit(solution)/shard_map/ppermute | solution.py:34
  115.6 4.9 %collective-permute-done.8 = bf16[14368]{0:T(1024)(128)(2,1)S(1)} collective-permute-done((bf16[14368]{0:T(1024)(128)(2,1)S(1)}, bf16[14368]{0:T(1024)(128)(2,1)S(1)}, u32[]{:S(2)}, u32[]{:S(2)}) %collective-permute-start.8) | collective-permute-done | bytes 28768 | tf_op jit(solution)/shard_map/ppermute | solution.py:34
  120.5 3.2 %collective-permute-start.9 = (bf16[14368]{0:T(1024)(128)(2,1)S(1)}, bf16[14368]{0:T(1024)(128)(2,1)S(1)}, u32[]{:S(2)}, u32[]{:S(2)}) collective-permute-start(bf16[14368]{0:T(1024)(128)(2,1)S(1)} %add_convert_fusion.4), channel_id=1, source_target_pairs={{0,16},{1,17},{2,18},{3,19},{4,20},{5,21},{6,22},{7,23},{8,24},{9,... | collective-permute-start | bytes 86216 | tf_op jit(solution)/shard_map/ppermute | solution.py:34
  123.7 2.5 %collective-permute-done.9 = bf16[14368]{0:T(1024)(128)(2,1)S(1)} collective-permute-done((bf16[14368]{0:T(1024)(128)(2,1)S(1)}, bf16[14368]{0:T(1024)(128)(2,1)S(1)}, u32[]{:S(2)}, u32[]{:S(2)}) %collective-permute-start.9) | collective-permute-done | bytes 28768 | tf_op jit(solution)/shard_map/ppermute | solution.py:34
  126.3 1.9 %collective-permute-start.10 = (bf16[14368]{0:T(1024)(128)(2,1)S(1)}, bf16[14368]{0:T(1024)(128)(2,1)S(1)}, u32[]{:S(2)}, u32[]{:S(2)}) collective-permute-start(bf16[14368]{0:T(1024)(128)(2,1)S(1)} %get-tuple-element.30), channel_id=1, source_target_pairs={{0,1},{1,0},{2,3},{3,2},{4,5},{5,4},{6,7},{7,6},{8,9},{9,8},{10,11... | collective-permute-start | bytes 86216 | tf_op jit(solution)/shard_map/ppermute | solution.py:34
  128.2 1.2 collective-permute-done.10
  130.8 4.3 %collective-permute-start.11 = (bf16[34848]{0:T(1024)(128)(2,1)S(1)}, bf16[34848]{0:T(1024)(128)(2,1)S(1)}, u32[]{:S(2)}, u32[]{:S(2)}) collective-permute-start(bf16[34848]{0:T(1024)(128)(2,1)S(1)} %pad_maximum_fusion.3), channel_id=1, source_target_pairs={{0,32},{32,0},{64,96},{96,64},{128,160},{160,128},{192,224},{224,1... | collective-permute-start | bytes 209096 | tf_op jit(solution)/shard_map/ppermute | solution.py:34
  135.1 4.3 %collective-permute-done.11 = bf16[34848]{0:T(1024)(128)(2,1)S(1)} collective-permute-done((bf16[34848]{0:T(1024)(128)(2,1)S(1)}, bf16[34848]{0:T(1024)(128)(2,1)S(1)}, u32[]{:S(2)}, u32[]{:S(2)}) %collective-permute-start.11) | collective-permute-done | bytes 69728 | tf_op jit(solution)/shard_map/ppermute | solution.py:34
  139.4 4.6 %collective-permute-start.12 = (bf16[34848]{0:T(1024)(128)(2,1)S(1)}, bf16[34848]{0:T(1024)(128)(2,1)S(1)}, u32[]{:S(2)}, u32[]{:S(2)}) collective-permute-start(bf16[34848]{0:T(1024)(128)(2,1)S(1)} %add_convert_fusion.2), channel_id=1, source_target_pairs={{0,64},{32,96},{64,0},{96,32},{128,192},{160,224},{192,128},{224,1... | collective-permute-start | bytes 209096 | tf_op jit(solution)/shard_map/ppermute | solution.py:34
  144.1 6.3 %collective-permute-done.12 = bf16[34848]{0:T(1024)(128)(2,1)S(1)} collective-permute-done((bf16[34848]{0:T(1024)(128)(2,1)S(1)}, bf16[34848]{0:T(1024)(128)(2,1)S(1)}, u32[]{:S(2)}, u32[]{:S(2)}) %collective-permute-start.12) | collective-permute-done | bytes 69728 | tf_op jit(solution)/shard_map/ppermute | solution.py:34
  150.4 1.9 %collective-permute-start.13 = (bf16[34848]{0:T(1024)(128)(2,1)S(1)}, bf16[34848]{0:T(1024)(128)(2,1)S(1)}, u32[]{:S(2)}, u32[]{:S(2)}) collective-permute-start(bf16[34848]{0:T(1024)(128)(2,1)S(1)} %add_convert_fusion.1), channel_id=1, source_target_pairs={{0,128},{32,160},{64,192},{96,224},{128,0},{160,32},{192,64},{224,... | collective-permute-start | bytes 209096 | tf_op jit(solution)/shard_map/ppermute | solution.py:34
  152.5 4.1 %collective-permute-done.13 = bf16[34848]{0:T(1024)(128)(2,1)S(1)} collective-permute-done((bf16[34848]{0:T(1024)(128)(2,1)S(1)}, bf16[34848]{0:T(1024)(128)(2,1)S(1)}, u32[]{:S(2)}, u32[]{:S(2)}) %collective-permute-start.13) | collective-permute-done | bytes 69728 | tf_op jit(solution)/shard_map/ppermute | solution.py:34
  156.6 2.9 %collective-permute-start.14 = (bf16[34848]{0:T(1024)(128)(2,1)S(1)}, bf16[34848]{0:T(1024)(128)(2,1)S(1)}, u32[]{:S(2)}, u32[]{:S(2)}) collective-permute-start(bf16[34848]{0:T(1024)(128)(2,1)S(1)} %add_convert_fusion), channel_id=1, source_target_pairs={{0,256},{32,288},{64,320},{96,352},{128,384},{160,416},{192,448},{... | collective-permute-start | bytes 209096 | tf_op jit(solution)/shard_map/ppermute | solution.py:34
  159.5 1.0 fusion.29
  160.5 3.9 %collective-permute-done.14 = bf16[34848]{0:T(1024)(128)(2,1)S(1)} collective-permute-done((bf16[34848]{0:T(1024)(128)(2,1)S(1)}, bf16[34848]{0:T(1024)(128)(2,1)S(1)}, u32[]{:S(2)}, u32[]{:S(2)}) %collective-permute-start.14) | collective-permute-done | bytes 69728 | tf_op jit(solution)/shard_map/ppermute | solution.py:34
  164.7 0.7 copy.57
  165.5 0.7 copy.58
  166.9 0.7 mul.329
  (122 shorter events, 7.9 us)
Async XLA Ops:
  0.6 1.0 copy-start
  4.9 17.4 %collective-permute-start = (bf16[12800]{0:T(1024)(128)(2,1)S(1)}, bf16[12800]{0:T(1024)(128)(2,1)S(1)}, u32[]{:S(2)}, u32[]{:S(2)}) collective-permute-start(bf16[12800]{0:T(1024)(128)(2,1)S(1)} %pad_maximum_fusion.4), channel_id=1, source_target_pairs={{0,32},{32,64},{64,96},{96,128},{128,160},{160,192},{192,224},{224... | collective-permute-start | bytes 76808 | tf_op jit(solution)/shard_map/ppermute | solution.py:18
  11.3 11.2 %collective-permute-start.1 = (bf16[12800]{0:T(1024)(128)(2,1)S(1)}, bf16[12800]{0:T(1024)(128)(2,1)S(1)}, u32[]{:S(2)}, u32[]{:S(2)}) collective-permute-start(bf16[12800]{0:T(1024)(128)(2,1)S(1)} %pad_maximum_fusion.5), channel_id=1, source_target_pairs={{32,0},{64,32},{96,64},{128,96},{160,128},{192,160},{224,192},{256... | collective-permute-start | bytes 76808 | tf_op jit(solution)/shard_map/ppermute | solution.py:18
  22.3 33.4 %copy-start.4 = (bf16[24,256,128]{1,0,2:T(8,128)(2,1)}, bf16[24,256,128]{1,0,2:T(8,128)(2,1)S(1)}, u32[]{:S(2)}) copy-start(bf16[24,256,128]{1,0,2:T(8,128)(2,1)S(1)} %copy.42) | copy-start | bytes 4718596
  22.8 14.4 %collective-permute-start.4 = (bf16[144,32]{0,1:T(8,128)(2,1)S(1)}, bf16[144,32]{0,1:T(8,128)(2,1)S(1)}, u32[]{:S(2)}, u32[]{:S(2)}) collective-permute-start(bf16[144,32]{0,1:T(8,128)(2,1)S(1)} %fusion.42), channel_id=1, source_target_pairs={{0,0},{1,1},{2,32},{3,33},{4,64},{5,65},{6,96},{7,97},{8,128},{9,1... | collective-permute-start | bytes 27656 | tf_op jit(solution)/shard_map/ppermute | solution.py:78
  30.6 19.7 %copy-start.5 = (bf16[24,4,128]{1,0,2:T(8,128)(2,1)}, bf16[24,4,128]{1,0,2:T(8,128)(2,1)S(1)}, u32[]{:S(2)}) copy-start(bf16[24,4,128]{1,0,2:T(8,128)(2,1)S(1)} %copy.41) | copy-start | bytes 73732
  31.5 29.0 %collective-permute-start.3 = (bf16[24,264,4]{1,0,2:T(8,128)(2,1)}, bf16[24,264,4]{1,0,2:T(8,128)(2,1)}, u32[]{:S(2)}, u32[]{:S(2)}) collective-permute-start(bf16[24,264,4]{1,0,2:T(8,128)(2,1)} %get-tuple-element.32), channel_id=1, source_target_pairs={{1,0},{2,1},{3,2},{4,3},{5,4},{6,5},{7,6},{8,7},{9,8},{10,9},{11,1... | collective-permute-start | bytes 152072 | tf_op jit(solution)/shard_map/ppermute | solution.py:18
  32.8 27.7 %collective-permute-start.2 = (bf16[24,264,4]{1,0,2:T(8,128)(2,1)}, bf16[24,264,4]{1,0,2:T(8,128)(2,1)}, u32[]{:S(2)}, u32[]{:S(2)}) collective-permute-start(bf16[24,264,4]{1,0,2:T(8,128)(2,1)} %get-tuple-element.31), channel_id=1, source_target_pairs={{0,1},{1,2},{2,3},{3,4},{4,5},{5,6},{6,7},{7,8},{8,9},{9,10},{10,1... | collective-permute-start | bytes 152072 | tf_op jit(solution)/shard_map/ppermute | solution.py:18
  40.9 9.4 %copy-start.1 = (bf16[32,272,144]{1,0,2:T(8,128)(2,1)}, bf16[32,272,144]{1,0,2:T(8,128)(2,1)S(1)}, u32[]{:S(2)}) copy-start(bf16[32,272,144]{1,0,2:T(8,128)(2,1)S(1)} %select_convert_fusion) | copy-start | bytes 7520260
  50.3 2.8 %copy-start.3 = (f32[32,264,136]{1,0,2:T(8,128)}, f32[32,264,136]{1,0,2:T(8,128)S(1)}, u32[]{:S(2)}) copy-start(f32[32,264,136]{1,0,2:T(8,128)S(1)} %multiply_add_fusion) | copy-start | bytes 13787140
  53.1 2.6 %copy-start.18 = (bf16[32,32]{1,0:T(8,128)(2,1)S(1)}, bf16[32,32]{1,0:T(8,128)(2,1)}, u32[]{:S(2)}) copy-start(bf16[32,32]{1,0:T(8,128)(2,1)} %param.11) | copy-start | bytes 6148
  60.3 3.7 %slice-start = ((s8[6684672]{0:T(1024)(128)(4,1)}), s8[2490368]{0:T(1024)(128)(4,1)S(1)}, s32[]{:S(2)}) async-start(s8[6684672]{0:T(1024)(128)(4,1)} %bitcast.107), calls=%async_computation | async-start | bytes 4980736
  60.4 3.7 %slice-start.1 = ((s8[6684672]{0:T(1024)(128)(4,1)}), s8[4194304]{0:T(1024)(128)(4,1)S(1)}, s32[]{:S(2)}) async-start(s8[6684672]{0:T(1024)(128)(4,1)} %bitcast.107), calls=%async_computation.1 | async-start | bytes 8388608
  60.5 3.6 %copy-start.19 = (bf16[32,32]{1,0:T(8,128)(2,1)S(1)}, bf16[32,32]{1,0:T(8,128)(2,1)}, u32[]{:S(2)}) copy-start(bf16[32,32]{1,0:T(8,128)(2,1)} %param.11) | copy-start | bytes 6148
  64.1 3.4 %copy-start.9 = (f32[32]{0:T(128)S(1)}, f32[32]{0:T(128)}, u32[]{:S(2)}) copy-start(f32[32]{0:T(128)} %get-tuple-element.47) | copy-start | bytes 388
  64.1 3.4 %copy-start.10 = (f32[32]{0:T(128)S(1)}, f32[32]{0:T(128)}, u32[]{:S(2)}) copy-start(f32[32]{0:T(128)} %get-tuple-element.48) | copy-start | bytes 388
  64.1 3.4 %copy-start.11 = (f32[32]{0:T(128)S(1)}, f32[32]{0:T(128)}, u32[]{:S(2)}) copy-start(f32[32]{0:T(128)} %get-tuple-element.49) | copy-start | bytes 388
  64.1 3.4 %copy-start.12 = (f32[32]{0:T(128)S(1)}, f32[32]{0:T(128)}, u32[]{:S(2)}) copy-start(f32[32]{0:T(128)} %get-tuple-element.50) | copy-start | bytes 388
  64.1 3.4 %copy-start.13 = (f32[32]{0:T(128)S(1)}, f32[32]{0:T(128)}, u32[]{:S(2)}) copy-start(f32[32]{0:T(128)} %get-tuple-element.51) | copy-start | bytes 388
  64.1 3.4 %copy-start.14 = (f32[32]{0:T(128)S(1)}, f32[32]{0:T(128)}, u32[]{:S(2)}) copy-start(f32[32]{0:T(128)} %get-tuple-element.52) | copy-start | bytes 388
  64.1 3.4 %copy-start.15 = (f32[32]{0:T(128)S(1)}, f32[32]{0:T(128)}, u32[]{:S(2)}) copy-start(f32[32]{0:T(128)} %get-tuple-element.53) | copy-start | bytes 388
  64.2 3.4 %copy-start.16 = (f32[32]{0:T(128)S(1)}, f32[32]{0:T(128)}, u32[]{:S(2)}) copy-start(f32[32]{0:T(128)} %get-tuple-element.54) | copy-start | bytes 388
  64.2 3.4 %copy-start.17 = (f32[32]{0:T(128)S(1)}, f32[32]{0:T(128)}, u32[]{:S(2)}) copy-start(f32[32]{0:T(128)} %get-tuple-element.55) | copy-start | bytes 388
  67.6 7.0 %copy-start.2 = (bf16[32,272,144]{1,0,2:T(8,128)(2,1)S(1)}, bf16[32,272,144]{1,0,2:T(8,128)(2,1)}, u32[]{:S(2)}) copy-start(bf16[32,272,144]{1,0,2:T(8,128)(2,1)} %copy-done.1) | copy-start | bytes 7520260
  74.5 14.5 %copy-start.6 = (bf16[32,256,128]{1,0,2:T(8,128)(2,1)S(1)}, bf16[32,256,128]{1,0,2:T(8,128)(2,1)}, u32[]{:S(2)}) copy-start(bf16[32,256,128]{1,0,2:T(8,128)(2,1)} %multiply_convert_fusion.1) | copy-start | bytes 6291460
  82.0 70.2 %copy-start.7 = (bf16[512,32]{0,1:T(8,128)(2,1)S(1)}, bf16[512,32]{0,1:T(8,128)(2,1)}, u32[]{:S(2)}) copy-start(bf16[512,32]{0,1:T(8,128)(2,1)} %param.8) | copy-start | bytes 98308
  82.1 77.5 %copy-start.8 = (bf16[512,32]{0,1:T(8,128)(2,1)S(1)}, bf16[512,32]{0,1:T(8,128)(2,1)}, u32[]{:S(2)}) copy-start(bf16[512,32]{0,1:T(8,128)(2,1)} %param.9) | copy-start | bytes 98308
  82.1 13.0 %collective-permute-start.5 = (bf16[128,32]{1,0:T(8,128)(2,1)S(1)}, bf16[128,32]{1,0:T(8,128)(2,1)S(1)}, u32[]{:S(2)}, u32[]{:S(2)}) collective-permute-start(bf16[128,32]{1,0:T(8,128)(2,1)S(1)} %bitcast.114), channel_id=1, source_target_pairs={{0,0},{1,1},{2,32},{3,33},{4,64},{5,65},{6,96},{7,97},{8,128},{9,1... | collective-permute-start | bytes 24584 | tf_op jit(solution)/shard_map/ppermute | solution.py:128
  95.2 8.9 %collective-permute-start.6 = (bf16[14368]{0:T(1024)(128)(2,1)S(1)}, bf16[14368]{0:T(1024)(128)(2,1)S(1)}, u32[]{:S(2)}, u32[]{:S(2)}) collective-permute-start(bf16[14368]{0:T(1024)(128)(2,1)S(1)} %concatenate.52), channel_id=1, source_target_pairs={{0,2},{1,3},{2,0},{3,1},{4,6},{5,7},{6,4},{7,5},{8,10},{9,11},{10,... | collective-permute-start | bytes 86216 | tf_op jit(solution)/shard_map/ppermute | solution.py:34
  104.1 6.7 %collective-permute-start.7 = (bf16[14368]{0:T(1024)(128)(2,1)S(1)}, bf16[14368]{0:T(1024)(128)(2,1)S(1)}, u32[]{:S(2)}, u32[]{:S(2)}) collective-permute-start(bf16[14368]{0:T(1024)(128)(2,1)S(1)} %add_convert_fusion.6), channel_id=1, source_target_pairs={{0,4},{1,5},{2,6},{3,7},{4,0},{5,1},{6,2},{7,3},{8,12},{9,13},{10,... | collective-permute-start | bytes 86216 | tf_op jit(solution)/shard_map/ppermute | solution.py:34
  110.8 9.7 %collective-permute-start.8 = (bf16[14368]{0:T(1024)(128)(2,1)S(1)}, bf16[14368]{0:T(1024)(128)(2,1)S(1)}, u32[]{:S(2)}, u32[]{:S(2)}) collective-permute-start(bf16[14368]{0:T(1024)(128)(2,1)S(1)} %add_convert_fusion.5), channel_id=1, source_target_pairs={{0,8},{1,9},{2,10},{3,11},{4,12},{5,13},{6,14},{7,15},{8,0},{9,1},... | collective-permute-start | bytes 86216 | tf_op jit(solution)/shard_map/ppermute | solution.py:34
  120.5 5.8 %collective-permute-start.9 = (bf16[14368]{0:T(1024)(128)(2,1)S(1)}, bf16[14368]{0:T(1024)(128)(2,1)S(1)}, u32[]{:S(2)}, u32[]{:S(2)}) collective-permute-start(bf16[14368]{0:T(1024)(128)(2,1)S(1)} %add_convert_fusion.4), channel_id=1, source_target_pairs={{0,16},{1,17},{2,18},{3,19},{4,20},{5,21},{6,22},{7,23},{8,24},{9,... | collective-permute-start | bytes 86216 | tf_op jit(solution)/shard_map/ppermute | solution.py:34
  126.3 3.1 %collective-permute-start.10 = (bf16[14368]{0:T(1024)(128)(2,1)S(1)}, bf16[14368]{0:T(1024)(128)(2,1)S(1)}, u32[]{:S(2)}, u32[]{:S(2)}) collective-permute-start(bf16[14368]{0:T(1024)(128)(2,1)S(1)} %get-tuple-element.30), channel_id=1, source_target_pairs={{0,1},{1,0},{2,3},{3,2},{4,5},{5,4},{6,7},{7,6},{8,9},{9,8},{10,11... | collective-permute-start | bytes 86216 | tf_op jit(solution)/shard_map/ppermute | solution.py:34
  130.8 8.6 %collective-permute-start.11 = (bf16[34848]{0:T(1024)(128)(2,1)S(1)}, bf16[34848]{0:T(1024)(128)(2,1)S(1)}, u32[]{:S(2)}, u32[]{:S(2)}) collective-permute-start(bf16[34848]{0:T(1024)(128)(2,1)S(1)} %pad_maximum_fusion.3), channel_id=1, source_target_pairs={{0,32},{32,0},{64,96},{96,64},{128,160},{160,128},{192,224},{224,1... | collective-permute-start | bytes 209096 | tf_op jit(solution)/shard_map/ppermute | solution.py:34
  139.4 10.9 %collective-permute-start.12 = (bf16[34848]{0:T(1024)(128)(2,1)S(1)}, bf16[34848]{0:T(1024)(128)(2,1)S(1)}, u32[]{:S(2)}, u32[]{:S(2)}) collective-permute-start(bf16[34848]{0:T(1024)(128)(2,1)S(1)} %add_convert_fusion.2), channel_id=1, source_target_pairs={{0,64},{32,96},{64,0},{96,32},{128,192},{160,224},{192,128},{224,1... | collective-permute-start | bytes 209096 | tf_op jit(solution)/shard_map/ppermute | solution.py:34
  150.4 6.2 %collective-permute-start.13 = (bf16[34848]{0:T(1024)(128)(2,1)S(1)}, bf16[34848]{0:T(1024)(128)(2,1)S(1)}, u32[]{:S(2)}, u32[]{:S(2)}) collective-permute-start(bf16[34848]{0:T(1024)(128)(2,1)S(1)} %add_convert_fusion.1), channel_id=1, source_target_pairs={{0,128},{32,160},{64,192},{96,224},{128,0},{160,32},{192,64},{224,... | collective-permute-start | bytes 209096 | tf_op jit(solution)/shard_map/ppermute | solution.py:34
  156.6 7.7 %collective-permute-start.14 = (bf16[34848]{0:T(1024)(128)(2,1)S(1)}, bf16[34848]{0:T(1024)(128)(2,1)S(1)}, u32[]{:S(2)}, u32[]{:S(2)}) collective-permute-start(bf16[34848]{0:T(1024)(128)(2,1)S(1)} %add_convert_fusion), channel_id=1, source_target_pairs={{0,256},{32,288},{64,320},{96,352},{128,384},{160,416},{192,448},{... | collective-permute-start | bytes 209096 | tf_op jit(solution)/shard_map/ppermute | solution.py:34

commit v9 on v8

--- a/solution.py
+++ b/solution.py
@@ -158,6 +158,7 @@
     contract = (((0,), (0,)), ((), ()))
     wleft_part = lax.dot_general(bin_features, grad_left, contract, preferred_element_type=jnp.float32)
     wright_part = lax.dot_general(bin_features, grad_right, contract, preferred_element_type=jnp.float32)
+    wleft_part, wright_part, small = (grad_scale * wleft_part, grad_scale * wright_part, grad_scale * small)
     bit = 1
     while bit < row_count:
         likes = (wleft_part, wright_part, small)
@@ -168,14 +169,7 @@
         bit *= 2
 
     kernel_sum, point_sum, head_sum = unpacked(small, (kernel_part, point_part, head_part))
-    return (
-        grad_features,
-        grad_scale * wleft_part,
-        grad_scale * wright_part,
-        grad_scale * kernel_sum,
-        grad_scale * point_sum,
-        grad_scale * head_sum,
-    )
+    return (grad_features, wleft_part, wright_part, kernel_sum, point_sum, head_sum)
 
 
 def solution(mesh):

time: 169 us -> 169 us (level)
    slice x6 -> x15, local copies, waits for them, and re-layouts: 0.94 us -> 2.76 us  [unpacked(): out.append(flat[at:at + like.size].reshape(like.shape))]
where the time goes in v9:
time: 169 us; the launch traced here: 168 us
  starting transfers between devices  67 us (40%)
  waiting for transfers between devices  35.4 us (21%)
  other arithmetic  31.2 us (18%)
  local copies, waits for them, and re-layouts  17.7 us (10%)
  matrix products  15.7 us (9%)
    ppermute x9, starting transfers between devices, xor_round(): return lax.ppermute(flat, axis, [(i, i ^ bit) for i in range(count)])  35.5 us
    ppermute x9, waiting for transfers between devices, xor_round(): return lax.ppermute(flat, axis, [(i, i ^ bit) for i in range(count)])  30.9 us
    ppermute x4, starting transfers between devices, shifted(): return lax.ppermute(x, axis, pairs)  18.1 us
    add x1, other arithmetic, body(): conv_ext + depth_kernel[3 * a + b][:, None, None] * pair_ext[:, step * a:...  9.35 us
    unnamed x48, local copies, waits for them, and re-layouts  8.19 us
    reduce_sum x1, other arithmetic, body(): kern_terms.append(jnp.sum(conv_grad_tile * window, axis=(1, 2)))  7.48 us
    ppermute x1, starting transfers between devices, body(): right_moved = lax.ppermute(right_part, ('row', 'col'), transpose_pairs())  6.98 us
    reduce_sum x1, other arithmetic, body(): right_part = jnp.sum(backward_pass, axis=1).T  6.96 us
  transfers between devices with their start and end apart: 15, of which 10 were waited for; matrix products, arithmetic and copies ran while one was open for 18% of the time, Pallas kernels for 0%

profile of v9, /device:TPU:6, one launch (start us, length us, event | category | flops | bytes accessed | tf_op | source)
XLA Modules:
  0.0 168.4 jit_solution(11520808733130250928)
XLA Ops:
  0.6 0.9 copy-done
  1.6 0.9 convolution_convert_fusion
  2.8 0.9 convolution_convert_fusion.1
  4.0 0.9 fusion.61
  4.9 6.1 %collective-permute-start = (bf16[12800]{0:T(1024)(128)(2,1)S(1)}, bf16[12800]{0:T(1024)(128)(2,1)S(1)}, u32[]{:S(2)}, u32[]{:S(2)}) collective-permute-start(bf16[12800]{0:T(1024)(128)(2,1)S(1)} %pad_maximum_fusion.4), channel_id=1, source_target_pairs={{0,32},{32,64},{64,96},{96,128},{128,160},{160,192},{192,224},{224... | collective-permute-start | bytes 76808 | tf_op jit(solution)/shard_map/ppermute | solution.py:18
  11.3 7.0 %collective-permute-start.1 = (bf16[12800]{0:T(1024)(128)(2,1)S(1)}, bf16[12800]{0:T(1024)(128)(2,1)S(1)}, u32[]{:S(2)}, u32[]{:S(2)}) collective-permute-start(bf16[12800]{0:T(1024)(128)(2,1)S(1)} %pad_maximum_fusion.5), channel_id=1, source_target_pairs={{32,0},{64,32},{96,64},{128,96},{160,128},{192,160},{224,192},{256... | collective-permute-start | bytes 76808 | tf_op jit(solution)/shard_map/ppermute | solution.py:18
  18.5 1.6 slice_bitcast_fusion.8
  20.1 2.2 %copy.42 = bf16[24,256,128]{1,0,2:T(8,128)(2,1)S(1)} copy(bf16[24,256,128]{2,1,0:T(8,128)(2,1)} %param.13) | data formatting | bytes 3145728 | tf_op args[6]
  22.8 6.5 %collective-permute-start.4 = (bf16[144,32]{0,1:T(8,128)(2,1)S(1)}, bf16[144,32]{0,1:T(8,128)(2,1)S(1)}, u32[]{:S(2)}, u32[]{:S(2)}) collective-permute-start(bf16[144,32]{0,1:T(8,128)(2,1)S(1)} %fusion.44), channel_id=1, source_target_pairs={{0,0},{1,1},{2,32},{3,33},{4,64},{5,65},{6,96},{7,97},{8,128},{9,1... | collective-permute-start | bytes 27656 | tf_op jit(solution)/shard_map/ppermute | solution.py:78
  30.6 0.9 pad_maximum_fusion.2
  31.5 1.3 collective-permute-start.3
  32.8 3.7 %collective-permute-start.2 = (bf16[24,264,4]{1,0,2:T(8,128)(2,1)}, bf16[24,264,4]{1,0,2:T(8,128)(2,1)}, u32[]{:S(2)}, u32[]{:S(2)}) collective-permute-start(bf16[24,264,4]{1,0,2:T(8,128)(2,1)} %get-tuple-element.31), channel_id=1, source_target_pairs={{0,1},{1,2},{2,3},{3,4},{4,5},{5,6},{6,7},{7,8},{8,9},{9,10},{10,1... | collective-permute-start | bytes 152072 | tf_op jit(solution)/shard_map/ppermute | solution.py:18
  36.5 0.7 convert_bitcast_fusion
  37.8 0.9 copy.48
  38.6 2.2 %select_convert_fusion = bf16[32,272,144]{1,0,2:T(8,128)(2,1)S(1)} fusion(f32[32,144]{0,1:T(8,128)S(1)} %copy.48, f32[32,272]{1,0:T(8,128)} %convert_bitcast_fusion, pred[272,144]{0,1:T(8,128)(4,1)S(1)} %and_and_fusion), kind=kLoop, calls=%fused_computation.10 | loop fusion | flops 3760128 | bytes 2599168 | tf_op jit(solution)/shard_map/convert_element_type | solution.py:84
  40.9 9.4 %multiply_add_fusion = f32[32,264,136]{1,0,2:T(8,128)S(1)} fusion(bf16[32,272,144]{1,0,2:T(8,128)(2,1)S(1)} %select_convert_fusion, f32[32]{0:T(128)} %get-tuple-element.54, f32[32]{0:T(128)} %get-tuple-element.55, f32[32]{0:T(128)} %get-tuple-element.48, f32[32]{0:T(128)} %get-tuple-element.49, f32[32]{0:T(128)} %get-tuple-element.50, ...), kind=kLoop, calls=%fused_computation.13 | loop fusion | flops 29872128 | bytes 25277568 | tf_op jit(solution)/shard_map/add | solution.py:91
  50.3 2.8 %copy-done.3 = f32[32,264,136]{1,0,2:T(8,128)} copy-done((f32[32,264,136]{1,0,2:T(8,128)}, f32[32,264,136]{1,0,2:T(8,128)S(1)}, u32[]{:S(2)}) %copy-start.3) | copy-done | bytes 4595736
  53.1 2.6 %multiply_convert_fusion.1 = bf16[32,256,128]{1,0,2:T(8,128)(2,1)} fusion(f32[32,264,136]{1,0,2:T(8,128)S(1)} %multiply_add_fusion), kind=kLoop, calls=%fused_computation.31 | loop fusion | flops 5242880 | bytes 6291456 | tf_op jit(solution)/shard_map/convert_element_type | solution.py:95
  55.6 4.6 %fusion.41 = bf16[32,24]{0,1:T(8,128)(2,1)S(1)} fusion(bf16[24,256,128]{1,0,2:T(8,128)(2,1)S(1)} %copy.42, bf16[32,256,128]{1,0,2:T(8,128)(2,1)} %multiply_convert_fusion.1, bf16[32,272,144]{1,0,2:T(8,128)(2,1)} %copy-done.1, bf16[32,32]{1,0:T(8,128)(2,1)S(1)} %copy-done.18), kind=kOutput, calls=%fused_computation.58 | convolution fusion | flops 120587008 | bytes 5770752 | tf_op jit(solution)/shard_map/ydq,gdq->yg/dot_general | solution.py:125
  60.5 3.5 %fusion.16 = bf16[32,264,136]{1,0,2:T(8,128)(2,1)S(1)} fusion(bf16[24,264,4]{1,0,2:T(8,128)(2,1)} %collective-permute-done.3, bf16[24,4,128]{1,0,2:T(8,128)(2,1)S(1)} %copy.43, bf16[24,256,128]{1,0,2:T(8,128)(2,1)} %copy-done.4, bf16[24,4,128]{1,0,2:T(8,128)(2,1)} %copy-done.5, bf16[24,264,4]{1,0,2:T(8,128)(2,1)} %collective-permute-done.2, ...), kind=kOutput, calls=%fused_computation.32 | convolution fusion | flops 66063360 | bytes 4022784 | tf_op jit(solution)/shard_map/ch,hij->cij/dot_general | solution.py:101
  64.2 3.3 %fusion = bf16[32,264,136]{1,0,2:T(8,128)(2,1)S(1)} fusion(f32[32,264,136]{1,0,2:T(8,128)S(1)} %bitcast.108, bf16[32,264,136]{1,0,2:T(8,128)(2,1)S(1)} %fusion.16, bf16[32,32]{1,0:T(8,128)(2,1)S(1)} %copy-done.19), kind=kOutput, calls=%fused_computation.12 | convolution fusion | flops 83871744 | bytes 9193472 | tf_op jit(solution)/shard_map/co,oij->cij/dot_general | solution.py:103
  67.6 7.0 %fusion.59 = (bf16[32,128]{0,1:T(8,128)(2,1)S(1)}, bf16[32,256]{1,0:T(8,128)(2,1)S(1)}) fusion(bf16[32,264,136]{1,0,2:T(8,128)(2,1)S(1)} %fusion, f32[32]{0:T(128)S(1)} %copy-done.16, f32[32]{0:T(128)S(1)} %copy-done.17, f32[32]{0:T(128)S(1)} %copy-done.10, f32[32]{0:T(128)S(1)} %copy-done.11, f32[32]{0:T(128)S(1)} %copy-done.12, f32[32]{0:T(128)S(1)} %copy-done.13, ...), kind=kLoop, calls=%fused_computation.121 | loop fusion | flops 31444992 | bytes 20997248 | tf_op jit(solution)/shard_map/reduce_sum | solution.py:121
  74.6 7.5 %fusion.15 = (bf16[32]{0:T(256)(128)(2,1)S(1)}, bf16[32]{0:T(256)(128)(2,1)S(1)}, bf16[32]{0:T(256)(128)(2,1)S(1)}, bf16[32]{0:T(256)(128)(2,1)S(1)}, bf16[32]{0...) fusion(bf16[32,272,144]{1,0,2:T(8,128)(2,1)S(1)} %copy-done.2, ...), kind=kLoop, calls=%fused_computation.30 | loop fusion | flops 29359840 | bytes 20972096 | tf_op jit(solution)/shard_map/reduce_sum | solution.py:118
  82.1 7.0 %collective-permute-start.5 = (bf16[128,32]{1,0:T(8,128)(2,1)S(1)}, bf16[128,32]{1,0:T(8,128)(2,1)S(1)}, u32[]{:S(2)}, u32[]{:S(2)}) collective-permute-start(bf16[128,32]{1,0:T(8,128)(2,1)S(1)} %bitcast.114), channel_id=1, source_target_pairs={{0,0},{1,1},{2,32},{3,33},{4,64},{5,65},{6,96},{7,97},{8,128},{9,1... | collective-permute-start | bytes 24584 | tf_op jit(solution)/shard_map/ppermute | solution.py:128
  89.1 1.0 fusion.37
  90.6 4.5 %collective-permute-done.5 = bf16[128,32]{1,0:T(8,128)(2,1)S(1)} collective-permute-done((bf16[128,32]{1,0:T(8,128)(2,1)S(1)}, bf16[128,32]{1,0:T(8,128)(2,1)S(1)}, u32[]{:S(2)}, u32[]{:S(2)}) %collective-permute-start.5) | collective-permute-done | bytes 8224 | tf_op jit(solution)/shard_map/ppermute | solution.py:128
  95.2 7.0 %collective-permute-start.6 = (bf16[14368]{0:T(1024)(128)(2,1)S(1)}, bf16[14368]{0:T(1024)(128)(2,1)S(1)}, u32[]{:S(2)}, u32[]{:S(2)}) collective-permute-start(bf16[14368]{0:T(1024)(128)(2,1)S(1)} %concatenate.52), channel_id=1, source_target_pairs={{0,2},{1,3},{2,0},{3,1},{4,6},{5,7},{6,4},{7,5},{8,10},{9,11},{10,... | collective-permute-start | bytes 86216 | tf_op jit(solution)/shard_map/ppermute | solution.py:34
  102.2 1.9 %collective-permute-done.6 = bf16[14368]{0:T(1024)(128)(2,1)S(1)} collective-permute-done((bf16[14368]{0:T(1024)(128)(2,1)S(1)}, bf16[14368]{0:T(1024)(128)(2,1)S(1)}, u32[]{:S(2)}, u32[]{:S(2)}) %collective-permute-start.6) | collective-permute-done | bytes 28768 | tf_op jit(solution)/shard_map/ppermute | solution.py:34
  104.1 4.8 %collective-permute-start.7 = (bf16[14368]{0:T(1024)(128)(2,1)S(1)}, bf16[14368]{0:T(1024)(128)(2,1)S(1)}, u32[]{:S(2)}, u32[]{:S(2)}) collective-permute-start(bf16[14368]{0:T(1024)(128)(2,1)S(1)} %add_convert_fusion.6), channel_id=1, source_target_pairs={{0,4},{1,5},{2,6},{3,7},{4,0},{5,1},{6,2},{7,3},{8,12},{9,13},{10,... | collective-permute-start | bytes 86216 | tf_op jit(solution)/shard_map/ppermute | solution.py:34
  108.9 1.9 %collective-permute-done.7 = bf16[14368]{0:T(1024)(128)(2,1)S(1)} collective-permute-done((bf16[14368]{0:T(1024)(128)(2,1)S(1)}, bf16[14368]{0:T(1024)(128)(2,1)S(1)}, u32[]{:S(2)}, u32[]{:S(2)}) %collective-permute-start.7) | collective-permute-done | bytes 28768 | tf_op jit(solution)/shard_map/ppermute | solution.py:34
  110.8 4.8 %collective-permute-start.8 = (bf16[14368]{0:T(1024)(128)(2,1)S(1)}, bf16[14368]{0:T(1024)(128)(2,1)S(1)}, u32[]{:S(2)}, u32[]{:S(2)}) collective-permute-start(bf16[14368]{0:T(1024)(128)(2,1)S(1)} %add_convert_fusion.5), channel_id=1, source_target_pairs={{0,8},{1,9},{2,10},{3,11},{4,12},{5,13},{6,14},{7,15},{8,0},{9,1},... | collective-permute-start | bytes 86216 | tf_op jit(solution)/shard_map/ppermute | solution.py:34
  115.6 4.9 %collective-permute-done.8 = bf16[14368]{0:T(1024)(128)(2,1)S(1)} collective-permute-done((bf16[14368]{0:T(1024)(128)(2,1)S(1)}, bf16[14368]{0:T(1024)(128)(2,1)S(1)}, u32[]{:S(2)}, u32[]{:S(2)}) %collective-permute-start.8) | collective-permute-done | bytes 28768 | tf_op jit(solution)/shard_map/ppermute | solution.py:34
  120.5 3.2 %collective-permute-start.9 = (bf16[14368]{0:T(1024)(128)(2,1)S(1)}, bf16[14368]{0:T(1024)(128)(2,1)S(1)}, u32[]{:S(2)}, u32[]{:S(2)}) collective-permute-start(bf16[14368]{0:T(1024)(128)(2,1)S(1)} %add_convert_fusion.4), channel_id=1, source_target_pairs={{0,16},{1,17},{2,18},{3,19},{4,20},{5,21},{6,22},{7,23},{8,24},{9,... | collective-permute-start | bytes 86216 | tf_op jit(solution)/shard_map/ppermute | solution.py:34
  123.7 2.5 %collective-permute-done.9 = bf16[14368]{0:T(1024)(128)(2,1)S(1)} collective-permute-done((bf16[14368]{0:T(1024)(128)(2,1)S(1)}, bf16[14368]{0:T(1024)(128)(2,1)S(1)}, u32[]{:S(2)}, u32[]{:S(2)}) %collective-permute-start.9) | collective-permute-done | bytes 28768 | tf_op jit(solution)/shard_map/ppermute | solution.py:34
  126.3 1.9 %collective-permute-start.10 = (bf16[14368]{0:T(1024)(128)(2,1)S(1)}, bf16[14368]{0:T(1024)(128)(2,1)S(1)}, u32[]{:S(2)}, u32[]{:S(2)}) collective-permute-start(bf16[14368]{0:T(1024)(128)(2,1)S(1)} %get-tuple-element.30), channel_id=1, source_target_pairs={{0,1},{1,0},{2,3},{3,2},{4,5},{5,4},{6,7},{7,6},{8,9},{9,8},{10,11... | collective-permute-start | bytes 86216 | tf_op jit(solution)/shard_map/ppermute | solution.py:34
  128.2 1.2 collective-permute-done.10
  130.8 4.3 %collective-permute-start.11 = (bf16[34848]{0:T(1024)(128)(2,1)S(1)}, bf16[34848]{0:T(1024)(128)(2,1)S(1)}, u32[]{:S(2)}, u32[]{:S(2)}) collective-permute-start(bf16[34848]{0:T(1024)(128)(2,1)S(1)} %pad_maximum_fusion.3), channel_id=1, source_target_pairs={{0,32},{32,0},{64,96},{96,64},{128,160},{160,128},{192,224},{224,1... | collective-permute-start | bytes 209096 | tf_op jit(solution)/shard_map/ppermute | solution.py:34
  135.1 4.3 %collective-permute-done.11 = bf16[34848]{0:T(1024)(128)(2,1)S(1)} collective-permute-done((bf16[34848]{0:T(1024)(128)(2,1)S(1)}, bf16[34848]{0:T(1024)(128)(2,1)S(1)}, u32[]{:S(2)}, u32[]{:S(2)}) %collective-permute-start.11) | collective-permute-done | bytes 69728 | tf_op jit(solution)/shard_map/ppermute | solution.py:34
  139.4 4.6 %collective-permute-start.12 = (bf16[34848]{0:T(1024)(128)(2,1)S(1)}, bf16[34848]{0:T(1024)(128)(2,1)S(1)}, u32[]{:S(2)}, u32[]{:S(2)}) collective-permute-start(bf16[34848]{0:T(1024)(128)(2,1)S(1)} %add_convert_fusion.2), channel_id=1, source_target_pairs={{0,64},{32,96},{64,0},{96,32},{128,192},{160,224},{192,128},{224,1... | collective-permute-start | bytes 209096 | tf_op jit(solution)/shard_map/ppermute | solution.py:34
  144.1 6.3 %collective-permute-done.12 = bf16[34848]{0:T(1024)(128)(2,1)S(1)} collective-permute-done((bf16[34848]{0:T(1024)(128)(2,1)S(1)}, bf16[34848]{0:T(1024)(128)(2,1)S(1)}, u32[]{:S(2)}, u32[]{:S(2)}) %collective-permute-start.12) | collective-permute-done | bytes 69728 | tf_op jit(solution)/shard_map/ppermute | solution.py:34
  150.4 1.9 %collective-permute-start.13 = (bf16[34848]{0:T(1024)(128)(2,1)S(1)}, bf16[34848]{0:T(1024)(128)(2,1)S(1)}, u32[]{:S(2)}, u32[]{:S(2)}) collective-permute-start(bf16[34848]{0:T(1024)(128)(2,1)S(1)} %add_convert_fusion.1), channel_id=1, source_target_pairs={{0,128},{32,160},{64,192},{96,224},{128,0},{160,32},{192,64},{224,... | collective-permute-start | bytes 209096 | tf_op jit(solution)/shard_map/ppermute | solution.py:34
  152.5 4.1 %collective-permute-done.13 = bf16[34848]{0:T(1024)(128)(2,1)S(1)} collective-permute-done((bf16[34848]{0:T(1024)(128)(2,1)S(1)}, bf16[34848]{0:T(1024)(128)(2,1)S(1)}, u32[]{:S(2)}, u32[]{:S(2)}) %collective-permute-start.13) | collective-permute-done | bytes 69728 | tf_op jit(solution)/shard_map/ppermute | solution.py:34
  156.6 2.9 %collective-permute-start.14 = (bf16[34848]{0:T(1024)(128)(2,1)S(1)}, bf16[34848]{0:T(1024)(128)(2,1)S(1)}, u32[]{:S(2)}, u32[]{:S(2)}) collective-permute-start(bf16[34848]{0:T(1024)(128)(2,1)S(1)} %add_convert_fusion), channel_id=1, source_target_pairs={{0,256},{32,288},{64,320},{96,352},{128,384},{160,416},{192,448},{... | collective-permute-start | bytes 209096 | tf_op jit(solution)/shard_map/ppermute | solution.py:34
  159.5 1.0 fusion.29
  160.5 3.8 %collective-permute-done.14 = bf16[34848]{0:T(1024)(128)(2,1)S(1)} collective-permute-done((bf16[34848]{0:T(1024)(128)(2,1)S(1)}, bf16[34848]{0:T(1024)(128)(2,1)S(1)}, u32[]{:S(2)}, u32[]{:S(2)}) %collective-permute-start.14) | collective-permute-done | bytes 69728 | tf_op jit(solution)/shard_map/ppermute | solution.py:34
  164.7 0.7 copy.57
  165.5 0.7 copy.58
  166.9 0.7 slice.427
  (122 shorter events, 7.9 us)
Async XLA Ops:
  0.6 1.0 copy-start
  4.9 17.4 %collective-permute-start = (bf16[12800]{0:T(1024)(128)(2,1)S(1)}, bf16[12800]{0:T(1024)(128)(2,1)S(1)}, u32[]{:S(2)}, u32[]{:S(2)}) collective-permute-start(bf16[12800]{0:T(1024)(128)(2,1)S(1)} %pad_maximum_fusion.4), channel_id=1, source_target_pairs={{0,32},{32,64},{64,96},{96,128},{128,160},{160,192},{192,224},{224... | collective-permute-start | bytes 76808 | tf_op jit(solution)/shard_map/ppermute | solution.py:18
  11.3 11.2 %collective-permute-start.1 = (bf16[12800]{0:T(1024)(128)(2,1)S(1)}, bf16[12800]{0:T(1024)(128)(2,1)S(1)}, u32[]{:S(2)}, u32[]{:S(2)}) collective-permute-start(bf16[12800]{0:T(1024)(128)(2,1)S(1)} %pad_maximum_fusion.5), channel_id=1, source_target_pairs={{32,0},{64,32},{96,64},{128,96},{160,128},{192,160},{224,192},{256... | collective-permute-start | bytes 76808 | tf_op jit(solution)/shard_map/ppermute | solution.py:18
  22.3 33.4 %copy-start.4 = (bf16[24,256,128]{1,0,2:T(8,128)(2,1)}, bf16[24,256,128]{1,0,2:T(8,128)(2,1)S(1)}, u32[]{:S(2)}) copy-start(bf16[24,256,128]{1,0,2:T(8,128)(2,1)S(1)} %copy.42) | copy-start | bytes 4718596
  22.8 14.4 %collective-permute-start.4 = (bf16[144,32]{0,1:T(8,128)(2,1)S(1)}, bf16[144,32]{0,1:T(8,128)(2,1)S(1)}, u32[]{:S(2)}, u32[]{:S(2)}) collective-permute-start(bf16[144,32]{0,1:T(8,128)(2,1)S(1)} %fusion.44), channel_id=1, source_target_pairs={{0,0},{1,1},{2,32},{3,33},{4,64},{5,65},{6,96},{7,97},{8,128},{9,1... | collective-permute-start | bytes 27656 | tf_op jit(solution)/shard_map/ppermute | solution.py:78
  30.6 19.7 %copy-start.5 = (bf16[24,4,128]{1,0,2:T(8,128)(2,1)}, bf16[24,4,128]{1,0,2:T(8,128)(2,1)S(1)}, u32[]{:S(2)}) copy-start(bf16[24,4,128]{1,0,2:T(8,128)(2,1)S(1)} %copy.41) | copy-start | bytes 73732
  31.5 29.0 %collective-permute-start.3 = (bf16[24,264,4]{1,0,2:T(8,128)(2,1)}, bf16[24,264,4]{1,0,2:T(8,128)(2,1)}, u32[]{:S(2)}, u32[]{:S(2)}) collective-permute-start(bf16[24,264,4]{1,0,2:T(8,128)(2,1)} %get-tuple-element.32), channel_id=1, source_target_pairs={{1,0},{2,1},{3,2},{4,3},{5,4},{6,5},{7,6},{8,7},{9,8},{10,9},{11,1... | collective-permute-start | bytes 152072 | tf_op jit(solution)/shard_map/ppermute | solution.py:18
  32.8 27.7 %collective-permute-start.2 = (bf16[24,264,4]{1,0,2:T(8,128)(2,1)}, bf16[24,264,4]{1,0,2:T(8,128)(2,1)}, u32[]{:S(2)}, u32[]{:S(2)}) collective-permute-start(bf16[24,264,4]{1,0,2:T(8,128)(2,1)} %get-tuple-element.31), channel_id=1, source_target_pairs={{0,1},{1,2},{2,3},{3,4},{4,5},{5,6},{6,7},{7,8},{8,9},{9,10},{10,1... | collective-permute-start | bytes 152072 | tf_op jit(solution)/shard_map/ppermute | solution.py:18
  40.9 9.4 %copy-start.1 = (bf16[32,272,144]{1,0,2:T(8,128)(2,1)}, bf16[32,272,144]{1,0,2:T(8,128)(2,1)S(1)}, u32[]{:S(2)}) copy-start(bf16[32,272,144]{1,0,2:T(8,128)(2,1)S(1)} %select_convert_fusion) | copy-start | bytes 7520260
  50.3 2.8 %copy-start.3 = (f32[32,264,136]{1,0,2:T(8,128)}, f32[32,264,136]{1,0,2:T(8,128)S(1)}, u32[]{:S(2)}) copy-start(f32[32,264,136]{1,0,2:T(8,128)S(1)} %multiply_add_fusion) | copy-start | bytes 13787140
  53.1 2.6 %copy-start.18 = (bf16[32,32]{1,0:T(8,128)(2,1)S(1)}, bf16[32,32]{1,0:T(8,128)(2,1)}, u32[]{:S(2)}) copy-start(bf16[32,32]{1,0:T(8,128)(2,1)} %param.11) | copy-start | bytes 6148
  60.3 3.7 %slice-start = ((s8[6684672]{0:T(1024)(128)(4,1)}), s8[2490368]{0:T(1024)(128)(4,1)S(1)}, s32[]{:S(2)}) async-start(s8[6684672]{0:T(1024)(128)(4,1)} %bitcast.107), calls=%async_computation | async-start | bytes 4980736
  60.4 3.7 %slice-start.1 = ((s8[6684672]{0:T(1024)(128)(4,1)}), s8[4194304]{0:T(1024)(128)(4,1)S(1)}, s32[]{:S(2)}) async-start(s8[6684672]{0:T(1024)(128)(4,1)} %bitcast.107), calls=%async_computation.1 | async-start | bytes 8388608
  60.5 3.6 %copy-start.19 = (bf16[32,32]{1,0:T(8,128)(2,1)S(1)}, bf16[32,32]{1,0:T(8,128)(2,1)}, u32[]{:S(2)}) copy-start(bf16[32,32]{1,0:T(8,128)(2,1)} %param.11) | copy-start | bytes 6148
  64.1 3.4 %copy-start.9 = (f32[32]{0:T(128)S(1)}, f32[32]{0:T(128)}, u32[]{:S(2)}) copy-start(f32[32]{0:T(128)} %get-tuple-element.47) | copy-start | bytes 388
  64.1 3.4 %copy-start.10 = (f32[32]{0:T(128)S(1)}, f32[32]{0:T(128)}, u32[]{:S(2)}) copy-start(f32[32]{0:T(128)} %get-tuple-element.48) | copy-start | bytes 388
  64.1 3.4 %copy-start.11 = (f32[32]{0:T(128)S(1)}, f32[32]{0:T(128)}, u32[]{:S(2)}) copy-start(f32[32]{0:T(128)} %get-tuple-element.49) | copy-start | bytes 388
  64.1 3.4 %copy-start.12 = (f32[32]{0:T(128)S(1)}, f32[32]{0:T(128)}, u32[]{:S(2)}) copy-start(f32[32]{0:T(128)} %get-tuple-element.50) | copy-start | bytes 388
  64.1 3.4 %copy-start.13 = (f32[32]{0:T(128)S(1)}, f32[32]{0:T(128)}, u32[]{:S(2)}) copy-start(f32[32]{0:T(128)} %get-tuple-element.51) | copy-start | bytes 388
  64.1 3.4 %copy-start.14 = (f32[32]{0:T(128)S(1)}, f32[32]{0:T(128)}, u32[]{:S(2)}) copy-start(f32[32]{0:T(128)} %get-tuple-element.52) | copy-start | bytes 388
  64.1 3.4 %copy-start.15 = (f32[32]{0:T(128)S(1)}, f32[32]{0:T(128)}, u32[]{:S(2)}) copy-start(f32[32]{0:T(128)} %get-tuple-element.53) | copy-start | bytes 388
  64.2 3.4 %copy-start.16 = (f32[32]{0:T(128)S(1)}, f32[32]{0:T(128)}, u32[]{:S(2)}) copy-start(f32[32]{0:T(128)} %get-tuple-element.54) | copy-start | bytes 388
  64.2 3.4 %copy-start.17 = (f32[32]{0:T(128)S(1)}, f32[32]{0:T(128)}, u32[]{:S(2)}) copy-start(f32[32]{0:T(128)} %get-tuple-element.55) | copy-start | bytes 388
  67.6 7.0 %copy-start.2 = (bf16[32,272,144]{1,0,2:T(8,128)(2,1)S(1)}, bf16[32,272,144]{1,0,2:T(8,128)(2,1)}, u32[]{:S(2)}) copy-start(bf16[32,272,144]{1,0,2:T(8,128)(2,1)} %copy-done.1) | copy-start | bytes 7520260
  74.5 14.5 %copy-start.6 = (bf16[32,256,128]{1,0,2:T(8,128)(2,1)S(1)}, bf16[32,256,128]{1,0,2:T(8,128)(2,1)}, u32[]{:S(2)}) copy-start(bf16[32,256,128]{1,0,2:T(8,128)(2,1)} %multiply_convert_fusion.1) | copy-start | bytes 6291460
  82.0 70.2 %copy-start.7 = (bf16[512,32]{0,1:T(8,128)(2,1)S(1)}, bf16[512,32]{0,1:T(8,128)(2,1)}, u32[]{:S(2)}) copy-start(bf16[512,32]{0,1:T(8,128)(2,1)} %param.8) | copy-start | bytes 98308
  82.1 77.5 %copy-start.8 = (bf16[512,32]{0,1:T(8,128)(2,1)S(1)}, bf16[512,32]{0,1:T(8,128)(2,1)}, u32[]{:S(2)}) copy-start(bf16[512,32]{0,1:T(8,128)(2,1)} %param.9) | copy-start | bytes 98308
  82.1 13.0 %collective-permute-start.5 = (bf16[128,32]{1,0:T(8,128)(2,1)S(1)}, bf16[128,32]{1,0:T(8,128)(2,1)S(1)}, u32[]{:S(2)}, u32[]{:S(2)}) collective-permute-start(bf16[128,32]{1,0:T(8,128)(2,1)S(1)} %bitcast.114), channel_id=1, source_target_pairs={{0,0},{1,1},{2,32},{3,33},{4,64},{5,65},{6,96},{7,97},{8,128},{9,1... | collective-permute-start | bytes 24584 | tf_op jit(solution)/shard_map/ppermute | solution.py:128
  95.2 8.9 %collective-permute-start.6 = (bf16[14368]{0:T(1024)(128)(2,1)S(1)}, bf16[14368]{0:T(1024)(128)(2,1)S(1)}, u32[]{:S(2)}, u32[]{:S(2)}) collective-permute-start(bf16[14368]{0:T(1024)(128)(2,1)S(1)} %concatenate.52), channel_id=1, source_target_pairs={{0,2},{1,3},{2,0},{3,1},{4,6},{5,7},{6,4},{7,5},{8,10},{9,11},{10,... | collective-permute-start | bytes 86216 | tf_op jit(solution)/shard_map/ppermute | solution.py:34
  104.1 6.7 %collective-permute-start.7 = (bf16[14368]{0:T(1024)(128)(2,1)S(1)}, bf16[14368]{0:T(1024)(128)(2,1)S(1)}, u32[]{:S(2)}, u32[]{:S(2)}) collective-permute-start(bf16[14368]{0:T(1024)(128)(2,1)S(1)} %add_convert_fusion.6), channel_id=1, source_target_pairs={{0,4},{1,5},{2,6},{3,7},{4,0},{5,1},{6,2},{7,3},{8,12},{9,13},{10,... | collective-permute-start | bytes 86216 | tf_op jit(solution)/shard_map/ppermute | solution.py:34
  110.8 9.7 %collective-permute-start.8 = (bf16[14368]{0:T(1024)(128)(2,1)S(1)}, bf16[14368]{0:T(1024)(128)(2,1)S(1)}, u32[]{:S(2)}, u32[]{:S(2)}) collective-permute-start(bf16[14368]{0:T(1024)(128)(2,1)S(1)} %add_convert_fusion.5), channel_id=1, source_target_pairs={{0,8},{1,9},{2,10},{3,11},{4,12},{5,13},{6,14},{7,15},{8,0},{9,1},... | collective-permute-start | bytes 86216 | tf_op jit(solution)/shard_map/ppermute | solution.py:34
  120.5 5.8 %collective-permute-start.9 = (bf16[14368]{0:T(1024)(128)(2,1)S(1)}, bf16[14368]{0:T(1024)(128)(2,1)S(1)}, u32[]{:S(2)}, u32[]{:S(2)}) collective-permute-start(bf16[14368]{0:T(1024)(128)(2,1)S(1)} %add_convert_fusion.4), channel_id=1, source_target_pairs={{0,16},{1,17},{2,18},{3,19},{4,20},{5,21},{6,22},{7,23},{8,24},{9,... | collective-permute-start | bytes 86216 | tf_op jit(solution)/shard_map/ppermute | solution.py:34
  126.3 3.1 %collective-permute-start.10 = (bf16[14368]{0:T(1024)(128)(2,1)S(1)}, bf16[14368]{0:T(1024)(128)(2,1)S(1)}, u32[]{:S(2)}, u32[]{:S(2)}) collective-permute-start(bf16[14368]{0:T(1024)(128)(2,1)S(1)} %get-tuple-element.30), channel_id=1, source_target_pairs={{0,1},{1,0},{2,3},{3,2},{4,5},{5,4},{6,7},{7,6},{8,9},{9,8},{10,11... | collective-permute-start | bytes 86216 | tf_op jit(solution)/shard_map/ppermute | solution.py:34
  130.8 8.6 %collective-permute-start.11 = (bf16[34848]{0:T(1024)(128)(2,1)S(1)}, bf16[34848]{0:T(1024)(128)(2,1)S(1)}, u32[]{:S(2)}, u32[]{:S(2)}) collective-permute-start(bf16[34848]{0:T(1024)(128)(2,1)S(1)} %pad_maximum_fusion.3), channel_id=1, source_target_pairs={{0,32},{32,0},{64,96},{96,64},{128,160},{160,128},{192,224},{224,1... | collective-permute-start | bytes 209096 | tf_op jit(solution)/shard_map/ppermute | solution.py:34
  139.4 10.9 %collective-permute-start.12 = (bf16[34848]{0:T(1024)(128)(2,1)S(1)}, bf16[34848]{0:T(1024)(128)(2,1)S(1)}, u32[]{:S(2)}, u32[]{:S(2)}) collective-permute-start(bf16[34848]{0:T(1024)(128)(2,1)S(1)} %add_convert_fusion.2), channel_id=1, source_target_pairs={{0,64},{32,96},{64,0},{96,32},{128,192},{160,224},{192,128},{224,1... | collective-permute-start | bytes 209096 | tf_op jit(solution)/shard_map/ppermute | solution.py:34
  150.4 6.2 %collective-permute-start.13 = (bf16[34848]{0:T(1024)(128)(2,1)S(1)}, bf16[34848]{0:T(1024)(128)(2,1)S(1)}, u32[]{:S(2)}, u32[]{:S(2)}) collective-permute-start(bf16[34848]{0:T(1024)(128)(2,1)S(1)} %add_convert_fusion.1), channel_id=1, source_target_pairs={{0,128},{32,160},{64,192},{96,224},{128,0},{160,32},{192,64},{224,... | collective-permute-start | bytes 209096 | tf_op jit(solution)/shard_map/ppermute | solution.py:34
  156.6 7.7 %collective-permute-start.14 = (bf16[34848]{0:T(1024)(128)(2,1)S(1)}, bf16[34848]{0:T(1024)(128)(2,1)S(1)}, u32[]{:S(2)}, u32[]{:S(2)}) collective-permute-start(bf16[34848]{0:T(1024)(128)(2,1)S(1)} %add_convert_fusion), channel_id=1, source_target_pairs={{0,256},{32,288},{64,320},{96,352},{128,384},{160,416},{192,448},{... | collective-permute-start | bytes 209096 | tf_op jit(solution)/shard_map/ppermute | solution.py:34

commit v10 on v8

--- a/solution.py
+++ b/solution.py
@@ -58,14 +58,6 @@
     cot_rows = jnp.concatenate([before[0], cotangent, after[0]], axis=1)
     left_ext = jnp.concatenate([before[1], left_proj, after[1]], axis=0)
     right_panel = jnp.concatenate([before[2], right_proj, after[2]], axis=0)
-    cot_ext = jnp.concatenate(
-        [
-            shifted(cot_rows[:, :, cols - step :], "col", 1, col_count),
-            cot_rows,
-            shifted(cot_rows[:, :, :step], "col", -1, col_count),
-        ],
-        axis=2,
-    )
 
     def transpose_pairs():
         pairs = []
@@ -91,6 +83,13 @@
             conv_ext = conv_ext + depth_kernel[3 * a + b][:, None, None] * pair_ext[
                 :, step * a : step * a + ext_rows, step * b : step * b + ext_cols
             ].astype(jnp.float32)
+    left_strip, right_strip, conv_ext = lax.optimization_barrier(
+        (cot_rows[:, :, cols - step :], cot_rows[:, :, :step], conv_ext)
+    )
+    cot_ext = jnp.concatenate(
+        [shifted(left_strip, "col", 1, col_count), cot_rows, shifted(right_strip, "col", -1, col_count)],
+        axis=2,
+    )
     conv_tile = conv_ext[:, step : step + rows, step : step + cols]
     hidden_state = jax.nn.silu(conv_tile).astype(jnp.bfloat16)
     mixed_out = jnp.einsum("co,cij->oij", w_point, hidden_state, preferred_element_type=jnp.float32)

time: 169 us -> 171 us (1.012)
  starting transfers between devices: 67 us -> 71.5 us
  local copies, waits for them, and re-layouts: 17.5 us -> 14.7 us
    ppermute x1, waiting for transfers between devices: 0.01 us -> 3.11 us  [body(): right_ext = lax.ppermute(own_tile, ('row', 'col'), transpose_pairs())]
    unnamed x48, local copies, waits for them, and re-layouts: 8.19 us -> 5.4 us
    ppermute x9, starting transfers between devices: 35.5 us -> 38.2 us  [xor_round(): return lax.ppermute(flat, axis, [(i, i ^ bit) for i in range(count)])]
    ppermute x1, waiting for transfers between devices: 4.46 us -> 1.84 us  [body(): right_moved = lax.ppermute(right_part, ('row', 'col'), transpose_pairs())]
    ppermute x1, starting transfers between devices: 6.98 us -> 9.46 us  [body(): right_moved = lax.ppermute(right_part, ('row', 'col'), transpose_pairs())]
  transfers between devices with their start and end apart: 15 -> 15, of which waited for: 10 -> 11; matrix products, arithmetic and copies ran while one was open for 18% -> 10% of each run, Pallas kernels for 0% -> 0%
where the time goes in v10:
time: 171 us; the launch traced here: 170 us
  starting transfers between devices  71.5 us (42%)
  waiting for transfers between devices  35.6 us (21%)
  other arithmetic  31.2 us (18%)
  matrix products  15.7 us (9%)
  local copies, waits for them, and re-layouts  14.7 us (9%)
    ppermute x9, starting transfers between devices, xor_round(): return lax.ppermute(flat, axis, [(i, i ^ bit) for i in range(count)])  38.2 us
    ppermute x9, waiting for transfers between devices, xor_round(): return lax.ppermute(flat, axis, [(i, i ^ bit) for i in range(count)])  30.6 us
    ppermute x4, starting transfers between devices, shifted(): return lax.ppermute(x, axis, pairs)  17.3 us
    ppermute x1, starting transfers between devices, body(): right_moved = lax.ppermute(right_part, ('row', 'col'), transpose_pairs())  9.46 us
    add x1, other arithmetic, body(): conv_ext + depth_kernel[3 * a + b][:, None, None] * pair_ext[:, step * a:...  9.35 us
    reduce_sum x1, other arithmetic, body(): kern_terms.append(jnp.sum(conv_grad_tile * window, axis=(1, 2)))  7.28 us
    reduce_sum x1, other arithmetic, body(): right_part = jnp.sum(backward_pass, axis=1).T  6.96 us
    ppermute x1, starting transfers between devices, body(): right_ext = lax.ppermute(own_tile, ('row', 'col'), transpose_pairs())  6.5 us
  transfers between devices with their start and end apart: 15, of which 11 were waited for; matrix products, arithmetic and copies ran while one was open for 10% of the time, Pallas kernels for 0%

profile of v10, /device:TPU:6, one launch (start us, length us, event | category | flops | bytes accessed | tf_op | source)
XLA Modules:
  0.0 170.1 jit_solution(1402527072468783015)
XLA Ops:
  0.6 0.9 copy-done
  1.6 0.9 convolution_convert_fusion.3
  2.8 0.9 convolution_convert_fusion.2
  4.0 0.9 fusion.58
  4.9 6.1 %collective-permute-start = (bf16[12800]{0:T(1024)(128)(2,1)S(1)}, bf16[12800]{0:T(1024)(128)(2,1)S(1)}, u32[]{:S(2)}, u32[]{:S(2)}) collective-permute-start(bf16[12800]{0:T(1024)(128)(2,1)S(1)} %pad_maximum_fusion.4), channel_id=1, source_target_pairs={{0,32},{32,64},{64,96},{96,128},{128,160},{160,192},{192,224},{224... | collective-permute-start | bytes 76808 | tf_op jit(solution)/shard_map/ppermute | solution.py:18
  11.3 7.0 %collective-permute-start.1 = (bf16[12800]{0:T(1024)(128)(2,1)S(1)}, bf16[12800]{0:T(1024)(128)(2,1)S(1)}, u32[]{:S(2)}, u32[]{:S(2)}) collective-permute-start(bf16[12800]{0:T(1024)(128)(2,1)S(1)} %pad_maximum_fusion.5), channel_id=1, source_target_pairs={{32,0},{64,32},{96,64},{128,96},{160,128},{192,160},{224,192},{256... | collective-permute-start | bytes 76808 | tf_op jit(solution)/shard_map/ppermute | solution.py:18
  18.5 1.6 slice_bitcast_fusion.8
  20.1 2.2 %copy.42 = bf16[24,256,128]{1,0,2:T(8,128)(2,1)S(1)} copy(bf16[24,256,128]{2,1,0:T(8,128)(2,1)} %param.13) | data formatting | bytes 3145728 | tf_op args[6]
  22.8 6.5 %collective-permute-start.2 = (bf16[144,32]{0,1:T(8,128)(2,1)S(1)}, bf16[144,32]{0,1:T(8,128)(2,1)S(1)}, u32[]{:S(2)}, u32[]{:S(2)}) collective-permute-start(bf16[144,32]{0,1:T(8,128)(2,1)S(1)} %fusion.42), channel_id=1, source_target_pairs={{0,0},{1,1},{2,32},{3,33},{4,64},{5,65},{6,96},{7,97},{8,128},{9,1... | collective-permute-start | bytes 27656 | tf_op jit(solution)/shard_map/ppermute | solution.py:70
  30.6 0.9 pad_maximum_fusion
  31.5 0.7 convert_bitcast_fusion
  32.2 3.1 %collective-permute-done.2 = bf16[144,32]{0,1:T(8,128)(2,1)S(1)} collective-permute-done((bf16[144,32]{0,1:T(8,128)(2,1)S(1)}, bf16[144,32]{0,1:T(8,128)(2,1)S(1)}, u32[]{:S(2)}, u32[]{:S(2)}) %collective-permute-start.2) | collective-permute-done | bytes 9248 | tf_op jit(solution)/shard_map/ppermute | solution.py:70
  35.9 0.9 copy.48
  36.8 2.2 %select_convert_fusion = bf16[32,272,144]{1,0,2:T(8,128)(2,1)S(1)} fusion(f32[32,144]{0,1:T(8,128)S(1)} %copy.48, f32[32,272]{1,0:T(8,128)} %convert_bitcast_fusion, pred[272,144]{0,1:T(8,128)(4,1)S(1)} %and_and_fusion), kind=kLoop, calls=%fused_computation.10 | loop fusion | flops 3760128 | bytes 2599168 | tf_op jit(solution)/shard_map/convert_element_type | solution.py:76
  39.1 9.4 %multiply_add_fusion = f32[32,264,136]{1,0,2:T(8,128)S(1)} fusion(bf16[32,272,144]{1,0,2:T(8,128)(2,1)S(1)} %select_convert_fusion, f32[32]{0:T(128)} %get-tuple-element.60, f32[32]{0:T(128)} %get-tuple-element.61, f32[32]{0:T(128)} %get-tuple-element.54, f32[32]{0:T(128)} %get-tuple-element.55, f32[32]{0:T(128)} %get-tuple-element.56, ...), kind=kLoop, calls=%fused_computation.14 | loop fusion | flops 29872128 | bytes 25277568 | tf_op jit(solution)/shard_map/add | solution.py:83
  48.5 2.7 %collective-permute-start.3 = (bf16[24,264,4]{1,0,2:T(8,128)(2,1)}, bf16[24,264,4]{1,0,2:T(8,128)(2,1)}, u32[]{:S(2)}, u32[]{:S(2)}) collective-permute-start(bf16[24,264,4]{1,0,2:T(8,128)(2,1)} %get-tuple-element.9), channel_id=1, source_target_pairs={{0,1},{1,2},{2,3},{3,4},{4,5},{5,6},{6,7},{7,8},{8,9},{9,10},{10,1... | collective-permute-start | bytes 152072 | tf_op jit(solution)/shard_map/ppermute | solution.py:18
  51.1 1.5 collective-permute-start.4
  52.6 2.6 %multiply_convert_fusion.1 = bf16[32,256,128]{1,0,2:T(8,128)(2,1)} fusion(f32[32,264,136]{1,0,2:T(8,128)S(1)} %multiply_add_fusion), kind=kLoop, calls=%fused_computation.31 | loop fusion | flops 5242880 | bytes 6291456 | tf_op jit(solution)/shard_map/convert_element_type | solution.py:94
  55.2 4.6 %fusion.39 = bf16[32,24]{0,1:T(8,128)(2,1)S(1)} fusion(bf16[24,256,128]{1,0,2:T(8,128)(2,1)S(1)} %copy.42, bf16[32,256,128]{1,0,2:T(8,128)(2,1)} %multiply_convert_fusion.1, bf16[32,272,144]{1,0,2:T(8,128)(2,1)} %copy-done.1, bf16[32,32]{1,0:T(8,128)(2,1)S(1)} %copy-done.18), kind=kOutput, calls=%fused_computation.56 | convolution fusion | flops 120587008 | bytes 5770752 | tf_op jit(solution)/shard_map/ydq,gdq->yg/dot_general | solution.py:124
  60.1 3.5 %fusion.16 = bf16[32,264,136]{1,0,2:T(8,128)(2,1)S(1)} fusion(bf16[24,264,4]{1,0,2:T(8,128)(2,1)} %collective-permute-done.4, bf16[24,4,128]{1,0,2:T(8,128)(2,1)} %copy-done.5, bf16[24,256,128]{1,0,2:T(8,128)(2,1)} %copy-done.4, bf16[24,4,128]{1,0,2:T(8,128)(2,1)S(1)} %copy.41, bf16[24,264,4]{1,0,2:T(8,128)(2,1)} %collective-permute-done.3, ...), kind=kOutput, calls=%fused_computation.32 | convolution fusion | flops 66063360 | bytes 4022784 | tf_op jit(solution)/shard_map/ch,hij->cij/dot_general | solution.py:100
  63.7 3.3 %fusion = bf16[32,264,136]{1,0,2:T(8,128)(2,1)S(1)} fusion(f32[32,264,136]{1,0,2:T(8,128)S(1)} %bitcast.108, bf16[32,264,136]{1,0,2:T(8,128)(2,1)S(1)} %fusion.16, bf16[32,32]{1,0:T(8,128)(2,1)S(1)} %copy-done.19), kind=kOutput, calls=%fused_computation.12 | convolution fusion | flops 83871744 | bytes 9193472 | tf_op jit(solution)/shard_map/co,oij->cij/dot_general | solution.py:102
  67.1 7.3 %fusion.15 = (bf16[32]{0:T(256)(128)(2,1)S(1)}, bf16[32]{0:T(256)(128)(2,1)S(1)}, bf16[32]{0:T(256)(128)(2,1)S(1)}, bf16[32]{0:T(256)(128)(2,1)S(1)}, bf16[32]{0...) fusion(bf16[32,272,144]{1,0,2:T(8,128)(2,1)S(1)} %copy-done.2, ...), kind=kLoop, calls=%fused_computation.30 | loop fusion | flops 29359840 | bytes 20972096 | tf_op jit(solution)/shard_map/reduce_sum | solution.py:117
  74.5 7.0 %fusion.56 = (bf16[32,128]{0,1:T(8,128)(2,1)S(1)}, bf16[32,256]{1,0:T(8,128)(2,1)S(1)}) fusion(bf16[32,264,136]{1,0,2:T(8,128)(2,1)S(1)} %fusion, f32[32]{0:T(128)S(1)} %copy-done.16, f32[32]{0:T(128)S(1)} %copy-done.17, f32[32]{0:T(128)S(1)} %copy-done.10, f32[32]{0:T(128)S(1)} %copy-done.11, f32[32]{0:T(128)S(1)} %copy-done.12, f32[32]{0:T(128)S(1)} %copy-done.13, ...), kind=kLoop, calls=%fused_computation.123 | loop fusion | flops 31444992 | bytes 20997248 | tf_op jit(solution)/shard_map/reduce_sum | solution.py:120
  81.4 9.5 %collective-permute-start.5 = (bf16[128,32]{1,0:T(8,128)(2,1)S(1)}, bf16[128,32]{1,0:T(8,128)(2,1)S(1)}, u32[]{:S(2)}, u32[]{:S(2)}) collective-permute-start(bf16[128,32]{1,0:T(8,128)(2,1)S(1)} %bitcast.114), channel_id=1, source_target_pairs={{0,0},{1,1},{2,32},{3,33},{4,64},{5,65},{6,96},{7,97},{8,128},{9,1... | collective-permute-start | bytes 24584 | tf_op jit(solution)/shard_map/ppermute | solution.py:127
  90.9 1.0 fusion.35
  92.4 1.8 %collective-permute-done.5 = bf16[128,32]{1,0:T(8,128)(2,1)S(1)} collective-permute-done((bf16[128,32]{1,0:T(8,128)(2,1)S(1)}, bf16[128,32]{1,0:T(8,128)(2,1)S(1)}, u32[]{:S(2)}, u32[]{:S(2)}) %collective-permute-start.5) | collective-permute-done | bytes 8224 | tf_op jit(solution)/shard_map/ppermute | solution.py:127
  94.4 7.1 %collective-permute-start.6 = (bf16[14368]{0:T(1024)(128)(2,1)S(1)}, bf16[14368]{0:T(1024)(128)(2,1)S(1)}, u32[]{:S(2)}, u32[]{:S(2)}) collective-permute-start(bf16[14368]{0:T(1024)(128)(2,1)S(1)} %concatenate.52), channel_id=1, source_target_pairs={{0,2},{1,3},{2,0},{3,1},{4,6},{5,7},{6,4},{7,5},{8,10},{9,11},{10,... | collective-permute-start | bytes 86216 | tf_op jit(solution)/shard_map/ppermute | solution.py:34
  101.5 1.9 %collective-permute-done.6 = bf16[14368]{0:T(1024)(128)(2,1)S(1)} collective-permute-done((bf16[14368]{0:T(1024)(128)(2,1)S(1)}, bf16[14368]{0:T(1024)(128)(2,1)S(1)}, u32[]{:S(2)}, u32[]{:S(2)}) %collective-permute-start.6) | collective-permute-done | bytes 28768 | tf_op jit(solution)/shard_map/ppermute | solution.py:34
  103.4 5.5 %collective-permute-start.7 = (bf16[14368]{0:T(1024)(128)(2,1)S(1)}, bf16[14368]{0:T(1024)(128)(2,1)S(1)}, u32[]{:S(2)}, u32[]{:S(2)}) collective-permute-start(bf16[14368]{0:T(1024)(128)(2,1)S(1)} %add_convert_fusion.6), channel_id=1, source_target_pairs={{0,4},{1,5},{2,6},{3,7},{4,0},{5,1},{6,2},{7,3},{8,12},{9,13},{10,... | collective-permute-start | bytes 86216 | tf_op jit(solution)/shard_map/ppermute | solution.py:34
  109.0 1.9 %collective-permute-done.7 = bf16[14368]{0:T(1024)(128)(2,1)S(1)} collective-permute-done((bf16[14368]{0:T(1024)(128)(2,1)S(1)}, bf16[14368]{0:T(1024)(128)(2,1)S(1)}, u32[]{:S(2)}, u32[]{:S(2)}) %collective-permute-start.7) | collective-permute-done | bytes 28768 | tf_op jit(solution)/shard_map/ppermute | solution.py:34
  110.8 4.5 %collective-permute-start.8 = (bf16[14368]{0:T(1024)(128)(2,1)S(1)}, bf16[14368]{0:T(1024)(128)(2,1)S(1)}, u32[]{:S(2)}, u32[]{:S(2)}) collective-permute-start(bf16[14368]{0:T(1024)(128)(2,1)S(1)} %add_convert_fusion.5), channel_id=1, source_target_pairs={{0,8},{1,9},{2,10},{3,11},{4,12},{5,13},{6,14},{7,15},{8,0},{9,1},... | collective-permute-start | bytes 86216 | tf_op jit(solution)/shard_map/ppermute | solution.py:34
  115.3 5.2 %collective-permute-done.8 = bf16[14368]{0:T(1024)(128)(2,1)S(1)} collective-permute-done((bf16[14368]{0:T(1024)(128)(2,1)S(1)}, bf16[14368]{0:T(1024)(128)(2,1)S(1)}, u32[]{:S(2)}, u32[]{:S(2)}) %collective-permute-start.8) | collective-permute-done | bytes 28768 | tf_op jit(solution)/shard_map/ppermute | solution.py:34
  120.5 3.3 %collective-permute-start.9 = (bf16[14368]{0:T(1024)(128)(2,1)S(1)}, bf16[14368]{0:T(1024)(128)(2,1)S(1)}, u32[]{:S(2)}, u32[]{:S(2)}) collective-permute-start(bf16[14368]{0:T(1024)(128)(2,1)S(1)} %add_convert_fusion.4), channel_id=1, source_target_pairs={{0,16},{1,17},{2,18},{3,19},{4,20},{5,21},{6,22},{7,23},{8,24},{9,... | collective-permute-start | bytes 86216 | tf_op jit(solution)/shard_map/ppermute | solution.py:34
  123.9 2.5 %collective-permute-done.9 = bf16[14368]{0:T(1024)(128)(2,1)S(1)} collective-permute-done((bf16[14368]{0:T(1024)(128)(2,1)S(1)}, bf16[14368]{0:T(1024)(128)(2,1)S(1)}, u32[]{:S(2)}, u32[]{:S(2)}) %collective-permute-start.9) | collective-permute-done | bytes 28768 | tf_op jit(solution)/shard_map/ppermute | solution.py:34
  126.3 1.9 %collective-permute-start.10 = (bf16[14368]{0:T(1024)(128)(2,1)S(1)}, bf16[14368]{0:T(1024)(128)(2,1)S(1)}, u32[]{:S(2)}, u32[]{:S(2)}) collective-permute-start(bf16[14368]{0:T(1024)(128)(2,1)S(1)} %get-tuple-element.36), channel_id=1, source_target_pairs={{0,1},{1,0},{2,3},{3,2},{4,5},{5,4},{6,7},{7,6},{8,9},{9,8},{10,11... | collective-permute-start | bytes 86216 | tf_op jit(solution)/shard_map/ppermute | solution.py:34
  128.3 1.2 collective-permute-done.10
  130.8 6.2 %collective-permute-start.11 = (bf16[34848]{0:T(1024)(128)(2,1)S(1)}, bf16[34848]{0:T(1024)(128)(2,1)S(1)}, u32[]{:S(2)}, u32[]{:S(2)}) collective-permute-start(bf16[34848]{0:T(1024)(128)(2,1)S(1)} %pad_maximum_fusion.3), channel_id=1, source_target_pairs={{0,32},{32,0},{64,96},{96,64},{128,160},{160,128},{192,224},{224,1... | collective-permute-start | bytes 209096 | tf_op jit(solution)/shard_map/ppermute | solution.py:34
  137.0 3.5 %collective-permute-done.11 = bf16[34848]{0:T(1024)(128)(2,1)S(1)} collective-permute-done((bf16[34848]{0:T(1024)(128)(2,1)S(1)}, bf16[34848]{0:T(1024)(128)(2,1)S(1)}, u32[]{:S(2)}, u32[]{:S(2)}) %collective-permute-start.11) | collective-permute-done | bytes 69728 | tf_op jit(solution)/shard_map/ppermute | solution.py:34
  140.6 5.8 %collective-permute-start.12 = (bf16[34848]{0:T(1024)(128)(2,1)S(1)}, bf16[34848]{0:T(1024)(128)(2,1)S(1)}, u32[]{:S(2)}, u32[]{:S(2)}) collective-permute-start(bf16[34848]{0:T(1024)(128)(2,1)S(1)} %add_convert_fusion.2), channel_id=1, source_target_pairs={{0,64},{32,96},{64,0},{96,32},{128,192},{160,224},{192,128},{224,1... | collective-permute-start | bytes 209096 | tf_op jit(solution)/shard_map/ppermute | solution.py:34
  146.4 5.7 %collective-permute-done.12 = bf16[34848]{0:T(1024)(128)(2,1)S(1)} collective-permute-done((bf16[34848]{0:T(1024)(128)(2,1)S(1)}, bf16[34848]{0:T(1024)(128)(2,1)S(1)}, u32[]{:S(2)}, u32[]{:S(2)}) %collective-permute-start.12) | collective-permute-done | bytes 69728 | tf_op jit(solution)/shard_map/ppermute | solution.py:34
  152.1 1.9 %collective-permute-start.13 = (bf16[34848]{0:T(1024)(128)(2,1)S(1)}, bf16[34848]{0:T(1024)(128)(2,1)S(1)}, u32[]{:S(2)}, u32[]{:S(2)}) collective-permute-start(bf16[34848]{0:T(1024)(128)(2,1)S(1)} %add_convert_fusion.1), channel_id=1, source_target_pairs={{0,128},{32,160},{64,192},{96,224},{128,0},{160,32},{192,64},{224,... | collective-permute-start | bytes 209096 | tf_op jit(solution)/shard_map/ppermute | solution.py:34
  154.2 4.1 %collective-permute-done.13 = bf16[34848]{0:T(1024)(128)(2,1)S(1)} collective-permute-done((bf16[34848]{0:T(1024)(128)(2,1)S(1)}, bf16[34848]{0:T(1024)(128)(2,1)S(1)}, u32[]{:S(2)}, u32[]{:S(2)}) %collective-permute-start.13) | collective-permute-done | bytes 69728 | tf_op jit(solution)/shard_map/ppermute | solution.py:34
  158.3 1.9 %collective-permute-start.14 = (bf16[34848]{0:T(1024)(128)(2,1)S(1)}, bf16[34848]{0:T(1024)(128)(2,1)S(1)}, u32[]{:S(2)}, u32[]{:S(2)}) collective-permute-start(bf16[34848]{0:T(1024)(128)(2,1)S(1)} %add_convert_fusion), channel_id=1, source_target_pairs={{0,256},{32,288},{64,320},{96,352},{128,384},{160,416},{192,448},{... | collective-permute-start | bytes 209096 | tf_op jit(solution)/shard_map/ppermute | solution.py:34
  160.2 1.0 fusion.29
  161.2 4.8 %collective-permute-done.14 = bf16[34848]{0:T(1024)(128)(2,1)S(1)} collective-permute-done((bf16[34848]{0:T(1024)(128)(2,1)S(1)}, bf16[34848]{0:T(1024)(128)(2,1)S(1)}, u32[]{:S(2)}, u32[]{:S(2)}) %collective-permute-start.14) | collective-permute-done | bytes 69728 | tf_op jit(solution)/shard_map/ppermute | solution.py:34
  166.4 0.7 copy.57
  167.2 0.7 copy.58
  168.7 0.7 mul.329
  (122 shorter events, 7.9 us)
Async XLA Ops:
  0.6 1.0 copy-start
  4.9 17.4 %collective-permute-start = (bf16[12800]{0:T(1024)(128)(2,1)S(1)}, bf16[12800]{0:T(1024)(128)(2,1)S(1)}, u32[]{:S(2)}, u32[]{:S(2)}) collective-permute-start(bf16[12800]{0:T(1024)(128)(2,1)S(1)} %pad_maximum_fusion.4), channel_id=1, source_target_pairs={{0,32},{32,64},{64,96},{96,128},{128,160},{160,192},{192,224},{224... | collective-permute-start | bytes 76808 | tf_op jit(solution)/shard_map/ppermute | solution.py:18
  11.3 11.2 %collective-permute-start.1 = (bf16[12800]{0:T(1024)(128)(2,1)S(1)}, bf16[12800]{0:T(1024)(128)(2,1)S(1)}, u32[]{:S(2)}, u32[]{:S(2)}) collective-permute-start(bf16[12800]{0:T(1024)(128)(2,1)S(1)} %pad_maximum_fusion.5), channel_id=1, source_target_pairs={{32,0},{64,32},{96,64},{128,96},{160,128},{192,160},{224,192},{256... | collective-permute-start | bytes 76808 | tf_op jit(solution)/shard_map/ppermute | solution.py:18
  22.3 32.9 %copy-start.4 = (bf16[24,256,128]{1,0,2:T(8,128)(2,1)}, bf16[24,256,128]{1,0,2:T(8,128)(2,1)S(1)}, u32[]{:S(2)}) copy-start(bf16[24,256,128]{1,0,2:T(8,128)(2,1)S(1)} %copy.42) | copy-start | bytes 4718596
  22.8 12.5 %collective-permute-start.2 = (bf16[144,32]{0,1:T(8,128)(2,1)S(1)}, bf16[144,32]{0,1:T(8,128)(2,1)S(1)}, u32[]{:S(2)}, u32[]{:S(2)}) collective-permute-start(bf16[144,32]{0,1:T(8,128)(2,1)S(1)} %fusion.42), channel_id=1, source_target_pairs={{0,0},{1,1},{2,32},{3,33},{4,64},{5,65},{6,96},{7,97},{8,128},{9,1... | collective-permute-start | bytes 27656 | tf_op jit(solution)/shard_map/ppermute | solution.py:70
  30.6 17.8 %copy-start.5 = (bf16[24,4,128]{1,0,2:T(8,128)(2,1)}, bf16[24,4,128]{1,0,2:T(8,128)(2,1)S(1)}, u32[]{:S(2)}) copy-start(bf16[24,4,128]{1,0,2:T(8,128)(2,1)S(1)} %copy.43) | copy-start | bytes 73732
  39.1 9.4 %copy-start.1 = (bf16[32,272,144]{1,0,2:T(8,128)(2,1)}, bf16[32,272,144]{1,0,2:T(8,128)(2,1)S(1)}, u32[]{:S(2)}) copy-start(bf16[32,272,144]{1,0,2:T(8,128)(2,1)S(1)} %select_convert_fusion) | copy-start | bytes 7520260
  48.4 4.2 %copy-start.3 = (f32[32,264,136]{1,0,2:T(8,128)}, f32[32,264,136]{1,0,2:T(8,128)S(1)}, u32[]{:S(2)}) copy-start(f32[32,264,136]{1,0,2:T(8,128)S(1)} %multiply_add_fusion) | copy-start | bytes 13787140
  48.5 6.7 %copy-start.18 = (bf16[32,32]{1,0:T(8,128)(2,1)S(1)}, bf16[32,32]{1,0:T(8,128)(2,1)}, u32[]{:S(2)}) copy-start(bf16[32,32]{1,0:T(8,128)(2,1)} %param.11) | copy-start | bytes 6148
  48.5 11.6 %collective-permute-start.3 = (bf16[24,264,4]{1,0,2:T(8,128)(2,1)}, bf16[24,264,4]{1,0,2:T(8,128)(2,1)}, u32[]{:S(2)}, u32[]{:S(2)}) collective-permute-start(bf16[24,264,4]{1,0,2:T(8,128)(2,1)} %get-tuple-element.9), channel_id=1, source_target_pairs={{0,1},{1,2},{2,3},{3,4},{4,5},{5,6},{6,7},{7,8},{8,9},{9,10},{10,1... | collective-permute-start | bytes 152072 | tf_op jit(solution)/shard_map/ppermute | solution.py:18
  51.1 8.9 %collective-permute-start.4 = (bf16[24,264,4]{1,0,2:T(8,128)(2,1)}, bf16[24,264,4]{1,0,2:T(8,128)(2,1)}, u32[]{:S(2)}, u32[]{:S(2)}) collective-permute-start(bf16[24,264,4]{1,0,2:T(8,128)(2,1)} %get-tuple-element.10), channel_id=1, source_target_pairs={{1,0},{2,1},{3,2},{4,3},{5,4},{6,5},{7,6},{8,7},{9,8},{10,9},{11,1... | collective-permute-start | bytes 152072 | tf_op jit(solution)/shard_map/ppermute | solution.py:18
  59.9 3.7 %slice-start = ((s8[6684672]{0:T(1024)(128)(4,1)}), s8[2490368]{0:T(1024)(128)(4,1)S(1)}, s32[]{:S(2)}) async-start(s8[6684672]{0:T(1024)(128)(4,1)} %bitcast.107), calls=%async_computation | async-start | bytes 4980736
  60.0 3.7 %slice-start.1 = ((s8[6684672]{0:T(1024)(128)(4,1)}), s8[4194304]{0:T(1024)(128)(4,1)S(1)}, s32[]{:S(2)}) async-start(s8[6684672]{0:T(1024)(128)(4,1)} %bitcast.107), calls=%async_computation.1 | async-start | bytes 8388608
  60.0 3.6 %copy-start.19 = (bf16[32,32]{1,0:T(8,128)(2,1)S(1)}, bf16[32,32]{1,0:T(8,128)(2,1)}, u32[]{:S(2)}) copy-start(bf16[32,32]{1,0:T(8,128)(2,1)} %param.11) | copy-start | bytes 6148
  63.7 3.3 %copy-start.2 = (bf16[32,272,144]{1,0,2:T(8,128)(2,1)S(1)}, bf16[32,272,144]{1,0,2:T(8,128)(2,1)}, u32[]{:S(2)}) copy-start(bf16[32,272,144]{1,0,2:T(8,128)(2,1)} %copy-done.1) | copy-start | bytes 7520260
  67.0 7.4 %copy-start.9 = (f32[32]{0:T(128)S(1)}, f32[32]{0:T(128)}, u32[]{:S(2)}) copy-start(f32[32]{0:T(128)} %get-tuple-element.53) | copy-start | bytes 388
  67.0 7.4 %copy-start.10 = (f32[32]{0:T(128)S(1)}, f32[32]{0:T(128)}, u32[]{:S(2)}) copy-start(f32[32]{0:T(128)} %get-tuple-element.54) | copy-start | bytes 388
  67.0 7.4 %copy-start.11 = (f32[32]{0:T(128)S(1)}, f32[32]{0:T(128)}, u32[]{:S(2)}) copy-start(f32[32]{0:T(128)} %get-tuple-element.55) | copy-start | bytes 388
  67.0 7.4 %copy-start.12 = (f32[32]{0:T(128)S(1)}, f32[32]{0:T(128)}, u32[]{:S(2)}) copy-start(f32[32]{0:T(128)} %get-tuple-element.56) | copy-start | bytes 388
  67.0 7.4 %copy-start.13 = (f32[32]{0:T(128)S(1)}, f32[32]{0:T(128)}, u32[]{:S(2)}) copy-start(f32[32]{0:T(128)} %get-tuple-element.57) | copy-start | bytes 388
  67.0 7.4 %copy-start.14 = (f32[32]{0:T(128)S(1)}, f32[32]{0:T(128)}, u32[]{:S(2)}) copy-start(f32[32]{0:T(128)} %get-tuple-element.58) | copy-start | bytes 388
  67.0 7.4 %copy-start.15 = (f32[32]{0:T(128)S(1)}, f32[32]{0:T(128)}, u32[]{:S(2)}) copy-start(f32[32]{0:T(128)} %get-tuple-element.59) | copy-start | bytes 388
  67.1 7.4 %copy-start.16 = (f32[32]{0:T(128)S(1)}, f32[32]{0:T(128)}, u32[]{:S(2)}) copy-start(f32[32]{0:T(128)} %get-tuple-element.60) | copy-start | bytes 388
  67.1 7.4 %copy-start.17 = (f32[32]{0:T(128)S(1)}, f32[32]{0:T(128)}, u32[]{:S(2)}) copy-start(f32[32]{0:T(128)} %get-tuple-element.61) | copy-start | bytes 388
  74.4 16.5 %copy-start.6 = (bf16[32,256,128]{1,0,2:T(8,128)(2,1)S(1)}, bf16[32,256,128]{1,0,2:T(8,128)(2,1)}, u32[]{:S(2)}) copy-start(bf16[32,256,128]{1,0,2:T(8,128)(2,1)} %multiply_convert_fusion.1) | copy-start | bytes 6291460
  81.4 72.6 %copy-start.7 = (bf16[512,32]{0,1:T(8,128)(2,1)S(1)}, bf16[512,32]{0,1:T(8,128)(2,1)}, u32[]{:S(2)}) copy-start(bf16[512,32]{0,1:T(8,128)(2,1)} %param.8) | copy-start | bytes 98308
  81.4 78.8 %copy-start.8 = (bf16[512,32]{0,1:T(8,128)(2,1)S(1)}, bf16[512,32]{0,1:T(8,128)(2,1)}, u32[]{:S(2)}) copy-start(bf16[512,32]{0,1:T(8,128)(2,1)} %param.9) | copy-start | bytes 98308
  81.4 12.8 %collective-permute-start.5 = (bf16[128,32]{1,0:T(8,128)(2,1)S(1)}, bf16[128,32]{1,0:T(8,128)(2,1)S(1)}, u32[]{:S(2)}, u32[]{:S(2)}) collective-permute-start(bf16[128,32]{1,0:T(8,128)(2,1)S(1)} %bitcast.114), channel_id=1, source_target_pairs={{0,0},{1,1},{2,32},{3,33},{4,64},{5,65},{6,96},{7,97},{8,128},{9,1... | collective-permute-start | bytes 24584 | tf_op jit(solution)/shard_map/ppermute | solution.py:127
  94.4 9.0 %collective-permute-start.6 = (bf16[14368]{0:T(1024)(128)(2,1)S(1)}, bf16[14368]{0:T(1024)(128)(2,1)S(1)}, u32[]{:S(2)}, u32[]{:S(2)}) collective-permute-start(bf16[14368]{0:T(1024)(128)(2,1)S(1)} %concatenate.52), channel_id=1, source_target_pairs={{0,2},{1,3},{2,0},{3,1},{4,6},{5,7},{6,4},{7,5},{8,10},{9,11},{10,... | collective-permute-start | bytes 86216 | tf_op jit(solution)/shard_map/ppermute | solution.py:34
  103.4 7.4 %collective-permute-start.7 = (bf16[14368]{0:T(1024)(128)(2,1)S(1)}, bf16[14368]{0:T(1024)(128)(2,1)S(1)}, u32[]{:S(2)}, u32[]{:S(2)}) collective-permute-start(bf16[14368]{0:T(1024)(128)(2,1)S(1)} %add_convert_fusion.6), channel_id=1, source_target_pairs={{0,4},{1,5},{2,6},{3,7},{4,0},{5,1},{6,2},{7,3},{8,12},{9,13},{10,... | collective-permute-start | bytes 86216 | tf_op jit(solution)/shard_map/ppermute | solution.py:34
  110.8 9.7 %collective-permute-start.8 = (bf16[14368]{0:T(1024)(128)(2,1)S(1)}, bf16[14368]{0:T(1024)(128)(2,1)S(1)}, u32[]{:S(2)}, u32[]{:S(2)}) collective-permute-start(bf16[14368]{0:T(1024)(128)(2,1)S(1)} %add_convert_fusion.5), channel_id=1, source_target_pairs={{0,8},{1,9},{2,10},{3,11},{4,12},{5,13},{6,14},{7,15},{8,0},{9,1},... | collective-permute-start | bytes 86216 | tf_op jit(solution)/shard_map/ppermute | solution.py:34
  120.5 5.8 %collective-permute-start.9 = (bf16[14368]{0:T(1024)(128)(2,1)S(1)}, bf16[14368]{0:T(1024)(128)(2,1)S(1)}, u32[]{:S(2)}, u32[]{:S(2)}) collective-permute-start(bf16[14368]{0:T(1024)(128)(2,1)S(1)} %add_convert_fusion.4), channel_id=1, source_target_pairs={{0,16},{1,17},{2,18},{3,19},{4,20},{5,21},{6,22},{7,23},{8,24},{9,... | collective-permute-start | bytes 86216 | tf_op jit(solution)/shard_map/ppermute | solution.py:34
  126.3 3.1 %collective-permute-start.10 = (bf16[14368]{0:T(1024)(128)(2,1)S(1)}, bf16[14368]{0:T(1024)(128)(2,1)S(1)}, u32[]{:S(2)}, u32[]{:S(2)}) collective-permute-start(bf16[14368]{0:T(1024)(128)(2,1)S(1)} %get-tuple-element.36), channel_id=1, source_target_pairs={{0,1},{1,0},{2,3},{3,2},{4,5},{5,4},{6,7},{7,6},{8,9},{9,8},{10,11... | collective-permute-start | bytes 86216 | tf_op jit(solution)/shard_map/ppermute | solution.py:34
  130.8 9.7 %collective-permute-start.11 = (bf16[34848]{0:T(1024)(128)(2,1)S(1)}, bf16[34848]{0:T(1024)(128)(2,1)S(1)}, u32[]{:S(2)}, u32[]{:S(2)}) collective-permute-start(bf16[34848]{0:T(1024)(128)(2,1)S(1)} %pad_maximum_fusion.3), channel_id=1, source_target_pairs={{0,32},{32,0},{64,96},{96,64},{128,160},{160,128},{192,224},{224,1... | collective-permute-start | bytes 209096 | tf_op jit(solution)/shard_map/ppermute | solution.py:34
  140.6 11.5 %collective-permute-start.12 = (bf16[34848]{0:T(1024)(128)(2,1)S(1)}, bf16[34848]{0:T(1024)(128)(2,1)S(1)}, u32[]{:S(2)}, u32[]{:S(2)}) collective-permute-start(bf16[34848]{0:T(1024)(128)(2,1)S(1)} %add_convert_fusion.2), channel_id=1, source_target_pairs={{0,64},{32,96},{64,0},{96,32},{128,192},{160,224},{192,128},{224,1... | collective-permute-start | bytes 209096 | tf_op jit(solution)/shard_map/ppermute | solution.py:34
  152.1 6.2 %collective-permute-start.13 = (bf16[34848]{0:T(1024)(128)(2,1)S(1)}, bf16[34848]{0:T(1024)(128)(2,1)S(1)}, u32[]{:S(2)}, u32[]{:S(2)}) collective-permute-start(bf16[34848]{0:T(1024)(128)(2,1)S(1)} %add_convert_fusion.1), channel_id=1, source_target_pairs={{0,128},{32,160},{64,192},{96,224},{128,0},{160,32},{192,64},{224,... | collective-permute-start | bytes 209096 | tf_op jit(solution)/shard_map/ppermute | solution.py:34
  158.3 7.7 %collective-permute-start.14 = (bf16[34848]{0:T(1024)(128)(2,1)S(1)}, bf16[34848]{0:T(1024)(128)(2,1)S(1)}, u32[]{:S(2)}, u32[]{:S(2)}) collective-permute-start(bf16[34848]{0:T(1024)(128)(2,1)S(1)} %add_convert_fusion), channel_id=1, source_target_pairs={{0,256},{32,288},{64,320},{96,352},{128,384},{160,416},{192,448},{... | collective-permute-start | bytes 209096 | tf_op jit(solution)/shard_map/ppermute | solution.py:34

commit v11 on v10

--- a/solution.py
+++ b/solution.py
@@ -51,23 +51,31 @@
     left_proj = jnp.dot(bin_features, w_left, preferred_element_type=jnp.float32).astype(jnp.bfloat16)
     right_proj = jnp.dot(bin_features, w_right, preferred_element_type=jnp.float32).astype(jnp.bfloat16)
 
-    tail = (cotangent[:, rows - step :, :], left_proj[rows - halo :], right_proj[rows - halo :])
-    head = (cotangent[:, :step, :], left_proj[:halo], right_proj[:halo])
+    tail = (cotangent[:, rows - step :, :], left_proj[rows - halo :])
+    head = (cotangent[:, :step, :], left_proj[:halo])
     before = unpacked(shifted(packed(tail), "row", 1, row_count), tail)
     after = unpacked(shifted(packed(head), "row", -1, row_count), head)
     cot_rows = jnp.concatenate([before[0], cotangent, after[0]], axis=1)
     left_ext = jnp.concatenate([before[1], left_proj, after[1]], axis=0)
-    right_panel = jnp.concatenate([before[2], right_proj, after[2]], axis=0)
 
-    def transpose_pairs():
+    def transpose_pairs(shift=0):
         pairs = []
         for a in range(row_count):
             for b in range(col_count):
-                pairs.append((a * col_count + b, (b // ratio) * col_count + ratio * a + b % ratio))
+                tile = ratio * a + b % ratio + shift
+                if 0 <= tile < col_count:
+                    pairs.append((a * col_count + b, (b // ratio) * col_count + tile))
         return pairs
 
-    own_tile = lax.dynamic_slice_in_dim(right_panel, part * cols, cols + 2 * halo, 0)
-    right_ext = lax.ppermute(own_tile, ("row", "col"), transpose_pairs())
+    own_tile = lax.dynamic_slice_in_dim(right_proj, part * cols, cols, 0)
+    right_ext = jnp.concatenate(
+        [
+            lax.ppermute(own_tile[cols - halo :], ("row", "col"), transpose_pairs(1)),
+            lax.ppermute(own_tile, ("row", "col"), transpose_pairs()),
+            lax.ppermute(own_tile[:halo], ("row", "col"), transpose_pairs(-1)),
+        ],
+        axis=0,
+    )
 
     row_place = r * rows - halo + lax.broadcasted_iota(jnp.int32, (rows + 2 * halo, 1), 0)
     col_place = k * cols - halo + lax.broadcasted_iota(jnp.int32, (1, cols + 2 * halo), 1)

time: 171 us -> 180 us (1.053)
  starting transfers between devices: 71.5 us -> 78.8 us
    ppermute x1 -> x3, starting transfers between devices: 6.5 us -> 22.7 us  [the longest x1 10.8 us: body(): lax.ppermute(own_tile[:halo], ('row', 'col'), transpose_pairs(-1))]
    ppermute x4, starting transfers between devices: 17.3 us -> 13 us  [shifted(): return lax.ppermute(x, axis, pairs)]
    ppermute x1 -> x3, waiting for transfers between devices: 3.11 us -> 0.01 us  [the longest x1 0.01 us: body(): lax.ppermute(own_tile[cols - halo:], ('row', 'col'), transpose_pairs(1))]
    ppermute x1, waiting for transfers between devices: 1.84 us -> 4.77 us  [body(): right_moved = lax.ppermute(right_part, ('row', 'col'), transpose_pairs())]
    reshape x8 -> x6, local copies, waits for them, and re-layouts: 0.71 us -> 3.3 us  [unpacked(): out.append(flat[at:at + like.size].reshape(like.shape))]
    ppermute x1, starting transfers between devices: 9.46 us -> 6.91 us  [body(): right_moved = lax.ppermute(right_part, ('row', 'col'), transpose_pairs())]
    ppermute x9, starting transfers between devices: 38.2 us -> 36.2 us  [xor_round(): return lax.ppermute(flat, axis, [(i, i ^ bit) for i in range(count)])]
  transfers between devices with their start and end apart: 15 -> 17, of which waited for: 11 -> 10; matrix products, arithmetic and copies ran while one was open for 10% -> 10% of each run, Pallas kernels for 0% -> 0%
where the time goes in v11:
time: 180 us; the launch traced here: 179 us
  starting transfers between devices  78.8 us (44%)
  waiting for transfers between devices  37.1 us (21%)
  other arithmetic  29.9 us (17%)
  local copies, waits for them, and re-layouts  15.9 us (9%)
  matrix products  15.7 us (9%)
    ppermute x9, starting transfers between devices, xor_round(): return lax.ppermute(flat, axis, [(i, i ^ bit) for i in range(count)])  36.2 us
    ppermute x9, waiting for transfers between devices, xor_round(): return lax.ppermute(flat, axis, [(i, i ^ bit) for i in range(count)])  32.3 us
    ppermute x4, starting transfers between devices, shifted(): return lax.ppermute(x, axis, pairs)  13 us
    ppermute x1, starting transfers between devices, body(): lax.ppermute(own_tile[:halo], ('row', 'col'), transpose_pairs(-1))  10.8 us
    ppermute x1, starting transfers between devices, body(): lax.ppermute(own_tile, ('row', 'col'), transpose_pairs())  9.46 us
    add x1, other arithmetic, body(): conv_ext + depth_kernel[3 * a + b][:, None, None] * pair_ext[:, step * a:...  9.31 us
    reduce_sum x1, other arithmetic, body(): kern_terms.append(jnp.sum(conv_grad_tile * window, axis=(1, 2)))  7.28 us
    reduce_sum x1, other arithmetic, body(): right_part = jnp.sum(backward_pass, axis=1).T  6.96 us
  transfers between devices with their start and end apart: 17, of which 10 were waited for; matrix products, arithmetic and copies ran while one was open for 10% of the time, Pallas kernels for 0%

profile of v11, /device:TPU:6, one launch (start us, length us, event | category | flops | bytes accessed | tf_op | source)
XLA Modules:
  0.0 178.7 jit_solution(3139296342222284179)
XLA Ops:
  0.7 0.9 copy-done
  1.6 0.9 fusion.59
  2.5 9.5 %collective-permute-start.3 = (bf16[128,32]{0,1:T(8,128)(2,1)S(1)}, bf16[128,32]{0,1:T(8,128)(2,1)S(1)}, u32[]{:S(2)}, u32[]{:S(2)}) collective-permute-start(bf16[128,32]{0,1:T(8,128)(2,1)S(1)} %dynamic-slice_convert_fusion), channel_id=1, source_target_pairs={{0,0},{1,1},{2,32},{3,33},{4,64},{5,65},{6,96},{7,97},{8,128},{9,1... | collective-permute-start | bytes 24584 | tf_op jit(solution)/shard_map/ppermute | solution.py:74
  12.1 2.4 %collective-permute-start.2 = (bf16[8,32]{0,1:T(8,128)(2,1)S(1)}, bf16[8,32]{0,1:T(8,128)(2,1)S(1)}, u32[]{:S(2)}, u32[]{:S(2)}) collective-permute-start(bf16[8,32]{0,1:T(8,128)(2,1)S(1)} %get-tuple-element.56), channel_id=1, source_target_pairs={{0,1},{1,2},{2,33},{3,34},{4,65},{5,66},{6,97},{7,98},{8,129},{9,1... | collective-permute-start | bytes 1544 | tf_op jit(solution)/shard_map/ppermute | solution.py:73
  14.5 10.8 %collective-permute-start.4 = (bf16[8,32]{0,1:T(8,128)(2,1)S(1)}, bf16[8,32]{0,1:T(8,128)(2,1)S(1)}, u32[]{:S(2)}, u32[]{:S(2)}) collective-permute-start(bf16[8,32]{0,1:T(8,128)(2,1)S(1)} %get-tuple-element.57), channel_id=1, source_target_pairs={{1,0},{3,32},{5,64},{7,96},{9,128},{11,160},{13,192},{15,224},{17,... | collective-permute-start | bytes 1544 | tf_op jit(solution)/shard_map/ppermute | solution.py:75
  25.4 0.9 convolution_convert_fusion.2
  26.5 0.9 fusion.56
  27.4 5.3 %collective-permute-start = (bf16[12544]{0:T(1024)(128)(2,1)S(1)}, bf16[12544]{0:T(1024)(128)(2,1)S(1)}, u32[]{:S(2)}, u32[]{:S(2)}) collective-permute-start(bf16[12544]{0:T(1024)(128)(2,1)S(1)} %pad_maximum_fusion.4), channel_id=1, source_target_pairs={{0,32},{32,64},{64,96},{96,128},{128,160},{160,192},{192,224},{224... | collective-permute-start | bytes 75272 | tf_op jit(solution)/shard_map/ppermute | solution.py:18
  32.9 3.5 %collective-permute-start.1 = (bf16[12544]{0:T(1024)(128)(2,1)S(1)}, bf16[12544]{0:T(1024)(128)(2,1)S(1)}, u32[]{:S(2)}, u32[]{:S(2)}) collective-permute-start(bf16[12544]{0:T(1024)(128)(2,1)S(1)} %pad_maximum_fusion.5), channel_id=1, source_target_pairs={{32,0},{64,32},{96,64},{128,96},{160,128},{192,160},{224,192},{256... | collective-permute-start | bytes 75272 | tf_op jit(solution)/shard_map/ppermute | solution.py:18
  36.6 1.6 slice_bitcast_fusion.8
  38.2 2.1 %copy.36 = bf16[24,256,128]{1,0,2:T(8,128)(2,1)S(1)} copy(bf16[24,256,128]{2,1,0:T(8,128)(2,1)} %param.13) | data formatting | bytes 3145728 | tf_op args[6]
  40.7 0.8 copy.38
  43.4 1.2 copy.37
  44.6 0.9 convert_bitcast_fusion
  45.4 1.4 select_convert_fusion
  46.9 0.9 pad_maximum_fusion
  47.8 9.3 %multiply_add_fusion = f32[32,264,136]{1,0,2:T(8,128)S(1)} fusion(bf16[32,272,144]{1,0,2:T(8,128)(2,1)S(1)} %select_convert_fusion, f32[32]{0:T(128)} %get-tuple-element.54, f32[32]{0:T(128)} %get-tuple-element.55, f32[32]{0:T(128)} %get-tuple-element.48, f32[32]{0:T(128)} %get-tuple-element.49, f32[32]{0:T(128)} %get-tuple-element.50, ...), kind=kLoop, calls=%fused_computation.14 | loop fusion | flops 29872128 | bytes 25277568 | tf_op jit(solution)/shard_map/add | solution.py:91
  57.2 2.7 %collective-permute-start.5 = (bf16[24,264,4]{1,0,2:T(8,128)(2,1)}, bf16[24,264,4]{1,0,2:T(8,128)(2,1)}, u32[]{:S(2)}, u32[]{:S(2)}) collective-permute-start(bf16[24,264,4]{1,0,2:T(8,128)(2,1)} %get-tuple-element.9), channel_id=1, source_target_pairs={{0,1},{1,2},{2,3},{3,4},{4,5},{5,6},{6,7},{7,8},{8,9},{9,10},{10,1... | collective-permute-start | bytes 152072 | tf_op jit(solution)/shard_map/ppermute | solution.py:18
  59.9 1.5 collective-permute-start.6
  61.3 2.6 %multiply_convert_fusion.1 = bf16[32,256,128]{1,0,2:T(8,128)(2,1)} fusion(f32[32,264,136]{1,0,2:T(8,128)S(1)} %multiply_add_fusion), kind=kLoop, calls=%fused_computation.31 | loop fusion | flops 5242880 | bytes 6291456 | tf_op jit(solution)/shard_map/convert_element_type | solution.py:102
  63.9 4.6 %fusion.39 = bf16[32,24]{0,1:T(8,128)(2,1)S(1)} fusion(bf16[24,256,128]{1,0,2:T(8,128)(2,1)S(1)} %copy.36, bf16[32,256,128]{1,0,2:T(8,128)(2,1)} %multiply_convert_fusion.1, bf16[32,272,144]{1,0,2:T(8,128)(2,1)} %copy-done.1, bf16[32,32]{1,0:T(8,128)(2,1)S(1)} %copy-done.18), kind=kOutput, calls=%fused_computation.55 | convolution fusion | flops 120587008 | bytes 5770752 | tf_op jit(solution)/shard_map/ydq,gdq->yg/dot_general | solution.py:132
  68.8 3.5 %fusion.16 = bf16[32,264,136]{1,0,2:T(8,128)(2,1)S(1)} fusion(bf16[24,264,4]{1,0,2:T(8,128)(2,1)} %collective-permute-done.6, bf16[24,4,128]{1,0,2:T(8,128)(2,1)} %copy-done.5, bf16[24,256,128]{1,0,2:T(8,128)(2,1)} %copy-done.4, bf16[24,4,128]{1,0,2:T(8,128)(2,1)S(1)} %copy.35, bf16[24,264,4]{1,0,2:T(8,128)(2,1)} %collective-permute-done.5, ...), kind=kOutput, calls=%fused_computation.32 | convolution fusion | flops 66063360 | bytes 4022784 | tf_op jit(solution)/shard_map/ch,hij->cij/dot_general | solution.py:108
  72.4 3.3 %fusion = bf16[32,264,136]{1,0,2:T(8,128)(2,1)S(1)} fusion(f32[32,264,136]{1,0,2:T(8,128)S(1)} %bitcast.108, bf16[32,264,136]{1,0,2:T(8,128)(2,1)S(1)} %fusion.16, bf16[32,32]{1,0:T(8,128)(2,1)S(1)} %copy-done.19), kind=kOutput, calls=%fused_computation.12 | convolution fusion | flops 83871744 | bytes 9193472 | tf_op jit(solution)/shard_map/co,oij->cij/dot_general | solution.py:110
  75.8 7.3 %fusion.15 = (bf16[32]{0:T(256)(128)(2,1)S(1)}, bf16[32]{0:T(256)(128)(2,1)S(1)}, bf16[32]{0:T(256)(128)(2,1)S(1)}, bf16[32]{0:T(256)(128)(2,1)S(1)}, bf16[32]{0...) fusion(bf16[32,272,144]{1,0,2:T(8,128)(2,1)S(1)} %copy-done.2, ...), kind=kLoop, calls=%fused_computation.30 | loop fusion | flops 29359840 | bytes 20972096 | tf_op jit(solution)/shard_map/reduce_sum | solution.py:125
  83.2 7.0 %fusion.54 = (bf16[32,128]{0,1:T(8,128)(2,1)S(1)}, bf16[32,256]{1,0:T(8,128)(2,1)S(1)}) fusion(bf16[32,264,136]{1,0,2:T(8,128)(2,1)S(1)} %fusion, f32[32]{0:T(128)S(1)} %copy-done.16, f32[32]{0:T(128)S(1)} %copy-done.17, f32[32]{0:T(128)S(1)} %copy-done.10, f32[32]{0:T(128)S(1)} %copy-done.11, f32[32]{0:T(128)S(1)} %copy-done.12, f32[32]{0:T(128)S(1)} %copy-done.13, ...), kind=kLoop, calls=%fused_computation.118 | loop fusion | flops 31444992 | bytes 20997248 | tf_op jit(solution)/shard_map/reduce_sum | solution.py:128
  90.1 6.9 %collective-permute-start.7 = (bf16[128,32]{1,0:T(8,128)(2,1)S(1)}, bf16[128,32]{1,0:T(8,128)(2,1)S(1)}, u32[]{:S(2)}, u32[]{:S(2)}) collective-permute-start(bf16[128,32]{1,0:T(8,128)(2,1)S(1)} %bitcast.114), channel_id=1, source_target_pairs={{0,0},{1,1},{2,32},{3,33},{4,64},{5,65},{6,96},{7,97},{8,128},{9,1... | collective-permute-start | bytes 24584 | tf_op jit(solution)/shard_map/ppermute | solution.py:135
  97.1 1.0 fusion.35
  98.5 4.8 %collective-permute-done.7 = bf16[128,32]{1,0:T(8,128)(2,1)S(1)} collective-permute-done((bf16[128,32]{1,0:T(8,128)(2,1)S(1)}, bf16[128,32]{1,0:T(8,128)(2,1)S(1)}, u32[]{:S(2)}, u32[]{:S(2)}) %collective-permute-start.7) | collective-permute-done | bytes 8224 | tf_op jit(solution)/shard_map/ppermute | solution.py:135
  103.5 6.1 %collective-permute-start.8 = (bf16[14368]{0:T(1024)(128)(2,1)S(1)}, bf16[14368]{0:T(1024)(128)(2,1)S(1)}, u32[]{:S(2)}, u32[]{:S(2)}) collective-permute-start(bf16[14368]{0:T(1024)(128)(2,1)S(1)} %concatenate.52), channel_id=1, source_target_pairs={{0,2},{1,3},{2,0},{3,1},{4,6},{5,7},{6,4},{7,5},{8,10},{9,11},{10,... | collective-permute-start | bytes 86216 | tf_op jit(solution)/shard_map/ppermute | solution.py:34
  109.5 1.9 %collective-permute-done.8 = bf16[14368]{0:T(1024)(128)(2,1)S(1)} collective-permute-done((bf16[14368]{0:T(1024)(128)(2,1)S(1)}, bf16[14368]{0:T(1024)(128)(2,1)S(1)}, u32[]{:S(2)}, u32[]{:S(2)}) %collective-permute-start.8) | collective-permute-done | bytes 28768 | tf_op jit(solution)/shard_map/ppermute | solution.py:34
  111.4 7.9 %collective-permute-start.9 = (bf16[14368]{0:T(1024)(128)(2,1)S(1)}, bf16[14368]{0:T(1024)(128)(2,1)S(1)}, u32[]{:S(2)}, u32[]{:S(2)}) collective-permute-start(bf16[14368]{0:T(1024)(128)(2,1)S(1)} %add_convert_fusion.6), channel_id=1, source_target_pairs={{0,4},{1,5},{2,6},{3,7},{4,0},{5,1},{6,2},{7,3},{8,12},{9,13},{10,... | collective-permute-start | bytes 86216 | tf_op jit(solution)/shard_map/ppermute | solution.py:34
  119.4 1.9 %collective-permute-done.9 = bf16[14368]{0:T(1024)(128)(2,1)S(1)} collective-permute-done((bf16[14368]{0:T(1024)(128)(2,1)S(1)}, bf16[14368]{0:T(1024)(128)(2,1)S(1)}, u32[]{:S(2)}, u32[]{:S(2)}) %collective-permute-start.9) | collective-permute-done | bytes 28768 | tf_op jit(solution)/shard_map/ppermute | solution.py:34
  121.2 4.7 %collective-permute-start.10 = (bf16[14368]{0:T(1024)(128)(2,1)S(1)}, bf16[14368]{0:T(1024)(128)(2,1)S(1)}, u32[]{:S(2)}, u32[]{:S(2)}) collective-permute-start(bf16[14368]{0:T(1024)(128)(2,1)S(1)} %add_convert_fusion.5), channel_id=1, source_target_pairs={{0,8},{1,9},{2,10},{3,11},{4,12},{5,13},{6,14},{7,15},{8,0},{9,1},... | collective-permute-start | bytes 86216 | tf_op jit(solution)/shard_map/ppermute | solution.py:34
  126.0 5.0 %collective-permute-done.10 = bf16[14368]{0:T(1024)(128)(2,1)S(1)} collective-permute-done((bf16[14368]{0:T(1024)(128)(2,1)S(1)}, bf16[14368]{0:T(1024)(128)(2,1)S(1)}, u32[]{:S(2)}, u32[]{:S(2)}) %collective-permute-start.10) | collective-permute-done | bytes 28768 | tf_op jit(solution)/shard_map/ppermute | solution.py:34
  131.0 2.4 %collective-permute-start.11 = (bf16[14368]{0:T(1024)(128)(2,1)S(1)}, bf16[14368]{0:T(1024)(128)(2,1)S(1)}, u32[]{:S(2)}, u32[]{:S(2)}) collective-permute-start(bf16[14368]{0:T(1024)(128)(2,1)S(1)} %add_convert_fusion.4), channel_id=1, source_target_pairs={{0,16},{1,17},{2,18},{3,19},{4,20},{5,21},{6,22},{7,23},{8,24},{9,... | collective-permute-start | bytes 86216 | tf_op jit(solution)/shard_map/ppermute | solution.py:34
  133.3 3.4 %collective-permute-done.11 = bf16[14368]{0:T(1024)(128)(2,1)S(1)} collective-permute-done((bf16[14368]{0:T(1024)(128)(2,1)S(1)}, bf16[14368]{0:T(1024)(128)(2,1)S(1)}, u32[]{:S(2)}, u32[]{:S(2)}) %collective-permute-start.11) | collective-permute-done | bytes 28768 | tf_op jit(solution)/shard_map/ppermute | solution.py:34
  136.8 1.9 %collective-permute-start.12 = (bf16[14368]{0:T(1024)(128)(2,1)S(1)}, bf16[14368]{0:T(1024)(128)(2,1)S(1)}, u32[]{:S(2)}, u32[]{:S(2)}) collective-permute-start(bf16[14368]{0:T(1024)(128)(2,1)S(1)} %get-tuple-element.36), channel_id=1, source_target_pairs={{0,1},{1,0},{2,3},{3,2},{4,5},{5,4},{6,7},{7,6},{8,9},{9,8},{10,11... | collective-permute-start | bytes 86216 | tf_op jit(solution)/shard_map/ppermute | solution.py:34
  138.7 1.2 collective-permute-done.12
  141.2 3.7 %collective-permute-start.13 = (bf16[34848]{0:T(1024)(128)(2,1)S(1)}, bf16[34848]{0:T(1024)(128)(2,1)S(1)}, u32[]{:S(2)}, u32[]{:S(2)}) collective-permute-start(bf16[34848]{0:T(1024)(128)(2,1)S(1)} %pad_maximum_fusion.3), channel_id=1, source_target_pairs={{0,32},{32,0},{64,96},{96,64},{128,160},{160,128},{192,224},{224,1... | collective-permute-start | bytes 209096 | tf_op jit(solution)/shard_map/ppermute | solution.py:34
  144.9 4.8 %collective-permute-done.13 = bf16[34848]{0:T(1024)(128)(2,1)S(1)} collective-permute-done((bf16[34848]{0:T(1024)(128)(2,1)S(1)}, bf16[34848]{0:T(1024)(128)(2,1)S(1)}, u32[]{:S(2)}, u32[]{:S(2)}) %collective-permute-start.13) | collective-permute-done | bytes 69728 | tf_op jit(solution)/shard_map/ppermute | solution.py:34
  149.8 5.1 %collective-permute-start.14 = (bf16[34848]{0:T(1024)(128)(2,1)S(1)}, bf16[34848]{0:T(1024)(128)(2,1)S(1)}, u32[]{:S(2)}, u32[]{:S(2)}) collective-permute-start(bf16[34848]{0:T(1024)(128)(2,1)S(1)} %add_convert_fusion.2), channel_id=1, source_target_pairs={{0,64},{32,96},{64,0},{96,32},{128,192},{160,224},{192,128},{224,1... | collective-permute-start | bytes 209096 | tf_op jit(solution)/shard_map/ppermute | solution.py:34
  154.9 5.8 %collective-permute-done.14 = bf16[34848]{0:T(1024)(128)(2,1)S(1)} collective-permute-done((bf16[34848]{0:T(1024)(128)(2,1)S(1)}, bf16[34848]{0:T(1024)(128)(2,1)S(1)}, u32[]{:S(2)}, u32[]{:S(2)}) %collective-permute-start.14) | collective-permute-done | bytes 69728 | tf_op jit(solution)/shard_map/ppermute | solution.py:34
  160.7 2.0 %collective-permute-start.15 = (bf16[34848]{0:T(1024)(128)(2,1)S(1)}, bf16[34848]{0:T(1024)(128)(2,1)S(1)}, u32[]{:S(2)}, u32[]{:S(2)}) collective-permute-start(bf16[34848]{0:T(1024)(128)(2,1)S(1)} %add_convert_fusion.1), channel_id=1, source_target_pairs={{0,128},{32,160},{64,192},{96,224},{128,0},{160,32},{192,64},{224,... | collective-permute-start | bytes 209096 | tf_op jit(solution)/shard_map/ppermute | solution.py:34
  162.9 4.0 %collective-permute-done.15 = bf16[34848]{0:T(1024)(128)(2,1)S(1)} collective-permute-done((bf16[34848]{0:T(1024)(128)(2,1)S(1)}, bf16[34848]{0:T(1024)(128)(2,1)S(1)}, u32[]{:S(2)}, u32[]{:S(2)}) %collective-permute-start.15) | collective-permute-done | bytes 69728 | tf_op jit(solution)/shard_map/ppermute | solution.py:34
  166.9 2.4 %collective-permute-start.16 = (bf16[34848]{0:T(1024)(128)(2,1)S(1)}, bf16[34848]{0:T(1024)(128)(2,1)S(1)}, u32[]{:S(2)}, u32[]{:S(2)}) collective-permute-start(bf16[34848]{0:T(1024)(128)(2,1)S(1)} %add_convert_fusion), channel_id=1, source_target_pairs={{0,256},{32,288},{64,320},{96,352},{128,384},{160,416},{192,448},{... | collective-permute-start | bytes 209096 | tf_op jit(solution)/shard_map/ppermute | solution.py:34
  169.4 1.0 fusion.29
  170.3 4.4 %collective-permute-done.16 = bf16[34848]{0:T(1024)(128)(2,1)S(1)} collective-permute-done((bf16[34848]{0:T(1024)(128)(2,1)S(1)}, bf16[34848]{0:T(1024)(128)(2,1)S(1)}, u32[]{:S(2)}, u32[]{:S(2)}) %collective-permute-start.16) | collective-permute-done | bytes 69728 | tf_op jit(solution)/shard_map/ppermute | solution.py:34
  175.0 0.7 copy.49
  (118 shorter events, 8.7 us)
Async XLA Ops:
  0.6 1.0 copy-start
  2.5 37.9 %collective-permute-start.3 = (bf16[128,32]{0,1:T(8,128)(2,1)S(1)}, bf16[128,32]{0,1:T(8,128)(2,1)S(1)}, u32[]{:S(2)}, u32[]{:S(2)}) collective-permute-start(bf16[128,32]{0,1:T(8,128)(2,1)S(1)} %dynamic-slice_convert_fusion), channel_id=1, source_target_pairs={{0,0},{1,1},{2,32},{3,33},{4,64},{5,65},{6,96},{7,97},{8,128},{9,1... | collective-permute-start | bytes 24584 | tf_op jit(solution)/shard_map/ppermute | solution.py:74
  12.1 28.3 %collective-permute-start.2 = (bf16[8,32]{0,1:T(8,128)(2,1)S(1)}, bf16[8,32]{0,1:T(8,128)(2,1)S(1)}, u32[]{:S(2)}, u32[]{:S(2)}) collective-permute-start(bf16[8,32]{0,1:T(8,128)(2,1)S(1)} %get-tuple-element.56), channel_id=1, source_target_pairs={{0,1},{1,2},{2,33},{3,34},{4,65},{5,66},{6,97},{7,98},{8,129},{9,1... | collective-permute-start | bytes 1544 | tf_op jit(solution)/shard_map/ppermute | solution.py:73
  14.5 25.9 %collective-permute-start.4 = (bf16[8,32]{0,1:T(8,128)(2,1)S(1)}, bf16[8,32]{0,1:T(8,128)(2,1)S(1)}, u32[]{:S(2)}, u32[]{:S(2)}) collective-permute-start(bf16[8,32]{0,1:T(8,128)(2,1)S(1)} %get-tuple-element.57), channel_id=1, source_target_pairs={{1,0},{3,32},{5,64},{7,96},{9,128},{11,160},{13,192},{15,224},{17,... | collective-permute-start | bytes 1544 | tf_op jit(solution)/shard_map/ppermute | solution.py:75
  27.4 13.2 %collective-permute-start = (bf16[12544]{0:T(1024)(128)(2,1)S(1)}, bf16[12544]{0:T(1024)(128)(2,1)S(1)}, u32[]{:S(2)}, u32[]{:S(2)}) collective-permute-start(bf16[12544]{0:T(1024)(128)(2,1)S(1)} %pad_maximum_fusion.4), channel_id=1, source_target_pairs={{0,32},{32,64},{64,96},{96,128},{128,160},{160,192},{192,224},{224... | collective-permute-start | bytes 75272 | tf_op jit(solution)/shard_map/ppermute | solution.py:18
  32.9 8.6 %collective-permute-start.1 = (bf16[12544]{0:T(1024)(128)(2,1)S(1)}, bf16[12544]{0:T(1024)(128)(2,1)S(1)}, u32[]{:S(2)}, u32[]{:S(2)}) collective-permute-start(bf16[12544]{0:T(1024)(128)(2,1)S(1)} %pad_maximum_fusion.5), channel_id=1, source_target_pairs={{32,0},{64,32},{96,64},{128,96},{160,128},{192,160},{224,192},{256... | collective-permute-start | bytes 75272 | tf_op jit(solution)/shard_map/ppermute | solution.py:18
  40.4 23.5 %copy-start.4 = (bf16[24,256,128]{1,0,2:T(8,128)(2,1)}, bf16[24,256,128]{1,0,2:T(8,128)(2,1)S(1)}, u32[]{:S(2)}) copy-start(bf16[24,256,128]{1,0,2:T(8,128)(2,1)S(1)} %copy.36) | copy-start | bytes 4718596
  44.6 12.6 %copy-start.5 = (bf16[24,4,128]{1,0,2:T(8,128)(2,1)}, bf16[24,4,128]{1,0,2:T(8,128)(2,1)S(1)}, u32[]{:S(2)}) copy-start(bf16[24,4,128]{1,0,2:T(8,128)(2,1)S(1)} %copy.37) | copy-start | bytes 73732
  46.9 10.3 %copy-start.1 = (bf16[32,272,144]{1,0,2:T(8,128)(2,1)}, bf16[32,272,144]{1,0,2:T(8,128)(2,1)S(1)}, u32[]{:S(2)}) copy-start(bf16[32,272,144]{1,0,2:T(8,128)(2,1)S(1)} %select_convert_fusion) | copy-start | bytes 7520260
  57.1 4.2 %copy-start.3 = (f32[32,264,136]{1,0,2:T(8,128)}, f32[32,264,136]{1,0,2:T(8,128)S(1)}, u32[]{:S(2)}) copy-start(f32[32,264,136]{1,0,2:T(8,128)S(1)} %multiply_add_fusion) | copy-start | bytes 13787140
  57.2 6.7 %copy-start.18 = (bf16[32,32]{1,0:T(8,128)(2,1)S(1)}, bf16[32,32]{1,0:T(8,128)(2,1)}, u32[]{:S(2)}) copy-start(bf16[32,32]{1,0:T(8,128)(2,1)} %param.11) | copy-start | bytes 6148
  57.2 11.6 %collective-permute-start.5 = (bf16[24,264,4]{1,0,2:T(8,128)(2,1)}, bf16[24,264,4]{1,0,2:T(8,128)(2,1)}, u32[]{:S(2)}, u32[]{:S(2)}) collective-permute-start(bf16[24,264,4]{1,0,2:T(8,128)(2,1)} %get-tuple-element.9), channel_id=1, source_target_pairs={{0,1},{1,2},{2,3},{3,4},{4,5},{5,6},{6,7},{7,8},{8,9},{9,10},{10,1... | collective-permute-start | bytes 152072 | tf_op jit(solution)/shard_map/ppermute | solution.py:18
  59.9 8.9 %collective-permute-start.6 = (bf16[24,264,4]{1,0,2:T(8,128)(2,1)}, bf16[24,264,4]{1,0,2:T(8,128)(2,1)}, u32[]{:S(2)}, u32[]{:S(2)}) collective-permute-start(bf16[24,264,4]{1,0,2:T(8,128)(2,1)} %get-tuple-element.10), channel_id=1, source_target_pairs={{1,0},{2,1},{3,2},{4,3},{5,4},{6,5},{7,6},{8,7},{9,8},{10,9},{11,1... | collective-permute-start | bytes 152072 | tf_op jit(solution)/shard_map/ppermute | solution.py:18
  68.6 3.7 %slice-start = ((s8[6684672]{0:T(1024)(128)(4,1)}), s8[2490368]{0:T(1024)(128)(4,1)S(1)}, s32[]{:S(2)}) async-start(s8[6684672]{0:T(1024)(128)(4,1)} %bitcast.107), calls=%async_computation | async-start | bytes 4980736
  68.7 3.7 %slice-start.1 = ((s8[6684672]{0:T(1024)(128)(4,1)}), s8[4194304]{0:T(1024)(128)(4,1)S(1)}, s32[]{:S(2)}) async-start(s8[6684672]{0:T(1024)(128)(4,1)} %bitcast.107), calls=%async_computation.1 | async-start | bytes 8388608
  68.7 3.6 %copy-start.19 = (bf16[32,32]{1,0:T(8,128)(2,1)S(1)}, bf16[32,32]{1,0:T(8,128)(2,1)}, u32[]{:S(2)}) copy-start(bf16[32,32]{1,0:T(8,128)(2,1)} %param.11) | copy-start | bytes 6148
  72.4 3.3 %copy-start.2 = (bf16[32,272,144]{1,0,2:T(8,128)(2,1)S(1)}, bf16[32,272,144]{1,0,2:T(8,128)(2,1)}, u32[]{:S(2)}) copy-start(bf16[32,272,144]{1,0,2:T(8,128)(2,1)} %copy-done.1) | copy-start | bytes 7520260
  75.7 7.4 %copy-start.9 = (f32[32]{0:T(128)S(1)}, f32[32]{0:T(128)}, u32[]{:S(2)}) copy-start(f32[32]{0:T(128)} %get-tuple-element.47) | copy-start | bytes 388
  75.7 7.4 %copy-start.10 = (f32[32]{0:T(128)S(1)}, f32[32]{0:T(128)}, u32[]{:S(2)}) copy-start(f32[32]{0:T(128)} %get-tuple-element.48) | copy-start | bytes 388
  75.7 7.4 %copy-start.11 = (f32[32]{0:T(128)S(1)}, f32[32]{0:T(128)}, u32[]{:S(2)}) copy-start(f32[32]{0:T(128)} %get-tuple-element.49) | copy-start | bytes 388
  75.7 7.4 %copy-start.12 = (f32[32]{0:T(128)S(1)}, f32[32]{0:T(128)}, u32[]{:S(2)}) copy-start(f32[32]{0:T(128)} %get-tuple-element.50) | copy-start | bytes 388
  75.7 7.4 %copy-start.13 = (f32[32]{0:T(128)S(1)}, f32[32]{0:T(128)}, u32[]{:S(2)}) copy-start(f32[32]{0:T(128)} %get-tuple-element.51) | copy-start | bytes 388
  75.7 7.4 %copy-start.14 = (f32[32]{0:T(128)S(1)}, f32[32]{0:T(128)}, u32[]{:S(2)}) copy-start(f32[32]{0:T(128)} %get-tuple-element.52) | copy-start | bytes 388
  75.7 7.4 %copy-start.15 = (f32[32]{0:T(128)S(1)}, f32[32]{0:T(128)}, u32[]{:S(2)}) copy-start(f32[32]{0:T(128)} %get-tuple-element.53) | copy-start | bytes 388
  75.8 7.4 %copy-start.16 = (f32[32]{0:T(128)S(1)}, f32[32]{0:T(128)}, u32[]{:S(2)}) copy-start(f32[32]{0:T(128)} %get-tuple-element.54) | copy-start | bytes 388
  75.8 7.4 %copy-start.17 = (f32[32]{0:T(128)S(1)}, f32[32]{0:T(128)}, u32[]{:S(2)}) copy-start(f32[32]{0:T(128)} %get-tuple-element.55) | copy-start | bytes 388
  83.1 13.9 %copy-start.6 = (bf16[32,256,128]{1,0,2:T(8,128)(2,1)S(1)}, bf16[32,256,128]{1,0,2:T(8,128)(2,1)}, u32[]{:S(2)}) copy-start(bf16[32,256,128]{1,0,2:T(8,128)(2,1)} %multiply_convert_fusion.1) | copy-start | bytes 6291460
  90.1 72.6 %copy-start.7 = (bf16[512,32]{0,1:T(8,128)(2,1)S(1)}, bf16[512,32]{0,1:T(8,128)(2,1)}, u32[]{:S(2)}) copy-start(bf16[512,32]{0,1:T(8,128)(2,1)} %param.8) | copy-start | bytes 98308
  90.1 79.2 %copy-start.8 = (bf16[512,32]{0,1:T(8,128)(2,1)S(1)}, bf16[512,32]{0,1:T(8,128)(2,1)}, u32[]{:S(2)}) copy-start(bf16[512,32]{0,1:T(8,128)(2,1)} %param.9) | copy-start | bytes 98308
  90.1 13.2 %collective-permute-start.7 = (bf16[128,32]{1,0:T(8,128)(2,1)S(1)}, bf16[128,32]{1,0:T(8,128)(2,1)S(1)}, u32[]{:S(2)}, u32[]{:S(2)}) collective-permute-start(bf16[128,32]{1,0:T(8,128)(2,1)S(1)} %bitcast.114), channel_id=1, source_target_pairs={{0,0},{1,1},{2,32},{3,33},{4,64},{5,65},{6,96},{7,97},{8,128},{9,1... | collective-permute-start | bytes 24584 | tf_op jit(solution)/shard_map/ppermute | solution.py:135
  103.5 7.9 %collective-permute-start.8 = (bf16[14368]{0:T(1024)(128)(2,1)S(1)}, bf16[14368]{0:T(1024)(128)(2,1)S(1)}, u32[]{:S(2)}, u32[]{:S(2)}) collective-permute-start(bf16[14368]{0:T(1024)(128)(2,1)S(1)} %concatenate.52), channel_id=1, source_target_pairs={{0,2},{1,3},{2,0},{3,1},{4,6},{5,7},{6,4},{7,5},{8,10},{9,11},{10,... | collective-permute-start | bytes 86216 | tf_op jit(solution)/shard_map/ppermute | solution.py:34
  111.4 9.8 %collective-permute-start.9 = (bf16[14368]{0:T(1024)(128)(2,1)S(1)}, bf16[14368]{0:T(1024)(128)(2,1)S(1)}, u32[]{:S(2)}, u32[]{:S(2)}) collective-permute-start(bf16[14368]{0:T(1024)(128)(2,1)S(1)} %add_convert_fusion.6), channel_id=1, source_target_pairs={{0,4},{1,5},{2,6},{3,7},{4,0},{5,1},{6,2},{7,3},{8,12},{9,13},{10,... | collective-permute-start | bytes 86216 | tf_op jit(solution)/shard_map/ppermute | solution.py:34
  121.2 9.7 %collective-permute-start.10 = (bf16[14368]{0:T(1024)(128)(2,1)S(1)}, bf16[14368]{0:T(1024)(128)(2,1)S(1)}, u32[]{:S(2)}, u32[]{:S(2)}) collective-permute-start(bf16[14368]{0:T(1024)(128)(2,1)S(1)} %add_convert_fusion.5), channel_id=1, source_target_pairs={{0,8},{1,9},{2,10},{3,11},{4,12},{5,13},{6,14},{7,15},{8,0},{9,1},... | collective-permute-start | bytes 86216 | tf_op jit(solution)/shard_map/ppermute | solution.py:34
  131.0 5.8 %collective-permute-start.11 = (bf16[14368]{0:T(1024)(128)(2,1)S(1)}, bf16[14368]{0:T(1024)(128)(2,1)S(1)}, u32[]{:S(2)}, u32[]{:S(2)}) collective-permute-start(bf16[14368]{0:T(1024)(128)(2,1)S(1)} %add_convert_fusion.4), channel_id=1, source_target_pairs={{0,16},{1,17},{2,18},{3,19},{4,20},{5,21},{6,22},{7,23},{8,24},{9,... | collective-permute-start | bytes 86216 | tf_op jit(solution)/shard_map/ppermute | solution.py:34
  136.8 3.1 %collective-permute-start.12 = (bf16[14368]{0:T(1024)(128)(2,1)S(1)}, bf16[14368]{0:T(1024)(128)(2,1)S(1)}, u32[]{:S(2)}, u32[]{:S(2)}) collective-permute-start(bf16[14368]{0:T(1024)(128)(2,1)S(1)} %get-tuple-element.36), channel_id=1, source_target_pairs={{0,1},{1,0},{2,3},{3,2},{4,5},{5,4},{6,7},{7,6},{8,9},{9,8},{10,11... | collective-permute-start | bytes 86216 | tf_op jit(solution)/shard_map/ppermute | solution.py:34
  141.2 8.5 %collective-permute-start.13 = (bf16[34848]{0:T(1024)(128)(2,1)S(1)}, bf16[34848]{0:T(1024)(128)(2,1)S(1)}, u32[]{:S(2)}, u32[]{:S(2)}) collective-permute-start(bf16[34848]{0:T(1024)(128)(2,1)S(1)} %pad_maximum_fusion.3), channel_id=1, source_target_pairs={{0,32},{32,0},{64,96},{96,64},{128,160},{160,128},{192,224},{224,1... | collective-permute-start | bytes 209096 | tf_op jit(solution)/shard_map/ppermute | solution.py:34
  149.8 10.9 %collective-permute-start.14 = (bf16[34848]{0:T(1024)(128)(2,1)S(1)}, bf16[34848]{0:T(1024)(128)(2,1)S(1)}, u32[]{:S(2)}, u32[]{:S(2)}) collective-permute-start(bf16[34848]{0:T(1024)(128)(2,1)S(1)} %add_convert_fusion.2), channel_id=1, source_target_pairs={{0,64},{32,96},{64,0},{96,32},{128,192},{160,224},{192,128},{224,1... | collective-permute-start | bytes 209096 | tf_op jit(solution)/shard_map/ppermute | solution.py:34
  160.7 6.2 %collective-permute-start.15 = (bf16[34848]{0:T(1024)(128)(2,1)S(1)}, bf16[34848]{0:T(1024)(128)(2,1)S(1)}, u32[]{:S(2)}, u32[]{:S(2)}) collective-permute-start(bf16[34848]{0:T(1024)(128)(2,1)S(1)} %add_convert_fusion.1), channel_id=1, source_target_pairs={{0,128},{32,160},{64,192},{96,224},{128,0},{160,32},{192,64},{224,... | collective-permute-start | bytes 209096 | tf_op jit(solution)/shard_map/ppermute | solution.py:34
  166.9 7.7 %collective-permute-start.16 = (bf16[34848]{0:T(1024)(128)(2,1)S(1)}, bf16[34848]{0:T(1024)(128)(2,1)S(1)}, u32[]{:S(2)}, u32[]{:S(2)}) collective-permute-start(bf16[34848]{0:T(1024)(128)(2,1)S(1)} %add_convert_fusion), channel_id=1, source_target_pairs={{0,256},{32,288},{64,320},{96,352},{128,384},{160,416},{192,448},{... | collective-permute-start | bytes 209096 | tf_op jit(solution)/shard_map/ppermute | solution.py:34

commit v12 on v8

--- a/solution.py
+++ b/solution.py
@@ -126,14 +126,14 @@
     small = packed((kernel_part, point_part, head_part))
 
     right_moved = lax.ppermute(right_part, ("row", "col"), transpose_pairs())
-    bit = ratio
-    while bit < col_count:
+    bit = col_count // 2
+    while bit >= ratio:
         likes = (left_part, right_moved, small)
         flat = packed(likes).astype(jnp.bfloat16)
         got = xor_round(flat, "col", col_count, bit)
         total = flat.astype(jnp.float32) + got.astype(jnp.float32)
         left_part, right_moved, small = unpacked(total, likes)
-        bit *= 2
+        bit //= 2
     right_block = right_moved
     bit = 1
     while bit < ratio:
@@ -158,14 +158,14 @@
     contract = (((0,), (0,)), ((), ()))
     wleft_part = lax.dot_general(bin_features, grad_left, contract, preferred_element_type=jnp.float32)
     wright_part = lax.dot_general(bin_features, grad_right, contract, preferred_element_type=jnp.float32)
-    bit = 1
-    while bit < row_count:
+    bit = row_count // 2
+    while bit >= 1:
         likes = (wleft_part, wright_part, small)
         flat = packed(likes).astype(jnp.bfloat16)
         got = xor_round(flat, "row", row_count, bit)
         total = flat.astype(jnp.float32) + got.astype(jnp.float32)
         wleft_part, wright_part, small = unpacked(total, likes)
-        bit *= 2
+        bit //= 2
 
     kernel_sum, point_sum, head_sum = unpacked(small, (kernel_part, point_part, head_part))
     return (

time: 169 us -> 168 us (level)
  starting transfers between devices: 67 us -> 65.2 us
    ppermute x9, starting transfers between devices: 35.5 us -> 33.6 us  [xor_round(): return lax.ppermute(flat, axis, [(i, i ^ bit) for i in range(count)])]
where the time goes in v12:
time: 168 us; the launch traced here: 166 us
  starting transfers between devices  65.2 us (39%)
  waiting for transfers between devices  35.2 us (21%)
  other arithmetic  31.4 us (19%)
  local copies, waits for them, and re-layouts  17.5 us (10%)
  matrix products  15.7 us (9%)
    ppermute x9, starting transfers between devices, xor_round(): return lax.ppermute(flat, axis, [(i, i ^ bit) for i in range(count)])  33.6 us
    ppermute x9, waiting for transfers between devices, xor_round(): return lax.ppermute(flat, axis, [(i, i ^ bit) for i in range(count)])  30.7 us
    ppermute x4, starting transfers between devices, shifted(): return lax.ppermute(x, axis, pairs)  18.1 us
    add x1, other arithmetic, body(): conv_ext + depth_kernel[3 * a + b][:, None, None] * pair_ext[:, step * a:...  9.35 us
    unnamed x48, local copies, waits for them, and re-layouts  8.19 us
    reduce_sum x1, other arithmetic, body(): kern_terms.append(jnp.sum(conv_grad_tile * window, axis=(1, 2)))  7.48 us
    ppermute x1, starting transfers between devices, body(): right_moved = lax.ppermute(right_part, ('row', 'col'), transpose_pairs())  6.98 us
    reduce_sum x1, other arithmetic, body(): right_part = jnp.sum(backward_pass, axis=1).T  6.96 us
  transfers between devices with their start and end apart: 15, of which 10 were waited for; matrix products, arithmetic and copies ran while one was open for 18% of the time, Pallas kernels for 0%

profile of v12, /device:TPU:6, one launch (start us, length us, event | category | flops | bytes accessed | tf_op | source)
XLA Modules:
  0.0 166.3 jit_solution(162951304278521943)
XLA Ops:
  0.6 0.9 copy-done
  1.6 0.9 convolution_convert_fusion.2
  2.8 0.9 convolution_convert_fusion.3
  4.0 0.9 fusion.58
  4.9 6.1 %collective-permute-start = (bf16[12800]{0:T(1024)(128)(2,1)S(1)}, bf16[12800]{0:T(1024)(128)(2,1)S(1)}, u32[]{:S(2)}, u32[]{:S(2)}) collective-permute-start(bf16[12800]{0:T(1024)(128)(2,1)S(1)} %pad_maximum_fusion.4), channel_id=1, source_target_pairs={{0,32},{32,64},{64,96},{96,128},{128,160},{160,192},{192,224},{224... | collective-permute-start | bytes 76808 | tf_op jit(solution)/shard_map/ppermute | solution.py:18
  11.3 7.0 %collective-permute-start.1 = (bf16[12800]{0:T(1024)(128)(2,1)S(1)}, bf16[12800]{0:T(1024)(128)(2,1)S(1)}, u32[]{:S(2)}, u32[]{:S(2)}) collective-permute-start(bf16[12800]{0:T(1024)(128)(2,1)S(1)} %pad_maximum_fusion.5), channel_id=1, source_target_pairs={{32,0},{64,32},{96,64},{128,96},{160,128},{192,160},{224,192},{256... | collective-permute-start | bytes 76808 | tf_op jit(solution)/shard_map/ppermute | solution.py:18
  18.5 1.6 slice_bitcast_fusion.8
  20.1 2.2 %copy.42 = bf16[24,256,128]{1,0,2:T(8,128)(2,1)S(1)} copy(bf16[24,256,128]{2,1,0:T(8,128)(2,1)} %param.13) | data formatting | bytes 3145728 | tf_op args[6]
  22.8 6.5 %collective-permute-start.4 = (bf16[144,32]{0,1:T(8,128)(2,1)S(1)}, bf16[144,32]{0,1:T(8,128)(2,1)S(1)}, u32[]{:S(2)}, u32[]{:S(2)}) collective-permute-start(bf16[144,32]{0,1:T(8,128)(2,1)S(1)} %fusion.42), channel_id=1, source_target_pairs={{0,0},{1,1},{2,32},{3,33},{4,64},{5,65},{6,96},{7,97},{8,128},{9,1... | collective-permute-start | bytes 27656 | tf_op jit(solution)/shard_map/ppermute | solution.py:78
  30.6 0.9 pad_maximum_fusion.2
  31.5 1.3 collective-permute-start.3
  32.8 3.7 %collective-permute-start.2 = (bf16[24,264,4]{1,0,2:T(8,128)(2,1)}, bf16[24,264,4]{1,0,2:T(8,128)(2,1)}, u32[]{:S(2)}, u32[]{:S(2)}) collective-permute-start(bf16[24,264,4]{1,0,2:T(8,128)(2,1)} %get-tuple-element.31), channel_id=1, source_target_pairs={{0,1},{1,2},{2,3},{3,4},{4,5},{5,6},{6,7},{7,8},{8,9},{9,10},{10,1... | collective-permute-start | bytes 152072 | tf_op jit(solution)/shard_map/ppermute | solution.py:18
  36.5 0.7 convert_bitcast_fusion
  37.8 0.9 copy.48
  38.6 2.2 %select_convert_fusion = bf16[32,272,144]{1,0,2:T(8,128)(2,1)S(1)} fusion(f32[32,144]{0,1:T(8,128)S(1)} %copy.48, f32[32,272]{1,0:T(8,128)} %convert_bitcast_fusion, pred[272,144]{0,1:T(8,128)(4,1)S(1)} %and_and_fusion), kind=kLoop, calls=%fused_computation.10 | loop fusion | flops 3760128 | bytes 2599168 | tf_op jit(solution)/shard_map/convert_element_type | solution.py:84
  40.9 9.4 %multiply_add_fusion = f32[32,264,136]{1,0,2:T(8,128)S(1)} fusion(bf16[32,272,144]{1,0,2:T(8,128)(2,1)S(1)} %select_convert_fusion, f32[32]{0:T(128)} %get-tuple-element.54, f32[32]{0:T(128)} %get-tuple-element.55, f32[32]{0:T(128)} %get-tuple-element.48, f32[32]{0:T(128)} %get-tuple-element.49, f32[32]{0:T(128)} %get-tuple-element.50, ...), kind=kLoop, calls=%fused_computation.13 | loop fusion | flops 29872128 | bytes 25277568 | tf_op jit(solution)/shard_map/add | solution.py:91
  50.3 2.8 %copy-done.3 = f32[32,264,136]{1,0,2:T(8,128)} copy-done((f32[32,264,136]{1,0,2:T(8,128)}, f32[32,264,136]{1,0,2:T(8,128)S(1)}, u32[]{:S(2)}) %copy-start.3) | copy-done | bytes 4595736
  53.1 2.6 %multiply_convert_fusion.1 = bf16[32,256,128]{1,0,2:T(8,128)(2,1)} fusion(f32[32,264,136]{1,0,2:T(8,128)S(1)} %multiply_add_fusion), kind=kLoop, calls=%fused_computation.31 | loop fusion | flops 5242880 | bytes 6291456 | tf_op jit(solution)/shard_map/convert_element_type | solution.py:95
  55.6 4.6 %fusion.39 = bf16[32,24]{0,1:T(8,128)(2,1)S(1)} fusion(bf16[24,256,128]{1,0,2:T(8,128)(2,1)S(1)} %copy.42, bf16[32,256,128]{1,0,2:T(8,128)(2,1)} %multiply_convert_fusion.1, bf16[32,272,144]{1,0,2:T(8,128)(2,1)} %copy-done.1, bf16[32,32]{1,0:T(8,128)(2,1)S(1)} %copy-done.18), kind=kOutput, calls=%fused_computation.56 | convolution fusion | flops 120587008 | bytes 5770752 | tf_op jit(solution)/shard_map/ydq,gdq->yg/dot_general | solution.py:125
  60.5 3.5 %fusion.16 = bf16[32,264,136]{1,0,2:T(8,128)(2,1)S(1)} fusion(bf16[24,264,4]{1,0,2:T(8,128)(2,1)} %collective-permute-done.3, bf16[24,4,128]{1,0,2:T(8,128)(2,1)S(1)} %copy.43, bf16[24,256,128]{1,0,2:T(8,128)(2,1)} %copy-done.4, bf16[24,4,128]{1,0,2:T(8,128)(2,1)} %copy-done.5, bf16[24,264,4]{1,0,2:T(8,128)(2,1)} %collective-permute-done.2, ...), kind=kOutput, calls=%fused_computation.32 | convolution fusion | flops 66063360 | bytes 4022784 | tf_op jit(solution)/shard_map/ch,hij->cij/dot_general | solution.py:101
  64.2 3.3 %fusion = bf16[32,264,136]{1,0,2:T(8,128)(2,1)S(1)} fusion(f32[32,264,136]{1,0,2:T(8,128)S(1)} %bitcast.108, bf16[32,264,136]{1,0,2:T(8,128)(2,1)S(1)} %fusion.16, bf16[32,32]{1,0:T(8,128)(2,1)S(1)} %copy-done.19), kind=kOutput, calls=%fused_computation.12 | convolution fusion | flops 83871744 | bytes 9193472 | tf_op jit(solution)/shard_map/co,oij->cij/dot_general | solution.py:103
  67.6 7.0 %fusion.56 = (bf16[32,128]{0,1:T(8,128)(2,1)S(1)}, bf16[32,256]{1,0:T(8,128)(2,1)S(1)}) fusion(bf16[32,264,136]{1,0,2:T(8,128)(2,1)S(1)} %fusion, f32[32]{0:T(128)S(1)} %copy-done.16, f32[32]{0:T(128)S(1)} %copy-done.17, f32[32]{0:T(128)S(1)} %copy-done.10, f32[32]{0:T(128)S(1)} %copy-done.11, f32[32]{0:T(128)S(1)} %copy-done.12, f32[32]{0:T(128)S(1)} %copy-done.13, ...), kind=kLoop, calls=%fused_computation.123 | loop fusion | flops 31444992 | bytes 20997248 | tf_op jit(solution)/shard_map/reduce_sum | solution.py:121
  74.6 7.5 %fusion.15 = (bf16[32]{0:T(256)(128)(2,1)S(1)}, bf16[32]{0:T(256)(128)(2,1)S(1)}, bf16[32]{0:T(256)(128)(2,1)S(1)}, bf16[32]{0:T(256)(128)(2,1)S(1)}, bf16[32]{0...) fusion(bf16[32,272,144]{1,0,2:T(8,128)(2,1)S(1)} %copy-done.2, ...), kind=kLoop, calls=%fused_computation.30 | loop fusion | flops 29359840 | bytes 20972096 | tf_op jit(solution)/shard_map/reduce_sum | solution.py:118
  82.1 7.0 %collective-permute-start.5 = (bf16[128,32]{1,0:T(8,128)(2,1)S(1)}, bf16[128,32]{1,0:T(8,128)(2,1)S(1)}, u32[]{:S(2)}, u32[]{:S(2)}) collective-permute-start(bf16[128,32]{1,0:T(8,128)(2,1)S(1)} %bitcast.114), channel_id=1, source_target_pairs={{0,0},{1,1},{2,32},{3,33},{4,64},{5,65},{6,96},{7,97},{8,128},{9,1... | collective-permute-start | bytes 24584 | tf_op jit(solution)/shard_map/ppermute | solution.py:128
  89.1 1.0 fusion.35
  90.6 4.5 %collective-permute-done.5 = bf16[128,32]{1,0:T(8,128)(2,1)S(1)} collective-permute-done((bf16[128,32]{1,0:T(8,128)(2,1)S(1)}, bf16[128,32]{1,0:T(8,128)(2,1)S(1)}, u32[]{:S(2)}, u32[]{:S(2)}) %collective-permute-start.5) | collective-permute-done | bytes 8224 | tf_op jit(solution)/shard_map/ppermute | solution.py:128
  95.2 3.6 %collective-permute-start.6 = (bf16[14368]{0:T(1024)(128)(2,1)S(1)}, bf16[14368]{0:T(1024)(128)(2,1)S(1)}, u32[]{:S(2)}, u32[]{:S(2)}) collective-permute-start(bf16[14368]{0:T(1024)(128)(2,1)S(1)} %concatenate.52), channel_id=1, source_target_pairs={{0,16},{1,17},{2,18},{3,19},{4,20},{5,21},{6,22},{7,23},{8,24},{9,... | collective-permute-start | bytes 86216 | tf_op jit(solution)/shard_map/ppermute | solution.py:34
  98.9 2.1 %collective-permute-done.6 = bf16[14368]{0:T(1024)(128)(2,1)S(1)} collective-permute-done((bf16[14368]{0:T(1024)(128)(2,1)S(1)}, bf16[14368]{0:T(1024)(128)(2,1)S(1)}, u32[]{:S(2)}, u32[]{:S(2)}) %collective-permute-start.6) | collective-permute-done | bytes 28768 | tf_op jit(solution)/shard_map/ppermute | solution.py:34
  101.0 1.9 %collective-permute-start.7 = (bf16[14368]{0:T(1024)(128)(2,1)S(1)}, bf16[14368]{0:T(1024)(128)(2,1)S(1)}, u32[]{:S(2)}, u32[]{:S(2)}) collective-permute-start(bf16[14368]{0:T(1024)(128)(2,1)S(1)} %add_convert_fusion.6), channel_id=1, source_target_pairs={{0,8},{1,9},{2,10},{3,11},{4,12},{5,13},{6,14},{7,15},{8,0},{9,1},... | collective-permute-start | bytes 86216 | tf_op jit(solution)/shard_map/ppermute | solution.py:34
  103.0 8.0 %collective-permute-done.7 = bf16[14368]{0:T(1024)(128)(2,1)S(1)} collective-permute-done((bf16[14368]{0:T(1024)(128)(2,1)S(1)}, bf16[14368]{0:T(1024)(128)(2,1)S(1)}, u32[]{:S(2)}, u32[]{:S(2)}) %collective-permute-start.7) | collective-permute-done | bytes 28768 | tf_op jit(solution)/shard_map/ppermute | solution.py:34
  111.0 7.6 %collective-permute-start.8 = (bf16[14368]{0:T(1024)(128)(2,1)S(1)}, bf16[14368]{0:T(1024)(128)(2,1)S(1)}, u32[]{:S(2)}, u32[]{:S(2)}) collective-permute-start(bf16[14368]{0:T(1024)(128)(2,1)S(1)} %add_convert_fusion.5), channel_id=1, source_target_pairs={{0,4},{1,5},{2,6},{3,7},{4,0},{5,1},{6,2},{7,3},{8,12},{9,13},{10,... | collective-permute-start | bytes 86216 | tf_op jit(solution)/shard_map/ppermute | solution.py:34
  118.6 1.9 %collective-permute-done.8 = bf16[14368]{0:T(1024)(128)(2,1)S(1)} collective-permute-done((bf16[14368]{0:T(1024)(128)(2,1)S(1)}, bf16[14368]{0:T(1024)(128)(2,1)S(1)}, u32[]{:S(2)}, u32[]{:S(2)}) %collective-permute-start.8) | collective-permute-done | bytes 28768 | tf_op jit(solution)/shard_map/ppermute | solution.py:34
  120.5 4.0 %collective-permute-start.9 = (bf16[14368]{0:T(1024)(128)(2,1)S(1)}, bf16[14368]{0:T(1024)(128)(2,1)S(1)}, u32[]{:S(2)}, u32[]{:S(2)}) collective-permute-start(bf16[14368]{0:T(1024)(128)(2,1)S(1)} %add_convert_fusion.4), channel_id=1, source_target_pairs={{0,2},{1,3},{2,0},{3,1},{4,6},{5,7},{6,4},{7,5},{8,10},{9,11},{10,... | collective-permute-start | bytes 86216 | tf_op jit(solution)/shard_map/ppermute | solution.py:34
  124.4 1.9 %collective-permute-done.9 = bf16[14368]{0:T(1024)(128)(2,1)S(1)} collective-permute-done((bf16[14368]{0:T(1024)(128)(2,1)S(1)}, bf16[14368]{0:T(1024)(128)(2,1)S(1)}, u32[]{:S(2)}, u32[]{:S(2)}) %collective-permute-start.9) | collective-permute-done | bytes 28768 | tf_op jit(solution)/shard_map/ppermute | solution.py:34
  126.3 1.9 %collective-permute-start.10 = (bf16[14368]{0:T(1024)(128)(2,1)S(1)}, bf16[14368]{0:T(1024)(128)(2,1)S(1)}, u32[]{:S(2)}, u32[]{:S(2)}) collective-permute-start(bf16[14368]{0:T(1024)(128)(2,1)S(1)} %get-tuple-element.30), channel_id=1, source_target_pairs={{0,1},{1,0},{2,3},{3,2},{4,5},{5,4},{6,7},{7,6},{8,9},{9,8},{10,11... | collective-permute-start | bytes 86216 | tf_op jit(solution)/shard_map/ppermute | solution.py:34
  128.2 1.2 collective-permute-done.10
  130.8 3.1 %collective-permute-start.11 = (bf16[34848]{0:T(1024)(128)(2,1)S(1)}, bf16[34848]{0:T(1024)(128)(2,1)S(1)}, u32[]{:S(2)}, u32[]{:S(2)}) collective-permute-start(bf16[34848]{0:T(1024)(128)(2,1)S(1)} %pad_maximum_fusion.3), channel_id=1, source_target_pairs={{0,256},{32,288},{64,320},{96,352},{128,384},{160,416},{192,448},{... | collective-permute-start | bytes 209096 | tf_op jit(solution)/shard_map/ppermute | solution.py:34
  133.9 4.6 %collective-permute-done.11 = bf16[34848]{0:T(1024)(128)(2,1)S(1)} collective-permute-done((bf16[34848]{0:T(1024)(128)(2,1)S(1)}, bf16[34848]{0:T(1024)(128)(2,1)S(1)}, u32[]{:S(2)}, u32[]{:S(2)}) %collective-permute-start.11) | collective-permute-done | bytes 69728 | tf_op jit(solution)/shard_map/ppermute | solution.py:34
  138.5 1.9 %collective-permute-start.12 = (bf16[34848]{0:T(1024)(128)(2,1)S(1)}, bf16[34848]{0:T(1024)(128)(2,1)S(1)}, u32[]{:S(2)}, u32[]{:S(2)}) collective-permute-start(bf16[34848]{0:T(1024)(128)(2,1)S(1)} %add_convert_fusion.2), channel_id=1, source_target_pairs={{0,128},{32,160},{64,192},{96,224},{128,0},{160,32},{192,64},{224,... | collective-permute-start | bytes 209096 | tf_op jit(solution)/shard_map/ppermute | solution.py:34
  140.5 4.3 %collective-permute-done.12 = bf16[34848]{0:T(1024)(128)(2,1)S(1)} collective-permute-done((bf16[34848]{0:T(1024)(128)(2,1)S(1)}, bf16[34848]{0:T(1024)(128)(2,1)S(1)}, u32[]{:S(2)}, u32[]{:S(2)}) %collective-permute-start.12) | collective-permute-done | bytes 69728 | tf_op jit(solution)/shard_map/ppermute | solution.py:34
  144.8 4.6 %collective-permute-start.13 = (bf16[34848]{0:T(1024)(128)(2,1)S(1)}, bf16[34848]{0:T(1024)(128)(2,1)S(1)}, u32[]{:S(2)}, u32[]{:S(2)}) collective-permute-start(bf16[34848]{0:T(1024)(128)(2,1)S(1)} %add_convert_fusion.1), channel_id=1, source_target_pairs={{0,64},{32,96},{64,0},{96,32},{128,192},{160,224},{192,128},{224,1... | collective-permute-start | bytes 209096 | tf_op jit(solution)/shard_map/ppermute | solution.py:34
  149.6 5.4 %collective-permute-done.13 = bf16[34848]{0:T(1024)(128)(2,1)S(1)} collective-permute-done((bf16[34848]{0:T(1024)(128)(2,1)S(1)}, bf16[34848]{0:T(1024)(128)(2,1)S(1)}, u32[]{:S(2)}, u32[]{:S(2)}) %collective-permute-start.13) | collective-permute-done | bytes 69728 | tf_op jit(solution)/shard_map/ppermute | solution.py:34
  155.0 5.0 %collective-permute-start.14 = (bf16[34848]{0:T(1024)(128)(2,1)S(1)}, bf16[34848]{0:T(1024)(128)(2,1)S(1)}, u32[]{:S(2)}, u32[]{:S(2)}) collective-permute-start(bf16[34848]{0:T(1024)(128)(2,1)S(1)} %add_convert_fusion), channel_id=1, source_target_pairs={{0,32},{32,0},{64,96},{96,64},{128,160},{160,128},{192,224},{224,1... | collective-permute-start | bytes 209096 | tf_op jit(solution)/shard_map/ppermute | solution.py:34
  160.0 1.0 fusion.29
  161.0 1.3 collective-permute-done.14
  162.6 0.7 copy.57
  163.5 0.7 copy.58
  164.9 0.7 mul.329
  (122 shorter events, 7.9 us)
Async XLA Ops:
  0.6 1.0 copy-start
  4.9 17.4 %collective-permute-start = (bf16[12800]{0:T(1024)(128)(2,1)S(1)}, bf16[12800]{0:T(1024)(128)(2,1)S(1)}, u32[]{:S(2)}, u32[]{:S(2)}) collective-permute-start(bf16[12800]{0:T(1024)(128)(2,1)S(1)} %pad_maximum_fusion.4), channel_id=1, source_target_pairs={{0,32},{32,64},{64,96},{96,128},{128,160},{160,192},{192,224},{224... | collective-permute-start | bytes 76808 | tf_op jit(solution)/shard_map/ppermute | solution.py:18
  11.3 11.2 %collective-permute-start.1 = (bf16[12800]{0:T(1024)(128)(2,1)S(1)}, bf16[12800]{0:T(1024)(128)(2,1)S(1)}, u32[]{:S(2)}, u32[]{:S(2)}) collective-permute-start(bf16[12800]{0:T(1024)(128)(2,1)S(1)} %pad_maximum_fusion.5), channel_id=1, source_target_pairs={{32,0},{64,32},{96,64},{128,96},{160,128},{192,160},{224,192},{256... | collective-permute-start | bytes 76808 | tf_op jit(solution)/shard_map/ppermute | solution.py:18
  22.3 33.4 %copy-start.4 = (bf16[24,256,128]{1,0,2:T(8,128)(2,1)}, bf16[24,256,128]{1,0,2:T(8,128)(2,1)S(1)}, u32[]{:S(2)}) copy-start(bf16[24,256,128]{1,0,2:T(8,128)(2,1)S(1)} %copy.42) | copy-start | bytes 4718596
  22.8 14.4 %collective-permute-start.4 = (bf16[144,32]{0,1:T(8,128)(2,1)S(1)}, bf16[144,32]{0,1:T(8,128)(2,1)S(1)}, u32[]{:S(2)}, u32[]{:S(2)}) collective-permute-start(bf16[144,32]{0,1:T(8,128)(2,1)S(1)} %fusion.42), channel_id=1, source_target_pairs={{0,0},{1,1},{2,32},{3,33},{4,64},{5,65},{6,96},{7,97},{8,128},{9,1... | collective-permute-start | bytes 27656 | tf_op jit(solution)/shard_map/ppermute | solution.py:78
  30.6 19.7 %copy-start.5 = (bf16[24,4,128]{1,0,2:T(8,128)(2,1)}, bf16[24,4,128]{1,0,2:T(8,128)(2,1)S(1)}, u32[]{:S(2)}) copy-start(bf16[24,4,128]{1,0,2:T(8,128)(2,1)S(1)} %copy.41) | copy-start | bytes 73732
  31.5 29.0 %collective-permute-start.3 = (bf16[24,264,4]{1,0,2:T(8,128)(2,1)}, bf16[24,264,4]{1,0,2:T(8,128)(2,1)}, u32[]{:S(2)}, u32[]{:S(2)}) collective-permute-start(bf16[24,264,4]{1,0,2:T(8,128)(2,1)} %get-tuple-element.32), channel_id=1, source_target_pairs={{1,0},{2,1},{3,2},{4,3},{5,4},{6,5},{7,6},{8,7},{9,8},{10,9},{11,1... | collective-permute-start | bytes 152072 | tf_op jit(solution)/shard_map/ppermute | solution.py:18
  32.8 27.7 %collective-permute-start.2 = (bf16[24,264,4]{1,0,2:T(8,128)(2,1)}, bf16[24,264,4]{1,0,2:T(8,128)(2,1)}, u32[]{:S(2)}, u32[]{:S(2)}) collective-permute-start(bf16[24,264,4]{1,0,2:T(8,128)(2,1)} %get-tuple-element.31), channel_id=1, source_target_pairs={{0,1},{1,2},{2,3},{3,4},{4,5},{5,6},{6,7},{7,8},{8,9},{9,10},{10,1... | collective-permute-start | bytes 152072 | tf_op jit(solution)/shard_map/ppermute | solution.py:18
  40.9 9.4 %copy-start.1 = (bf16[32,272,144]{1,0,2:T(8,128)(2,1)}, bf16[32,272,144]{1,0,2:T(8,128)(2,1)S(1)}, u32[]{:S(2)}) copy-start(bf16[32,272,144]{1,0,2:T(8,128)(2,1)S(1)} %select_convert_fusion) | copy-start | bytes 7520260
  50.3 2.8 %copy-start.3 = (f32[32,264,136]{1,0,2:T(8,128)}, f32[32,264,136]{1,0,2:T(8,128)S(1)}, u32[]{:S(2)}) copy-start(f32[32,264,136]{1,0,2:T(8,128)S(1)} %multiply_add_fusion) | copy-start | bytes 13787140
  53.1 2.6 %copy-start.18 = (bf16[32,32]{1,0:T(8,128)(2,1)S(1)}, bf16[32,32]{1,0:T(8,128)(2,1)}, u32[]{:S(2)}) copy-start(bf16[32,32]{1,0:T(8,128)(2,1)} %param.11) | copy-start | bytes 6148
  60.3 3.7 %slice-start = ((s8[6684672]{0:T(1024)(128)(4,1)}), s8[2490368]{0:T(1024)(128)(4,1)S(1)}, s32[]{:S(2)}) async-start(s8[6684672]{0:T(1024)(128)(4,1)} %bitcast.107), calls=%async_computation | async-start | bytes 4980736
  60.4 3.7 %slice-start.1 = ((s8[6684672]{0:T(1024)(128)(4,1)}), s8[4194304]{0:T(1024)(128)(4,1)S(1)}, s32[]{:S(2)}) async-start(s8[6684672]{0:T(1024)(128)(4,1)} %bitcast.107), calls=%async_computation.1 | async-start | bytes 8388608
  60.5 3.6 %copy-start.19 = (bf16[32,32]{1,0:T(8,128)(2,1)S(1)}, bf16[32,32]{1,0:T(8,128)(2,1)}, u32[]{:S(2)}) copy-start(bf16[32,32]{1,0:T(8,128)(2,1)} %param.11) | copy-start | bytes 6148
  64.1 3.4 %copy-start.9 = (f32[32]{0:T(128)S(1)}, f32[32]{0:T(128)}, u32[]{:S(2)}) copy-start(f32[32]{0:T(128)} %get-tuple-element.47) | copy-start | bytes 388
  64.1 3.4 %copy-start.10 = (f32[32]{0:T(128)S(1)}, f32[32]{0:T(128)}, u32[]{:S(2)}) copy-start(f32[32]{0:T(128)} %get-tuple-element.48) | copy-start | bytes 388
  64.1 3.4 %copy-start.11 = (f32[32]{0:T(128)S(1)}, f32[32]{0:T(128)}, u32[]{:S(2)}) copy-start(f32[32]{0:T(128)} %get-tuple-element.49) | copy-start | bytes 388
  64.1 3.4 %copy-start.12 = (f32[32]{0:T(128)S(1)}, f32[32]{0:T(128)}, u32[]{:S(2)}) copy-start(f32[32]{0:T(128)} %get-tuple-element.50) | copy-start | bytes 388
  64.1 3.4 %copy-start.13 = (f32[32]{0:T(128)S(1)}, f32[32]{0:T(128)}, u32[]{:S(2)}) copy-start(f32[32]{0:T(128)} %get-tuple-element.51) | copy-start | bytes 388
  64.1 3.4 %copy-start.14 = (f32[32]{0:T(128)S(1)}, f32[32]{0:T(128)}, u32[]{:S(2)}) copy-start(f32[32]{0:T(128)} %get-tuple-element.52) | copy-start | bytes 388
  64.1 3.4 %copy-start.15 = (f32[32]{0:T(128)S(1)}, f32[32]{0:T(128)}, u32[]{:S(2)}) copy-start(f32[32]{0:T(128)} %get-tuple-element.53) | copy-start | bytes 388
  64.2 3.4 %copy-start.16 = (f32[32]{0:T(128)S(1)}, f32[32]{0:T(128)}, u32[]{:S(2)}) copy-start(f32[32]{0:T(128)} %get-tuple-element.54) | copy-start | bytes 388
  64.2 3.4 %copy-start.17 = (f32[32]{0:T(128)S(1)}, f32[32]{0:T(128)}, u32[]{:S(2)}) copy-start(f32[32]{0:T(128)} %get-tuple-element.55) | copy-start | bytes 388
  67.6 7.0 %copy-start.2 = (bf16[32,272,144]{1,0,2:T(8,128)(2,1)S(1)}, bf16[32,272,144]{1,0,2:T(8,128)(2,1)}, u32[]{:S(2)}) copy-start(bf16[32,272,144]{1,0,2:T(8,128)(2,1)} %copy-done.1) | copy-start | bytes 7520260
  74.5 14.5 %copy-start.6 = (bf16[32,256,128]{1,0,2:T(8,128)(2,1)S(1)}, bf16[32,256,128]{1,0,2:T(8,128)(2,1)}, u32[]{:S(2)}) copy-start(bf16[32,256,128]{1,0,2:T(8,128)(2,1)} %multiply_convert_fusion.1) | copy-start | bytes 6291460
  82.0 67.3 %copy-start.7 = (bf16[512,32]{0,1:T(8,128)(2,1)S(1)}, bf16[512,32]{0,1:T(8,128)(2,1)}, u32[]{:S(2)}) copy-start(bf16[512,32]{0,1:T(8,128)(2,1)} %param.8) | copy-start | bytes 98308
  82.1 77.9 %copy-start.8 = (bf16[512,32]{0,1:T(8,128)(2,1)S(1)}, bf16[512,32]{0,1:T(8,128)(2,1)}, u32[]{:S(2)}) copy-start(bf16[512,32]{0,1:T(8,128)(2,1)} %param.9) | copy-start | bytes 98308
  82.1 13.0 %collective-permute-start.5 = (bf16[128,32]{1,0:T(8,128)(2,1)S(1)}, bf16[128,32]{1,0:T(8,128)(2,1)S(1)}, u32[]{:S(2)}, u32[]{:S(2)}) collective-permute-start(bf16[128,32]{1,0:T(8,128)(2,1)S(1)} %bitcast.114), channel_id=1, source_target_pairs={{0,0},{1,1},{2,32},{3,33},{4,64},{5,65},{6,96},{7,97},{8,128},{9,1... | collective-permute-start | bytes 24584 | tf_op jit(solution)/shard_map/ppermute | solution.py:128
  95.2 5.8 %collective-permute-start.6 = (bf16[14368]{0:T(1024)(128)(2,1)S(1)}, bf16[14368]{0:T(1024)(128)(2,1)S(1)}, u32[]{:S(2)}, u32[]{:S(2)}) collective-permute-start(bf16[14368]{0:T(1024)(128)(2,1)S(1)} %concatenate.52), channel_id=1, source_target_pairs={{0,16},{1,17},{2,18},{3,19},{4,20},{5,21},{6,22},{7,23},{8,24},{9,... | collective-permute-start | bytes 86216 | tf_op jit(solution)/shard_map/ppermute | solution.py:34
  101.0 9.9 %collective-permute-start.7 = (bf16[14368]{0:T(1024)(128)(2,1)S(1)}, bf16[14368]{0:T(1024)(128)(2,1)S(1)}, u32[]{:S(2)}, u32[]{:S(2)}) collective-permute-start(bf16[14368]{0:T(1024)(128)(2,1)S(1)} %add_convert_fusion.6), channel_id=1, source_target_pairs={{0,8},{1,9},{2,10},{3,11},{4,12},{5,13},{6,14},{7,15},{8,0},{9,1},... | collective-permute-start | bytes 86216 | tf_op jit(solution)/shard_map/ppermute | solution.py:34
  111.0 9.5 %collective-permute-start.8 = (bf16[14368]{0:T(1024)(128)(2,1)S(1)}, bf16[14368]{0:T(1024)(128)(2,1)S(1)}, u32[]{:S(2)}, u32[]{:S(2)}) collective-permute-start(bf16[14368]{0:T(1024)(128)(2,1)S(1)} %add_convert_fusion.5), channel_id=1, source_target_pairs={{0,4},{1,5},{2,6},{3,7},{4,0},{5,1},{6,2},{7,3},{8,12},{9,13},{10,... | collective-permute-start | bytes 86216 | tf_op jit(solution)/shard_map/ppermute | solution.py:34
  120.5 5.8 %collective-permute-start.9 = (bf16[14368]{0:T(1024)(128)(2,1)S(1)}, bf16[14368]{0:T(1024)(128)(2,1)S(1)}, u32[]{:S(2)}, u32[]{:S(2)}) collective-permute-start(bf16[14368]{0:T(1024)(128)(2,1)S(1)} %add_convert_fusion.4), channel_id=1, source_target_pairs={{0,2},{1,3},{2,0},{3,1},{4,6},{5,7},{6,4},{7,5},{8,10},{9,11},{10,... | collective-permute-start | bytes 86216 | tf_op jit(solution)/shard_map/ppermute | solution.py:34
  126.3 3.1 %collective-permute-start.10 = (bf16[14368]{0:T(1024)(128)(2,1)S(1)}, bf16[14368]{0:T(1024)(128)(2,1)S(1)}, u32[]{:S(2)}, u32[]{:S(2)}) collective-permute-start(bf16[14368]{0:T(1024)(128)(2,1)S(1)} %get-tuple-element.30), channel_id=1, source_target_pairs={{0,1},{1,0},{2,3},{3,2},{4,5},{5,4},{6,7},{7,6},{8,9},{9,8},{10,11... | collective-permute-start | bytes 86216 | tf_op jit(solution)/shard_map/ppermute | solution.py:34
  130.8 7.7 %collective-permute-start.11 = (bf16[34848]{0:T(1024)(128)(2,1)S(1)}, bf16[34848]{0:T(1024)(128)(2,1)S(1)}, u32[]{:S(2)}, u32[]{:S(2)}) collective-permute-start(bf16[34848]{0:T(1024)(128)(2,1)S(1)} %pad_maximum_fusion.3), channel_id=1, source_target_pairs={{0,256},{32,288},{64,320},{96,352},{128,384},{160,416},{192,448},{... | collective-permute-start | bytes 209096 | tf_op jit(solution)/shard_map/ppermute | solution.py:34
  138.5 6.2 %collective-permute-start.12 = (bf16[34848]{0:T(1024)(128)(2,1)S(1)}, bf16[34848]{0:T(1024)(128)(2,1)S(1)}, u32[]{:S(2)}, u32[]{:S(2)}) collective-permute-start(bf16[34848]{0:T(1024)(128)(2,1)S(1)} %add_convert_fusion.2), channel_id=1, source_target_pairs={{0,128},{32,160},{64,192},{96,224},{128,0},{160,32},{192,64},{224,... | collective-permute-start | bytes 209096 | tf_op jit(solution)/shard_map/ppermute | solution.py:34
  144.8 10.2 %collective-permute-start.13 = (bf16[34848]{0:T(1024)(128)(2,1)S(1)}, bf16[34848]{0:T(1024)(128)(2,1)S(1)}, u32[]{:S(2)}, u32[]{:S(2)}) collective-permute-start(bf16[34848]{0:T(1024)(128)(2,1)S(1)} %add_convert_fusion.1), channel_id=1, source_target_pairs={{0,64},{32,96},{64,0},{96,32},{128,192},{160,224},{192,128},{224,1... | collective-permute-start | bytes 209096 | tf_op jit(solution)/shard_map/ppermute | solution.py:34
  155.0 7.3 %collective-permute-start.14 = (bf16[34848]{0:T(1024)(128)(2,1)S(1)}, bf16[34848]{0:T(1024)(128)(2,1)S(1)}, u32[]{:S(2)}, u32[]{:S(2)}) collective-permute-start(bf16[34848]{0:T(1024)(128)(2,1)S(1)} %add_convert_fusion), channel_id=1, source_target_pairs={{0,32},{32,0},{64,96},{96,64},{128,160},{160,128},{192,224},{224,1... | collective-permute-start | bytes 209096 | tf_op jit(solution)/shard_map/ppermute | solution.py:34

commit v13 on v12

--- a/solution.py
+++ b/solution.py
@@ -158,6 +158,7 @@
     contract = (((0,), (0,)), ((), ()))
     wleft_part = lax.dot_general(bin_features, grad_left, contract, preferred_element_type=jnp.float32)
     wright_part = lax.dot_general(bin_features, grad_right, contract, preferred_element_type=jnp.float32)
+    wleft_part, wright_part, small = (grad_scale * wleft_part, grad_scale * wright_part, grad_scale * small)
     bit = row_count // 2
     while bit >= 1:
         likes = (wleft_part, wright_part, small)
@@ -168,14 +169,7 @@
         bit //= 2
 
     kernel_sum, point_sum, head_sum = unpacked(small, (kernel_part, point_part, head_part))
-    return (
-        grad_features,
-        grad_scale * wleft_part,
-        grad_scale * wright_part,
-        grad_scale * kernel_sum,
-        grad_scale * point_sum,
-        grad_scale * head_sum,
-    )
+    return (grad_features, wleft_part, wright_part, kernel_sum, point_sum, head_sum)
 
 
 def solution(mesh):

time: 168 us -> 168 us (level)
    slice x6 -> x15, local copies, waits for them, and re-layouts: 0.94 us -> 2.76 us  [unpacked(): out.append(flat[at:at + like.size].reshape(like.shape))]
where the time goes in v13:
time: 168 us; the launch traced here: 166 us
  starting transfers between devices  65.2 us (39%)
  waiting for transfers between devices  35.2 us (21%)
  other arithmetic  31.2 us (19%)
  local copies, waits for them, and re-layouts  17.7 us (11%)
  matrix products  15.7 us (9%)
    ppermute x9, starting transfers between devices, xor_round(): return lax.ppermute(flat, axis, [(i, i ^ bit) for i in range(count)])  33.6 us
    ppermute x9, waiting for transfers between devices, xor_round(): return lax.ppermute(flat, axis, [(i, i ^ bit) for i in range(count)])  30.7 us
    ppermute x4, starting transfers between devices, shifted(): return lax.ppermute(x, axis, pairs)  18.1 us
    add x1, other arithmetic, body(): conv_ext + depth_kernel[3 * a + b][:, None, None] * pair_ext[:, step * a:...  9.35 us
    unnamed x48, local copies, waits for them, and re-layouts  8.19 us
    reduce_sum x1, other arithmetic, body(): kern_terms.append(jnp.sum(conv_grad_tile * window, axis=(1, 2)))  7.48 us
    ppermute x1, starting transfers between devices, body(): right_moved = lax.ppermute(right_part, ('row', 'col'), transpose_pairs())  6.98 us
    reduce_sum x1, other arithmetic, body(): right_part = jnp.sum(backward_pass, axis=1).T  6.96 us
  transfers between devices with their start and end apart: 15, of which 10 were waited for; matrix products, arithmetic and copies ran while one was open for 18% of the time, Pallas kernels for 0%

profile of v13, /device:TPU:6, one launch (start us, length us, event | category | flops | bytes accessed | tf_op | source)
XLA Modules:
  0.0 166.3 jit_solution(2671085206555015872)
XLA Ops:
  0.6 0.9 copy-done
  1.6 0.9 convolution_convert_fusion
  2.8 0.9 convolution_convert_fusion.1
  4.0 0.9 fusion.61
  4.9 6.1 %collective-permute-start = (bf16[12800]{0:T(1024)(128)(2,1)S(1)}, bf16[12800]{0:T(1024)(128)(2,1)S(1)}, u32[]{:S(2)}, u32[]{:S(2)}) collective-permute-start(bf16[12800]{0:T(1024)(128)(2,1)S(1)} %pad_maximum_fusion.4), channel_id=1, source_target_pairs={{0,32},{32,64},{64,96},{96,128},{128,160},{160,192},{192,224},{224... | collective-permute-start | bytes 76808 | tf_op jit(solution)/shard_map/ppermute | solution.py:18
  11.3 7.0 %collective-permute-start.1 = (bf16[12800]{0:T(1024)(128)(2,1)S(1)}, bf16[12800]{0:T(1024)(128)(2,1)S(1)}, u32[]{:S(2)}, u32[]{:S(2)}) collective-permute-start(bf16[12800]{0:T(1024)(128)(2,1)S(1)} %pad_maximum_fusion.5), channel_id=1, source_target_pairs={{32,0},{64,32},{96,64},{128,96},{160,128},{192,160},{224,192},{256... | collective-permute-start | bytes 76808 | tf_op jit(solution)/shard_map/ppermute | solution.py:18
  18.5 1.6 slice_bitcast_fusion.8
  20.1 2.2 %copy.42 = bf16[24,256,128]{1,0,2:T(8,128)(2,1)S(1)} copy(bf16[24,256,128]{2,1,0:T(8,128)(2,1)} %param.13) | data formatting | bytes 3145728 | tf_op args[6]
  22.8 6.5 %collective-permute-start.4 = (bf16[144,32]{0,1:T(8,128)(2,1)S(1)}, bf16[144,32]{0,1:T(8,128)(2,1)S(1)}, u32[]{:S(2)}, u32[]{:S(2)}) collective-permute-start(bf16[144,32]{0,1:T(8,128)(2,1)S(1)} %fusion.44), channel_id=1, source_target_pairs={{0,0},{1,1},{2,32},{3,33},{4,64},{5,65},{6,96},{7,97},{8,128},{9,1... | collective-permute-start | bytes 27656 | tf_op jit(solution)/shard_map/ppermute | solution.py:78
  30.6 0.9 pad_maximum_fusion.2
  31.5 1.3 collective-permute-start.3
  32.8 3.7 %collective-permute-start.2 = (bf16[24,264,4]{1,0,2:T(8,128)(2,1)}, bf16[24,264,4]{1,0,2:T(8,128)(2,1)}, u32[]{:S(2)}, u32[]{:S(2)}) collective-permute-start(bf16[24,264,4]{1,0,2:T(8,128)(2,1)} %get-tuple-element.31), channel_id=1, source_target_pairs={{0,1},{1,2},{2,3},{3,4},{4,5},{5,6},{6,7},{7,8},{8,9},{9,10},{10,1... | collective-permute-start | bytes 152072 | tf_op jit(solution)/shard_map/ppermute | solution.py:18
  36.5 0.7 convert_bitcast_fusion
  37.8 0.9 copy.48
  38.6 2.2 %select_convert_fusion = bf16[32,272,144]{1,0,2:T(8,128)(2,1)S(1)} fusion(f32[32,144]{0,1:T(8,128)S(1)} %copy.48, f32[32,272]{1,0:T(8,128)} %convert_bitcast_fusion, pred[272,144]{0,1:T(8,128)(4,1)S(1)} %and_and_fusion), kind=kLoop, calls=%fused_computation.10 | loop fusion | flops 3760128 | bytes 2599168 | tf_op jit(solution)/shard_map/convert_element_type | solution.py:84
  40.9 9.4 %multiply_add_fusion = f32[32,264,136]{1,0,2:T(8,128)S(1)} fusion(bf16[32,272,144]{1,0,2:T(8,128)(2,1)S(1)} %select_convert_fusion, f32[32]{0:T(128)} %get-tuple-element.54, f32[32]{0:T(128)} %get-tuple-element.55, f32[32]{0:T(128)} %get-tuple-element.48, f32[32]{0:T(128)} %get-tuple-element.49, f32[32]{0:T(128)} %get-tuple-element.50, ...), kind=kLoop, calls=%fused_computation.13 | loop fusion | flops 29872128 | bytes 25277568 | tf_op jit(solution)/shard_map/add | solution.py:91
  50.3 2.8 %copy-done.3 = f32[32,264,136]{1,0,2:T(8,128)} copy-done((f32[32,264,136]{1,0,2:T(8,128)}, f32[32,264,136]{1,0,2:T(8,128)S(1)}, u32[]{:S(2)}) %copy-start.3) | copy-done | bytes 4595736
  53.1 2.6 %multiply_convert_fusion.1 = bf16[32,256,128]{1,0,2:T(8,128)(2,1)} fusion(f32[32,264,136]{1,0,2:T(8,128)S(1)} %multiply_add_fusion), kind=kLoop, calls=%fused_computation.31 | loop fusion | flops 5242880 | bytes 6291456 | tf_op jit(solution)/shard_map/convert_element_type | solution.py:95
  55.6 4.6 %fusion.41 = bf16[32,24]{0,1:T(8,128)(2,1)S(1)} fusion(bf16[24,256,128]{1,0,2:T(8,128)(2,1)S(1)} %copy.42, bf16[32,256,128]{1,0,2:T(8,128)(2,1)} %multiply_convert_fusion.1, bf16[32,272,144]{1,0,2:T(8,128)(2,1)} %copy-done.1, bf16[32,32]{1,0:T(8,128)(2,1)S(1)} %copy-done.18), kind=kOutput, calls=%fused_computation.58 | convolution fusion | flops 120587008 | bytes 5770752 | tf_op jit(solution)/shard_map/ydq,gdq->yg/dot_general | solution.py:125
  60.5 3.5 %fusion.16 = bf16[32,264,136]{1,0,2:T(8,128)(2,1)S(1)} fusion(bf16[24,264,4]{1,0,2:T(8,128)(2,1)} %collective-permute-done.3, bf16[24,4,128]{1,0,2:T(8,128)(2,1)S(1)} %copy.43, bf16[24,256,128]{1,0,2:T(8,128)(2,1)} %copy-done.4, bf16[24,4,128]{1,0,2:T(8,128)(2,1)} %copy-done.5, bf16[24,264,4]{1,0,2:T(8,128)(2,1)} %collective-permute-done.2, ...), kind=kOutput, calls=%fused_computation.32 | convolution fusion | flops 66063360 | bytes 4022784 | tf_op jit(solution)/shard_map/ch,hij->cij/dot_general | solution.py:101
  64.2 3.3 %fusion = bf16[32,264,136]{1,0,2:T(8,128)(2,1)S(1)} fusion(f32[32,264,136]{1,0,2:T(8,128)S(1)} %bitcast.108, bf16[32,264,136]{1,0,2:T(8,128)(2,1)S(1)} %fusion.16, bf16[32,32]{1,0:T(8,128)(2,1)S(1)} %copy-done.19), kind=kOutput, calls=%fused_computation.12 | convolution fusion | flops 83871744 | bytes 9193472 | tf_op jit(solution)/shard_map/co,oij->cij/dot_general | solution.py:103
  67.6 7.0 %fusion.59 = (bf16[32,128]{0,1:T(8,128)(2,1)S(1)}, bf16[32,256]{1,0:T(8,128)(2,1)S(1)}) fusion(bf16[32,264,136]{1,0,2:T(8,128)(2,1)S(1)} %fusion, f32[32]{0:T(128)S(1)} %copy-done.16, f32[32]{0:T(128)S(1)} %copy-done.17, f32[32]{0:T(128)S(1)} %copy-done.10, f32[32]{0:T(128)S(1)} %copy-done.11, f32[32]{0:T(128)S(1)} %copy-done.12, f32[32]{0:T(128)S(1)} %copy-done.13, ...), kind=kLoop, calls=%fused_computation.121 | loop fusion | flops 31444992 | bytes 20997248 | tf_op jit(solution)/shard_map/reduce_sum | solution.py:121
  74.6 7.5 %fusion.15 = (bf16[32]{0:T(256)(128)(2,1)S(1)}, bf16[32]{0:T(256)(128)(2,1)S(1)}, bf16[32]{0:T(256)(128)(2,1)S(1)}, bf16[32]{0:T(256)(128)(2,1)S(1)}, bf16[32]{0...) fusion(bf16[32,272,144]{1,0,2:T(8,128)(2,1)S(1)} %copy-done.2, ...), kind=kLoop, calls=%fused_computation.30 | loop fusion | flops 29359840 | bytes 20972096 | tf_op jit(solution)/shard_map/reduce_sum | solution.py:118
  82.1 7.0 %collective-permute-start.5 = (bf16[128,32]{1,0:T(8,128)(2,1)S(1)}, bf16[128,32]{1,0:T(8,128)(2,1)S(1)}, u32[]{:S(2)}, u32[]{:S(2)}) collective-permute-start(bf16[128,32]{1,0:T(8,128)(2,1)S(1)} %bitcast.114), channel_id=1, source_target_pairs={{0,0},{1,1},{2,32},{3,33},{4,64},{5,65},{6,96},{7,97},{8,128},{9,1... | collective-permute-start | bytes 24584 | tf_op jit(solution)/shard_map/ppermute | solution.py:128
  89.1 1.0 fusion.37
  90.6 4.5 %collective-permute-done.5 = bf16[128,32]{1,0:T(8,128)(2,1)S(1)} collective-permute-done((bf16[128,32]{1,0:T(8,128)(2,1)S(1)}, bf16[128,32]{1,0:T(8,128)(2,1)S(1)}, u32[]{:S(2)}, u32[]{:S(2)}) %collective-permute-start.5) | collective-permute-done | bytes 8224 | tf_op jit(solution)/shard_map/ppermute | solution.py:128
  95.2 3.6 %collective-permute-start.6 = (bf16[14368]{0:T(1024)(128)(2,1)S(1)}, bf16[14368]{0:T(1024)(128)(2,1)S(1)}, u32[]{:S(2)}, u32[]{:S(2)}) collective-permute-start(bf16[14368]{0:T(1024)(128)(2,1)S(1)} %concatenate.52), channel_id=1, source_target_pairs={{0,16},{1,17},{2,18},{3,19},{4,20},{5,21},{6,22},{7,23},{8,24},{9,... | collective-permute-start | bytes 86216 | tf_op jit(solution)/shard_map/ppermute | solution.py:34
  98.9 2.1 %collective-permute-done.6 = bf16[14368]{0:T(1024)(128)(2,1)S(1)} collective-permute-done((bf16[14368]{0:T(1024)(128)(2,1)S(1)}, bf16[14368]{0:T(1024)(128)(2,1)S(1)}, u32[]{:S(2)}, u32[]{:S(2)}) %collective-permute-start.6) | collective-permute-done | bytes 28768 | tf_op jit(solution)/shard_map/ppermute | solution.py:34
  101.0 1.9 %collective-permute-start.7 = (bf16[14368]{0:T(1024)(128)(2,1)S(1)}, bf16[14368]{0:T(1024)(128)(2,1)S(1)}, u32[]{:S(2)}, u32[]{:S(2)}) collective-permute-start(bf16[14368]{0:T(1024)(128)(2,1)S(1)} %add_convert_fusion.6), channel_id=1, source_target_pairs={{0,8},{1,9},{2,10},{3,11},{4,12},{5,13},{6,14},{7,15},{8,0},{9,1},... | collective-permute-start | bytes 86216 | tf_op jit(solution)/shard_map/ppermute | solution.py:34
  103.0 8.0 %collective-permute-done.7 = bf16[14368]{0:T(1024)(128)(2,1)S(1)} collective-permute-done((bf16[14368]{0:T(1024)(128)(2,1)S(1)}, bf16[14368]{0:T(1024)(128)(2,1)S(1)}, u32[]{:S(2)}, u32[]{:S(2)}) %collective-permute-start.7) | collective-permute-done | bytes 28768 | tf_op jit(solution)/shard_map/ppermute | solution.py:34
  111.0 7.6 %collective-permute-start.8 = (bf16[14368]{0:T(1024)(128)(2,1)S(1)}, bf16[14368]{0:T(1024)(128)(2,1)S(1)}, u32[]{:S(2)}, u32[]{:S(2)}) collective-permute-start(bf16[14368]{0:T(1024)(128)(2,1)S(1)} %add_convert_fusion.5), channel_id=1, source_target_pairs={{0,4},{1,5},{2,6},{3,7},{4,0},{5,1},{6,2},{7,3},{8,12},{9,13},{10,... | collective-permute-start | bytes 86216 | tf_op jit(solution)/shard_map/ppermute | solution.py:34
  118.6 1.9 %collective-permute-done.8 = bf16[14368]{0:T(1024)(128)(2,1)S(1)} collective-permute-done((bf16[14368]{0:T(1024)(128)(2,1)S(1)}, bf16[14368]{0:T(1024)(128)(2,1)S(1)}, u32[]{:S(2)}, u32[]{:S(2)}) %collective-permute-start.8) | collective-permute-done | bytes 28768 | tf_op jit(solution)/shard_map/ppermute | solution.py:34
  120.5 4.0 %collective-permute-start.9 = (bf16[14368]{0:T(1024)(128)(2,1)S(1)}, bf16[14368]{0:T(1024)(128)(2,1)S(1)}, u32[]{:S(2)}, u32[]{:S(2)}) collective-permute-start(bf16[14368]{0:T(1024)(128)(2,1)S(1)} %add_convert_fusion.4), channel_id=1, source_target_pairs={{0,2},{1,3},{2,0},{3,1},{4,6},{5,7},{6,4},{7,5},{8,10},{9,11},{10,... | collective-permute-start | bytes 86216 | tf_op jit(solution)/shard_map/ppermute | solution.py:34
  124.4 1.9 %collective-permute-done.9 = bf16[14368]{0:T(1024)(128)(2,1)S(1)} collective-permute-done((bf16[14368]{0:T(1024)(128)(2,1)S(1)}, bf16[14368]{0:T(1024)(128)(2,1)S(1)}, u32[]{:S(2)}, u32[]{:S(2)}) %collective-permute-start.9) | collective-permute-done | bytes 28768 | tf_op jit(solution)/shard_map/ppermute | solution.py:34
  126.3 1.9 %collective-permute-start.10 = (bf16[14368]{0:T(1024)(128)(2,1)S(1)}, bf16[14368]{0:T(1024)(128)(2,1)S(1)}, u32[]{:S(2)}, u32[]{:S(2)}) collective-permute-start(bf16[14368]{0:T(1024)(128)(2,1)S(1)} %get-tuple-element.30), channel_id=1, source_target_pairs={{0,1},{1,0},{2,3},{3,2},{4,5},{5,4},{6,7},{7,6},{8,9},{9,8},{10,11... | collective-permute-start | bytes 86216 | tf_op jit(solution)/shard_map/ppermute | solution.py:34
  128.2 1.2 collective-permute-done.10
  130.8 3.1 %collective-permute-start.11 = (bf16[34848]{0:T(1024)(128)(2,1)S(1)}, bf16[34848]{0:T(1024)(128)(2,1)S(1)}, u32[]{:S(2)}, u32[]{:S(2)}) collective-permute-start(bf16[34848]{0:T(1024)(128)(2,1)S(1)} %pad_maximum_fusion.3), channel_id=1, source_target_pairs={{0,256},{32,288},{64,320},{96,352},{128,384},{160,416},{192,448},{... | collective-permute-start | bytes 209096 | tf_op jit(solution)/shard_map/ppermute | solution.py:34
  133.9 4.6 %collective-permute-done.11 = bf16[34848]{0:T(1024)(128)(2,1)S(1)} collective-permute-done((bf16[34848]{0:T(1024)(128)(2,1)S(1)}, bf16[34848]{0:T(1024)(128)(2,1)S(1)}, u32[]{:S(2)}, u32[]{:S(2)}) %collective-permute-start.11) | collective-permute-done | bytes 69728 | tf_op jit(solution)/shard_map/ppermute | solution.py:34
  138.5 1.9 %collective-permute-start.12 = (bf16[34848]{0:T(1024)(128)(2,1)S(1)}, bf16[34848]{0:T(1024)(128)(2,1)S(1)}, u32[]{:S(2)}, u32[]{:S(2)}) collective-permute-start(bf16[34848]{0:T(1024)(128)(2,1)S(1)} %add_convert_fusion.2), channel_id=1, source_target_pairs={{0,128},{32,160},{64,192},{96,224},{128,0},{160,32},{192,64},{224,... | collective-permute-start | bytes 209096 | tf_op jit(solution)/shard_map/ppermute | solution.py:34
  140.5 4.3 %collective-permute-done.12 = bf16[34848]{0:T(1024)(128)(2,1)S(1)} collective-permute-done((bf16[34848]{0:T(1024)(128)(2,1)S(1)}, bf16[34848]{0:T(1024)(128)(2,1)S(1)}, u32[]{:S(2)}, u32[]{:S(2)}) %collective-permute-start.12) | collective-permute-done | bytes 69728 | tf_op jit(solution)/shard_map/ppermute | solution.py:34
  144.8 4.6 %collective-permute-start.13 = (bf16[34848]{0:T(1024)(128)(2,1)S(1)}, bf16[34848]{0:T(1024)(128)(2,1)S(1)}, u32[]{:S(2)}, u32[]{:S(2)}) collective-permute-start(bf16[34848]{0:T(1024)(128)(2,1)S(1)} %add_convert_fusion.1), channel_id=1, source_target_pairs={{0,64},{32,96},{64,0},{96,32},{128,192},{160,224},{192,128},{224,1... | collective-permute-start | bytes 209096 | tf_op jit(solution)/shard_map/ppermute | solution.py:34
  149.6 5.4 %collective-permute-done.13 = bf16[34848]{0:T(1024)(128)(2,1)S(1)} collective-permute-done((bf16[34848]{0:T(1024)(128)(2,1)S(1)}, bf16[34848]{0:T(1024)(128)(2,1)S(1)}, u32[]{:S(2)}, u32[]{:S(2)}) %collective-permute-start.13) | collective-permute-done | bytes 69728 | tf_op jit(solution)/shard_map/ppermute | solution.py:34
  155.0 5.0 %collective-permute-start.14 = (bf16[34848]{0:T(1024)(128)(2,1)S(1)}, bf16[34848]{0:T(1024)(128)(2,1)S(1)}, u32[]{:S(2)}, u32[]{:S(2)}) collective-permute-start(bf16[34848]{0:T(1024)(128)(2,1)S(1)} %add_convert_fusion), channel_id=1, source_target_pairs={{0,32},{32,0},{64,96},{96,64},{128,160},{160,128},{192,224},{224,1... | collective-permute-start | bytes 209096 | tf_op jit(solution)/shard_map/ppermute | solution.py:34
  160.0 1.0 fusion.29
  161.0 1.3 collective-permute-done.14
  162.6 0.7 copy.57
  163.5 0.7 copy.58
  164.9 0.7 slice.427
  (122 shorter events, 7.9 us)
Async XLA Ops:
  0.6 1.0 copy-start
  4.9 17.4 %collective-permute-start = (bf16[12800]{0:T(1024)(128)(2,1)S(1)}, bf16[12800]{0:T(1024)(128)(2,1)S(1)}, u32[]{:S(2)}, u32[]{:S(2)}) collective-permute-start(bf16[12800]{0:T(1024)(128)(2,1)S(1)} %pad_maximum_fusion.4), channel_id=1, source_target_pairs={{0,32},{32,64},{64,96},{96,128},{128,160},{160,192},{192,224},{224... | collective-permute-start | bytes 76808 | tf_op jit(solution)/shard_map/ppermute | solution.py:18
  11.3 11.2 %collective-permute-start.1 = (bf16[12800]{0:T(1024)(128)(2,1)S(1)}, bf16[12800]{0:T(1024)(128)(2,1)S(1)}, u32[]{:S(2)}, u32[]{:S(2)}) collective-permute-start(bf16[12800]{0:T(1024)(128)(2,1)S(1)} %pad_maximum_fusion.5), channel_id=1, source_target_pairs={{32,0},{64,32},{96,64},{128,96},{160,128},{192,160},{224,192},{256... | collective-permute-start | bytes 76808 | tf_op jit(solution)/shard_map/ppermute | solution.py:18
  22.3 33.4 %copy-start.4 = (bf16[24,256,128]{1,0,2:T(8,128)(2,1)}, bf16[24,256,128]{1,0,2:T(8,128)(2,1)S(1)}, u32[]{:S(2)}) copy-start(bf16[24,256,128]{1,0,2:T(8,128)(2,1)S(1)} %copy.42) | copy-start | bytes 4718596
  22.8 14.4 %collective-permute-start.4 = (bf16[144,32]{0,1:T(8,128)(2,1)S(1)}, bf16[144,32]{0,1:T(8,128)(2,1)S(1)}, u32[]{:S(2)}, u32[]{:S(2)}) collective-permute-start(bf16[144,32]{0,1:T(8,128)(2,1)S(1)} %fusion.44), channel_id=1, source_target_pairs={{0,0},{1,1},{2,32},{3,33},{4,64},{5,65},{6,96},{7,97},{8,128},{9,1... | collective-permute-start | bytes 27656 | tf_op jit(solution)/shard_map/ppermute | solution.py:78
  30.6 19.7 %copy-start.5 = (bf16[24,4,128]{1,0,2:T(8,128)(2,1)}, bf16[24,4,128]{1,0,2:T(8,128)(2,1)S(1)}, u32[]{:S(2)}) copy-start(bf16[24,4,128]{1,0,2:T(8,128)(2,1)S(1)} %copy.41) | copy-start | bytes 73732
  31.5 29.0 %collective-permute-start.3 = (bf16[24,264,4]{1,0,2:T(8,128)(2,1)}, bf16[24,264,4]{1,0,2:T(8,128)(2,1)}, u32[]{:S(2)}, u32[]{:S(2)}) collective-permute-start(bf16[24,264,4]{1,0,2:T(8,128)(2,1)} %get-tuple-element.32), channel_id=1, source_target_pairs={{1,0},{2,1},{3,2},{4,3},{5,4},{6,5},{7,6},{8,7},{9,8},{10,9},{11,1... | collective-permute-start | bytes 152072 | tf_op jit(solution)/shard_map/ppermute | solution.py:18
  32.8 27.7 %collective-permute-start.2 = (bf16[24,264,4]{1,0,2:T(8,128)(2,1)}, bf16[24,264,4]{1,0,2:T(8,128)(2,1)}, u32[]{:S(2)}, u32[]{:S(2)}) collective-permute-start(bf16[24,264,4]{1,0,2:T(8,128)(2,1)} %get-tuple-element.31), channel_id=1, source_target_pairs={{0,1},{1,2},{2,3},{3,4},{4,5},{5,6},{6,7},{7,8},{8,9},{9,10},{10,1... | collective-permute-start | bytes 152072 | tf_op jit(solution)/shard_map/ppermute | solution.py:18
  40.9 9.4 %copy-start.1 = (bf16[32,272,144]{1,0,2:T(8,128)(2,1)}, bf16[32,272,144]{1,0,2:T(8,128)(2,1)S(1)}, u32[]{:S(2)}) copy-start(bf16[32,272,144]{1,0,2:T(8,128)(2,1)S(1)} %select_convert_fusion) | copy-start | bytes 7520260
  50.3 2.8 %copy-start.3 = (f32[32,264,136]{1,0,2:T(8,128)}, f32[32,264,136]{1,0,2:T(8,128)S(1)}, u32[]{:S(2)}) copy-start(f32[32,264,136]{1,0,2:T(8,128)S(1)} %multiply_add_fusion) | copy-start | bytes 13787140
  53.1 2.6 %copy-start.18 = (bf16[32,32]{1,0:T(8,128)(2,1)S(1)}, bf16[32,32]{1,0:T(8,128)(2,1)}, u32[]{:S(2)}) copy-start(bf16[32,32]{1,0:T(8,128)(2,1)} %param.11) | copy-start | bytes 6148
  60.3 3.7 %slice-start = ((s8[6684672]{0:T(1024)(128)(4,1)}), s8[2490368]{0:T(1024)(128)(4,1)S(1)}, s32[]{:S(2)}) async-start(s8[6684672]{0:T(1024)(128)(4,1)} %bitcast.107), calls=%async_computation | async-start | bytes 4980736
  60.4 3.7 %slice-start.1 = ((s8[6684672]{0:T(1024)(128)(4,1)}), s8[4194304]{0:T(1024)(128)(4,1)S(1)}, s32[]{:S(2)}) async-start(s8[6684672]{0:T(1024)(128)(4,1)} %bitcast.107), calls=%async_computation.1 | async-start | bytes 8388608
  60.5 3.6 %copy-start.19 = (bf16[32,32]{1,0:T(8,128)(2,1)S(1)}, bf16[32,32]{1,0:T(8,128)(2,1)}, u32[]{:S(2)}) copy-start(bf16[32,32]{1,0:T(8,128)(2,1)} %param.11) | copy-start | bytes 6148
  64.1 3.4 %copy-start.9 = (f32[32]{0:T(128)S(1)}, f32[32]{0:T(128)}, u32[]{:S(2)}) copy-start(f32[32]{0:T(128)} %get-tuple-element.47) | copy-start | bytes 388
  64.1 3.4 %copy-start.10 = (f32[32]{0:T(128)S(1)}, f32[32]{0:T(128)}, u32[]{:S(2)}) copy-start(f32[32]{0:T(128)} %get-tuple-element.48) | copy-start | bytes 388
  64.1 3.4 %copy-start.11 = (f32[32]{0:T(128)S(1)}, f32[32]{0:T(128)}, u32[]{:S(2)}) copy-start(f32[32]{0:T(128)} %get-tuple-element.49) | copy-start | bytes 388
  64.1 3.4 %copy-start.12 = (f32[32]{0:T(128)S(1)}, f32[32]{0:T(128)}, u32[]{:S(2)}) copy-start(f32[32]{0:T(128)} %get-tuple-element.50) | copy-start | bytes 388
  64.1 3.4 %copy-start.13 = (f32[32]{0:T(128)S(1)}, f32[32]{0:T(128)}, u32[]{:S(2)}) copy-start(f32[32]{0:T(128)} %get-tuple-element.51) | copy-start | bytes 388
  64.1 3.4 %copy-start.14 = (f32[32]{0:T(128)S(1)}, f32[32]{0:T(128)}, u32[]{:S(2)}) copy-start(f32[32]{0:T(128)} %get-tuple-element.52) | copy-start | bytes 388
  64.1 3.4 %copy-start.15 = (f32[32]{0:T(128)S(1)}, f32[32]{0:T(128)}, u32[]{:S(2)}) copy-start(f32[32]{0:T(128)} %get-tuple-element.53) | copy-start | bytes 388
  64.2 3.4 %copy-start.16 = (f32[32]{0:T(128)S(1)}, f32[32]{0:T(128)}, u32[]{:S(2)}) copy-start(f32[32]{0:T(128)} %get-tuple-element.54) | copy-start | bytes 388
  64.2 3.4 %copy-start.17 = (f32[32]{0:T(128)S(1)}, f32[32]{0:T(128)}, u32[]{:S(2)}) copy-start(f32[32]{0:T(128)} %get-tuple-element.55) | copy-start | bytes 388
  67.6 7.0 %copy-start.2 = (bf16[32,272,144]{1,0,2:T(8,128)(2,1)S(1)}, bf16[32,272,144]{1,0,2:T(8,128)(2,1)}, u32[]{:S(2)}) copy-start(bf16[32,272,144]{1,0,2:T(8,128)(2,1)} %copy-done.1) | copy-start | bytes 7520260
  74.5 14.5 %copy-start.6 = (bf16[32,256,128]{1,0,2:T(8,128)(2,1)S(1)}, bf16[32,256,128]{1,0,2:T(8,128)(2,1)}, u32[]{:S(2)}) copy-start(bf16[32,256,128]{1,0,2:T(8,128)(2,1)} %multiply_convert_fusion.1) | copy-start | bytes 6291460
  82.0 67.3 %copy-start.7 = (bf16[512,32]{0,1:T(8,128)(2,1)S(1)}, bf16[512,32]{0,1:T(8,128)(2,1)}, u32[]{:S(2)}) copy-start(bf16[512,32]{0,1:T(8,128)(2,1)} %param.8) | copy-start | bytes 98308
  82.1 77.9 %copy-start.8 = (bf16[512,32]{0,1:T(8,128)(2,1)S(1)}, bf16[512,32]{0,1:T(8,128)(2,1)}, u32[]{:S(2)}) copy-start(bf16[512,32]{0,1:T(8,128)(2,1)} %param.9) | copy-start | bytes 98308
  82.1 13.0 %collective-permute-start.5 = (bf16[128,32]{1,0:T(8,128)(2,1)S(1)}, bf16[128,32]{1,0:T(8,128)(2,1)S(1)}, u32[]{:S(2)}, u32[]{:S(2)}) collective-permute-start(bf16[128,32]{1,0:T(8,128)(2,1)S(1)} %bitcast.114), channel_id=1, source_target_pairs={{0,0},{1,1},{2,32},{3,33},{4,64},{5,65},{6,96},{7,97},{8,128},{9,1... | collective-permute-start | bytes 24584 | tf_op jit(solution)/shard_map/ppermute | solution.py:128
  95.2 5.8 %collective-permute-start.6 = (bf16[14368]{0:T(1024)(128)(2,1)S(1)}, bf16[14368]{0:T(1024)(128)(2,1)S(1)}, u32[]{:S(2)}, u32[]{:S(2)}) collective-permute-start(bf16[14368]{0:T(1024)(128)(2,1)S(1)} %concatenate.52), channel_id=1, source_target_pairs={{0,16},{1,17},{2,18},{3,19},{4,20},{5,21},{6,22},{7,23},{8,24},{9,... | collective-permute-start | bytes 86216 | tf_op jit(solution)/shard_map/ppermute | solution.py:34
  101.0 9.9 %collective-permute-start.7 = (bf16[14368]{0:T(1024)(128)(2,1)S(1)}, bf16[14368]{0:T(1024)(128)(2,1)S(1)}, u32[]{:S(2)}, u32[]{:S(2)}) collective-permute-start(bf16[14368]{0:T(1024)(128)(2,1)S(1)} %add_convert_fusion.6), channel_id=1, source_target_pairs={{0,8},{1,9},{2,10},{3,11},{4,12},{5,13},{6,14},{7,15},{8,0},{9,1},... | collective-permute-start | bytes 86216 | tf_op jit(solution)/shard_map/ppermute | solution.py:34
  111.0 9.5 %collective-permute-start.8 = (bf16[14368]{0:T(1024)(128)(2,1)S(1)}, bf16[14368]{0:T(1024)(128)(2,1)S(1)}, u32[]{:S(2)}, u32[]{:S(2)}) collective-permute-start(bf16[14368]{0:T(1024)(128)(2,1)S(1)} %add_convert_fusion.5), channel_id=1, source_target_pairs={{0,4},{1,5},{2,6},{3,7},{4,0},{5,1},{6,2},{7,3},{8,12},{9,13},{10,... | collective-permute-start | bytes 86216 | tf_op jit(solution)/shard_map/ppermute | solution.py:34
  120.5 5.8 %collective-permute-start.9 = (bf16[14368]{0:T(1024)(128)(2,1)S(1)}, bf16[14368]{0:T(1024)(128)(2,1)S(1)}, u32[]{:S(2)}, u32[]{:S(2)}) collective-permute-start(bf16[14368]{0:T(1024)(128)(2,1)S(1)} %add_convert_fusion.4), channel_id=1, source_target_pairs={{0,2},{1,3},{2,0},{3,1},{4,6},{5,7},{6,4},{7,5},{8,10},{9,11},{10,... | collective-permute-start | bytes 86216 | tf_op jit(solution)/shard_map/ppermute | solution.py:34
  126.3 3.1 %collective-permute-start.10 = (bf16[14368]{0:T(1024)(128)(2,1)S(1)}, bf16[14368]{0:T(1024)(128)(2,1)S(1)}, u32[]{:S(2)}, u32[]{:S(2)}) collective-permute-start(bf16[14368]{0:T(1024)(128)(2,1)S(1)} %get-tuple-element.30), channel_id=1, source_target_pairs={{0,1},{1,0},{2,3},{3,2},{4,5},{5,4},{6,7},{7,6},{8,9},{9,8},{10,11... | collective-permute-start | bytes 86216 | tf_op jit(solution)/shard_map/ppermute | solution.py:34
  130.8 7.7 %collective-permute-start.11 = (bf16[34848]{0:T(1024)(128)(2,1)S(1)}, bf16[34848]{0:T(1024)(128)(2,1)S(1)}, u32[]{:S(2)}, u32[]{:S(2)}) collective-permute-start(bf16[34848]{0:T(1024)(128)(2,1)S(1)} %pad_maximum_fusion.3), channel_id=1, source_target_pairs={{0,256},{32,288},{64,320},{96,352},{128,384},{160,416},{192,448},{... | collective-permute-start | bytes 209096 | tf_op jit(solution)/shard_map/ppermute | solution.py:34
  138.5 6.2 %collective-permute-start.12 = (bf16[34848]{0:T(1024)(128)(2,1)S(1)}, bf16[34848]{0:T(1024)(128)(2,1)S(1)}, u32[]{:S(2)}, u32[]{:S(2)}) collective-permute-start(bf16[34848]{0:T(1024)(128)(2,1)S(1)} %add_convert_fusion.2), channel_id=1, source_target_pairs={{0,128},{32,160},{64,192},{96,224},{128,0},{160,32},{192,64},{224,... | collective-permute-start | bytes 209096 | tf_op jit(solution)/shard_map/ppermute | solution.py:34
  144.8 10.2 %collective-permute-start.13 = (bf16[34848]{0:T(1024)(128)(2,1)S(1)}, bf16[34848]{0:T(1024)(128)(2,1)S(1)}, u32[]{:S(2)}, u32[]{:S(2)}) collective-permute-start(bf16[34848]{0:T(1024)(128)(2,1)S(1)} %add_convert_fusion.1), channel_id=1, source_target_pairs={{0,64},{32,96},{64,0},{96,32},{128,192},{160,224},{192,128},{224,1... | collective-permute-start | bytes 209096 | tf_op jit(solution)/shard_map/ppermute | solution.py:34
  155.0 7.3 %collective-permute-start.14 = (bf16[34848]{0:T(1024)(128)(2,1)S(1)}, bf16[34848]{0:T(1024)(128)(2,1)S(1)}, u32[]{:S(2)}, u32[]{:S(2)}) collective-permute-start(bf16[34848]{0:T(1024)(128)(2,1)S(1)} %add_convert_fusion), channel_id=1, source_target_pairs={{0,32},{32,0},{64,96},{96,64},{128,160},{160,128},{192,224},{224,1... | collective-permute-start | bytes 209096 | tf_op jit(solution)/shard_map/ppermute | solution.py:34
